TPU v7x, 32 devices: a whole 2x2x4 slice. The times are simulated.
32 devices in a mesh: wide: 8 (over z, y), narrow: 4 (over x, core).
Axes of the slice: x: 2, y: 2, z: 4, core: 2. Of those that a mesh axis runs over, the one named last changes fastest.
Arguments:
- clips: bfloat16 [128, 16, 64, 768], P(('wide', 'narrow')), may hold values from -6 to 6
- t_emb: bfloat16 [128, 2, 768], P(('wide', 'narrow')), may hold values from -6 to 6
- lengths: int32 [128], P('wide'), may hold values from 1 to 16, as said below
- task: int32 [128, 16], P('wide'), may hold values 0 or 1
- w_mod: bfloat16 [768, 6912], P(('wide', 'narrow')), may hold values from -0.21875 to 0.21875
- b_mod: bfloat16 [6912], P(('wide', 'narrow')), may hold values from -3 to 3
- w_qkv_s: bfloat16 [768, 2304], P(('wide', 'narrow')), may hold values from -0.21875 to 0.21875
- w_o_s: bfloat16 [768, 768], P(('wide', 'narrow')), may hold values from -0.625 to 0.625
- b_o_s: bfloat16 [768], P(('wide', 'narrow')), may hold values from -3 to 3
- w_qkv_t: bfloat16 [768, 2304], P(('wide', 'narrow')), may hold values from -0.21875 to 0.21875
- w_o_t: bfloat16 [768, 768], P(('wide', 'narrow')), may hold values from -0.375 to 0.375
- b_o_t: bfloat16 [768], P(('wide', 'narrow')), may hold values from -3 to 3
- w_in: bfloat16 [768, 3072], P(('wide', 'narrow')), may hold values from -0.21875 to 0.21875
- b_in: bfloat16 [3072], P(('wide', 'narrow')), may hold values from -3 to 3
- w_out: bfloat16 [3072, 768], P(('wide', 'narrow')), may hold values from -0.109375 to 0.109375
- b_out: bfloat16 [768], P(('wide', 'narrow')), may hold values from -3 to 3
- cotangent: bfloat16 [128, 16, 64, 768], P(('wide', 'narrow')), may hold values from -6 to 6
Outputs:
- layer_out: bfloat16 [128, 16, 64, 768], P(('wide', 'narrow'))
- grad_clips: bfloat16 [128, 16, 64, 768], P(('wide', 'narrow'))
- grad_t_emb: bfloat16 [128, 2, 768], P(('wide', 'narrow'))
- grad_w_mod: float32 [768, 6912], P(('wide', 'narrow'))
- grad_b_mod: float32 [6912], P(('wide', 'narrow'))
- grad_w_qkv_s: float32 [768, 2304], P(('wide', 'narrow'))
- grad_w_o_s: float32 [768, 768], P(('wide', 'narrow'))
- grad_b_o_s: float32 [768], P(('wide', 'narrow'))
- grad_w_qkv_t: float32 [768, 2304], P(('wide', 'narrow'))
- grad_w_o_t: float32 [768, 768], P(('wide', 'narrow'))
- grad_b_o_t: float32 [768], P(('wide', 'narrow'))
- grad_w_in: float32 [768, 3072], P(('wide', 'narrow'))
- grad_b_in: float32 [3072], P(('wide', 'narrow'))
- grad_w_out: float32 [3072, 768], P(('wide', 'narrow'))
- grad_b_out: float32 [768], P(('wide', 'narrow'))
Inputs may be any that keep to these rules, and one draw needn't show every extreme that they name: `lengths`: write clip i as g * 4 * 4 + s * 4 + c with s, c below 4. For every g and every k, the clips with (s + c) % 4 == k hold exactly 32 live frames together.
All inputs are finite; a program needn't handle non-finite values. No bound on the sum of `task` on one device may be relied on, other than what follows from the above.
Results may differ from a plain program's by a relative error of at most 0.025.
The roundings to bfloat16 on the way count: a program that leaves them out, or rounds other values in their place, can miss the bound.
Values may be sent and summed in bfloat16 or wider, within the bound.
A program may use at most 384 MiB of HBM per device.

v0:
```python
import jax
import jax.numpy as jnp
from jax import lax
from jax.sharding import PartitionSpec as P

D = 768
HEADS = 12
HEAD = 64
FR = 16
PATCHES = 64


norm_eps = 1e-06
precise = lax.Precision.HIGHEST
frame_forms = (
    "fphc,fqhc->fhpq",
    "fhpq,fqhc->fphc",
    "fhpq,fqhc->fphc",
    "fhpq,fphc->fqhc",
    "fhpq,fphc->fqhc",
    "fphc,fqhc->fhpq",
)
time_forms = (
    "fphc,gphc->phfg",
    "phfg,gphc->fphc",
    "phfg,gphc->fphc",
    "phfg,fphc->gphc",
    "phfg,fphc->gphc",
    "fphc,gphc->phfg",
)


def layer_norm(values):
    mean_value = jnp.mean(values, axis=-1, keepdims=True)
    centred = values - mean_value
    variance = jnp.mean(centred * centred, axis=-1, keepdims=True)
    return centred * lax.rsqrt(variance + norm_eps)


def silu_fn(values):
    return values * jax.nn.sigmoid(values)


def gelu_fn(values):
    return jax.nn.gelu(values, approximate=True)


def modulate(values, shift, scale):
    return layer_norm(values) * (1.0 + scale[:, None, :]) + shift[:, None, :]


def product(matrix_a, matrix_b):
    return jnp.dot(matrix_a, matrix_b, preferred_element_type=jnp.float32)


def product_tn(matrix_a, matrix_b):
    return lax.dot_general(
        matrix_a, matrix_b, (((0,), (0,)), ((), ())), preferred_element_type=jnp.float32
    )


def product_nt(matrix_a, matrix_b):
    return lax.dot_general(
        matrix_a, matrix_b, (((1,), (1,)), ((), ())), preferred_element_type=jnp.float32
    )


def heads_of(qkv_rows):
    split = qkv_rows.reshape(-1, PATCHES, 3, HEADS, HEAD)
    return (split[:, :, 0], split[:, :, 1], split[:, :, 2])


def masked_scores(forms, queries, key_part, mask):
    scores = jnp.einsum(forms[0], queries, key_part, preferred_element_type=jnp.float32) * HEAD ** (
        -0.5
    )
    return jnp.where(mask, scores, -1e30)


def attend_forward(h_low, w_qkv, w_proj, b_proj, forms, mask):
    qkv_rows = product(h_low.reshape(-1, D), w_qkv).astype(jnp.bfloat16)
    queries, key_part, value_part = heads_of(qkv_rows)
    scores = masked_scores(forms, queries, key_part, mask)
    row_top = jnp.max(scores, axis=-1, keepdims=True)
    exp_terms = jnp.exp(scores - row_top)
    totals = jnp.sum(exp_terms, axis=-1, keepdims=True)
    probabilities = (exp_terms / totals).astype(jnp.bfloat16)
    mixture = jnp.einsum(forms[1], probabilities, value_part, preferred_element_type=jnp.float32)
    mixture = mixture.astype(jnp.bfloat16).reshape(-1, D)
    branch = product(mixture, w_proj) + b_proj.astype(jnp.float32)
    return (branch.reshape(h_low.shape), (qkv_rows, row_top + jnp.log(totals), mixture))


def attend_backward(h_low, grad_branch, kept, w_qkv, w_proj, forms, mask):
    qkv_rows, log_total, mixture = kept
    queries, key_part, value_part = heads_of(qkv_rows)
    grad_proj = product_tn(mixture, grad_branch)
    grad_bias = jnp.sum(grad_branch.astype(jnp.float32), axis=0)
    grad_mixture = (
        product_nt(grad_branch, w_proj).astype(jnp.bfloat16).reshape(-1, PATCHES, HEADS, HEAD)
    )
    probabilities = jnp.exp(masked_scores(forms, queries, key_part, mask) - log_total)
    grad_probs = jnp.einsum(forms[5], grad_mixture, value_part, preferred_element_type=jnp.float32)
    grad_scores = probabilities * (
        grad_probs - jnp.sum(probabilities * grad_probs, axis=-1, keepdims=True)
    )
    grad_scores = grad_scores.astype(jnp.bfloat16)
    grad_query = jnp.einsum(
        forms[2], grad_scores, key_part, preferred_element_type=jnp.float32
    ) * HEAD ** (-0.5)
    grad_key = jnp.einsum(
        forms[3], grad_scores, queries, preferred_element_type=jnp.float32
    ) * HEAD ** (-0.5)
    grad_value = jnp.einsum(
        forms[4],
        probabilities.astype(jnp.bfloat16),
        grad_mixture,
        preferred_element_type=jnp.float32,
    )
    grad_qkv = (
        jnp.stack([grad_query, grad_key, grad_value], axis=2)
        .reshape(-1, 3 * D)
        .astype(jnp.bfloat16)
    )
    grad_w_qkv = product_tn(h_low.reshape(-1, D), grad_qkv)
    grad_h = product_nt(grad_qkv, w_qkv).reshape(h_low.shape)
    return (grad_h, grad_w_qkv, grad_proj, grad_bias)


def local(
    clips,
    t_emb,
    lengths,
    task,
    w_mod,
    b_mod,
    w_qkv_s,
    w_o_s,
    b_o_s,
    w_qkv_t,
    w_o_t,
    b_o_t,
    w_in,
    b_in,
    w_out,
    b_out,
    cotangent,
):
    gathered = (
        lax.all_gather(w_mod, ("wide", "narrow"), axis=0, tiled=True),
        lax.all_gather(b_mod, ("wide", "narrow"), axis=0, tiled=True),
        lax.all_gather(w_qkv_s, ("wide", "narrow"), axis=0, tiled=True),
        lax.all_gather(w_o_s, ("wide", "narrow"), axis=0, tiled=True),
        lax.all_gather(b_o_s, ("wide", "narrow"), axis=0, tiled=True),
        lax.all_gather(w_qkv_t, ("wide", "narrow"), axis=0, tiled=True),
        lax.all_gather(w_o_t, ("wide", "narrow"), axis=0, tiled=True),
        lax.all_gather(b_o_t, ("wide", "narrow"), axis=0, tiled=True),
        lax.all_gather(w_in, ("wide", "narrow"), axis=0, tiled=True),
        lax.all_gather(b_in, ("wide", "narrow"), axis=0, tiled=True),
        lax.all_gather(w_out, ("wide", "narrow"), axis=0, tiled=True),
        lax.all_gather(b_out, ("wide", "narrow"), axis=0, tiled=True),
    )
    (
        mod_weight,
        mod_bias,
        frame_qkv,
        frame_proj,
        frame_bias,
        time_qkv,
        time_proj,
        time_bias,
        mlp_in,
        mlp_in_bias,
        mlp_out,
        mlp_out_bias,
    ) = gathered
    group_size = lax.axis_size("narrow")
    my_rank = lax.axis_index("narrow")
    slot_ids = jnp.arange(group_size, dtype=jnp.int32)
    send_order = (slot_ids - my_rank) % group_size
    back_order = (slot_ids + my_rank) % group_size
    from_clip = (my_rank - slot_ids) % group_size
    group_len = lengths.reshape(group_size, group_size)
    group_task = task.reshape(group_size, group_size, FR)
    recv_len = jnp.take_along_axis(group_len, from_clip[:, None], axis=1)[:, 0]
    recv_task = jnp.take_along_axis(group_task, from_clip[:, None, None], axis=1)[:, 0]
    len_ends = jnp.cumsum(recv_len)
    len_starts = len_ends - recv_len
    packed_ids = jnp.arange(2 * FR, dtype=jnp.int32)
    source = jnp.sum((len_ends[None, :] <= packed_ids[:, None]).astype(jnp.int32), axis=1)
    within = packed_ids - len_starts[source]
    pack_rows = source * FR + within
    row_choice = source * 2 + recv_task[source, within]
    chooser = (row_choice[:, None] == jnp.arange(2 * group_size, dtype=jnp.int32)[None, :]).astype(
        jnp.float32
    )
    segment_mask = (source[:, None] == source[None, :])[None, None]
    all_true = jnp.ones((1, 1, 1, 1), dtype=jnp.bool_)
    frame_ids = jnp.arange(FR, dtype=jnp.int32)
    live_back = frame_ids[None, :] < recv_len[:, None]
    unpack_rows = jnp.where(live_back, len_starts[:, None] + frame_ids[None, :], 0).reshape(-1)

    def pack_frames(received):
        return jnp.take(received.reshape(group_size * FR, PATCHES, D), pack_rows, axis=0)

    def unpack_frames(packed):
        spread = jnp.take(packed, unpack_rows, axis=0).reshape(group_size, FR, PATCHES, D)
        return jnp.where(live_back[:, :, None, None], spread, jnp.zeros((), packed.dtype))

    send_clips = jnp.take(clips, send_order, axis=0)
    send_emb = jnp.take(t_emb, send_order, axis=0)
    recv_clips, recv_emb = (
        lax.all_to_all(send_clips, "narrow", split_axis=0, concat_axis=0, tiled=True),
        lax.all_to_all(send_emb, "narrow", split_axis=0, concat_axis=0, tiled=True),
    )
    x_zero = pack_frames(recv_clips).astype(jnp.float32)
    emb_flat = recv_emb.astype(jnp.float32).reshape(2 * group_size, D)
    silu_value, silu_back = jax.vjp(silu_fn, emb_flat)
    silu_low = silu_value.astype(jnp.bfloat16)
    mod_rows = product(silu_low, mod_weight) + mod_bias.astype(jnp.float32)
    mod_frames = jnp.dot(chooser, mod_rows, precision=precise)
    pieces = [mod_frames[:, i * D : (i + 1) * D] for i in range(9)]
    h_one, norm_back_one = jax.vjp(modulate, x_zero, pieces[0], pieces[1])
    h_one_low = h_one.astype(jnp.bfloat16)
    branch_one, kept_one = attend_forward(
        h_one_low, frame_qkv, frame_proj, frame_bias, frame_forms, all_true
    )
    x_one = x_zero + pieces[2][:, None, :] * branch_one
    h_two, norm_back_two = jax.vjp(modulate, x_one, pieces[3], pieces[4])
    h_two_low = h_two.astype(jnp.bfloat16)
    branch_two, kept_two = attend_forward(
        h_two_low, time_qkv, time_proj, time_bias, time_forms, segment_mask
    )
    x_two = x_one + pieces[5][:, None, :] * branch_two
    h_three, norm_back_three = jax.vjp(modulate, x_two, pieces[6], pieces[7])
    h_three_low = h_three.astype(jnp.bfloat16)
    hidden = product(h_three_low.reshape(-1, D), mlp_in) + mlp_in_bias.astype(jnp.float32)
    active, gelu_back = jax.vjp(gelu_fn, hidden)
    active_low = active.astype(jnp.bfloat16)
    branch_three = (product(active_low, mlp_out) + mlp_out_bias.astype(jnp.float32)).reshape(
        x_two.shape
    )
    result = x_two + pieces[8][:, None, :] * branch_three
    send_result = unpack_frames(result.astype(jnp.bfloat16))
    back_result = lax.all_to_all(send_result, "narrow", split_axis=0, concat_axis=0, tiled=True)
    layer_out = jnp.take(back_result, back_order, axis=0)
    recv_grad = lax.all_to_all(
        jnp.take(cotangent, send_order, axis=0), "narrow", split_axis=0, concat_axis=0, tiled=True
    )
    grad_out = pack_frames(recv_grad).astype(jnp.float32)
    grad_gate_three = jnp.sum(grad_out * branch_three, axis=1)
    grad_branch_three = (grad_out * pieces[8][:, None, :]).astype(jnp.bfloat16).reshape(-1, D)
    grad_mlp_out = product_tn(active_low, grad_branch_three)
    grad_mlp_out_bias = jnp.sum(grad_branch_three.astype(jnp.float32), axis=0)
    grad_hidden = gelu_back(product_nt(grad_branch_three, mlp_out))[0].astype(jnp.bfloat16)
    grad_mlp_in = product_tn(h_three_low.reshape(-1, D), grad_hidden)
    grad_mlp_in_bias = jnp.sum(grad_hidden.astype(jnp.float32), axis=0)
    grad_h_three = product_nt(grad_hidden, mlp_in).reshape(x_two.shape)
    grad_x_two, grad_shift_three, grad_scale_three = norm_back_three(grad_h_three)
    grad_x_two = grad_x_two + grad_out
    grad_gate_two = jnp.sum(grad_x_two * branch_two, axis=1)
    grad_branch_two = (grad_x_two * pieces[5][:, None, :]).astype(jnp.bfloat16).reshape(-1, D)
    grad_h_two, grad_time_qkv, grad_time_proj, grad_time_bias = attend_backward(
        h_two_low, grad_branch_two, kept_two, time_qkv, time_proj, time_forms, segment_mask
    )
    grad_x_one, grad_shift_two, grad_scale_two = norm_back_two(grad_h_two)
    grad_x_one = grad_x_one + grad_x_two
    grad_gate_one = jnp.sum(grad_x_one * branch_one, axis=1)
    grad_branch_one = (grad_x_one * pieces[2][:, None, :]).astype(jnp.bfloat16).reshape(-1, D)
    grad_h_one, grad_frame_qkv, grad_frame_proj, grad_frame_bias = attend_backward(
        h_one_low, grad_branch_one, kept_one, frame_qkv, frame_proj, frame_forms, all_true
    )
    grad_x_zero, grad_shift_one, grad_scale_one = norm_back_one(grad_h_one)
    grad_x_zero = grad_x_zero + grad_x_one
    grad_frames = jnp.concatenate(
        [
            grad_shift_one,
            grad_scale_one,
            grad_gate_one,
            grad_shift_two,
            grad_scale_two,
            grad_gate_two,
            grad_shift_three,
            grad_scale_three,
            grad_gate_three,
        ],
        axis=1,
    )
    grad_rows = lax.dot_general(
        chooser, grad_frames, (((0,), (0,)), ((), ())), precision=precise
    ).astype(jnp.bfloat16)
    grad_mod_weight = product_tn(silu_low, grad_rows)
    grad_mod_bias = jnp.sum(grad_rows.astype(jnp.float32), axis=0)
    grad_emb = (
        silu_back(product_nt(grad_rows, mod_weight))[0]
        .astype(jnp.bfloat16)
        .reshape(group_size, 2, D)
    )
    send_input_grad = unpack_frames(grad_x_zero.astype(jnp.bfloat16))
    back_input, back_emb = (
        lax.all_to_all(send_input_grad, "narrow", split_axis=0, concat_axis=0, tiled=True),
        lax.all_to_all(grad_emb, "narrow", split_axis=0, concat_axis=0, tiled=True),
    )
    grad_clips = jnp.take(back_input, back_order, axis=0)
    grad_t_emb = jnp.take(back_emb, back_order, axis=0)
    summed = (
        lax.psum_scatter(grad_mod_weight, ("wide", "narrow"), scatter_dimension=0, tiled=True),
        lax.psum_scatter(grad_mod_bias, ("wide", "narrow"), scatter_dimension=0, tiled=True),
        lax.psum_scatter(grad_frame_qkv, ("wide", "narrow"), scatter_dimension=0, tiled=True),
        lax.psum_scatter(grad_frame_proj, ("wide", "narrow"), scatter_dimension=0, tiled=True),
        lax.psum_scatter(grad_frame_bias, ("wide", "narrow"), scatter_dimension=0, tiled=True),
        lax.psum_scatter(grad_time_qkv, ("wide", "narrow"), scatter_dimension=0, tiled=True),
        lax.psum_scatter(grad_time_proj, ("wide", "narrow"), scatter_dimension=0, tiled=True),
        lax.psum_scatter(grad_time_bias, ("wide", "narrow"), scatter_dimension=0, tiled=True),
        lax.psum_scatter(grad_mlp_in, ("wide", "narrow"), scatter_dimension=0, tiled=True),
        lax.psum_scatter(grad_mlp_in_bias, ("wide", "narrow"), scatter_dimension=0, tiled=True),
        lax.psum_scatter(grad_mlp_out, ("wide", "narrow"), scatter_dimension=0, tiled=True),
        lax.psum_scatter(grad_mlp_out_bias, ("wide", "narrow"), scatter_dimension=0, tiled=True),
    )
    return (
        layer_out,
        grad_clips,
        grad_t_emb,
        summed[0],
        summed[1],
        summed[2],
        summed[3],
        summed[4],
        summed[5],
        summed[6],
        summed[7],
        summed[8],
        summed[9],
        summed[10],
        summed[11],
    )


def solution(mesh):
    placed = (
        P(("wide", "narrow"), None, None, None),
        P(("wide", "narrow"), None, None),
        P("wide"),
        P("wide", None),
        P(("wide", "narrow"), None),
        P(("wide", "narrow")),
        P(("wide", "narrow"), None),
        P(("wide", "narrow"), None),
        P(("wide", "narrow")),
        P(("wide", "narrow"), None),
        P(("wide", "narrow"), None),
        P(("wide", "narrow")),
        P(("wide", "narrow"), None),
        P(("wide", "narrow")),
        P(("wide", "narrow"), None),
        P(("wide", "narrow")),
        P(("wide", "narrow"), None, None, None),
    )
    return jax.shard_map(
        local,
        mesh=mesh,
        in_specs=placed,
        out_specs=(
            P(("wide", "narrow"), None, None, None),
            P(("wide", "narrow"), None, None, None),
            P(("wide", "narrow"), None, None),
            P(("wide", "narrow"), None),
            P(("wide", "narrow")),
            P(("wide", "narrow"), None),
            P(("wide", "narrow"), None),
            P(("wide", "narrow")),
            P(("wide", "narrow"), None),
            P(("wide", "narrow"), None),
            P(("wide", "narrow")),
            P(("wide", "narrow"), None),
            P(("wide", "narrow")),
            P(("wide", "narrow"), None),
            P(("wide", "narrow")),
        ),
        check_vma=False,
    )
```

profile of v0, /device:TPU:1, one launch (start us, length us, event | category | flops | bytes accessed | tf_op | source)
XLA Modules:
  0.0 1767.2 jit_solution(11569477264813007603)
XLA Ops:
  32.2 10.6 broadcast_select_fusion.4
  42.8 96.0 %all_to_all.30 = bf16[4,16,64,768]{3,2,1,0:T(8,128)(2,1)} all-to-all(bf16[4,16,64,768]{3,2,1,0:T(8,128)(2,1)} %get-tuple-element.83), channel_id=1, replica_groups=mesh['wide'=8,'narrow'=4] {'narrow'}, dimensions={0} | all-to-all | bytes 12582912 | tf_op jit(solution)/shard_map/all_to_all | solution.py:247
  147.9 112.7 %all-reduce.11 = (bf16[6912]{0:T(1024)(128)(2,1)S(1)}, bf16[768]{0:T(1024)(128)(2,1)S(1)}, bf16[768]{0:T(1024)(128)(2,1)S(1)}, bf16[3072]{0:T(1024)(128)(2,1)S(1)}, bf16[768]{0:T(1024)(128)(2,1)S(1)}) all-reduce(bf16[6912]{0:T(1024)(128)(2,1)S(1)} %dynamic-update-slice, ...), channel_id=1, replica_groups=mesh['wide'=8,'narrow'=4] {'wide','narrow'}, use_global_device_ids=true, to_apply=%add | all-reduce | flops 12288 | bytes 49152
  290.8 12.3 convolution_convert_fusion.1
  303.1 12.6 copy.118
  315.8 27.2 %reshape.559 = bf16[32,64,3,12,64]{1,0,4,3,2:T(8,128)(2,1)} reshape(bf16[2048,2304]{0,1:T(8,128)(2,1)} %copy.118) | data formatting | bytes 18874368 | tf_op jit(solution)/shard_map/reshape | solution.py:69
  343.0 14.0 fusion.97
  375.2 12.5 multiply_reduce_fusion.2
  397.5 16.2 convert_bitcast_fusion.1
  447.8 12.9 convolution_convert_fusion
  460.7 28.8 %reshape.753 = bf16[32,64,3,12,64]{4,3,2,1,0:T(8,128)(2,1)} reshape(bf16[2048,2304]{1,0:T(8,128)(2,1)} %convolution_convert_fusion) | data formatting | bytes 18874368 | tf_op jit(solution)/shard_map/reshape | solution.py:69
  489.5 17.5 fusion.96
  507.0 16.2 fusion.42
  529.6 12.5 convert_bitcast_fusion
  542.2 12.2 copy.129
  579.4 24.9 %multiply_convert_fusion = (bf16[2048,3072]{1,0:T(8,128)(2,1)}, f32[2048,3072]{1,0:T(8,128)}) fusion(f32[3072]{0:T(1024)S(1)} %copy-done.74, bf16[2048,768]{1,0:T(8,128)(2,1)} %bitcast.226, bf16[768,3072]{1,0:T(8,128)(2,1)} %all-gather.18.cloned.1.call-done), kind=kOutput, calls=%fused_computation.25 | convolution fusion | flops 9726590976 | bytes 45625344 | tf_op jit(solution)/shard_map/dot_general | solution.py:53
  604.3 33.8 %convert_reduce_fusion = (f32[3072]{0:T(1024)}, bf16[2048,3072]{1,0:T(8,128)(2,1)}) fusion(f32[2048,3072]{1,0:T(8,128)} %get-tuple-element.94, f32[3072]{0:T(1024)S(1)} %copy-done.74, bf16[2048,768]{1,0:T(8,128)(2,1)} %bitcast.220, bf16[3072,768]{1,0:T(8,128)(2,1)} %all-gather.20.cloned.1.call-done), kind=kOutput, calls=%fused_computation.24 | convolution fusion | flops 9808376832 | bytes 45637632 | tf_op jit(solution)/shard_map/dot_general | solution.py:63
  638.1 13.0 fusion.100
  655.4 12.9 convolution_add_fusion.1
  693.8 10.9 reshape.754
  704.7 20.9 %multiply_reduce_fusion.1 = (f32[64,12,32]{2,1,0:T(8,128)S(1)}, f32[64,12,32,32]{2,3,1,0:T(8,128)}) fusion(f32[64,12,32]{2,1,0:T(8,128)S(1)} %copy-done.14, f32[64,12,32,32]{2,3,1,0:T(8,128)} %copy-done.3, pred[32,32]{0,1:T(8,128)(4,1)S(1)} %copy-done.66, bf16[32,64,1,12,64]{4,3,2,1,0:T(8,128)(2,1)} %get-tuple-element.56, bf16[32,64,12,64]{3,2,1,0:T(8,128)(2,1)} %reshape.754), kind=kOutput, calls=%fused_computation.33 | convolution fusion | flops 104570880 | bytes 12780544 | tf_op jit(solution)/shard_map/fphc,gphc->phfg/dot_general | solution.py:103
  725.6 12.3 fusion.53
  737.8 10.6 multiply_convert_fusion.2
  748.5 10.5 multiply_bitcast_fusion.2
  768.7 11.1 maximum_convert_fusion
  786.3 27.7 %copy.134 = bf16[32,64,3,12,64]{4,3,2,1,0:T(8,128)(2,1)} copy(bf16[32,64,3,12,64]{4,0,3,1,2:T(8,128)(2,1)S(1)} %maximum_convert_fusion) | data formatting | bytes 18874368 | tf_op jit(solution)/shard_map/convert_element_type | solution.py:123
  814.1 30.3 %convert_element_type.186 = bf16[32,64,2304]{2,1,0:T(8,128)(2,1)} reshape(bf16[32,64,3,12,64]{4,3,2,1,0:T(8,128)(2,1)} %copy.134) | data formatting | bytes 18874368 | tf_op jit(solution)/shard_map/convert_element_type | solution.py:123
  844.5 13.5 multiply_reduce_fusion.6
  876.9 32.6 %copy.149 = bf16[32,64,3,12,64]{1,0,4,3,2:T(8,128)(2,1)} copy(bf16[32,64,3,12,64]{4,0,3,1,2:T(8,128)(2,1)} %copy-done.4) | data formatting | bytes 18874368 | tf_op jit(solution)/shard_map/convert_element_type | solution.py:123
  909.5 26.5 %convert_element_type.199 = bf16[2048,2304]{0,1:T(8,128)(2,1)} reshape(bf16[32,64,3,12,64]{1,0,4,3,2:T(8,128)(2,1)} %copy.149) | data formatting | bytes 18874368 | tf_op jit(solution)/shard_map/convert_element_type | solution.py:123
  936.0 12.8 fusion.103
  956.2 10.6 reshape.755
  966.8 11.8 copy.144
  978.6 13.9 multiply_reduce_fusion
  992.5 13.5 multiply_convert_fusion.1
  1034.2 17.9 %maximum_convert_fusion.1 = bf16[32,64,3,12,64]{4,1,3,0,2:T(8,128)(2,1)} fusion(bf16[32,64,1,12,64]{4,1,3,0,2:T(8,128)(2,1)} %fusion.58, bf16[32,64,1,12,64]{4,1,3,0,2:T(8,128)(2,1)} %multiply_bitcast_fusion, bf16[32,64,1,12,64]{4,1,3,0,2:T(8,128)(2,1)} %multiply_bitcast_fusion.1), kind=kLoop, calls=%fused_computation.14 | loop fusion | flops 9437184 | bytes 18874368 | tf_op jit(solution)/shard_map/convert_element_type | solution.py:123
  1052.1 25.8 %copy.148 = bf16[32,64,3,12,64]{1,0,4,3,2:T(8,128)(2,1)} copy(bf16[32,64,3,12,64]{4,1,3,0,2:T(8,128)(2,1)} %maximum_convert_fusion.1) | data formatting | bytes 18874368 | tf_op jit(solution)/shard_map/convert_element_type | solution.py:123
  1077.9 26.6 %convert_element_type.197 = bf16[2048,2304]{0,1:T(8,128)(2,1)} reshape(bf16[32,64,3,12,64]{1,0,4,3,2:T(8,128)(2,1)} %copy.148) | data formatting | bytes 18874368 | tf_op jit(solution)/shard_map/convert_element_type | solution.py:123
  1104.5 12.8 fusion.101
  1119.1 15.7 fusion.106
  1136.8 15.4 fusion.105
  1152.4 21.8 %copy.147 = bf16[32,64,3,12,64]{4,3,2,1,0:T(8,128)(2,1)} copy(bf16[32,64,3,12,64]{4,1,3,0,2:T(8,128)(2,1)} %maximum_convert_fusion.1) | data formatting | bytes 18874368 | tf_op jit(solution)/shard_map/convert_element_type | solution.py:123
  1174.2 30.5 %convert_element_type.192 = bf16[32,64,2304]{2,1,0:T(8,128)(2,1)} reshape(bf16[32,64,3,12,64]{4,3,2,1,0:T(8,128)(2,1)} %copy.147) | data formatting | bytes 18874368 | tf_op jit(solution)/shard_map/convert_element_type | solution.py:123
  1204.7 19.6 %fusion.25 = (f32[32,768]{1,0:T(8,128)S(1)}, f32[32,768]{1,0:T(8,128)S(1)}, f32[32,64]{1,0:T(8,128)S(1)}, f32[32,64,768]{2,1,0:T(8,128)}) fusion(f32[2048,768]{1,0:T(8,128)} %copy-done.16, bf16[32,64,768]{2,1,0:T(8,128)(2,1)} %gather_fusion.9, pred[32]{0:T(512)(128)(4,1)S(1)} %copy-done.69, f32[2048,768]{1,0:T(8,128)} %copy-done.15, ...), kind=kOutput, calls=%fused_computation.72 | convolution fusion | flops 7269726208 | bytes 44752928 | tf_op jit(solution)/shard_map/dot_general | solution.py:63
  1282.0 97.3 %all_to_all.31 = bf16[4,16,64,768]{3,2,1,0:T(8,128)(2,1)} all-to-all(bf16[4,16,64,768]{3,2,1,0:T(8,128)(2,1)} %get-tuple-element.77), channel_id=1, replica_groups=mesh['wide'=8,'narrow'=4] {'narrow'}, dimensions={0} | all-to-all | bytes 12582912 | tf_op jit(solution)/shard_map/all_to_all | solution.py:301
  1385.9 109.7 %all-reduce.10 = (f32[6912]{0:T(1024)S(1)}, f32[768]{0:T(1024)S(1)}, f32[768]{0:T(1024)S(1)}, f32[3072]{0:T(1024)S(1)}, f32[768]{0:T(1024)S(1)}) all-reduce(f32[6912]{0:T(1024)S(1)} %get-tuple-element.102, f32[768]{0:T(1024)S(1)} %copy-done.73, f32[768]{0:T(1024)S(1)} %copy-done.72, ...), channel_id=3, replica_groups=mesh['wide'=8,'narrow'=4] {'wide','narrow'}, use_global_device_ids=true, to_apply=%region_31.36.clone | all-reduce | flops 12288 | bytes 98304
  1512.9 10.6 broadcast_select_fusion
  1533.4 227.0 %reduce-scatter.8.cloned.1.call-done = f32[24,6912]{1,0:T(8,128)} async-done(((f32[768,6912]{1,0:T(8,128)}), f32[24,6912]{1,0:T(8,128)}) %reduce-scatter.8.cloned.1.call-update) | async-done | bytes 663568 | tf_op jit(solution)/shard_map/reduce_scatter | solution.py:307
  (378 shorter events, 352.4 us)
Async XLA Ops:
  7.2 273.1 %all-gather.8.cloned.1.call-start = ((), (), s32[]{:S(2)}) async-start(), calls=%async_computation.13 | async-start | bytes 10948608 | tf_op jit(solution)/shard_map/all_gather | solution.py:150
  7.9 282.8 %all-gather.10.cloned.1.call-start = ((), (), s32[]{:S(2)}) async-start(), calls=%async_computation.14 | async-start | bytes 3649536 | tf_op jit(solution)/shard_map/all_gather | solution.py:152
  8.7 425.0 %all-gather.12.cloned.1.call-start = ((), (), s32[]{:S(2)}) async-start(), calls=%async_computation.15 | async-start | bytes 1216512 | tf_op jit(solution)/shard_map/all_gather | solution.py:153
  9.4 438.3 %all-gather.14.cloned.1.call-start = ((), (), s32[]{:S(2)}) async-start(), calls=%async_computation.16 | async-start | bytes 3649536 | tf_op jit(solution)/shard_map/all_gather | solution.py:155
  10.0 552.9 %all-gather.16.cloned.1.call-start = ((), (), s32[]{:S(2)}) async-start(), calls=%async_computation.17 | async-start | bytes 1216512 | tf_op jit(solution)/shard_map/all_gather | solution.py:156
  10.6 568.8 %all-gather.18.cloned.1.call-start = ((), (), s32[]{:S(2)}) async-start(), calls=%async_computation.18 | async-start | bytes 4866048 | tf_op jit(solution)/shard_map/all_gather | solution.py:158
  14.9 27.8 %all-to-all-start.1 = ((bf16[4,2,768]{2,1,0:T(2,128)(2,1)}), bf16[4,2,768]{2,1,0:T(2,128)(2,1)S(1)}, u32[]{:S(2)}, u32[]{:S(2)}) async-start(bf16[4,2,768]{2,1,0:T(2,128)(2,1)} %broadcast_select_fusion.11), calls=%async_computation.1 | async-start | bytes 24576 | tf_op jit(solution)/shard_map/all_to_all | solution.py:214
  138.8 135.7 %all-to-all-start = ((bf16[4,16,64,768]{3,2,1,0:T(8,128)(2,1)}), bf16[4,16,64,768]{3,2,1,0:T(8,128)(2,1)}, u32[]{:S(2)}, u32[]{:S(2)}) async-start(bf16[4,16,64,768]{3,2,1,0:T(8,128)(2,1)} %get-tuple-element.84), calls=%async_computation | async-start | bytes 12582912 | tf_op jit(solution)/shard_map/all_to_all | solution.py:213
  145.2 459.0 %all-gather.20.cloned.1.call-start = ((), (), s32[]{:S(2)}) async-start(), calls=%async_computation.19 | async-start | bytes 4866048 | tf_op jit(solution)/shard_map/all_gather | solution.py:160
  146.0 1377.5 %reduce-scatter.16.cloned.1.call-start = ((), (), s32[]{:S(2)}) async-start(), calls=%async_computation.24 | async-start | bytes 2433024 | tf_op jit(solution)/shard_map/reduce_scatter | solution.py:313
  269.1 169.7 %copy-start.67 = (pred[32]{0:T(512)(128)(4,1)}, pred[32]{0:T(512)(128)(4,1)S(1)}, u32[]{:S(2)}) copy-start(pred[32]{0:T(512)(128)(4,1)S(1)} %get-tuple-element.52) | copy-start | bytes 100
  269.2 16.6 copy-start.78
  269.2 260.4 %copy-start.65 = (pred[32,32]{0,1:T(8,128)(4,1)}, pred[32,32]{0,1:T(8,128)(4,1)S(1)}, u32[]{:S(2)}) copy-start(pred[32,32]{0,1:T(8,128)(4,1)S(1)} %broadcast_compare_fusion) | copy-start | bytes 3076
  278.1 160.8 %copy-start.6 = (bf16[32,64,768]{2,1,0:T(8,128)(2,1)}, bf16[32,64,768]{2,1,0:T(8,128)(2,1)S(1)}, u32[]{:S(2)}) copy-start(bf16[32,64,768]{2,1,0:T(8,128)(2,1)S(1)} %gather_fusion.4) | copy-start | bytes 9437188
  287.2 157.3 %copy-start.34 = (f32[32,768]{1,0:T(8,128)}, f32[32,768]{1,0:T(8,128)S(1)}, u32[]{:S(2)}) copy-start(f32[32,768]{1,0:T(8,128)S(1)} %get-tuple-element.70) | copy-start | bytes 294916
  444.4 16.3 copy-start.63
  444.4 16.2 copy-start.55
  447.7 13.0 copy-start.23
  579.3 71.7 %slice-start.2 = ((s8[6291456]{0:T(1024)(128)(4,1)}), s8[2097152]{0:T(1024)(128)(4,1)S(1)}, s32[]{:S(2)}) async-start(s8[6291456]{0:T(1024)(128)(4,1)} %bitcast.209), calls=%async_computation.29 | async-start | bytes 4194304
  604.3 33.9 %copy-start.84 = (bf16[768,3072]{1,0:T(8,128)(2,1)S(1)}, bf16[768,3072]{1,0:T(8,128)(2,1)}, u32[]{:S(2)}) copy-start(bf16[768,3072]{1,0:T(8,128)(2,1)} %all-gather.18.cloned.1.call-done) | copy-start | bytes 14155780
  604.3 46.8 %slice-start.3 = ((s8[6291456]{0:T(1024)(128)(4,1)}), s8[4194304]{0:T(1024)(128)(4,1)S(1)}, s32[]{:S(2)}) async-start(s8[6291456]{0:T(1024)(128)(4,1)} %bitcast.209), calls=%async_computation.30 | async-start | bytes 8388608
  677.5 185.3 %copy-start.59 = (f32[32,64]{1,0:T(8,128)}, f32[32,64]{1,0:T(8,128)S(1)}, u32[]{:S(2)}) copy-start(f32[32,64]{1,0:T(8,128)S(1)} %negate_multiply_fusion.2) | copy-start | bytes 24580
  768.7 754.8 %reduce-scatter.12.cloned.1.call-start = ((), (), s32[]{:S(2)}) async-start(), calls=%async_computation.22 | async-start | bytes 2433024 | tf_op jit(solution)/shard_map/reduce_scatter | solution.py:310
  814.1 30.4 %copy-start.35 = (f32[32,768]{1,0:T(8,128)S(1)}, f32[32,768]{1,0:T(8,128)}, u32[]{:S(2)}) copy-start(f32[32,768]{1,0:T(8,128)} %copy-done.34) | copy-start | bytes 294916
  814.1 30.4 %copy-start.46 = (f32[32,64]{1,0:T(8,128)S(1)}, f32[32,64]{1,0:T(8,128)}, u32[]{:S(2)}) copy-start(f32[32,64]{1,0:T(8,128)} %copy-done.45) | copy-start | bytes 24580
  814.1 44.0 %slice-start = ((s8[6291456]{0:T(1024)(128)(4,1)}), s8[2097152]{0:T(1024)(128)(4,1)S(1)}, s32[]{:S(2)}) async-start(s8[6291456]{0:T(1024)(128)(4,1)} %bitcast.207), calls=%async_computation.27 | async-start | bytes 4194304
  844.4 13.6 copy-start.64
  844.4 13.6 slice-start.1
  844.5 13.6 copy-start.56
  876.9 646.6 %reduce-scatter.14.cloned.1.call-start = ((), (), s32[]{:S(2)}) async-start(), calls=%async_computation.23 | async-start | bytes 7299072 | tf_op jit(solution)/shard_map/reduce_scatter | solution.py:312
  909.5 26.5 %copy-start.24 = (bf16[32,64,768]{2,1,0:T(8,128)(2,1)S(1)}, bf16[32,64,768]{2,1,0:T(8,128)(2,1)}, u32[]{:S(2)}) copy-start(bf16[32,64,768]{2,1,0:T(8,128)(2,1)} %copy-done.23) | copy-start | bytes 9437188
  948.8 574.6 %reduce-scatter.10.cloned.1.call-start = ((), (), s32[]{:S(2)}) async-start(), calls=%async_computation.21 | async-start | bytes 7299072 | tf_op jit(solution)/shard_map/reduce_scatter | solution.py:309
  1006.1 19.8 %slice-start.4 = ((s8[6291456]{0:T(1024)(128)(4,1)}), s8[2097152]{0:T(1024)(128)(4,1)S(1)}, s32[]{:S(2)}) async-start(s8[6291456]{0:T(1024)(128)(4,1)} %bitcast.211), calls=%async_computation.31 | async-start | bytes 4194304
  1077.9 26.6 %copy-start.20 = (bf16[32,64,768]{2,1,0:T(8,128)(2,1)S(1)}, bf16[32,64,768]{2,1,0:T(8,128)(2,1)}, u32[]{:S(2)}) copy-start(bf16[32,64,768]{2,1,0:T(8,128)(2,1)} %fusion.18) | copy-start | bytes 9437188
  1117.3 406.2 %reduce-scatter.20.cloned.1.call-start = ((), (), s32[]{:S(2)}) async-start(), calls=%async_computation.26 | async-start | bytes 9732096 | tf_op jit(solution)/shard_map/reduce_scatter | solution.py:317
  1134.9 398.6 %reduce-scatter.18.cloned.1.call-start = ((), (), s32[]{:S(2)}) async-start(), calls=%async_computation.25 | async-start | bytes 9732096 | tf_op jit(solution)/shard_map/reduce_scatter | solution.py:315
  1152.3 608.2 %reduce-scatter.8.cloned.1.call-start = ((), (), s32[]{:S(2)}) async-start(), calls=%async_computation.20 | async-start | bytes 21897216 | tf_op jit(solution)/shard_map/reduce_scatter | solution.py:307
  1174.2 30.5 %copy-start.7 = (bf16[32,64,768]{2,1,0:T(8,128)(2,1)S(1)}, bf16[32,64,768]{2,1,0:T(8,128)(2,1)}, u32[]{:S(2)}) copy-start(bf16[32,64,768]{2,1,0:T(8,128)(2,1)} %copy-done.6) | copy-start | bytes 9437188
  1174.2 30.5 %copy-start.33 = (f32[32,768]{1,0:T(8,128)S(1)}, f32[32,768]{1,0:T(8,128)}, u32[]{:S(2)}) copy-start(f32[32,768]{1,0:T(8,128)} %copy-done.32) | copy-start | bytes 294916
  1174.2 30.5 %copy-start.48 = (f32[32,64]{1,0:T(8,128)S(1)}, f32[32,64]{1,0:T(8,128)}, u32[]{:S(2)}) copy-start(f32[32,64]{1,0:T(8,128)} %copy-done.47) | copy-start | bytes 24580
  1174.2 30.5 %copy-start.60 = (f32[32,64]{1,0:T(8,128)S(1)}, f32[32,64]{1,0:T(8,128)}, u32[]{:S(2)}) copy-start(f32[32,64]{1,0:T(8,128)} %copy-done.59) | copy-start | bytes 24580
  1174.2 30.5 %copy-start.69 = (pred[32]{0:T(512)(128)(4,1)S(1)}, pred[32]{0:T(512)(128)(4,1)}, u32[]{:S(2)}) copy-start(pred[32]{0:T(512)(128)(4,1)} %copy-done.67) | copy-start | bytes 100
  1204.7 19.6 %copy-start.62 = (f32[32,64]{1,0:T(8,128)S(1)}, f32[32,64]{1,0:T(8,128)}, u32[]{:S(2)}) copy-start(f32[32,64]{1,0:T(8,128)} %copy-done.61) | copy-start | bytes 24580
  1204.7 19.6 %copy-start.58 = (f32[32,64]{1,0:T(8,128)S(1)}, f32[32,64]{1,0:T(8,128)}, u32[]{:S(2)}) copy-start(f32[32,64]{1,0:T(8,128)} %copy-done.57) | copy-start | bytes 24580
  1248.4 13.0 copy-start.11
  1256.6 25.4 %all-to-all-start.5 = ((bf16[4,2,768]{2,1,0:T(2,128)(2,1)}), bf16[4,2,768]{2,1,0:T(2,128)(2,1)S(1)}, u32[]{:S(2)}, u32[]{:S(2)}) async-start(bf16[4,2,768]{2,1,0:T(2,128)(2,1)} %reshape.577), calls=%async_computation.5 | async-start | bytes 24576 | tf_op jit(solution)/shard_map/all_to_all | solution.py:302
  1379.4 127.0 %all-to-all-start.2 = ((bf16[4,16,64,768]{3,2,1,0:T(8,128)(2,1)}), bf16[4,16,64,768]{3,2,1,0:T(8,128)(2,1)}, u32[]{:S(2)}, u32[]{:S(2)}) async-start(bf16[4,16,64,768]{3,2,1,0:T(8,128)(2,1)} %get-tuple-element.78), calls=%async_computation.2 | async-start | bytes 12582912 | tf_op jit(solution)/shard_map/all_to_all | solution.py:245
  1512.9 247.6 %copy-start.1 = (bf16[4,2,768]{2,1,0:T(2,128)(2,1)S(1)}, bf16[4,2,768]{2,1,0:T(2,128)(2,1)}, u32[]{:S(2)}) copy-start(bf16[4,2,768]{2,1,0:T(2,128)(2,1)} %param.26) | copy-start | bytes 36868
  (68 other events, 391.7 us)
Sparse Core Ops, SparseCore 0:
  10.9 108.3 all-gather.7
  122.2 66.0 all-gather.9
  191.2 53.5 all-gather.11
  247.5 59.0 all-gather.13
  309.4 52.6 all-gather.15
  364.9 62.5 all-gather.17
  430.3 61.9 all-gather.19
  768.8 97.1 reduce-scatter.15
  877.0 97.3 reduce-scatter.11
  980.5 118.5 reduce-scatter.13
  1117.4 117.4 reduce-scatter.9
  1241.2 149.7 reduce-scatter.19
  1397.5 135.9 reduce-scatter.17
  1540.3 220.1 reduce-scatter.7
where the time goes:
time: 1780 us; the launch traced here: 1770 us
  local copies, waits for them, and re-layouts  489 us (27%)
  blocking collectives  416 us (23%)
  matrix products  405 us (23%)
  waiting for transfers between devices  242 us (14%)
  other arithmetic  178 us (10%)
  starting transfers between devices  22.4 us (1%)
    reduce_scatter x1, waiting for transfers between devices, local(): lax.psum_scatter(grad_mod_weight, ('wide', 'narrow'), scatter_dimension=0...  227 us
    unnamed x2, blocking collectives  222 us
    convert_element_type x8, local copies, waits for them, and re-layouts, attend_backward(): grad_qkv = jnp.stack([grad_query, grad_key, grad_value], axis=2).reshape(...  222 us
    dot_general x7, matrix products, product_nt(): lax.dot_general(matrix_a, matrix_b, (((1,), (1,)), ((), ())), preferred_e...  99.1 us
    all_to_all x1, blocking collectives, local(): lax.all_to_all(send_input_grad, 'narrow', split_axis=0, concat_axis=0, ti...  97.3 us
    all_to_all x1, blocking collectives, local(): lax.all_to_all(jnp.take(cotangent, send_order, axis=0), 'narrow', split_a...  96 us
    dot_general x7, matrix products, product(): return jnp.dot(matrix_a, matrix_b, preferred_element_type=jnp.float32)  78.7 us
    dot_general x7, matrix products, product_tn(): lax.dot_general(matrix_a, matrix_b, (((0,), (0,)), ((), ())), preferred_e...  73.5 us
  transfers between devices with their start and end apart: 18, of which 2 were waited for; matrix products, arithmetic and copies ran while one was open for 50% of the time, Pallas kernels for 0%

commit v1 on v0

v1 whole, which is shorter than its diff:
```python
import functools

import jax
import jax.numpy as jnp
from jax import lax
from jax.experimental import pallas as pl
from jax.experimental.pallas import tpu as pltpu
from jax.sharding import PartitionSpec as P

D = 768
HEADS = 12
HEAD = 64
FF = 3072
FR = 16
PATCHES = 64
LIVE = 2 * FR
EPS = 1e-06
BF = jnp.bfloat16
F32 = jnp.float32
ALL = ("wide", "narrow")
PAIRS = HEADS // 2
LANES = 2 * HEAD
TILE = 512
FT = TILE // PATCHES
PT = TILE // LIVE
GRID = LIVE * PATCHES // TILE
GROUPS = TILE // 64
GELU_C = 0.7978845608028654
GELU_A = 0.044715
VMEM_LIMIT = 66 * 1000 * 1000


def dot(a, b):
    return lax.dot_general(a, b, (((1,), (0,)), ((), ())), preferred_element_type=F32)


def dot_nt(a, b):
    return lax.dot_general(a, b, (((1,), (1,)), ((), ())), preferred_element_type=F32)


def dot_tn(a, b):
    return lax.dot_general(a, b, (((0,), (0,)), ((), ())), preferred_element_type=F32)


def normalise(x):
    mean = jnp.mean(x, axis=-1, keepdims=True)
    centred = x - mean
    var = jnp.mean(centred * centred, axis=-1, keepdims=True)
    rstd = lax.rsqrt(var + EPS)
    return centred * rstd, rstd


def norm_back(dn, xhat, rstd):
    m1 = jnp.mean(dn, axis=-1, keepdims=True)
    m2 = jnp.mean(dn * xhat, axis=-1, keepdims=True)
    return rstd * (dn - m1 - xhat * m2)


def lane_masks():
    lane = lax.broadcasted_iota(jnp.int32, (64, LANES), 1)
    low_lanes = lane < HEAD
    low = jnp.where(low_lanes, 1.0, 0.0).astype(BF)
    high = jnp.where(low_lanes, 0.0, 1.0).astype(BF)
    return low_lanes, low, high


def softmax_keys(k, qb, mask):
    s = dot_nt(k, qb) * HEAD ** (-0.5)
    if mask is not None:
        s = jnp.where(mask, s, -1e30)
    top = jnp.max(s, axis=0, keepdims=True)
    e = jnp.exp(s - top)
    return e / jnp.sum(e, axis=0, keepdims=True)


def attend(qkv_ref, o_ref, mask):
    low_lanes, low, high = lane_masks()

    def body(g, carry):
        rows = pl.ds(pl.multiple_of(g * 64, 64), 64)
        for hp in range(PAIRS):
            cols = slice(hp * LANES, (hp + 1) * LANES)
            q = qkv_ref[rows, hp * LANES : (hp + 1) * LANES]
            k = qkv_ref[rows, D + hp * LANES : D + (hp + 1) * LANES]
            v = qkv_ref[rows, 2 * D + hp * LANES : 2 * D + (hp + 1) * LANES]
            qb = jnp.concatenate([q * low, q * high], axis=0)
            p = softmax_keys(k, qb, mask).astype(BF)
            r = dot_tn(p, v)
            o_ref[rows, cols] = jnp.where(low_lanes, r[:64], r[64:]).astype(BF)
        return carry

    lax.fori_loop(0, GROUPS, body, 0)


def attend_back(qkv_ref, do_ref, dqkv_ref, mask):
    low_lanes, low, high = lane_masks()

    def body(g, carry):
        rows = pl.ds(pl.multiple_of(g * 64, 64), 64)
        for hp in range(PAIRS):
            qc = slice(hp * LANES, (hp + 1) * LANES)
            kc = slice(D + hp * LANES, D + (hp + 1) * LANES)
            vc = slice(2 * D + hp * LANES, 2 * D + (hp + 1) * LANES)
            q = qkv_ref[rows, qc]
            k = qkv_ref[rows, kc]
            v = qkv_ref[rows, vc]
            do = do_ref[rows, qc]
            qb = jnp.concatenate([q * low, q * high], axis=0)
            dob = jnp.concatenate([do * low, do * high], axis=0)
            p = softmax_keys(k, qb, mask)
            dp = dot_nt(v, dob)
            delta = jnp.sum(p * dp, axis=0, keepdims=True)
            ds = (p * (dp - delta)).astype(BF)
            r = dot_tn(ds, k)
            dq = jnp.where(low_lanes, r[:64], r[64:]) * HEAD ** (-0.5)
            dqkv_ref[rows, qc] = dq.astype(BF)
            dqkv_ref[rows, kc] = (dot(ds, qb) * HEAD ** (-0.5)).astype(BF)
            dqkv_ref[rows, vc] = dot(p.astype(BF), dob).astype(BF)
        return carry

    lax.fori_loop(0, GROUPS, body, 0)


def swap_major(value, scratch, out_ref, first, second):
    for b in range(D // 128):
        cols = slice(b * 128, (b + 1) * 128)
        for i in range(first):
            scratch[b, pl.ds(i, second, stride=first), :] = value[i * second : (i + 1) * second, cols]
        out_ref[:, :, cols] = scratch[b].reshape(second, first, 128).astype(out_ref.dtype)


def frames_of(refs):
    return jnp.concatenate([r[0] for r in refs], axis=0).astype(F32)


def per_frame(piece):
    return jnp.broadcast_to(piece[:, None, :], (FT, PATCHES, D)).reshape(TILE, D)


def per_patch(piece):
    return jnp.broadcast_to(piece[None], (PT, LIVE, D)).reshape(TILE, D)


def sum_patches(value):
    return jnp.sum(value.reshape(FT, PATCHES, D), axis=1)


def sum_groups(value):
    return jnp.sum(value.reshape(PT, LIVE, D), axis=0)


def attn_mask(seg_ref):
    return seg_ref[...] > 0.0


def frame_forward(rows_ref, *refs):
    x_refs, (mod, wqkv, wo, bo, x1t, qkv, o, a1, scratch) = refs[:FT], refs[FT:]
    x = frames_of(x_refs)
    xhat, _ = normalise(x)
    h = (xhat * (1.0 + per_frame(mod[1])) + per_frame(mod[0])).astype(BF)
    qkv[...] = dot(h, wqkv[...]).astype(BF)
    attend(qkv, o, None)
    branch = dot(o[...], wo[...]) + bo[...]
    a1[...] = branch
    x1 = x + per_frame(mod[2]) * branch
    swap_major(x1, scratch, x1t, FT, PATCHES)


def turn_frames(rows_ref, *refs):
    x_refs, (out, scratch) = refs[:FT], refs[FT:]
    swap_major(frames_of(x_refs), scratch, out, FT, PATCHES)


def time_forward(x1, mod, seg, wqkv, wo, bo, x2, qkv, o, a2):
    x = x1[...].reshape(TILE, D)
    xhat, _ = normalise(x)
    h = (xhat * (1.0 + per_patch(mod[1])) + per_patch(mod[0])).astype(BF)
    qkv[...] = dot(h, wqkv[...]).astype(BF)
    attend(qkv, o, attn_mask(seg))
    branch = dot(o[...], wo[...]) + bo[...]
    a2[...] = branch
    x2[...] = (x + per_patch(mod[2]) * branch).reshape(PT, LIVE, D)


def mlp_both(x2, dy, mod, win, bin_, wout, bout, out, dx2, gwin, gwout, gbin, gbout, dmod, scratch):
    first = pl.program_id(0) == 0

    @pl.when(first)
    def _():
        gwin[...] = jnp.zeros_like(gwin)
        gwout[...] = jnp.zeros_like(gwout)
        gbin[...] = jnp.zeros_like(gbin)
        gbout[...] = jnp.zeros_like(gbout)
        dmod[...] = jnp.zeros_like(dmod)

    x = x2[...].reshape(TILE, D)
    xhat, rstd = normalise(x)
    h = (xhat * (1.0 + per_patch(mod[1])) + per_patch(mod[0])).astype(BF)
    gate = per_patch(mod[2])
    grad = dy[...].reshape(TILE, D)
    da = (grad * gate).astype(BF)
    gbout[...] += jnp.sum(da.astype(F32), axis=0, keepdims=True)
    branch = jnp.zeros((TILE, D), F32) + bout[...]
    dh = jnp.zeros((TILE, D), F32)
    for j in range(FF // D):
        cols = slice(j * D, (j + 1) * D)
        u = dot(h, win[:, cols]) + bin_[:, cols]
        u2 = u * u
        t = jnp.tanh(GELU_C * u * (1.0 + GELU_A * u2))
        half = 0.5 * (1.0 + t)
        g = (u * half).astype(BF)
        slope = half + (0.5 * GELU_C) * u * (1.0 - t * t) * (1.0 + 3.0 * GELU_A * u2)
        branch = branch + dot(g, wout[cols, :])
        du = (dot_nt(da, wout[cols, :]) * slope).astype(BF)
        gwout[cols, :] += dot_tn(g, da)
        gbin[:, cols] += jnp.sum(du.astype(F32), axis=0, keepdims=True)
        gwin[:, cols] += dot_tn(h, du)
        dh = dh + dot_nt(du, win[:, cols])
    swap_major(x + gate * branch, scratch, out, PT, LIVE)
    dmod[2] += sum_groups(grad * branch)
    dmod[0] += sum_groups(dh)
    dmod[1] += sum_groups(dh * xhat)
    back = norm_back(dh * (1.0 + per_patch(mod[1])), xhat, rstd)
    dx2[...] = (grad + back).reshape(PT, LIVE, D)


def attn_back_tile(x, grad, shift, scale, gate, branch, qkv, o, wqkv, wo, gwqkv, gwo, gbo, do, dqkv, mask):
    first = pl.program_id(0) == 0

    @pl.when(first)
    def _():
        gwqkv[...] = jnp.zeros_like(gwqkv)
        gwo[...] = jnp.zeros_like(gwo)
        gbo[...] = jnp.zeros_like(gbo)

    da = (grad * gate).astype(BF)
    do[...] = dot_nt(da, wo[...]).astype(BF)
    gwo[...] += dot_tn(o[...], da)
    gbo[...] += jnp.sum(da.astype(F32), axis=0, keepdims=True)
    attend_back(qkv, do, dqkv, mask)
    xhat, rstd = normalise(x)
    h = (xhat * (1.0 + scale) + shift).astype(BF)
    dh = jnp.zeros((TILE, D), F32)
    for j in range(3):
        cols = slice(j * D, (j + 1) * D)
        part = dqkv[:, cols]
        gwqkv[:, cols] += dot_tn(h, part)
        dh = dh + dot_nt(part, wqkv[:, cols])
    dx = grad + norm_back(dh * (1.0 + scale), xhat, rstd)
    return dx, dh, dh * xhat, grad * branch


def time_back(x1, dx2, mod, seg, qkv, o, a2, wqkv, wo, dx1, gwqkv, gwo, gbo, dmod, do, dqkv, scratch):
    @pl.when(pl.program_id(0) == 0)
    def _():
        dmod[...] = jnp.zeros_like(dmod)

    dx, d_shift, d_scale, d_gate = attn_back_tile(
        x1[...].reshape(TILE, D), dx2[...].reshape(TILE, D), per_patch(mod[0]), per_patch(mod[1]),
        per_patch(mod[2]), a2[...], qkv, o, wqkv, wo, gwqkv, gwo, gbo, do, dqkv, attn_mask(seg))
    dmod[0] += sum_groups(d_shift)
    dmod[1] += sum_groups(d_scale)
    dmod[2] += sum_groups(d_gate)
    swap_major(dx, scratch, dx1, PT, LIVE)


def frame_back(rows_ref, *refs):
    x_refs, (dx1, mod, qkv, o, a1, wqkv, wo, dx0, gwqkv, gwo, gbo, dmod, do, dqkv) = refs[:FT], refs[FT:]
    dx, d_shift, d_scale, d_gate = attn_back_tile(
        frames_of(x_refs), dx1[...].reshape(TILE, D), per_frame(mod[0]), per_frame(mod[1]),
        per_frame(mod[2]), a1[...], qkv, o, wqkv, wo, gwqkv, gwo, gbo, do, dqkv, None)
    dmod[0] = sum_patches(d_shift)
    dmod[1] = sum_patches(d_scale)
    dmod[2] = sum_patches(d_gate)
    dx0[...] = dx.reshape(FT, PATCHES, D).astype(BF)


def frame_specs():
    return [
        pl.BlockSpec((1, PATCHES, D), functools.partial(lambda j, i, rows: (rows[FT * i + j], 0, 0), j))
        for j in range(FT)
    ]


def whole(shape):
    return pl.BlockSpec(shape, lambda i, *_: (0,) * len(shape), pipeline_mode=pl.Buffered(1))


def tiles(shape, dim):
    return pl.BlockSpec(shape, lambda i, *_: tuple(i if a == dim else 0 for a in range(len(shape))))


def piece_spec(number, frames, by_tile):
    return pl.BlockSpec((3, frames, D), lambda i, *_: (number, i if by_tile else 0, 0))


ROWS = tiles((TILE, D), 0)
ROWS3 = tiles((TILE, 3 * D), 0)
TURNED = tiles((PT, LIVE, D), 0)


TURN = pltpu.VMEM((D // 128, TILE, 128), F32)


def shape_of(shape, dtype):
    return jax.ShapeDtypeStruct(shape, dtype)


def call(kernel, name, ins, in_specs, outs, out_specs, scratch, flops, prefetch=None):
    moved = sum(a.size * a.dtype.itemsize for a in tuple(ins) + tuple(outs))
    grid_spec = pltpu.PrefetchScalarGridSpec(
        num_scalar_prefetch=0 if prefetch is None else 1,
        grid=(GRID,),
        in_specs=in_specs,
        out_specs=out_specs,
        scratch_shapes=scratch,
    )
    fn = pl.pallas_call(
        kernel,
        grid_spec=grid_spec,
        out_shape=outs,
        name=name,
        cost_estimate=pl.CostEstimate(flops=flops, bytes_accessed=moved, transcendentals=0),
        compiler_params=pltpu.CompilerParams(
            dimension_semantics=("arbitrary",), vmem_limit_bytes=VMEM_LIMIT
        ),
    )
    return fn(*ins) if prefetch is None else fn(prefetch, *ins)


TOKENS = LIVE * PATCHES


def run_frame_forward(frames, rows, mod, wqkv, wo, bo):
    return call(
        frame_forward, "frame_forward",
        [frames] * FT + [mod, wqkv, wo, bo],
        frame_specs() + [piece_spec(0, FT, True), whole((D, 3 * D)), whole((D, D)), whole((1, D))],
        [shape_of((PATCHES, LIVE, D), F32), shape_of((TOKENS, 3 * D), BF), shape_of((TOKENS, D), BF),
         shape_of((TOKENS, D), F32)],
        [tiles((PATCHES, FT, D), 1), ROWS3, ROWS, ROWS],
        [TURN],
        2 * TOKENS * D * 4 * D, rows)


def run_turn_frames(frames, rows):
    return call(
        turn_frames, "turn_frames", [frames] * FT, frame_specs(),
        [shape_of((PATCHES, LIVE, D), F32)], [tiles((PATCHES, FT, D), 1)],
        [TURN], 1000, rows)[0]


def run_time_forward(x1, mod, seg, wqkv, wo, bo):
    return call(
        time_forward, "time_forward",
        [x1, mod, seg, wqkv, wo, bo],
        [TURNED, piece_spec(1, LIVE, False), whole((64, LANES)), whole((D, 3 * D)), whole((D, D)),
         whole((1, D))],
        [shape_of((PATCHES, LIVE, D), F32), shape_of((TOKENS, 3 * D), BF), shape_of((TOKENS, D), BF),
         shape_of((TOKENS, D), F32)],
        [TURNED, ROWS3, ROWS, ROWS],
        [], 2 * TOKENS * D * 4 * D)


def run_mlp(x2, dy, mod, win, bin_, wout, bout):
    return call(
        mlp_both, "mlp_both",
        [x2, dy, mod, win, bin_, wout, bout],
        [TURNED, TURNED, piece_spec(2, LIVE, False), whole((D, FF)), whole((1, FF)), whole((FF, D)),
         whole((1, D))],
        [shape_of((LIVE, PATCHES, D), BF), shape_of((PATCHES, LIVE, D), F32), shape_of((D, FF), F32),
         shape_of((FF, D), F32), shape_of((1, FF), F32), shape_of((1, D), F32), shape_of((3, LIVE, D), F32)],
        [tiles((LIVE, PT, D), 1), TURNED, whole((D, FF)), whole((FF, D)), whole((1, FF)), whole((1, D)),
         whole((3, LIVE, D))],
        [TURN],
        6 * 2 * TOKENS * D * FF)


def run_time_back(x1, dx2, mod, seg, qkv, o, a2, wqkv, wo):
    return call(
        time_back, "time_back",
        [x1, dx2, mod, seg, qkv, o, a2, wqkv, wo],
        [TURNED, TURNED, piece_spec(1, LIVE, False), whole((64, LANES)), ROWS3, ROWS, ROWS,
         whole((D, 3 * D)), whole((D, D))],
        [shape_of((LIVE, PATCHES, D), F32), shape_of((D, 3 * D), F32), shape_of((D, D), F32),
         shape_of((1, D), F32), shape_of((3, LIVE, D), F32)],
        [tiles((LIVE, PT, D), 1), whole((D, 3 * D)), whole((D, D)), whole((1, D)), whole((3, LIVE, D))],
        [pltpu.VMEM((TILE, D), BF), pltpu.VMEM((TILE, 3 * D), BF), TURN],
        2 * 2 * TOKENS * D * 4 * D)


def run_frame_back(frames, rows, dx1, mod, qkv, o, a1, wqkv, wo):
    return call(
        frame_back, "frame_back",
        [frames] * FT + [dx1, mod, qkv, o, a1, wqkv, wo],
        frame_specs() + [tiles((FT, PATCHES, D), 0), piece_spec(0, FT, True), ROWS3, ROWS, ROWS,
                         whole((D, 3 * D)), whole((D, D))],
        [shape_of((LIVE, PATCHES, D), BF), shape_of((D, 3 * D), F32), shape_of((D, D), F32),
         shape_of((1, D), F32), shape_of((3, LIVE, D), F32)],
        [tiles((FT, PATCHES, D), 0), whole((D, 3 * D)), whole((D, D)), whole((1, D)),
         piece_spec(0, FT, True)],
        [pltpu.VMEM((TILE, D), BF), pltpu.VMEM((TILE, 3 * D), BF)],
        2 * 2 * TOKENS * D * 4 * D, rows)


def exchange(x):
    return lax.all_to_all(x, ALL, split_axis=0, concat_axis=0, tiled=True)


def shift_clips(clips, back):
    n = lax.axis_size("narrow")
    parts = [clips[0]]
    for j in range(1, n):
        step = -j if back else j
        parts.append(lax.ppermute(clips[j], "narrow", [(s, (s + step) % n) for s in range(n)]))
    return jnp.stack(parts)


def local(clips, t_emb, lengths, task, w_mod, b_mod, w_qkv_s, w_o_s, b_o_s, w_qkv_t, w_o_t, b_o_t,
          w_in, b_in, w_out, b_out, cotangent):
    n = lax.axis_size("narrow")
    wide = lax.axis_size("wide")
    devices = n * wide
    part = w_mod.shape[0]
    mod_cols = w_mod.shape[1] // devices
    rank = lax.axis_index("narrow")
    slots = jnp.arange(n, dtype=jnp.int32)
    from_clip = (rank - slots) % n
    recv_len = lengths.reshape(n, n)[from_clip, slots]
    recv_task = task.reshape(n, n, FR)[from_clip, slots]
    ends = jnp.cumsum(recv_len)
    starts = ends - recv_len
    ids = jnp.arange(LIVE, dtype=jnp.int32)
    source = jnp.sum((ends[None, :] <= ids[:, None]).astype(jnp.int32), axis=1)
    within = ids - starts[source]
    pack_rows = source * FR + within
    row_choice = source * 2 + recv_task[source, within]
    frame_ids = jnp.arange(FR, dtype=jnp.int32)
    live_back = frame_ids[None, :] < recv_len[:, None]
    unpack_rows = jnp.where(live_back, starts[:, None] + frame_ids[None, :], 0).reshape(-1)
    row_id = jnp.arange(64, dtype=jnp.int32)
    col_id = jnp.arange(LANES, dtype=jnp.int32) % 64
    seg = (
        (row_id[:, None] // LIVE == col_id[None, :] // LIVE)
        & (source[row_id % LIVE][:, None] == source[col_id % LIVE][None, :])
    ).astype(F32)

    def gather(w):
        return lax.all_gather(w, ALL, axis=0, tiled=True)

    frames = shift_clips(clips, False).reshape(n * FR, PATCHES, D)

    wm = jnp.swapaxes(w_mod.reshape(part, devices, mod_cols), 0, 1).reshape(devices, -1)
    emb = jnp.broadcast_to(t_emb.reshape(1, -1), (devices, t_emb.size))
    small = jnp.concatenate([b_o_s, b_o_t, b_in, b_out])
    small_all = jnp.broadcast_to(small[None], (devices, small.size))
    got = exchange(jnp.concatenate([wm, emb, small_all], axis=1))
    wm_cols = got[:, : part * mod_cols].reshape(D, mod_cols)
    emb_all = got[:, part * mod_cols : part * mod_cols + t_emb.size].reshape(-1, D)
    small_got = got[:, part * mod_cols + t_emb.size :]
    b1 = b_o_s.size
    bias_s = small_got[:, :b1].reshape(1, -1).astype(F32)
    bias_t = small_got[:, b1 : 2 * b1].reshape(1, -1).astype(F32)
    bias_in = small_got[:, 2 * b1 : 2 * b1 + b_in.size].reshape(1, -1).astype(F32)
    bias_out = small_got[:, 2 * b1 + b_in.size :].reshape(1, -1).astype(F32)
    emb_f = emb_all.astype(F32)
    silu_low = (emb_f * jax.nn.sigmoid(emb_f)).astype(BF)
    mod_part = dot(silu_low, wm_cols) + b_mod.astype(F32)[None]
    mod_part = mod_part.reshape(wide, n, n, 2, mod_cols)
    mod_part = jnp.stack([jnp.roll(mod_part[:, :, c], c, axis=1) for c in range(n)], axis=2)
    mod_rows = exchange(mod_part.reshape(devices, -1)).reshape(devices, 2 * n, mod_cols)
    mod_rows = jnp.swapaxes(mod_rows, 0, 1).reshape(2 * n, 9, D)
    mod = jnp.swapaxes(mod_rows[row_choice], 0, 1)

    wqkv_s, wo_s = gather(w_qkv_s), gather(w_o_s)
    wqkv_t, wo_t = gather(w_qkv_t), gather(w_o_t)
    win, wout = gather(w_in), gather(w_out)

    x1, qkv1, o1, a1 = run_frame_forward(frames, pack_rows, mod, wqkv_s, wo_s, bias_s)
    x2, qkv2, o2, a2 = run_time_forward(x1, mod, seg, wqkv_t, wo_t, bias_t)
    cots = shift_clips(cotangent, False).reshape(n * FR, PATCHES, D)
    dy = run_turn_frames(cots, pack_rows)
    out, dx2, g_in, g_out, gb_in, gb_out, dmod3 = run_mlp(x2, dy, mod, win, bias_in, wout, bias_out)

    def unpack(packed):
        spread = jnp.take(packed, unpack_rows, axis=0).reshape(n, FR, PATCHES, D)
        spread = jnp.where(live_back[:, :, None, None], spread, jnp.zeros((), packed.dtype))
        return shift_clips(spread, True)

    def scatter(g):
        return lax.psum_scatter(g.astype(BF), ALL, scatter_dimension=0, tiled=True).astype(F32)

    layer_out = unpack(out)
    s_in, s_out = scatter(g_in), scatter(g_out)
    dx1, g_qkv_t, g_o_t, gb_t, dmod2 = run_time_back(x1, dx2, mod, seg, qkv2, o2, a2, wqkv_t, wo_t)
    s_qkv_t, s_o_t = scatter(g_qkv_t), scatter(g_o_t)
    dx0, g_qkv_s, g_o_s, gb_s, dmod1 = run_frame_back(
        frames, pack_rows, dx1, mod, qkv1, o1, a1, wqkv_s, wo_s)
    grad_clips = unpack(dx0)
    s_qkv_s, s_o_s = scatter(g_qkv_s), scatter(g_o_s)

    grad_frames = jnp.swapaxes(jnp.concatenate([dmod1, dmod2, dmod3], axis=0), 0, 1).reshape(LIVE, 9 * D)
    chooser = (row_choice[:, None] == jnp.arange(2 * n, dtype=jnp.int32)[None, :]).astype(F32)
    grad_rows = lax.dot_general(
        chooser, grad_frames, (((0,), (0,)), ((), ())), precision=lax.Precision.HIGHEST
    ).astype(BF)
    d_cols = exchange(jnp.swapaxes(grad_rows.reshape(2 * n, devices, mod_cols), 0, 1).reshape(devices, -1))
    d_cols = d_cols.reshape(wide, n, n, 2, mod_cols)
    d_cols = jnp.stack([jnp.roll(d_cols[:, :, c], -c, axis=1) for c in range(n)], axis=2)
    d_cols = d_cols.reshape(devices * 2 * n, mod_cols)
    grad_b_mod = jnp.sum(d_cols.astype(F32), axis=0)
    gwm_cols = dot_tn(silu_low, d_cols)
    g_emb = dot_nt(d_cols, wm_cols)
    gb_all = jnp.concatenate(
        [gb_s.reshape(devices, -1), gb_t.reshape(devices, -1), gb_in.reshape(devices, -1),
         gb_out.reshape(devices, -1)], axis=1)
    final = exchange(jnp.concatenate(
        [gwm_cols.reshape(devices, -1), g_emb.reshape(devices, -1), gb_all], axis=1))
    cut1 = part * mod_cols
    cut2 = cut1 + t_emb.size
    grad_w_mod = jnp.swapaxes(final[:, :cut1].reshape(devices, part, mod_cols), 0, 1).reshape(part, -1)
    emb_own = t_emb.astype(F32)
    sig = jax.nn.sigmoid(emb_own)
    grad_emb = jnp.sum(final[:, cut1:cut2], axis=0).reshape(t_emb.shape)
    grad_t_emb = (grad_emb * (sig * (1.0 + emb_own * (1.0 - sig)))).astype(BF)
    gb = jnp.sum(final[:, cut2:], axis=0)
    return (
        layer_out,
        grad_clips,
        grad_t_emb,
        grad_w_mod,
        grad_b_mod,
        s_qkv_s,
        s_o_s,
        gb[:b1],
        s_qkv_t,
        s_o_t,
        gb[b1 : 2 * b1],
        s_in,
        gb[2 * b1 : 2 * b1 + b_in.size],
        s_out,
        gb[2 * b1 + b_in.size :],
    )


def solution(mesh):
    full = P(ALL)
    placed = (full, full, P("wide"), P("wide")) + (full,) * 13
    return jax.shard_map(local, mesh=mesh, in_specs=placed, out_specs=(full,) * 15, check_vma=False)
```

time: 1780 us -> 1320 us (0.74)
  waiting for transfers between devices: 242 us -> 681 us
  local copies, waits for them, and re-layouts: 489 us -> 67.4 us
  Pallas kernels: 0 us -> 416 us
  blocking collectives: 416 us -> 0 us
  matrix products: 405 us -> 1.4 us
  other arithmetic: 178 us -> 96.4 us
    pallas_call x0 -> x6, Pallas kernels: none -> 416 us  [call(): return fn(*ins) if prefetch is None else fn(prefetch, *ins)]
    dot_general x34 -> x3, matrix products: 405 us -> 0.94 us  [the longest x1 0.33 us: dot(): lax.dot_general(a, b, (((1,), (0,)), ((), ())), preferred_element_type=F32)]
    reduce_scatter x7 -> x6, waiting for transfers between devices: 237 us -> 503 us  [scatter(): lax.psum_scatter(g.astype(BF), ALL, scatter_dimension=0, tiled=True)]
    convert_element_type x11 -> x5, local copies, waits for them, and re-layouts: 257 us -> 2.88 us  [the longest x1 0.69 us: local(): bias_in = small_got[:, 2 * b1:2 * b1 + b_in.size].reshape(1, -1).astype(F32)]
    unnamed x2 -> x0, blocking collectives: 222 us -> none
    all_to_all x2 -> x0, blocking collectives: 193 us -> none  [the longest x1 97.3 us: local(): lax.all_to_all(send_input_grad, 'narrow', split_axis=0, concat_axis=0, ti...]
    ppermute x0 -> x12, waiting for transfers between devices: none -> 136 us  [shift_clips(): lax.ppermute(clips[j], 'narrow', [(s, (s + step) % n) for s in range(n)])]
    reshape x10 -> x23, local copies, waits for them, and re-layouts: 109 us -> 9.58 us  [the longest x2 2.39 us: local(): w_mod.reshape(part, devices, mod_cols)]
  transfers between devices with their start and end apart: 18 -> 28, of which waited for: 2 -> 11; matrix products, arithmetic and copies ran while one was open for 50% -> 12% of each run, Pallas kernels for 0% -> 11%
where the time goes in v1:
time: 1320 us; the launch traced here: 1310 us
  waiting for transfers between devices  681 us (52%)
  Pallas kernels  416 us (32%)
  other arithmetic  96.4 us (7%)
  local copies, waits for them, and re-layouts  67.4 us (5%)
  starting transfers between devices  30.1 us (2%)
  between operations  15.3 us (1%)
    reduce_scatter x6, waiting for transfers between devices, scatter(): lax.psum_scatter(g.astype(BF), ALL, scatter_dimension=0, tiled=True)  503 us
    pallas_call x6, Pallas kernels, call(): return fn(*ins) if prefetch is None else fn(prefetch, *ins)  416 us
    ppermute x12, waiting for transfers between devices, shift_clips(): lax.ppermute(clips[j], 'narrow', [(s, (s + step) % n) for s in range(n)])  136 us
    all_gather x6, waiting for transfers between devices, gather(): return lax.all_gather(w, ALL, axis=0, tiled=True)  36.9 us
    convert_element_type x6, other arithmetic, scatter(): g.astype(BF)  27.6 us
  transfers between devices with their start and end apart: 28, of which 11 were waited for; matrix products, arithmetic and copies ran while one was open for 12% of the time, Pallas kernels for 11%

profile of v1, /device:TPU:1, one launch (start us, length us, event | category | flops | bytes accessed | tf_op | source)
XLA Modules:
  0.0 1306.7 jit_solution(15459827995277290978)
XLA Ops:
  11.2 2.2 reshape.533
  17.7 1.7 reshape.665
  19.4 7.1 all-to-all-start
  26.5 5.7 fusion.29
  32.2 1.6 collective-permute-start
  33.9 5.2 fusion.28
  45.5 2.6 fusion.25
  48.9 3.2 multiply_add_fusion
  52.8 5.1 reshape.666
  60.5 91.3 %collective-permute-done.3 = bf16[16,64,768]{2,1,0:T(8,128)(2,1)} collective-permute-done((bf16[16,64,768]{2,1,0:T(8,128)(2,1)}, bf16[16,64,768]{2,1,0:T(8,128)(2,1)}, u32[]{:S(2)}, u32[]{:S(2)}) %collective-permute-start.3) | collective-permute-done | bytes 1572896 | tf_op jit(solution)/shard_map/ppermute | solution.py:415
  155.1 4.1 all-to-all-start.1
  163.7 25.7 %collective-permute-done.4 = bf16[16,64,768]{2,1,0:T(8,128)(2,1)} collective-permute-done((bf16[16,64,768]{2,1,0:T(8,128)(2,1)}, bf16[16,64,768]{2,1,0:T(8,128)(2,1)}, u32[]{:S(2)}, u32[]{:S(2)}) %collective-permute-start.4) | collective-permute-done | bytes 1572896 | tf_op jit(solution)/shard_map/ppermute | solution.py:415
  189.5 5.9 pad_maximum_fusion.1
  195.4 7.0 turn_frames.1.dy
  202.4 6.5 pad_maximum_fusion
  212.2 72.0 %frame_forward.1 = (f32[64,32,768]{2,1,0:T(8,128)}, bf16[2048,2304]{1,0:T(8,128)(2,1)}, bf16[2048,768]{1,0:T(8,128)(2,1)}, f32[2048,768]{1,0:T(8,128)}) custom-call(s32[32]{0:T(128)} %get-tuple-element.103.rows_ref, bf16[64,64,768]{2,1,0:T(8,128)(2,1)} %bitcast.147, bf16[64,64,768]{2,1,0:T(8,128)(2,1)} %bitcast.148, bf16[64,64,768]{2,1,0:T(8,128)(2,1)} %bitcast.149, ...), custom_call_target="tpu_custom_call" | custom-call | flops 9663676416 | bytes 81103872 | tf_op jit(solution)/shard_map/frame_forward/pallas_call | solution.py:328
  284.3 69.9 %time_forward.1 = (f32[64,32,768]{2,1,0:T(8,128)}, bf16[2048,2304]{1,0:T(8,128)(2,1)}, bf16[2048,768]{1,0:T(8,128)(2,1)}, f32[2048,768]{1,0:T(8,128)}) custom-call(f32[64,32,768]{2,1,0:T(8,128)} %get-tuple-element.41.x1, f32[9,32,768]{2,1,0:T(8,128)} %bitcast.174, f32[64,128]{1,0:T(8,128)} %and_convert_fusion.seg, ...), custom_call_target="tpu_custom_call" | custom-call | flops 9663676416 | bytes 37096448 | tf_op jit(solution)/shard_map/time_forward/pallas_call | solution.py:328
  354.2 36.9 %all-gather.17.cloned.1.call-done.wout = bf16[3072,768]{1,0:T(8,128)(2,1)} async-done(((bf16[96,768]{1,0:T(8,128)(2,1)}), bf16[3072,768]{1,0:T(8,128)(2,1)}) %all-gather.17.cloned.1.call-update) | async-done | bytes 4718608 | tf_op jit(solution)/shard_map/all_gather | solution.py:449
  391.1 85.3 %mlp_both.1 = (bf16[32,64,768]{2,1,0:T(8,128)(2,1)}, f32[64,32,768]{2,1,0:T(8,128)}, f32[768,3072]{1,0:T(8,128)}, f32[3072,768]{1,0:T(8,128)}, f32[1,3072]{1,0:T...) custom-call(f32[64,32,768]{2,1,0:T(8,128)} %get-tuple-element.42.x2, f32[64,32,768]{2,1,0:T(8,128)} %turn_frames.1.dy, ...), custom_call_target="tpu_custom_call" | custom-call | flops 57982058496 | bytes 51542016 | tf_op jit(solution)/shard_map/mlp_both/pallas_call | solution.py:328
  476.5 93.2 %time_back.1 = (f32[32,64,768]{2,1,0:T(8,128)}, f32[768,2304]{1,0:T(8,128)}, f32[768,768]{1,0:T(8,128)}, f32[1,768]{1,0:T(1,128)}, f32[3,32,768]{2,1,0:T(8,128)}) custom-call(f32[64,32,768]{2,1,0:T(8,128)} %get-tuple-element.41.x1, f32[64,32,768]{2,1,0:T(8,128)} %get-tuple-element.44.dx2, f32[9,32,768]{2,1,0:T(8,128)} %bitcast.176, ...), custom_call_target="tpu_custom_call" | custom-call | flops 19327352832 | bytes 53120000 | tf_op jit(solution)/shard_map/time_back/pallas_call | solution.py:328
  569.6 88.1 %frame_back.1 = (bf16[32,64,768]{2,1,0:T(8,128)(2,1)}, f32[768,2304]{1,0:T(8,128)}, f32[768,768]{1,0:T(8,128)}, f32[1,768]{1,0:T(1,128)}, f32[3,32,768]{2,1,0:T(8,128)}) custom-call(s32[32]{0:T(128)} %get-tuple-element.103.rows_ref, bf16[64,64,768]{2,1,0:T(8,128)(2,1)} %bitcast.155, bf16[64,64,768]{2,1,0:T(8,128)(2,1)} %bitcast.156, ...), custom_call_target="tpu_custom_call" | custom-call | flops 19327352832 | bytes 93981696 | tf_op jit(solution)/shard_map/frame_back/pallas_call | solution.py:328
  657.8 3.0 convert_element_type.111
  662.0 5.2 convert_element_type.109
  667.3 5.3 convert_element_type.113
  672.7 6.6 convert_element_type.117
  683.9 2.9 all-to-all-start.2
  687.2 5.7 gather_fusion.7
  692.9 3.7 gather_fusion.6
  696.5 6.4 convert_element_type.119
  703.0 10.5 broadcast_select_fusion
  715.1 8.3 broadcast_select_fusion.2
  723.3 2.3 fusion.26
  731.4 1.7 concatenate.54
  733.1 2.1 all_to_all.35
  735.2 5.8 all-to-all-start.3
  743.1 5.2 fusion.27
  749.7 3.0 collective-permute-done.9
  752.7 3.5 reduce-scatter.9.cloned.1.call-done
  757.5 101.1 %reduce-scatter.13.cloned.1.call-done = bf16[24,768]{1,0:T(8,128)(2,1)} async-done(((bf16[768,768]{1,0:T(8,128)(2,1)}), bf16[24,768]{1,0:T(8,128)(2,1)}) %reduce-scatter.13.cloned.1.call-update) | async-done | bytes 36880 | tf_op jit(solution)/shard_map/reduce_scatter | solution.py:491
  860.0 5.9 pad_maximum_fusion.3
  865.9 16.3 %collective-permute-done.8 = bf16[16,64,768]{2,1,0:T(8,128)(2,1)} collective-permute-done((bf16[16,64,768]{2,1,0:T(8,128)(2,1)}, bf16[16,64,768]{2,1,0:T(8,128)(2,1)}, u32[]{:S(2)}, u32[]{:S(2)}) %collective-permute-start.8) | collective-permute-done | bytes 1572896 | tf_op jit(solution)/shard_map/ppermute | solution.py:415
  882.2 6.0 pad_maximum_fusion.2
  894.2 72.4 %reduce-scatter.7.cloned.1.call-done = bf16[24,2304]{1,0:T(8,128)(2,1)} async-done(((bf16[768,2304]{1,0:T(8,128)(2,1)}), bf16[24,2304]{1,0:T(8,128)(2,1)}) %reduce-scatter.7.cloned.1.call-update) | async-done | bytes 110608 | tf_op jit(solution)/shard_map/reduce_scatter | solution.py:491
  968.2 106.1 %reduce-scatter.11.cloned.1.call-done = bf16[24,2304]{1,0:T(8,128)(2,1)} async-done(((bf16[768,2304]{1,0:T(8,128)(2,1)}), bf16[24,2304]{1,0:T(8,128)(2,1)}) %reduce-scatter.11.cloned.1.call-update) | async-done | bytes 110608 | tf_op jit(solution)/shard_map/reduce_scatter | solution.py:491
  1075.9 110.3 %reduce-scatter.15.cloned.1.call-done = bf16[24,3072]{1,0:T(8,128)(2,1)} async-done(((bf16[768,3072]{1,0:T(8,128)(2,1)}), bf16[24,3072]{1,0:T(8,128)(2,1)}) %reduce-scatter.15.cloned.1.call-update) | async-done | bytes 147472 | tf_op jit(solution)/shard_map/reduce_scatter | solution.py:491
  1186.2 1.6 convert_element_type.118
  1187.9 110.1 %reduce-scatter.17.cloned.1.call-done = bf16[96,768]{1,0:T(8,128)(2,1)} async-done(((bf16[3072,768]{1,0:T(8,128)(2,1)}), bf16[96,768]{1,0:T(8,128)(2,1)}) %reduce-scatter.17.cloned.1.call-update) | async-done | bytes 147472 | tf_op jit(solution)/shard_map/reduce_scatter | solution.py:491
  1298.0 1.6 convert_element_type.120
  (219 shorter events, 58.5 us)
Async XLA Ops:
  7.2 34.8 %copy-start = (s32[16,16]{1,0:T(8,128)S(1)}, s32[16,16]{1,0:T(8,128)}, u32[]{:S(2)}) copy-start(s32[16,16]{1,0:T(8,128)} %param.22) | copy-start | bytes 3076
  7.2 205.0 %all-gather.9.cloned.1.call-start = ((), (), s32[]{:S(2)}) async-start(), calls=%async_computation.11 | async-start | bytes 1216512 | tf_op jit(solution)/shard_map/all_gather | solution.py:449
  7.9 204.3 %all-gather.7.cloned.1.call-start = ((), (), s32[]{:S(2)}) async-start(), calls=%async_computation.10 | async-start | bytes 3649536 | tf_op jit(solution)/shard_map/all_gather | solution.py:449
  8.7 275.6 %all-gather.13.cloned.1.call-start = ((), (), s32[]{:S(2)}) async-start(), calls=%async_computation.13 | async-start | bytes 1216512 | tf_op jit(solution)/shard_map/all_gather | solution.py:449
  9.4 274.9 %all-gather.11.cloned.1.call-start = ((), (), s32[]{:S(2)}) async-start(), calls=%async_computation.12 | async-start | bytes 3649536 | tf_op jit(solution)/shard_map/all_gather | solution.py:449
  10.0 344.2 %all-gather.15.cloned.1.call-start = ((), (), s32[]{:S(2)}) async-start(), calls=%async_computation.14 | async-start | bytes 4866048 | tf_op jit(solution)/shard_map/all_gather | solution.py:449
  10.6 380.5 %all-gather.17.cloned.1.call-start = ((), (), s32[]{:S(2)}) async-start(), calls=%async_computation.15 | async-start | bytes 4866048 | tf_op jit(solution)/shard_map/all_gather | solution.py:449
  19.4 33.4 %all-to-all-start = ((bf16[32,2,5748]{2,1,0:T(2,128)(2,1)}), bf16[32,2,5748]{2,1,0:T(2,128)(2,1)}, u32[]{:S(2)}, u32[]{:S(2)}) async-start(bf16[32,2,5748]{2,1,0:T(2,128)(2,1)} %reshape.665), calls=%async_computation | async-start | bytes 1474560 | tf_op jit(solution)/shard_map/all_to_all | solution.py:407
  32.2 170.2 %collective-permute-start = (bf16[16,64,768]{2,1,0:T(8,128)(2,1)}, bf16[16,64,768]{2,1,0:T(8,128)(2,1)}, u32[]{:S(2)}, u32[]{:S(2)}) collective-permute-start(bf16[16,64,768]{2,1,0:T(8,128)(2,1)} %get-tuple-element.81), channel_id=1, source_target_pairs={{0,1},{1,2},{2,3},{3,0},{4,5},{5,6},{6,7},{7,4},{8,9},{9,10},{10,1... | collective-permute-start | bytes 4718600 | tf_op jit(solution)/shard_map/ppermute | solution.py:415
  33.8 7.4 copy-start.23
  33.8 7.4 copy-start.22
  33.8 168.5 %collective-permute-start.1 = (bf16[16,64,768]{2,1,0:T(8,128)(2,1)}, bf16[16,64,768]{2,1,0:T(8,128)(2,1)}, u32[]{:S(2)}, u32[]{:S(2)}) collective-permute-start(bf16[16,64,768]{2,1,0:T(8,128)(2,1)} %get-tuple-element.83), channel_id=1, source_target_pairs={{0,2},{1,3},{2,0},{3,1},{4,6},{5,7},{6,4},{7,5},{8,10},{9,11},{10,... | collective-permute-start | bytes 4718600 | tf_op jit(solution)/shard_map/ppermute | solution.py:415
  39.1 112.8 %collective-permute-start.3 = (bf16[16,64,768]{2,1,0:T(8,128)(2,1)}, bf16[16,64,768]{2,1,0:T(8,128)(2,1)}, u32[]{:S(2)}, u32[]{:S(2)}) collective-permute-start(bf16[16,64,768]{2,1,0:T(8,128)(2,1)} %get-tuple-element.77), channel_id=1, source_target_pairs={{0,1},{1,2},{2,3},{3,0},{4,5},{5,6},{6,7},{7,4},{8,9},{9,10},{10,1... | collective-permute-start | bytes 4718600 | tf_op jit(solution)/shard_map/ppermute | solution.py:415
  39.5 150.0 %collective-permute-start.4 = (bf16[16,64,768]{2,1,0:T(8,128)(2,1)}, bf16[16,64,768]{2,1,0:T(8,128)(2,1)}, u32[]{:S(2)}, u32[]{:S(2)}) collective-permute-start(bf16[16,64,768]{2,1,0:T(8,128)(2,1)} %get-tuple-element.79), channel_id=1, source_target_pairs={{0,2},{1,3},{2,0},{3,1},{4,6},{5,7},{6,4},{7,5},{8,10},{9,11},{10,... | collective-permute-start | bytes 4718600 | tf_op jit(solution)/shard_map/ppermute | solution.py:415
  40.9 148.6 %collective-permute-start.5 = (bf16[16,64,768]{2,1,0:T(8,128)(2,1)}, bf16[16,64,768]{2,1,0:T(8,128)(2,1)}, u32[]{:S(2)}, u32[]{:S(2)}) collective-permute-start(bf16[16,64,768]{2,1,0:T(8,128)(2,1)} %get-tuple-element.78), channel_id=1, source_target_pairs={{0,3},{1,0},{2,1},{3,2},{4,7},{5,4},{6,5},{7,6},{8,11},{9,8},{10,9... | collective-permute-start | bytes 4718600 | tf_op jit(solution)/shard_map/ppermute | solution.py:415
  42.0 10.8 copy-start.20
  43.7 1.9 copy-start.13
  59.1 136.3 %copy-start.3 = (bf16[256,768]{1,0:T(8,128)(2,1)}, bf16[256,768]{1,0:T(8,128)(2,1)S(1)}, u32[]{:S(2)}) copy-start(bf16[256,768]{1,0:T(8,128)(2,1)S(1)} %convert_element_type.94) | copy-start | bytes 1179652
  59.8 135.6 %copy-start.5 = (bf16[768,216]{1,0:T(8,128)(2,1)}, bf16[768,216]{1,0:T(8,128)(2,1)S(1)}, u32[]{:S(2)}) copy-start(bf16[768,216]{1,0:T(8,128)(2,1)S(1)} %reshape.535) | copy-start | bytes 995332
  151.8 50.5 %collective-permute-start.2 = (bf16[16,64,768]{2,1,0:T(8,128)(2,1)}, bf16[16,64,768]{2,1,0:T(8,128)(2,1)}, u32[]{:S(2)}, u32[]{:S(2)}) collective-permute-start(bf16[16,64,768]{2,1,0:T(8,128)(2,1)} %get-tuple-element.82), channel_id=1, source_target_pairs={{0,3},{1,0},{2,1},{3,2},{4,7},{5,4},{6,5},{7,6},{8,11},{9,8},{10,9... | collective-permute-start | bytes 4718600 | tf_op jit(solution)/shard_map/ppermute | solution.py:415
  155.1 53.9 %all-to-all-start.1 = ((f32[32,1,1728]{2,1,0:T(1,128)}), f32[32,1,1728]{2,1,0:T(1,128)S(1)}, u32[]{:S(2)}, u32[]{:S(2)}) async-start(f32[32,1,1728]{2,1,0:T(1,128)} %all_to_all.38), calls=%async_computation.1 | async-start | bytes 458752 | tf_op jit(solution)/shard_map/all_to_all | solution.py:407
  159.2 596.9 %reduce-scatter.9.cloned.1.call-start = ((), (), s32[]{:S(2)}) async-start(), calls=%async_computation.17 | async-start | bytes 1216512 | tf_op jit(solution)/shard_map/reduce_scatter | solution.py:491
  657.8 3.0 copy-start.8
  660.8 197.8 %reduce-scatter.13.cloned.1.call-start = ((), (), s32[]{:S(2)}) async-start(), calls=%async_computation.19 | async-start | bytes 1216512 | tf_op jit(solution)/shard_map/reduce_scatter | solution.py:491
  662.0 304.6 %reduce-scatter.7.cloned.1.call-start = ((), (), s32[]{:S(2)}) async-start(), calls=%async_computation.16 | async-start | bytes 3649536 | tf_op jit(solution)/shard_map/reduce_scatter | solution.py:491
  667.3 407.0 %reduce-scatter.11.cloned.1.call-start = ((), (), s32[]{:S(2)}) async-start(), calls=%async_computation.18 | async-start | bytes 3649536 | tf_op jit(solution)/shard_map/reduce_scatter | solution.py:491
  672.6 513.6 %reduce-scatter.15.cloned.1.call-start = ((), (), s32[]{:S(2)}) async-start(), calls=%async_computation.20 | async-start | bytes 4866048 | tf_op jit(solution)/shard_map/reduce_scatter | solution.py:491
  679.3 1.1 copy-start.10
  679.3 1.1 copy-start.11
  679.3 1.3 copy-start.19
  683.9 42.0 %all-to-all-start.2 = ((bf16[32,2,864]{2,1,0:T(2,128)(2,1)}), bf16[32,2,864]{2,1,0:T(2,128)(2,1)S(1)}, u32[]{:S(2)}, u32[]{:S(2)}) async-start(bf16[32,2,864]{2,1,0:T(2,128)(2,1)} %reshape.667), calls=%async_computation.2 | async-start | bytes 229376 | tf_op jit(solution)/shard_map/all_to_all | solution.py:407
  686.9 611.1 %reduce-scatter.17.cloned.1.call-start = ((), (), s32[]{:S(2)}) async-start(), calls=%async_computation.21 | async-start | bytes 4866048 | tf_op jit(solution)/shard_map/reduce_scatter | solution.py:491
  687.2 5.7 copy-start.2
  702.9 10.5 copy-start.18
  702.9 10.6 copy-start.17
  703.0 11.2 copy-start.15
  703.0 12.0 copy-start.16
  723.3 5.2 copy-start.6
  725.6 4.2 copy-start.4
  725.6 27.0 %collective-permute-start.9 = (bf16[16,64,768]{2,1,0:T(8,128)(2,1)}, bf16[16,64,768]{2,1,0:T(8,128)(2,1)}, u32[]{:S(2)}, u32[]{:S(2)}) collective-permute-start(bf16[16,64,768]{2,1,0:T(8,128)(2,1)} %get-tuple-element.71), channel_id=1, source_target_pairs={{0,3},{1,0},{2,1},{3,2},{4,7},{5,4},{6,5},{7,6},{8,11},{9,8},{10,9... | collective-permute-start | bytes 4718600 | tf_op jit(solution)/shard_map/ppermute | solution.py:415
  735.2 153.0 %all-to-all-start.3 = ((f32[32,1,11496]{2,1,0:T(1,128)}), f32[32,1,11496]{2,1,0:T(1,128)}, u32[]{:S(2)}, u32[]{:S(2)}) async-start(f32[32,1,11496]{2,1,0:T(1,128)} %all_to_all.35), calls=%async_computation.3 | async-start | bytes 2949120 | tf_op jit(solution)/shard_map/all_to_all | solution.py:407
  741.1 118.9 %collective-permute-start.10 = (bf16[16,64,768]{2,1,0:T(8,128)(2,1)}, bf16[16,64,768]{2,1,0:T(8,128)(2,1)}, u32[]{:S(2)}, u32[]{:S(2)}) collective-permute-start(bf16[16,64,768]{2,1,0:T(8,128)(2,1)} %get-tuple-element.70), channel_id=1, source_target_pairs={{0,2},{1,3},{2,0},{3,1},{4,6},{5,7},{6,4},{7,5},{8,10},{9,11},{10,... | collective-permute-start | bytes 4718600 | tf_op jit(solution)/shard_map/ppermute | solution.py:415
  742.5 117.5 %collective-permute-start.11 = (bf16[16,64,768]{2,1,0:T(8,128)(2,1)}, bf16[16,64,768]{2,1,0:T(8,128)(2,1)}, u32[]{:S(2)}, u32[]{:S(2)}) collective-permute-start(bf16[16,64,768]{2,1,0:T(8,128)(2,1)} %get-tuple-element.69), channel_id=1, source_target_pairs={{0,1},{1,2},{2,3},{3,0},{4,5},{5,6},{6,7},{7,4},{8,9},{9,10},{10,1... | collective-permute-start | bytes 4718600 | tf_op jit(solution)/shard_map/ppermute | solution.py:415
  748.3 117.6 %collective-permute-start.6 = (bf16[16,64,768]{2,1,0:T(8,128)(2,1)}, bf16[16,64,768]{2,1,0:T(8,128)(2,1)}, u32[]{:S(2)}, u32[]{:S(2)}) collective-permute-start(bf16[16,64,768]{2,1,0:T(8,128)(2,1)} %get-tuple-element.75), channel_id=1, source_target_pairs={{0,3},{1,0},{2,1},{3,2},{4,7},{5,4},{6,5},{7,6},{8,11},{9,8},{10,9... | collective-permute-start | bytes 4718600 | tf_op jit(solution)/shard_map/ppermute | solution.py:415
  748.3 117.5 %collective-permute-start.7 = (bf16[16,64,768]{2,1,0:T(8,128)(2,1)}, bf16[16,64,768]{2,1,0:T(8,128)(2,1)}, u32[]{:S(2)}, u32[]{:S(2)}) collective-permute-start(bf16[16,64,768]{2,1,0:T(8,128)(2,1)} %get-tuple-element.74), channel_id=1, source_target_pairs={{0,2},{1,3},{2,0},{3,1},{4,6},{5,7},{6,4},{7,5},{8,10},{9,11},{10,... | collective-permute-start | bytes 4718600 | tf_op jit(solution)/shard_map/ppermute | solution.py:415
  752.7 129.5 %collective-permute-start.8 = (bf16[16,64,768]{2,1,0:T(8,128)(2,1)}, bf16[16,64,768]{2,1,0:T(8,128)(2,1)}, u32[]{:S(2)}, u32[]{:S(2)}) collective-permute-start(bf16[16,64,768]{2,1,0:T(8,128)(2,1)} %get-tuple-element.73), channel_id=1, source_target_pairs={{0,1},{1,2},{2,3},{3,0},{4,5},{5,6},{6,7},{7,4},{8,9},{9,10},{10,1... | collective-permute-start | bytes 4718600 | tf_op jit(solution)/shard_map/ppermute | solution.py:415
  889.7 3.8 copy-start.12
  889.7 410.0 %copy-start.1 = (s32[16,16]{1,0:T(8,128)S(1)}, s32[16,16]{1,0:T(8,128)}, u32[]{:S(2)}) copy-start(s32[16,16]{1,0:T(8,128)} %param.22) | copy-start | bytes 3076
  (4 other events, 3.1 us)
Sparse Core Ops, SparseCore 0:
  10.9 59.5 all-gather.8
  73.4 66.6 all-gather.6
  143.0 54.8 all-gather.12
  200.7 59.7 all-gather.10
  263.2 62.9 all-gather.14
  329.0 62.1 all-gather.16
  660.9 95.1 reduce-scatter.8
  761.2 97.3 reduce-scatter.12
  864.0 102.5 reduce-scatter.6
  971.8 102.4 reduce-scatter.10
  1079.8 106.4 reduce-scatter.14
  1191.6 106.4 reduce-scatter.16

commit v2 on v1

--- a/solution.py
+++ b/solution.py
@@ -224,18 +224,17 @@
     dx2[...] = (grad + back).reshape(PT, LIVE, D)
 
 
-def attn_back_tile(x, grad, shift, scale, gate, branch, qkv, o, wqkv, wo, gwqkv, gwo, gbo, do, dqkv, mask):
+def attn_back_tile(x, grad, shift, scale, gate, branch, qkv, o, wqkv, wo, gw, gbo, do, dqkv, mask):
     first = pl.program_id(0) == 0
 
     @pl.when(first)
     def _():
-        gwqkv[...] = jnp.zeros_like(gwqkv)
-        gwo[...] = jnp.zeros_like(gwo)
+        gw[...] = jnp.zeros_like(gw)
         gbo[...] = jnp.zeros_like(gbo)
 
     da = (grad * gate).astype(BF)
     do[...] = dot_nt(da, wo[...]).astype(BF)
-    gwo[...] += dot_tn(o[...], da)
+    gw[:, 3 * D :] += dot_tn(o[...], da)
     gbo[...] += jnp.sum(da.astype(F32), axis=0, keepdims=True)
     attend_back(qkv, do, dqkv, mask)
     xhat, rstd = normalise(x)
@@ -244,20 +243,20 @@
     for j in range(3):
         cols = slice(j * D, (j + 1) * D)
         part = dqkv[:, cols]
-        gwqkv[:, cols] += dot_tn(h, part)
+        gw[:, cols] += dot_tn(h, part)
         dh = dh + dot_nt(part, wqkv[:, cols])
     dx = grad + norm_back(dh * (1.0 + scale), xhat, rstd)
     return dx, dh, dh * xhat, grad * branch
 
 
-def time_back(x1, dx2, mod, seg, qkv, o, a2, wqkv, wo, dx1, gwqkv, gwo, gbo, dmod, do, dqkv, scratch):
+def time_back(x1, dx2, mod, seg, qkv, o, a2, wqkv, wo, dx1, gw, gbo, dmod, do, dqkv, scratch):
     @pl.when(pl.program_id(0) == 0)
     def _():
         dmod[...] = jnp.zeros_like(dmod)
 
     dx, d_shift, d_scale, d_gate = attn_back_tile(
         x1[...].reshape(TILE, D), dx2[...].reshape(TILE, D), per_patch(mod[0]), per_patch(mod[1]),
-        per_patch(mod[2]), a2[...], qkv, o, wqkv, wo, gwqkv, gwo, gbo, do, dqkv, attn_mask(seg))
+        per_patch(mod[2]), a2[...], qkv, o, wqkv, wo, gw, gbo, do, dqkv, attn_mask(seg))
     dmod[0] += sum_groups(d_shift)
     dmod[1] += sum_groups(d_scale)
     dmod[2] += sum_groups(d_gate)
@@ -265,10 +264,10 @@
 
 
 def frame_back(rows_ref, *refs):
-    x_refs, (dx1, mod, qkv, o, a1, wqkv, wo, dx0, gwqkv, gwo, gbo, dmod, do, dqkv) = refs[:FT], refs[FT:]
+    x_refs, (dx1, mod, qkv, o, a1, wqkv, wo, dx0, gw, gbo, dmod, do, dqkv) = refs[:FT], refs[FT:]
     dx, d_shift, d_scale, d_gate = attn_back_tile(
         frames_of(x_refs), dx1[...].reshape(TILE, D), per_frame(mod[0]), per_frame(mod[1]),
-        per_frame(mod[2]), a1[...], qkv, o, wqkv, wo, gwqkv, gwo, gbo, do, dqkv, None)
+        per_frame(mod[2]), a1[...], qkv, o, wqkv, wo, gw, gbo, do, dqkv, None)
     dmod[0] = sum_patches(d_shift)
     dmod[1] = sum_patches(d_scale)
     dmod[2] = sum_patches(d_gate)
@@ -382,9 +381,8 @@
         [x1, dx2, mod, seg, qkv, o, a2, wqkv, wo],
         [TURNED, TURNED, piece_spec(1, LIVE, False), whole((64, LANES)), ROWS3, ROWS, ROWS,
          whole((D, 3 * D)), whole((D, D))],
-        [shape_of((LIVE, PATCHES, D), F32), shape_of((D, 3 * D), F32), shape_of((D, D), F32),
-         shape_of((1, D), F32), shape_of((3, LIVE, D), F32)],
-        [tiles((LIVE, PT, D), 1), whole((D, 3 * D)), whole((D, D)), whole((1, D)), whole((3, LIVE, D))],
+        [shape_of((LIVE, PATCHES, D), F32), shape_of((D, 4 * D), F32), shape_of((1, D), F32), shape_of((3, LIVE, D), F32)],
+        [tiles((LIVE, PT, D), 1), whole((D, 4 * D)), whole((1, D)), whole((3, LIVE, D))],
         [pltpu.VMEM((TILE, D), BF), pltpu.VMEM((TILE, 3 * D), BF), TURN],
         2 * 2 * TOKENS * D * 4 * D)
 
@@ -395,12 +393,285 @@
         [frames] * FT + [dx1, mod, qkv, o, a1, wqkv, wo],
         frame_specs() + [tiles((FT, PATCHES, D), 0), piece_spec(0, FT, True), ROWS3, ROWS, ROWS,
                          whole((D, 3 * D)), whole((D, D))],
-        [shape_of((LIVE, PATCHES, D), BF), shape_of((D, 3 * D), F32), shape_of((D, D), F32),
-         shape_of((1, D), F32), shape_of((3, LIVE, D), F32)],
-        [tiles((FT, PATCHES, D), 0), whole((D, 3 * D)), whole((D, D)), whole((1, D)),
-         piece_spec(0, FT, True)],
+        [shape_of((LIVE, PATCHES, D), BF), shape_of((D, 4 * D), F32), shape_of((1, D), F32), shape_of((3, LIVE, D), F32)],
+        [tiles((FT, PATCHES, D), 0), whole((D, 4 * D)), whole((1, D)), piece_spec(0, FT, True)],
         [pltpu.VMEM((TILE, D), BF), pltpu.VMEM((TILE, 3 * D), BF)],
         2 * 2 * TOKENS * D * 4 * D, rows)
+
+
+MESH = pl.DeviceIdType.MESH
+ANY = pl.BlockSpec(memory_space=pl.ANY)
+
+
+def place_of(wide):
+    ring = wide
+    turn = ring // 2
+    w = lax.axis_index("wide")
+    k = lax.axis_index("narrow")
+    z, y = w // 2, w % 2
+    r = z + y * (ring - 1 - 2 * z)
+
+    def wide_at(position):
+        side = position // turn
+        return 2 * ((1 - side) * position + side * (ring - 1 - position)) + side
+
+    return w, k, r, k // 2, k % 2, wide_at
+
+
+def greet(peers):
+    barrier = pltpu.get_barrier_semaphore()
+    for peer in peers:
+        pl.semaphore_signal(barrier, inc=1, device_id=peer, device_id_type=MESH)
+    pl.semaphore_wait(barrier, len(peers))
+
+
+def send(src, dst, send_sem, recv_sem, peer):
+    return pltpu.make_async_remote_copy(
+        src_ref=src, dst_ref=dst, send_sem=send_sem, recv_sem=recv_sem, device_id=peer, device_id_type=MESH
+    )
+
+
+def gather_kernel(ring, n, heights, ways, *refs):
+    count = len(heights)
+    clips, shards = refs[0], refs[1 : 1 + count]
+    frames, full = refs[1 + count], refs[2 + count : 2 + 2 * count]
+    clip_buf, bufs = refs[2 + 2 * count], refs[3 + 2 * count : 3 + 3 * count]
+    ring_s, ring_r, core_s, core_r, x_s, x_r, clip_s, clip_r, load_sem, keep_sem = refs[3 + 3 * count :]
+    w, k, r, x, c, wide_at = place_of(ring)
+    other_x = (w, 2 * (1 - x) + c)
+    other_c = (w, 2 * x + 1 - c)
+    steps = ((wide_at((r + 1) % ring), k), (wide_at((r + ring - 1) % ring), k))
+    greet(steps + tuple((w, (k + j) % n) for j in range(1, n)))
+
+    def rows(t, position, column):
+        block = 4 * wide_at(position) + 2 * column + c
+        return pl.ds(pl.multiple_of(block * heights[t], 8), heights[t])
+
+    def ring_copy(t, b, s, src=None):
+        place = (r + ring - s) % ring if ways[t] == 0 else (r + s) % ring
+        dst = full[t].at[rows(t, place, x if b == 0 else 1 - x)]
+        return send(dst if src is None else src, dst, ring_s.at[t, b, s], ring_r.at[t, b, s], steps[ways[t]])
+
+    def core_copy(t, b, s, src=None):
+        place = (r + ring - s) % ring if ways[t] == 0 else (r + s) % ring
+        dst = full[t].at[rows(t, place, x if b == 0 else 1 - x)]
+        return send(dst if src is None else src, dst, core_s.at[t, b, s], core_r.at[t, b, s], other_c)
+
+    def x_copy(t):
+        dst = full[t].at[rows(t, r, x)]
+        return send(shards[t], dst, x_s.at[t], x_r.at[t], other_x)
+
+    def clip_copy(j):
+        return send(clips.at[j], frames.at[j], clip_s.at[j], clip_r.at[j], (w, (k + j) % n))
+
+    for t in range(count):
+        x_copy(t).start()
+        ring_copy(t, 0, 0, shards[t]).start()
+    for j in range(1, n):
+        clip_copy(j).start()
+    for t in range(count):
+        core_copy(t, 0, 0, shards[t]).start()
+    loads = [pltpu.make_async_copy(clips.at[0], clip_buf, load_sem.at[count])]
+    loads += [pltpu.make_async_copy(shards[t], bufs[t], load_sem.at[t]) for t in range(count)]
+    keeps = [pltpu.make_async_copy(clip_buf, frames.at[0], keep_sem.at[count])]
+    keeps += [pltpu.make_async_copy(bufs[t], full[t].at[rows(t, r, x)], keep_sem.at[t]) for t in range(count)]
+    for copy in loads:
+        copy.start()
+    for copy, keep in zip(loads, keeps):
+        copy.wait()
+        keep.start()
+    for t in range(count):
+        x_copy(t).wait_recv()
+        ring_copy(t, 1, 0).start()
+        core_copy(t, 1, 0).start()
+    for s in range(1, ring):
+        for b in range(2):
+            for t in range(count):
+                ring_copy(t, b, s - 1).wait_recv()
+                if s < ring - 1:
+                    ring_copy(t, b, s).start()
+                core_copy(t, b, s).start()
+    for copy in keeps:
+        copy.wait()
+    for t in range(count):
+        x_copy(t).wait_send()
+        for b in range(2):
+            for s in range(ring):
+                if s < ring - 1:
+                    ring_copy(t, b, s).wait_send()
+                core_copy(t, b, s).wait()
+    for j in range(1, n):
+        clip_copy(j).wait()
+
+
+def gather_all(clips, shards, ways, ring, n):
+    count = len(shards)
+    devices = ring * n
+    heights = tuple(a.shape[0] for a in shards)
+    sems = pltpu.SemaphoreType.DMA
+    got = pl.pallas_call(
+        functools.partial(gather_kernel, ring, n, heights, ways),
+        name="gather_all",
+        out_shape=[shape_of(clips.shape, clips.dtype)]
+        + [shape_of((a.shape[0] * devices, a.shape[1]), a.dtype) for a in shards],
+        in_specs=[ANY] * (1 + count),
+        out_specs=[ANY] * (1 + count),
+        scratch_shapes=[pltpu.VMEM(clips.shape[1:], clips.dtype)]
+        + [pltpu.VMEM(a.shape, a.dtype) for a in shards]
+        + [sems((count, 2, ring))] * 4
+        + [sems((count,))] * 2
+        + [sems((n,))] * 2
+        + [sems((count + 1,))] * 2,
+        compiler_params=pltpu.CompilerParams(collective_id=0, has_side_effects=True),
+    )(clips, *shards)
+    return got[0], got[1:]
+
+
+def scatter_kernel(ring, heights, ways, *refs):
+    count = len(heights)
+    grads, outs, stages = refs[:count], refs[count : 2 * count], refs[2 * count : 3 * count]
+    local, part, came, went, last, fin_s, fin_r = (
+        refs[(3 + i) * count : (4 + i) * count] for i in range(7)
+    )
+    ring_s, ring_r, core_s, core_r, x_s, x_r, load_sem, part_sem = refs[10 * count :]
+    w, k, r, x, c, wide_at = place_of(ring)
+    other_x = (w, 2 * (1 - x) + c)
+    other_c = (w, 2 * x + 1 - c)
+    steps = ((wide_at((r + 1) % ring), k), (wide_at((r + ring - 1) % ring), k))
+    greet(steps + (other_x, other_c))
+    final = ring - 1
+
+    def place(t, s):
+        return (r + 2 * ring - 1 - s) % ring if ways[t] == 0 else (r + 1 + s) % ring
+
+    def rows(t, s, column, core):
+        block = 4 * wide_at(place(t, s)) + 2 * column + core
+        return pl.ds(pl.multiple_of(block * heights[t], 8), heights[t])
+
+    def half(t, column):
+        return pl.ds(column * heights[t], heights[t])
+
+    def core_copy(t, s, column):
+        return send(grads[t].at[rows(t, s, column, 1 - c)], stages[t].at[s, half(t, column)],
+                    core_s.at[t, s, column], core_r.at[t, s, column], other_c)
+
+    def local_load(t, s, slot, column):
+        return pltpu.make_async_copy(grads[t].at[rows(t, s, column, c)], local[t].at[slot, half(t, column)],
+                                     load_sem.at[t, slot, column])
+
+    def part_load(t, s, slot):
+        return pltpu.make_async_copy(stages[t].at[s], part[t].at[slot], part_sem.at[t, slot])
+
+    def ring_copy(t, s):
+        return send(went[t].at[s], came[t].at[s], ring_s.at[t, s], ring_r.at[t, s], steps[ways[t]])
+
+    def x_copy(t):
+        return send(fin_s[t], fin_r[t], x_s.at[t], x_r.at[t], other_x)
+
+    order = (0, 2, 1, 3)
+
+    def fetch(t, s, slot):
+        for column in range(2):
+            core_copy(t, s, column).wait_recv()
+        part_load(t, s, slot).start()
+        for column in range(2):
+            local_load(t, s, slot, column).start()
+
+    def total(t, s, slot):
+        for column in range(2):
+            local_load(t, s, slot, column).wait()
+        part_load(t, s, slot).wait()
+        return local[t][slot] + part[t][slot]
+
+    for t in order:
+        for column in range(2):
+            core_copy(t, 0, column).start()
+    for s in range(1, ring):
+        for t in order:
+            for column in range(2):
+                core_copy(t, s, column).start()
+    for t in order:
+        fetch(t, 0, 0)
+    for t in order:
+        fetch(t, 1, 1)
+        went[t][0] = total(t, 0, 0).astype(BF)
+        ring_copy(t, 0).start()
+
+    def body(s, carry):
+        slot = s % 2
+        for t in order:
+            fetch(t, s + 1, 1 - slot)
+            value = total(t, s, slot)
+            ring_copy(t, s - 1).wait_recv()
+            went[t][s] = (value + came[t][s - 1].astype(F32)).astype(BF)
+            ring_copy(t, s).start()
+        return carry
+
+    lax.fori_loop(1, final, body, 0)
+    for t in order:
+        value = total(t, final, final % 2)
+        ring_copy(t, final - 1).wait_recv()
+        value = value + came[t][final - 1].astype(F32)
+        last[t][0] = value[: heights[t]]
+        last[t][1] = value[heights[t] :]
+        fin_s[t][...] = last[t][1 - x].astype(BF)
+        x_copy(t).start()
+    for t in order:
+        x_copy(t).wait_recv()
+        outs[t][...] = last[t][x] + fin_r[t][...].astype(F32)
+    for t in order:
+        x_copy(t).wait_send()
+        for s in range(final):
+            ring_copy(t, s).wait_send()
+        for s in range(ring):
+            for column in range(2):
+                core_copy(t, s, column).wait_send()
+
+
+def scatter_all(grads, ways, ring, n):
+    count = len(grads)
+    devices = ring * n
+    heights = tuple(g.shape[0] // devices for g in grads)
+    widths = tuple(g.shape[1] for g in grads)
+    each = tuple(zip(heights, widths))
+    sems = pltpu.SemaphoreType.DMA
+    vmem = pltpu.VMEM
+    got = pl.pallas_call(
+        functools.partial(scatter_kernel, ring, heights, ways),
+        name="scatter_all",
+        out_shape=[shape_of(hw, F32) for hw in each]
+        + [shape_of((ring, 2 * h, wd), F32) for h, wd in each],
+        in_specs=[ANY] * count,
+        out_specs=[pl.BlockSpec(memory_space=pltpu.VMEM)] * count + [ANY] * count,
+        scratch_shapes=[vmem((2, 2 * h, wd), F32) for h, wd in each]
+        + [vmem((2, 2 * h, wd), F32) for h, wd in each]
+        + [vmem((ring - 1, 2 * h, wd), BF) for h, wd in each]
+        + [vmem((ring - 1, 2 * h, wd), BF) for h, wd in each]
+        + [vmem((2, h, wd), F32) for h, wd in each]
+        + [vmem((h, wd), BF) for h, wd in each]
+        + [vmem((h, wd), BF) for h, wd in each]
+        + [sems((count, ring))] * 2
+        + [sems((count, ring, 2))] * 2
+        + [sems((count,))] * 2
+        + [sems((count, 2, 2)), sems((count, 2))],
+        compiler_params=pltpu.CompilerParams(
+            collective_id=1, has_side_effects=True, vmem_limit_bytes=VMEM_LIMIT
+        ),
+    )(*grads)
+    return got[:count]
+
+
+def tuned(mesh):
+    wide, n = mesh.shape["wide"], mesh.shape["narrow"]
+    if n != 4 or wide < 4 or wide % 2 or D % (8 * wide * n):
+        return False
+    for w in range(wide):
+        for k in range(n):
+            device = mesh.devices[w, k]
+            here = (getattr(device, "coords", None), getattr(device, "core_on_chip", None))
+            if here[0] is None or tuple(here[0]) != (k // 2, w % 2, w // 2) or here[1] != k % 2:
+                return False
+    return True
 
 
 def exchange(x):
@@ -416,7 +687,7 @@
     return jnp.stack(parts)
 
 
-def local(clips, t_emb, lengths, task, w_mod, b_mod, w_qkv_s, w_o_s, b_o_s, w_qkv_t, w_o_t, b_o_t,
+def local(fast, clips, t_emb, lengths, task, w_mod, b_mod, w_qkv_s, w_o_s, b_o_s, w_qkv_t, w_o_t, b_o_t,
           w_in, b_in, w_out, b_out, cotangent):
     n = lax.axis_size("narrow")
     wide = lax.axis_size("wide")
@@ -448,7 +719,14 @@
     def gather(w):
         return lax.all_gather(w, ALL, axis=0, tiled=True)
 
-    frames = shift_clips(clips, False).reshape(n * FR, PATCHES, D)
+    weights = (w_in, w_out, w_qkv_t, w_o_t, w_qkv_s, w_o_s)
+    if fast:
+        frames, weights = gather_all(clips, weights, (0, 0, 1, 1, 1, 1), wide, n)
+    else:
+        frames = shift_clips(clips, False)
+        weights = [gather(w) for w in weights]
+    win, wout, wqkv_t, wo_t, wqkv_s, wo_s = weights
+    frames = frames.reshape(n * FR, PATCHES, D)
 
     wm = jnp.swapaxes(w_mod.reshape(part, devices, mod_cols), 0, 1).reshape(devices, -1)
     emb = jnp.broadcast_to(t_emb.reshape(1, -1), (devices, t_emb.size))
@@ -472,10 +750,6 @@
     mod_rows = jnp.swapaxes(mod_rows, 0, 1).reshape(2 * n, 9, D)
     mod = jnp.swapaxes(mod_rows[row_choice], 0, 1)
 
-    wqkv_s, wo_s = gather(w_qkv_s), gather(w_o_s)
-    wqkv_t, wo_t = gather(w_qkv_t), gather(w_o_t)
-    win, wout = gather(w_in), gather(w_out)
-
     x1, qkv1, o1, a1 = run_frame_forward(frames, pack_rows, mod, wqkv_s, wo_s, bias_s)
     x2, qkv2, o2, a2 = run_time_forward(x1, mod, seg, wqkv_t, wo_t, bias_t)
     cots = shift_clips(cotangent, False).reshape(n * FR, PATCHES, D)
@@ -491,13 +765,15 @@
         return lax.psum_scatter(g.astype(BF), ALL, scatter_dimension=0, tiled=True).astype(F32)
 
     layer_out = unpack(out)
-    s_in, s_out = scatter(g_in), scatter(g_out)
-    dx1, g_qkv_t, g_o_t, gb_t, dmod2 = run_time_back(x1, dx2, mod, seg, qkv2, o2, a2, wqkv_t, wo_t)
-    s_qkv_t, s_o_t = scatter(g_qkv_t), scatter(g_o_t)
-    dx0, g_qkv_s, g_o_s, gb_s, dmod1 = run_frame_back(
+    dx1, g_t, gb_t, dmod2 = run_time_back(x1, dx2, mod, seg, qkv2, o2, a2, wqkv_t, wo_t)
+    dx0, g_s, gb_s, dmod1 = run_frame_back(
         frames, pack_rows, dx1, mod, qkv1, o1, a1, wqkv_s, wo_s)
     grad_clips = unpack(dx0)
-    s_qkv_s, s_o_s = scatter(g_qkv_s), scatter(g_o_s)
+    grads = (g_in, g_out, g_t, g_s)
+    if fast:
+        s_in, s_out, s_t, s_s = scatter_all(grads, (0, 0, 1, 1), wide, n)
+    else:
+        s_in, s_out, s_t, s_s = [scatter(g) for g in grads]
 
     grad_frames = jnp.swapaxes(jnp.concatenate([dmod1, dmod2, dmod3], axis=0), 0, 1).reshape(LIVE, 9 * D)
     chooser = (row_choice[:, None] == jnp.arange(2 * n, dtype=jnp.int32)[None, :]).astype(F32)
@@ -530,11 +806,11 @@
         grad_t_emb,
         grad_w_mod,
         grad_b_mod,
-        s_qkv_s,
-        s_o_s,
+        s_s[:, : 3 * D],
+        s_s[:, 3 * D :],
         gb[:b1],
-        s_qkv_t,
-        s_o_t,
+        s_t[:, : 3 * D],
+        s_t[:, 3 * D :],
         gb[b1 : 2 * b1],
         s_in,
         gb[2 * b1 : 2 * b1 + b_in.size],
@@ -546,4 +822,4 @@
 def solution(mesh):
     full = P(ALL)
     placed = (full, full, P("wide"), P("wide")) + (full,) * 13
-    return jax.shard_map(local, mesh=mesh, in_specs=placed, out_specs=(full,) * 15, check_vma=False)
+    return jax.shard_map(functools.partial(local, tuned(mesh)), mesh=mesh, in_specs=placed, out_specs=(full,) * 15, check_vma=False)

time: 1320 us -> 882 us (0.67)
  waiting for transfers between devices: 681 us -> 12.6 us
  Pallas kernels: 416 us -> 715 us
  other arithmetic: 96.4 us -> 46.6 us
  between operations: 15.3 us -> 1.74 us
    reduce_scatter x6 -> x0, waiting for transfers between devices: 503 us -> none  [scatter(): lax.psum_scatter(g.astype(BF), ALL, scatter_dimension=0, tiled=True)]
    pallas_call x0 -> x2, Pallas kernels: none -> 298 us  [the longest x1 163 us: gather_all(): pl.pallas_call(functools.partial(gather_kernel, ring, n, heights, ways),...]
    ppermute x12 -> x9, waiting for transfers between devices: 136 us -> 12.6 us  [shift_clips(): lax.ppermute(clips[j], 'narrow', [(s, (s + step) % n) for s in range(n)])]
    all_gather x6 -> x0, waiting for transfers between devices: 36.9 us -> none  [gather(): return lax.all_gather(w, ALL, axis=0, tiled=True)]
    convert_element_type x12 -> x0, other arithmetic: 36.9 us -> none  [the longest x6 27.6 us: scatter(): g.astype(BF)]
  transfers between devices with their start and end apart: 28 -> 13, of which waited for: 11 -> 1; matrix products, arithmetic and copies ran while one was open for 12% -> 10% of each run, Pallas kernels for 11% -> 35%
where the time goes in v2:
time: 882 us; the launch traced here: 873 us
  Pallas kernels  715 us (81%)
  local copies, waits for them, and re-layouts  67.3 us (8%)
  other arithmetic  46.6 us (5%)
  starting transfers between devices  29 us (3%)
  waiting for transfers between devices  12.6 us (1%)
    pallas_call x6, Pallas kernels, call(): return fn(*ins) if prefetch is None else fn(prefetch, *ins)  416 us
    pallas_call x1, Pallas kernels, gather_all(): pl.pallas_call(functools.partial(gather_kernel, ring, n, heights, ways),...  163 us
    pallas_call x1, Pallas kernels, scatter_all(): pl.pallas_call(functools.partial(scatter_kernel, ring, heights, ways), na...  135 us
    all_to_all x4, starting transfers between devices, exchange(): return lax.all_to_all(x, ALL, split_axis=0, concat_axis=0, tiled=True)  23 us
    another operation x3, other arithmetic, shift_clips(): return jnp.stack(parts)  18.4 us
  transfers between devices with their start and end apart: 13, of which 1 were waited for; matrix products, arithmetic and copies ran while one was open for 10% of the time, Pallas kernels for 35%

profile of v2, /device:TPU:1, one launch (start us, length us, event | category | flops | bytes accessed | tf_op | source)
XLA Modules:
  0.0 873.4 jit_solution(15694913608357784789)
XLA Ops:
  0.7 2.2 reshape.533
  6.1 1.2 reduce.10
  7.3 1.7 reshape.665
  9.0 7.1 all-to-all-start
  16.1 5.2 fusion.28
  21.3 1.6 collective-permute-start
  25.8 2.6 fusion.25
  29.9 1.2 gather_fusion.5
  31.3 163.0 %gather_all.1 = (bf16[4,16,64,768]{3,2,1,0:T(8,128)(2,1)}, bf16[768,3072]{1,0:T(8,128)(2,1)}, bf16[3072,768]{1,0:T(8,128)(2,1)}, bf16[768,2304]{1,0:T(8,128)(2,1...) custom-call(bf16[4,16,64,768]{3,2,1,0:T(8,128)(2,1)} %refs_0_.1, ...), custom_call_target="tpu_custom_call" | custom-call | tf_op jit(solution)/shard_map/gather_all/pallas_call | solution.py:512
  196.1 3.2 multiply_add_fusion
  200.0 5.1 reshape.666
  208.1 1.3 all_to_all.38
  209.4 4.1 all-to-all-start.1
  213.5 0.9 slice_convert_fusion
  216.3 0.8 slice_convert_fusion.1
  217.8 5.9 pad_maximum_fusion
  223.7 7.0 turn_frames.1.dy
  232.5 1.5 copy.129
  233.9 72.0 %frame_forward.1 = (f32[64,32,768]{2,1,0:T(8,128)}, bf16[2048,2304]{1,0:T(8,128)(2,1)}, bf16[2048,768]{1,0:T(8,128)(2,1)}, f32[2048,768]{1,0:T(8,128)}) custom-call(s32[32]{0:T(128)} %get-tuple-element.117.rows_ref, bf16[64,64,768]{2,1,0:T(8,128)(2,1)} %bitcast.138, bf16[64,64,768]{2,1,0:T(8,128)(2,1)} %bitcast.139, bf16[64,64,768]{2,1,0:T(8,128)(2,1)} %bitcast.140, ...), custom_call_target="tpu_custom_call" | custom-call | flops 9663676416 | bytes 81103872 | tf_op jit(solution)/shard_map/frame_forward/pallas_call | solution.py:327
  306.0 69.9 %time_forward.1 = (f32[64,32,768]{2,1,0:T(8,128)}, bf16[2048,2304]{1,0:T(8,128)(2,1)}, bf16[2048,768]{1,0:T(8,128)(2,1)}, f32[2048,768]{1,0:T(8,128)}) custom-call(f32[64,32,768]{2,1,0:T(8,128)} %get-tuple-element.53.x1, f32[9,32,768]{2,1,0:T(8,128)} %bitcast.165, f32[64,128]{1,0:T(8,128)} %and_convert_fusion.seg, bf16[768,2304]{1,0:T(8,128)(2,1)} %get-tuple-element.54.wqkv, ...), custom_call_target="tpu_custom_call" | custom-call | flops 9663676416 | bytes 37096448 | tf_op jit(solution)/shard_map/time_forward/pallas_call | solution.py:327
  375.9 85.5 %mlp_both.1 = (bf16[32,64,768]{2,1,0:T(8,128)(2,1)}, f32[64,32,768]{2,1,0:T(8,128)}, f32[768,3072]{1,0:T(8,128)}, f32[3072,768]{1,0:T(8,128)}, f32[1,3072]{1,0:T...) custom-call(f32[64,32,768]{2,1,0:T(8,128)} %get-tuple-element.56.x2, f32[64,32,768]{2,1,0:T(8,128)} %turn_frames.1.dy, ...), custom_call_target="tpu_custom_call" | custom-call | flops 57982058496 | bytes 51542016 | tf_op jit(solution)/shard_map/mlp_both/pallas_call | solution.py:327
  461.4 93.2 %time_back.1 = (f32[32,64,768]{2,1,0:T(8,128)}, f32[768,3072]{1,0:T(8,128)}, f32[1,768]{1,0:T(1,128)}, f32[3,32,768]{2,1,0:T(8,128)}) custom-call(f32[64,32,768]{2,1,0:T(8,128)} %get-tuple-element.53.x1, f32[64,32,768]{2,1,0:T(8,128)} %get-tuple-element.60.dx2, f32[9,32,768]{2,1,0:T(8,128)} %bitcast.167, f32[64,128]{1,0:T(8,128)} %and_convert_fusion.seg, ...), custom_call_target="tpu_custom_call" | custom-call | flops 19327352832 | bytes 53120000 | tf_op jit(solution)/shard_map/time_back/pallas_call | solution.py:327
  554.6 88.9 %frame_back.1 = (bf16[32,64,768]{2,1,0:T(8,128)(2,1)}, f32[768,3072]{1,0:T(8,128)}, f32[1,768]{1,0:T(1,128)}, f32[3,32,768]{2,1,0:T(8,128)}) custom-call(s32[32]{0:T(128)} %get-tuple-element.117.rows_ref, bf16[64,64,768]{2,1,0:T(8,128)(2,1)} %bitcast.146, bf16[64,64,768]{2,1,0:T(8,128)(2,1)} %bitcast.147, bf16[64,64,768]{2,1,0:T(8,128)(2,1)} %bitcast.148, ...), custom_call_target="tpu_custom_call" | custom-call | flops 19327352832 | bytes 93981696 | tf_op jit(solution)/shard_map/frame_back/pallas_call | solution.py:327
  643.6 1.0 maximum_bitcast_fusion
  645.9 1.4 reduce.11
  647.3 0.8 reshape.667
  648.1 5.8 all-to-all-start.2
  655.5 5.8 gather_fusion.7
  661.4 3.9 gather_fusion.6
  665.3 5.6 broadcast_select_fusion
  670.8 3.4 broadcast_select_fusion.2
  674.2 2.7 fusion.26
  678.9 0.8 convert_reduce_fusion
  681.7 2.1 all_to_all.35
  683.9 5.9 all-to-all-start.3
  689.8 1.4 collective-permute-start.7
  691.8 5.7 fusion.27
  697.6 1.4 collective-permute-start.4
  699.0 12.5 %collective-permute-done.6 = bf16[16,64,768]{2,1,0:T(8,128)(2,1)} collective-permute-done((bf16[16,64,768]{2,1,0:T(8,128)(2,1)}, bf16[16,64,768]{2,1,0:T(8,128)(2,1)}, u32[]{:S(2)}, u32[]{:S(2)}) %collective-permute-start.6) | collective-permute-done | bytes 1572896 | tf_op jit(solution)/shard_map/ppermute | solution.py:686
  711.5 135.3 %scatter_all.1 = (f32[24,3072]{1,0:T(8,128)}, f32[96,768]{1,0:T(8,128)}, f32[24,3072]{1,0:T(8,128)}, f32[24,3072]{1,0:T(8,128)}, f32[8,48,3072]{2,1,0:T(8,128)},...) custom-call(f32[768,3072]{1,0:T(8,128)} %get-tuple-element.76.refs_0_, ...), custom_call_target="tpu_custom_call" | custom-call | tf_op jit(solution)/shard_map/scatter_all/pallas_call | solution.py:639
  846.8 1.6 slice.204
  848.4 1.5 slice.205
  850.0 1.6 slice.208
  851.6 1.5 slice.209
  853.1 6.7 pad_maximum_fusion.2
  859.8 5.9 pad_maximum_fusion.1
  865.7 1.5 copy.128
  869.8 1.3 reshape.555
  (169 shorter events, 29.5 us)
Async XLA Ops:
  0.6 24.6 %copy-start = (s32[16,16]{1,0:T(8,128)S(1)}, s32[16,16]{1,0:T(8,128)}, u32[]{:S(2)}) copy-start(s32[16,16]{1,0:T(8,128)} %param.22) | copy-start | bytes 3076
  9.0 191.1 %all-to-all-start = ((bf16[32,2,5748]{2,1,0:T(2,128)(2,1)}), bf16[32,2,5748]{2,1,0:T(2,128)(2,1)}, u32[]{:S(2)}, u32[]{:S(2)}) async-start(bf16[32,2,5748]{2,1,0:T(2,128)(2,1)} %reshape.665), calls=%async_computation | async-start | bytes 1474560 | tf_op jit(solution)/shard_map/all_to_all | solution.py:678
  16.1 7.4 copy-start.21
  16.1 9.0 %copy-start.22 = (bf16[216]{0:T(256)(128)(2,1)S(1)}, bf16[216]{0:T(256)(128)(2,1)}, u32[]{:S(2)}) copy-start(bf16[216]{0:T(256)(128)(2,1)} %param.24) | copy-start | bytes 1300
  21.3 196.5 %collective-permute-start = (bf16[16,64,768]{2,1,0:T(8,128)(2,1)}, bf16[16,64,768]{2,1,0:T(8,128)(2,1)}, u32[]{:S(2)}, u32[]{:S(2)}) collective-permute-start(bf16[16,64,768]{2,1,0:T(8,128)(2,1)} %get-tuple-element.95), channel_id=1, source_target_pairs={{0,1},{1,2},{2,3},{3,0},{4,5},{5,6},{6,7},{7,4},{8,9},{9,10},{10,1... | collective-permute-start | bytes 4718600 | tf_op jit(solution)/shard_map/ppermute | solution.py:686
  23.0 194.8 %collective-permute-start.1 = (bf16[16,64,768]{2,1,0:T(8,128)(2,1)}, bf16[16,64,768]{2,1,0:T(8,128)(2,1)}, u32[]{:S(2)}, u32[]{:S(2)}) collective-permute-start(bf16[16,64,768]{2,1,0:T(8,128)(2,1)} %get-tuple-element.97), channel_id=1, source_target_pairs={{0,2},{1,3},{2,0},{3,1},{4,6},{5,7},{6,4},{7,5},{8,10},{9,11},{10,... | collective-permute-start | bytes 4718600 | tf_op jit(solution)/shard_map/ppermute | solution.py:686
  23.0 194.8 %collective-permute-start.2 = (bf16[16,64,768]{2,1,0:T(8,128)(2,1)}, bf16[16,64,768]{2,1,0:T(8,128)(2,1)}, u32[]{:S(2)}, u32[]{:S(2)}) collective-permute-start(bf16[16,64,768]{2,1,0:T(8,128)(2,1)} %get-tuple-element.96), channel_id=1, source_target_pairs={{0,3},{1,0},{2,1},{3,2},{4,7},{5,4},{6,5},{7,6},{8,11},{9,8},{10,9... | collective-permute-start | bytes 4718600 | tf_op jit(solution)/shard_map/ppermute | solution.py:686
  205.2 0.9 copy-start.8
  206.3 17.4 %copy-start.4 = (bf16[256,768]{1,0:T(8,128)(2,1)}, bf16[256,768]{1,0:T(8,128)(2,1)S(1)}, u32[]{:S(2)}) copy-start(bf16[256,768]{1,0:T(8,128)(2,1)S(1)} %convert_element_type.58) | copy-start | bytes 1179652
  207.0 16.7 %copy-start.6 = (bf16[768,216]{1,0:T(8,128)(2,1)}, bf16[768,216]{1,0:T(8,128)(2,1)S(1)}, u32[]{:S(2)}) copy-start(bf16[768,216]{1,0:T(8,128)(2,1)S(1)} %reshape.535) | copy-start | bytes 995332
  209.4 21.3 %all-to-all-start.1 = ((f32[32,1,1728]{2,1,0:T(1,128)}), f32[32,1,1728]{2,1,0:T(1,128)S(1)}, u32[]{:S(2)}, u32[]{:S(2)}) async-start(f32[32,1,1728]{2,1,0:T(1,128)} %all_to_all.38), calls=%async_computation.1 | async-start | bytes 458752 | tf_op jit(solution)/shard_map/all_to_all | solution.py:678
  554.6 89.0 %copy-start.9 = (f32[3,32,768]{2,1,0:T(8,128)S(1)}, f32[3,32,768]{2,1,0:T(8,128)}, u32[]{:S(2)}) copy-start(f32[3,32,768]{2,1,0:T(8,128)} %get-tuple-element.71) | copy-start | bytes 884740
  554.6 89.0 %copy-start.10 = (f32[3,32,768]{2,1,0:T(8,128)S(1)}, f32[3,32,768]{2,1,0:T(8,128)}, u32[]{:S(2)}) copy-start(f32[3,32,768]{2,1,0:T(8,128)} %get-tuple-element.70) | copy-start | bytes 884740
  554.6 90.1 %copy-start.18 = (s32[32]{0:T(128)S(1)}, s32[32]{0:T(128)}, u32[]{:S(2)}) copy-start(s32[32]{0:T(128)} %get-tuple-element.116) | copy-start | bytes 388
  643.5 10.4 %copy-start.17 = (f32[1,768]{1,0:T(1,128)S(1)}, f32[1,768]{1,0:T(1,128)}, u32[]{:S(2)}) copy-start(f32[1,768]{1,0:T(1,128)} %get-tuple-element.72) | copy-start | bytes 9220
  643.5 10.5 %copy-start.16 = (f32[1,768]{1,0:T(1,128)S(1)}, f32[1,768]{1,0:T(1,128)}, u32[]{:S(2)}) copy-start(f32[1,768]{1,0:T(1,128)} %get-tuple-element.73) | copy-start | bytes 9220
  643.5 11.1 %copy-start.14 = (f32[1,3072]{1,0:T(1,128)S(1)}, f32[1,3072]{1,0:T(1,128)}, u32[]{:S(2)}) copy-start(f32[1,3072]{1,0:T(1,128)} %get-tuple-element.74) | copy-start | bytes 36868
  643.5 11.9 %copy-start.15 = (f32[1,768]{1,0:T(1,128)S(1)}, f32[1,768]{1,0:T(1,128)}, u32[]{:S(2)}) copy-start(f32[1,768]{1,0:T(1,128)} %get-tuple-element.75) | copy-start | bytes 9220
  648.1 29.3 %all-to-all-start.2 = ((bf16[32,2,864]{2,1,0:T(2,128)(2,1)}), bf16[32,2,864]{2,1,0:T(2,128)(2,1)S(1)}, u32[]{:S(2)}, u32[]{:S(2)}) async-start(bf16[32,2,864]{2,1,0:T(2,128)(2,1)} %reshape.667), calls=%async_computation.2 | async-start | bytes 229376 | tf_op jit(solution)/shard_map/all_to_all | solution.py:678
  655.5 5.8 copy-start.2
  661.4 3.9 copy-start.20
  665.3 5.6 copy-start.19
  674.2 5.7 copy-start.7
  676.9 3.5 copy-start.5
  676.9 34.6 %collective-permute-start.6 = (bf16[16,64,768]{2,1,0:T(8,128)(2,1)}, bf16[16,64,768]{2,1,0:T(8,128)(2,1)}, u32[]{:S(2)}, u32[]{:S(2)}) collective-permute-start(bf16[16,64,768]{2,1,0:T(8,128)(2,1)} %get-tuple-element.89), channel_id=1, source_target_pairs={{0,3},{1,0},{2,1},{3,2},{4,7},{5,4},{6,5},{7,6},{8,11},{9,8},{10,9... | collective-permute-start | bytes 4718600 | tf_op jit(solution)/shard_map/ppermute | solution.py:686
  683.9 181.9 %all-to-all-start.3 = ((f32[32,1,11496]{2,1,0:T(1,128)}), f32[32,1,11496]{2,1,0:T(1,128)}, u32[]{:S(2)}, u32[]{:S(2)}) async-start(f32[32,1,11496]{2,1,0:T(1,128)} %all_to_all.35), calls=%async_computation.3 | async-start | bytes 2949120 | tf_op jit(solution)/shard_map/all_to_all | solution.py:678
  689.8 163.3 %collective-permute-start.7 = (bf16[16,64,768]{2,1,0:T(8,128)(2,1)}, bf16[16,64,768]{2,1,0:T(8,128)(2,1)}, u32[]{:S(2)}, u32[]{:S(2)}) collective-permute-start(bf16[16,64,768]{2,1,0:T(8,128)(2,1)} %get-tuple-element.88), channel_id=1, source_target_pairs={{0,2},{1,3},{2,0},{3,1},{4,6},{5,7},{6,4},{7,5},{8,10},{9,11},{10,... | collective-permute-start | bytes 4718600 | tf_op jit(solution)/shard_map/ppermute | solution.py:686
  691.2 161.9 %collective-permute-start.8 = (bf16[16,64,768]{2,1,0:T(8,128)(2,1)}, bf16[16,64,768]{2,1,0:T(8,128)(2,1)}, u32[]{:S(2)}, u32[]{:S(2)}) collective-permute-start(bf16[16,64,768]{2,1,0:T(8,128)(2,1)} %get-tuple-element.87), channel_id=1, source_target_pairs={{0,1},{1,2},{2,3},{3,0},{4,5},{5,6},{6,7},{7,4},{8,9},{9,10},{10,1... | collective-permute-start | bytes 4718600 | tf_op jit(solution)/shard_map/ppermute | solution.py:686
  697.5 162.3 %collective-permute-start.3 = (bf16[16,64,768]{2,1,0:T(8,128)(2,1)}, bf16[16,64,768]{2,1,0:T(8,128)(2,1)}, u32[]{:S(2)}, u32[]{:S(2)}) collective-permute-start(bf16[16,64,768]{2,1,0:T(8,128)(2,1)} %get-tuple-element.93), channel_id=1, source_target_pairs={{0,3},{1,0},{2,1},{3,2},{4,7},{5,4},{6,5},{7,6},{8,11},{9,8},{10,9... | collective-permute-start | bytes 4718600 | tf_op jit(solution)/shard_map/ppermute | solution.py:686
  697.6 162.2 %collective-permute-start.4 = (bf16[16,64,768]{2,1,0:T(8,128)(2,1)}, bf16[16,64,768]{2,1,0:T(8,128)(2,1)}, u32[]{:S(2)}, u32[]{:S(2)}) collective-permute-start(bf16[16,64,768]{2,1,0:T(8,128)(2,1)} %get-tuple-element.92), channel_id=1, source_target_pairs={{0,2},{1,3},{2,0},{3,1},{4,6},{5,7},{6,4},{7,5},{8,10},{9,11},{10,... | collective-permute-start | bytes 4718600 | tf_op jit(solution)/shard_map/ppermute | solution.py:686
  711.5 148.3 %collective-permute-start.5 = (bf16[16,64,768]{2,1,0:T(8,128)(2,1)}, bf16[16,64,768]{2,1,0:T(8,128)(2,1)}, u32[]{:S(2)}, u32[]{:S(2)}) collective-permute-start(bf16[16,64,768]{2,1,0:T(8,128)(2,1)} %get-tuple-element.91), channel_id=1, source_target_pairs={{0,1},{1,2},{2,3},{3,0},{4,5},{5,6},{6,7},{7,4},{8,9},{9,10},{10,1... | collective-permute-start | bytes 4718600 | tf_op jit(solution)/shard_map/ppermute | solution.py:686
  853.1 6.7 copy-start.3
  865.7 5.4 copy-start.13
  865.7 6.0 copy-start.12
  865.7 6.8 copy-start.11
  865.7 7.5 copy-start.1

commit v3 on v2

--- a/solution.py
+++ b/solution.py
@@ -20,6 +20,7 @@
 ALL = ("wide", "narrow")
 PAIRS = HEADS // 2
 LANES = 2 * HEAD
+BACK_PAIRS = 6
 TILE = 512
 FT = TILE // PATCHES
 PT = TILE // LIVE
@@ -28,6 +29,8 @@
 GELU_C = 0.7978845608028654
 GELU_A = 0.044715
 VMEM_LIMIT = 66 * 1000 * 1000
+MESH = pl.DeviceIdType.MESH
+ANY = pl.BlockSpec(memory_space=pl.ANY)
 
 
 def dot(a, b):
@@ -64,29 +67,35 @@
     return low_lanes, low, high
 
 
-def softmax_keys(k, qb, mask):
-    s = dot_nt(k, qb) * HEAD ** (-0.5)
+def split_heads(x, low, high):
+    return jnp.concatenate([x * low, x * high], axis=0)
+
+
+def softmax_keys(s, mask):
     if mask is not None:
         s = jnp.where(mask, s, -1e30)
     top = jnp.max(s, axis=0, keepdims=True)
     e = jnp.exp(s - top)
-    return e / jnp.sum(e, axis=0, keepdims=True)
+    return e * (1.0 / jnp.sum(e, axis=0, keepdims=True))
+
+
+def pair_cols(part, hp):
+    return slice(part * D + hp * LANES, part * D + (hp + 1) * LANES)
 
 
 def attend(qkv_ref, o_ref, mask):
     low_lanes, low, high = lane_masks()
+    scale = HEAD ** (-0.5)
 
     def body(g, carry):
         rows = pl.ds(pl.multiple_of(g * 64, 64), 64)
-        for hp in range(PAIRS):
-            cols = slice(hp * LANES, (hp + 1) * LANES)
-            q = qkv_ref[rows, hp * LANES : (hp + 1) * LANES]
-            k = qkv_ref[rows, D + hp * LANES : D + (hp + 1) * LANES]
-            v = qkv_ref[rows, 2 * D + hp * LANES : 2 * D + (hp + 1) * LANES]
-            qb = jnp.concatenate([q * low, q * high], axis=0)
-            p = softmax_keys(k, qb, mask).astype(BF)
-            r = dot_tn(p, v)
-            o_ref[rows, cols] = jnp.where(low_lanes, r[:64], r[64:]).astype(BF)
+        pairs = range(PAIRS)
+        s = [dot_nt(qkv_ref[rows, pair_cols(1, hp)], split_heads(qkv_ref[rows, pair_cols(0, hp)], low * scale, high * scale))
+             for hp in pairs]
+        p = [softmax_keys(t, mask).astype(BF) for t in s]
+        r = [dot_tn(p[hp], qkv_ref[rows, pair_cols(2, hp)]) for hp in pairs]
+        for hp in pairs:
+            o_ref[rows, pair_cols(0, hp)] = jnp.where(low_lanes, r[hp][:64], r[hp][64:]).astype(BF)
         return carry
 
     lax.fori_loop(0, GROUPS, body, 0)
@@ -94,28 +103,27 @@
 
 def attend_back(qkv_ref, do_ref, dqkv_ref, mask):
     low_lanes, low, high = lane_masks()
+    scale = HEAD ** (-0.5)
 
     def body(g, carry):
         rows = pl.ds(pl.multiple_of(g * 64, 64), 64)
-        for hp in range(PAIRS):
-            qc = slice(hp * LANES, (hp + 1) * LANES)
-            kc = slice(D + hp * LANES, D + (hp + 1) * LANES)
-            vc = slice(2 * D + hp * LANES, 2 * D + (hp + 1) * LANES)
-            q = qkv_ref[rows, qc]
-            k = qkv_ref[rows, kc]
-            v = qkv_ref[rows, vc]
-            do = do_ref[rows, qc]
-            qb = jnp.concatenate([q * low, q * high], axis=0)
-            dob = jnp.concatenate([do * low, do * high], axis=0)
-            p = softmax_keys(k, qb, mask)
-            dp = dot_nt(v, dob)
-            delta = jnp.sum(p * dp, axis=0, keepdims=True)
-            ds = (p * (dp - delta)).astype(BF)
-            r = dot_tn(ds, k)
-            dq = jnp.where(low_lanes, r[:64], r[64:]) * HEAD ** (-0.5)
-            dqkv_ref[rows, qc] = dq.astype(BF)
-            dqkv_ref[rows, kc] = (dot(ds, qb) * HEAD ** (-0.5)).astype(BF)
-            dqkv_ref[rows, vc] = dot(p.astype(BF), dob).astype(BF)
+        for first in range(0, PAIRS, BACK_PAIRS):
+            pairs = range(first, first + BACK_PAIRS)
+            qb = [split_heads(qkv_ref[rows, pair_cols(0, hp)], low * scale, high * scale) for hp in pairs]
+            dob = [split_heads(do_ref[rows, pair_cols(0, hp)], low, high) for hp in pairs]
+            s = [dot_nt(qkv_ref[rows, pair_cols(1, hp)], q) for hp, q in zip(pairs, qb)]
+            dp = [dot_nt(qkv_ref[rows, pair_cols(2, hp)], d) for hp, d in zip(pairs, dob)]
+            p = [softmax_keys(t, mask) for t in s]
+            delta = [jnp.sum(a * b, axis=0, keepdims=True) for a, b in zip(p, dp)]
+            ds = [(a * (b - c)).astype(BF) for a, b, c in zip(p, dp, delta)]
+            dv = [dot(a.astype(BF), d) for a, d in zip(p, dob)]
+            dk = [dot(a, q) for a, q in zip(ds, qb)]
+            r = [dot_tn(a, qkv_ref[rows, pair_cols(1, hp)]) for hp, a in zip(pairs, ds)]
+            for i, hp in enumerate(pairs):
+                dqkv_ref[rows, pair_cols(2, hp)] = dv[i].astype(BF)
+                dqkv_ref[rows, pair_cols(1, hp)] = dk[i].astype(BF)
+                dq = jnp.where(low_lanes, r[i][:64], r[i][64:]) * scale
+                dqkv_ref[rows, pair_cols(0, hp)] = dq.astype(BF)
         return carry
 
     lax.fori_loop(0, GROUPS, body, 0)
@@ -153,9 +161,8 @@
     return seg_ref[...] > 0.0
 
 
-def frame_forward(rows_ref, *refs):
-    x_refs, (mod, wqkv, wo, bo, x1t, qkv, o, a1, scratch) = refs[:FT], refs[FT:]
-    x = frames_of(x_refs)
+def frame_forward(frames, mod, wqkv, wo, bo, x1t, qkv, o, a1, scratch):
+    x = frames[...].reshape(TILE, D).astype(F32)
     xhat, _ = normalise(x)
     h = (xhat * (1.0 + per_frame(mod[1])) + per_frame(mod[0])).astype(BF)
     qkv[...] = dot(h, wqkv[...]).astype(BF)
@@ -263,10 +270,9 @@
     swap_major(dx, scratch, dx1, PT, LIVE)
 
 
-def frame_back(rows_ref, *refs):
-    x_refs, (dx1, mod, qkv, o, a1, wqkv, wo, dx0, gw, gbo, dmod, do, dqkv) = refs[:FT], refs[FT:]
+def frame_back(frames, dx1, mod, qkv, o, a1, wqkv, wo, dx0, gw, gbo, dmod, do, dqkv):
     dx, d_shift, d_scale, d_gate = attn_back_tile(
-        frames_of(x_refs), dx1[...].reshape(TILE, D), per_frame(mod[0]), per_frame(mod[1]),
+        frames[...].reshape(TILE, D).astype(F32), dx1[...].reshape(TILE, D), per_frame(mod[0]), per_frame(mod[1]),
         per_frame(mod[2]), a1[...], qkv, o, wqkv, wo, gw, gbo, do, dqkv, None)
     dmod[0] = sum_patches(d_shift)
     dmod[1] = sum_patches(d_scale)
@@ -305,8 +311,43 @@
     return jax.ShapeDtypeStruct(shape, dtype)
 
 
-def call(kernel, name, ins, in_specs, outs, out_specs, scratch, flops, prefetch=None):
+def clip_copies(n, js, back, src, dst, send_sem, recv_sem):
+    w, k = lax.axis_index("wide"), lax.axis_index("narrow")
+    return [
+        send(src.at[j], dst.at[i], send_sem.at[i], recv_sem.at[i], (w, (k + (n - j if back else j)) % n))
+        for i, j in enumerate(js)
+    ]
+
+
+def carrying(kernel, count, n, js, back, *refs):
+    src, ins, dst, rest = refs[0], refs[1 : 1 + count], refs[1 + count], refs[2 + count : -2]
+    copies = clip_copies(n, js, back, src, dst, *refs[-2:])
+
+    @pl.when(pl.program_id(0) == 0)
+    def _():
+        w, k = lax.axis_index("wide"), lax.axis_index("narrow")
+        greet([(w, (k + j) % n) for j in js])
+        for copy in copies:
+            copy.start()
+
+    kernel(*ins, *rest)
+
+    @pl.when(pl.program_id(0) == GRID - 1)
+    def _():
+        for copy in copies:
+            copy.wait()
+
+
+def call(kernel, name, ins, in_specs, outs, out_specs, scratch, flops, prefetch=None, carry=None):
     moved = sum(a.size * a.dtype.itemsize for a in tuple(ins) + tuple(outs))
+    params = {}
+    if carry is not None:
+        src, n, js, back, number = carry
+        kernel = functools.partial(carrying, kernel, len(ins), n, js, back)
+        ins, in_specs = [src] + ins, [ANY] + in_specs
+        outs, out_specs = [shape_of((len(js),) + src.shape[1:], src.dtype)] + outs, [ANY] + out_specs
+        scratch = scratch + [pltpu.SemaphoreType.DMA((len(js),))] * 2
+        params = dict(collective_id=number, has_side_effects=True)
     grid_spec = pltpu.PrefetchScalarGridSpec(
         num_scalar_prefetch=0 if prefetch is None else 1,
         grid=(GRID,),
@@ -321,7 +362,7 @@
         name=name,
         cost_estimate=pl.CostEstimate(flops=flops, bytes_accessed=moved, transcendentals=0),
         compiler_params=pltpu.CompilerParams(
-            dimension_semantics=("arbitrary",), vmem_limit_bytes=VMEM_LIMIT
+            dimension_semantics=("arbitrary",), vmem_limit_bytes=VMEM_LIMIT, **params
         ),
     )
     return fn(*ins) if prefetch is None else fn(prefetch, *ins)
@@ -330,16 +371,16 @@
 TOKENS = LIVE * PATCHES
 
 
-def run_frame_forward(frames, rows, mod, wqkv, wo, bo):
+def run_frame_forward(frames, mod, wqkv, wo, bo, carry=None):
     return call(
         frame_forward, "frame_forward",
-        [frames] * FT + [mod, wqkv, wo, bo],
-        frame_specs() + [piece_spec(0, FT, True), whole((D, 3 * D)), whole((D, D)), whole((1, D))],
+        [frames, mod, wqkv, wo, bo],
+        [tiles((FT, PATCHES, D), 0), piece_spec(0, FT, True), whole((D, 3 * D)), whole((D, D)), whole((1, D))],
         [shape_of((PATCHES, LIVE, D), F32), shape_of((TOKENS, 3 * D), BF), shape_of((TOKENS, D), BF),
          shape_of((TOKENS, D), F32)],
         [tiles((PATCHES, FT, D), 1), ROWS3, ROWS, ROWS],
         [TURN],
-        2 * TOKENS * D * 4 * D, rows)
+        2 * TOKENS * D * 4 * D, carry=carry)
 
 
 def run_turn_frames(frames, rows):
@@ -349,7 +390,7 @@
         [TURN], 1000, rows)[0]
 
 
-def run_time_forward(x1, mod, seg, wqkv, wo, bo):
+def run_time_forward(x1, mod, seg, wqkv, wo, bo, carry=None):
     return call(
         time_forward, "time_forward",
         [x1, mod, seg, wqkv, wo, bo],
@@ -358,7 +399,7 @@
         [shape_of((PATCHES, LIVE, D), F32), shape_of((TOKENS, 3 * D), BF), shape_of((TOKENS, D), BF),
          shape_of((TOKENS, D), F32)],
         [TURNED, ROWS3, ROWS, ROWS],
-        [], 2 * TOKENS * D * 4 * D)
+        [], 2 * TOKENS * D * 4 * D, carry=carry)
 
 
 def run_mlp(x2, dy, mod, win, bin_, wout, bout):
@@ -375,7 +416,7 @@
         6 * 2 * TOKENS * D * FF)
 
 
-def run_time_back(x1, dx2, mod, seg, qkv, o, a2, wqkv, wo):
+def run_time_back(x1, dx2, mod, seg, qkv, o, a2, wqkv, wo, carry=None):
     return call(
         time_back, "time_back",
         [x1, dx2, mod, seg, qkv, o, a2, wqkv, wo],
@@ -384,23 +425,19 @@
         [shape_of((LIVE, PATCHES, D), F32), shape_of((D, 4 * D), F32), shape_of((1, D), F32), shape_of((3, LIVE, D), F32)],
         [tiles((LIVE, PT, D), 1), whole((D, 4 * D)), whole((1, D)), whole((3, LIVE, D))],
         [pltpu.VMEM((TILE, D), BF), pltpu.VMEM((TILE, 3 * D), BF), TURN],
-        2 * 2 * TOKENS * D * 4 * D)
-
-
-def run_frame_back(frames, rows, dx1, mod, qkv, o, a1, wqkv, wo):
+        2 * 2 * TOKENS * D * 4 * D, carry=carry)
+
+
+def run_frame_back(frames, dx1, mod, qkv, o, a1, wqkv, wo, carry=None):
     return call(
         frame_back, "frame_back",
-        [frames] * FT + [dx1, mod, qkv, o, a1, wqkv, wo],
-        frame_specs() + [tiles((FT, PATCHES, D), 0), piece_spec(0, FT, True), ROWS3, ROWS, ROWS,
+        [frames, dx1, mod, qkv, o, a1, wqkv, wo],
+        [tiles((FT, PATCHES, D), 0), tiles((FT, PATCHES, D), 0), piece_spec(0, FT, True), ROWS3, ROWS, ROWS,
                          whole((D, 3 * D)), whole((D, D))],
         [shape_of((LIVE, PATCHES, D), BF), shape_of((D, 4 * D), F32), shape_of((1, D), F32), shape_of((3, LIVE, D), F32)],
         [tiles((FT, PATCHES, D), 0), whole((D, 4 * D)), whole((1, D)), piece_spec(0, FT, True)],
         [pltpu.VMEM((TILE, D), BF), pltpu.VMEM((TILE, 3 * D), BF)],
-        2 * 2 * TOKENS * D * 4 * D, rows)
-
-
-MESH = pl.DeviceIdType.MESH
-ANY = pl.BlockSpec(memory_space=pl.ANY)
+        2 * 2 * TOKENS * D * 4 * D, carry=carry)
 
 
 def place_of(wide):
@@ -726,7 +763,7 @@
         frames = shift_clips(clips, False)
         weights = [gather(w) for w in weights]
     win, wout, wqkv_t, wo_t, wqkv_s, wo_s = weights
-    frames = frames.reshape(n * FR, PATCHES, D)
+    frames = jnp.take(frames.reshape(n * FR, PATCHES, D), pack_rows, axis=0, mode="clip")
 
     wm = jnp.swapaxes(w_mod.reshape(part, devices, mod_cols), 0, 1).reshape(devices, -1)
     emb = jnp.broadcast_to(t_emb.reshape(1, -1), (devices, t_emb.size))
@@ -750,25 +787,40 @@
     mod_rows = jnp.swapaxes(mod_rows, 0, 1).reshape(2 * n, 9, D)
     mod = jnp.swapaxes(mod_rows[row_choice], 0, 1)
 
-    x1, qkv1, o1, a1 = run_frame_forward(frames, pack_rows, mod, wqkv_s, wo_s, bias_s)
-    x2, qkv2, o2, a2 = run_time_forward(x1, mod, seg, wqkv_t, wo_t, bias_t)
-    cots = shift_clips(cotangent, False).reshape(n * FR, PATCHES, D)
-    dy = run_turn_frames(cots, pack_rows)
+    def carry(clips, js, back, number):
+        return (clips, n, js, back, number) if fast else None
+
+    def regroup(clips, back, half, odd):
+        if fast:
+            return jnp.stack([clips[0], odd[0], half[0], odd[1]])
+        return shift_clips(clips, back)
+
+    *half, x1, qkv1, o1, a1 = run_frame_forward(
+        frames, mod, wqkv_s, wo_s, bias_s, carry(cotangent, (2,), False, 2))
+    *odd, x2, qkv2, o2, a2 = run_time_forward(
+        x1, mod, seg, wqkv_t, wo_t, bias_t, carry(cotangent, (1, 3), False, 3))
+    cots = regroup(cotangent, False, *(half or [None]), *(odd or [None]))
+    dy = run_turn_frames(cots.reshape(n * FR, PATCHES, D), pack_rows)
     out, dx2, g_in, g_out, gb_in, gb_out, dmod3 = run_mlp(x2, dy, mod, win, bias_in, wout, bias_out)
 
-    def unpack(packed):
-        spread = jnp.take(packed, unpack_rows, axis=0).reshape(n, FR, PATCHES, D)
-        spread = jnp.where(live_back[:, :, None, None], spread, jnp.zeros((), packed.dtype))
-        return shift_clips(spread, True)
+    own_live = frame_ids[None, :] < lengths.reshape(n, n)[rank][:, None]
+
+    def spread(packed):
+        return jnp.take(packed, unpack_rows, axis=0, mode="clip").reshape(n, FR, PATCHES, D)
+
+    def only_live(parts):
+        return jnp.where(own_live[:, :, None, None], parts, jnp.zeros((), parts.dtype))
 
     def scatter(g):
         return lax.psum_scatter(g.astype(BF), ALL, scatter_dimension=0, tiled=True).astype(F32)
 
-    layer_out = unpack(out)
-    dx1, g_t, gb_t, dmod2 = run_time_back(x1, dx2, mod, seg, qkv2, o2, a2, wqkv_t, wo_t)
-    dx0, g_s, gb_s, dmod1 = run_frame_back(
-        frames, pack_rows, dx1, mod, qkv1, o1, a1, wqkv_s, wo_s)
-    grad_clips = unpack(dx0)
+    out = spread(out)
+    *half, dx1, g_t, gb_t, dmod2 = run_time_back(
+        x1, dx2, mod, seg, qkv2, o2, a2, wqkv_t, wo_t, carry(out, (2,), True, 4))
+    *odd, dx0, g_s, gb_s, dmod1 = run_frame_back(
+        frames, dx1, mod, qkv1, o1, a1, wqkv_s, wo_s, carry(out, (1, 3), True, 5))
+    layer_out = only_live(regroup(out, True, *(half or [None]), *(odd or [None])))
+    grad_clips = only_live(shift_clips(spread(dx0), True))
     grads = (g_in, g_out, g_t, g_s)
     if fast:
         s_in, s_out, s_t, s_s = scatter_all(grads, (0, 0, 1, 1), wide, n)

time: 882 us -> 664 us (0.75)
  the two profiles are of different devices: /device:TPU:1 before, /device:TPU:12 now
where the time goes in v3:
time: 664 us; the launch traced here: 656 us
  Pallas kernels  533 us (80%)
  local copies, waits for them, and re-layouts  66.4 us (10%)
  other arithmetic  24.9 us (4%)
  starting transfers between devices  23.6 us (4%)
    pallas_call x6, Pallas kernels, call(): return fn(*ins) if prefetch is None else fn(prefetch, *ins)  295 us
    pallas_call x1, Pallas kernels, scatter_all(): pl.pallas_call(functools.partial(scatter_kernel, ring, heights, ways), na...  133 us
    pallas_call x1, Pallas kernels, gather_all(): pl.pallas_call(functools.partial(gather_kernel, ring, n, heights, ways),...  104 us
    all_to_all x4, starting transfers between devices, exchange(): return lax.all_to_all(x, ALL, split_axis=0, concat_axis=0, tiled=True)  21.7 us
  transfers between devices with their start and end apart: 7, of which 1 were waited for; matrix products, arithmetic and copies ran while one was open for 8% of the time, Pallas kernels for 36%

profile of v3, /device:TPU:12, one launch (start us, length us, event | category | flops | bytes accessed | tf_op | source)
XLA Modules:
  0.0 656.3 jit_solution(15477273189557309784)
XLA Ops:
  0.7 2.2 reshape.596
  3.5 0.7 broadcast_in_dim.25
  4.2 0.8 pad_maximum_fusion.3
  6.1 1.1 reduce.10
  7.2 1.7 reshape.731
  8.9 6.0 all-to-all-start
  17.3 0.8 gather_fusion.5
  18.0 1.2 gather_fusion.6
  19.4 3.1 fusion.23
  22.5 0.8 gather_fusion.3
  23.2 104.1 %gather_all.1 = (bf16[4,16,64,768]{3,2,1,0:T(8,128)(2,1)}, bf16[768,3072]{1,0:T(8,128)(2,1)}, bf16[3072,768]{1,0:T(8,128)(2,1)}, bf16[768,2304]{1,0:T(8,128)(2,1...) custom-call(bf16[4,16,64,768]{3,2,1,0:T(8,128)(2,1)} %refs_0_.3, ...), custom_call_target="tpu_custom_call" | custom-call | tf_op jit(solution)/shard_map/gather_all/pallas_call | solution.py:549
  127.4 5.3 gather_fusion.1
  133.9 1.0 reshape.732
  137.3 1.3 all_to_all.38
  138.6 4.5 all-to-all-start.1
  146.0 5.2 all-to-all-done.1
  153.0 1.4 copy.129
  154.5 41.8 %frame_forward.1 = (bf16[1,16,64,768]{3,2,1,0:T(8,128)(2,1)}, f32[64,32,768]{2,1,0:T(8,128)}, bf16[2048,2304]{1,0:T(8,128)(2,1)}, bf16[2048,768]{1,0:T(8,128)(2,1)}, f32[2048,768]{1,0:T(8,128)}) custom-call(bf16[4,16,64,768]{3,2,1,0:T(8,128)(2,1)} %refs_0_.5, bf16[32,64,768]{2,1,0:T(8,128)(2,1)} %gather_fusion.1, f32[9,32,768]{2,1,0:T(8,128)} %bitcast.146, ...), custom_call_target="tpu_custom_call" | custom-call | flops 9663676416 | bytes 33917952 | tf_op jit(solution)/shard_map/frame_forward/pallas_call | solution.py:368
  196.3 41.9 %time_forward.1 = (bf16[2,16,64,768]{3,2,1,0:T(8,128)(2,1)}, f32[64,32,768]{2,1,0:T(8,128)}, bf16[2048,2304]{1,0:T(8,128)(2,1)}, bf16[2048,768]{1,0:T(8,128)(2,1)}, f32[2048,768]{1,0:T(8,128)}) custom-call(bf16[4,16,64,768]{3,2,1,0:T(8,128)(2,1)} %refs_0_.5, f32[64,32,768]{2,1,0:T(8,128)} %get-tuple-element.56.refs_1_, f32[9,32,768]{2,1,0:T(8,128)} %bitcast.147, ...), custom_call_target="tpu_custom_call" | custom-call | flops 9663676416 | bytes 37096448 | tf_op jit(solution)/shard_map/time_forward/pallas_call | solution.py:368
  238.2 2.2 fusion.29
  241.0 3.2 pad_maximum_fusion
  244.2 6.9 %turn_frames.1.dy = f32[64,32,768]{2,1,0:T(8,128)} custom-call(s32[32]{0:T(128)} %get-tuple-element.93.rows_ref, bf16[64,64,768]{2,1,0:T(8,128)(2,1)} %bitcast.123, bf16[64,64,768]{2,1,0:T(8,128)(2,1)} %bitcast.124, bf16[64,64,768]{2,1,0:T(8,128)(2,1)} %bitcast.125, bf16[64,64,768]{2,1,0:T(8,128)(2,1)} %bitcast.126, bf16[64,64,768]{2,1,0:T(8,128)(2,1)} %bitcast.127, ...), custom_call_target="tpu_custom_call" | custom-call | flops 1000 | bytes 56623104 | tf_op jit(solution)/shard_map/turn_frames/pallas_call | solution.py:368
  251.1 85.4 %mlp_both.1 = (bf16[32,64,768]{2,1,0:T(8,128)(2,1)}, f32[64,32,768]{2,1,0:T(8,128)}, f32[768,3072]{1,0:T(8,128)}, f32[3072,768]{1,0:T(8,128)}, f32[1,3072]{1,0:T...) custom-call(f32[64,32,768]{2,1,0:T(8,128)} %get-tuple-element.59.x2, f32[64,32,768]{2,1,0:T(8,128)} %turn_frames.1.dy, ...), custom_call_target="tpu_custom_call" | custom-call | flops 57982058496 | bytes 51542016 | tf_op jit(solution)/shard_map/mlp_both/pallas_call | solution.py:368
  336.6 5.5 gather_fusion.7
  342.1 62.0 %time_back.1 = (bf16[1,16,64,768]{3,2,1,0:T(8,128)(2,1)}, f32[32,64,768]{2,1,0:T(8,128)}, f32[768,3072]{1,0:T(8,128)}, f32[1,768]{1,0:T(1,128)}, f32[3,32,768]{2,1,0:T(8,128)}) custom-call(bf16[4,16,64,768]{3,2,1,0:T(8,128)(2,1)} %bitcast.131, f32[64,32,768]{2,1,0:T(8,128)} %get-tuple-element.56.refs_1_, f32[64,32,768]{2,1,0:T(8,128)} %get-tuple-element.65.refs_2_, ...), custom_call_target="tpu_custom_call" | custom-call | flops 19327352832 | bytes 53120000 | tf_op jit(solution)/shard_map/time_back/pallas_call | solution.py:368
  404.1 57.3 %frame_back.1 = (bf16[2,16,64,768]{3,2,1,0:T(8,128)(2,1)}, bf16[32,64,768]{2,1,0:T(8,128)(2,1)}, f32[768,3072]{1,0:T(8,128)}, f32[1,768]{1,0:T(1,128)}, f32[3,32,768]{2,1,0:T(8,128)}) custom-call(bf16[4,16,64,768]{3,2,1,0:T(8,128)(2,1)} %bitcast.132, bf16[32,64,768]{2,1,0:T(8,128)(2,1)} %gather_fusion.1, f32[32,64,768]{2,1,0:T(8,128)} %get-tuple-element.69.refs_2_, ...), custom_call_target="tpu_custom_call" | custom-call | flops 19327352832 | bytes 46795776 | tf_op jit(solution)/shard_map/frame_back/pallas_call | solution.py:368
  461.5 1.3 maximum_bitcast_fusion
  464.0 1.3 reduce.11
  465.4 0.8 reshape.733
  466.2 5.0 all-to-all-start.2
  472.9 3.7 gather_fusion.8
  476.5 5.7 slice_bitcast_fusion
  482.2 1.2 collective-permute-start
  485.7 0.8 convert_reduce_fusion
  488.5 2.2 all_to_all.35
  490.6 6.2 all-to-all-start.3
  497.6 133.5 %scatter_all.1 = (f32[24,3072]{1,0:T(8,128)}, f32[96,768]{1,0:T(8,128)}, f32[24,3072]{1,0:T(8,128)}, f32[24,3072]{1,0:T(8,128)}, f32[8,48,3072]{2,1,0:T(8,128)},...) custom-call(f32[768,3072]{1,0:T(8,128)} %get-tuple-element.83.refs_0_, ...), custom_call_target="tpu_custom_call" | custom-call | tf_op jit(solution)/shard_map/scatter_all/pallas_call | solution.py:676
  631.1 1.8 slice.207
  632.8 1.5 slice.208
  634.4 1.6 slice.211
  636.0 1.5 slice.212
  637.5 1.5 slice_bitcast_fusion.1
  639.4 1.0 copy-done.4
  640.9 7.8 %maximum_select_fusion.1 = (bf16[4,16,64,768]{3,2,1,0:T(8,128)(2,1)}, bf16[4,16,64,768]{3,2,1,0:T(8,128)(2,1)}) fusion(bf16[1,16,64,768]{3,2,1,0:T(8,128)(2,1)} %bitcast.34, bf16[1,16,64,768]{3,2,1,0:T(8,128)(2,1)} %bitcast.33, bf16[1,16,64,768]{3,2,1,0:T(8,128)(2,1)} %bitcast.32, bf16[1,16,64,768]{3,2,1,0:T(8,128)(2,1)S(1)} %copy-done.4, ...), kind=kLoop, calls=%fused_computation.12 | loop fusion | flops 25165824 | bytes 25165888 | tf_op jit(solution)/shard_map/jit(_where)/select_n | solution.py:812
  648.7 1.5 copy.128
  652.7 1.3 reshape.617
  654.7 0.7 copy.137
  655.4 0.7 copy.138
  (159 shorter events, 24.5 us)
Async XLA Ops:
  0.6 16.0 %copy-start = (s32[16,16]{1,0:T(8,128)S(1)}, s32[16,16]{1,0:T(8,128)}, u32[]{:S(2)}) copy-start(s32[16,16]{1,0:T(8,128)} %param.20) | copy-start | bytes 3076
  5.0 10.0 %copy-start.21 = (s32[16]{0:T(128)S(1)}, s32[16]{0:T(128)}, u32[]{:S(2)}) copy-start(s32[16]{0:T(128)} %param.19) | copy-start | bytes 196
  5.0 11.5 %copy-start.22 = (bf16[216]{0:T(256)(128)(2,1)S(1)}, bf16[216]{0:T(256)(128)(2,1)}, u32[]{:S(2)}) copy-start(bf16[216]{0:T(256)(128)(2,1)} %param.22) | copy-start | bytes 1300
  8.9 125.0 %all-to-all-start = ((bf16[32,2,5748]{2,1,0:T(2,128)(2,1)}), bf16[32,2,5748]{2,1,0:T(2,128)(2,1)S(1)}, u32[]{:S(2)}, u32[]{:S(2)}) async-start(bf16[32,2,5748]{2,1,0:T(2,128)(2,1)} %reshape.731), calls=%async_computation | async-start | bytes 1474560 | tf_op jit(solution)/shard_map/all_to_all | solution.py:715
  15.1 1.5 copy-start.2
  135.5 16.2 %copy-start.5 = (bf16[256,768]{1,0:T(8,128)(2,1)}, bf16[256,768]{1,0:T(8,128)(2,1)S(1)}, u32[]{:S(2)}) copy-start(bf16[256,768]{1,0:T(8,128)(2,1)S(1)} %convert_element_type.58) | copy-start | bytes 1179652
  136.2 15.8 %copy-start.7 = (bf16[768,216]{1,0:T(8,128)(2,1)}, bf16[768,216]{1,0:T(8,128)(2,1)S(1)}, u32[]{:S(2)}) copy-start(bf16[768,216]{1,0:T(8,128)(2,1)S(1)} %reshape.598) | copy-start | bytes 995332
  138.6 12.6 %all-to-all-start.1 = ((f32[32,1,1728]{2,1,0:T(1,128)}), f32[32,1,1728]{2,1,0:T(1,128)S(1)}, u32[]{:S(2)}, u32[]{:S(2)}) async-start(f32[32,1,1728]{2,1,0:T(1,128)} %all_to_all.38), calls=%async_computation.1 | async-start | bytes 458752 | tf_op jit(solution)/shard_map/all_to_all | solution.py:715
  238.2 2.4 slice-start
  238.2 2.8 copy-start.10
  404.1 57.4 %copy-start.12 = (f32[3,32,768]{2,1,0:T(8,128)S(1)}, f32[3,32,768]{2,1,0:T(8,128)}, u32[]{:S(2)}) copy-start(f32[3,32,768]{2,1,0:T(8,128)} %get-tuple-element.78) | copy-start | bytes 884740
  461.4 1.4 copy-start.20
  461.4 9.8 %copy-start.19 = (f32[1,768]{1,0:T(1,128)S(1)}, f32[1,768]{1,0:T(1,128)}, u32[]{:S(2)}) copy-start(f32[1,768]{1,0:T(1,128)} %get-tuple-element.79) | copy-start | bytes 9220
  461.4 9.9 %copy-start.18 = (f32[1,768]{1,0:T(1,128)S(1)}, f32[1,768]{1,0:T(1,128)}, u32[]{:S(2)}) copy-start(f32[1,768]{1,0:T(1,128)} %get-tuple-element.80) | copy-start | bytes 9220
  461.4 10.5 %copy-start.16 = (f32[1,3072]{1,0:T(1,128)S(1)}, f32[1,3072]{1,0:T(1,128)}, u32[]{:S(2)}) copy-start(f32[1,3072]{1,0:T(1,128)} %get-tuple-element.81) | copy-start | bytes 36868
  461.5 11.3 %copy-start.17 = (f32[1,768]{1,0:T(1,128)S(1)}, f32[1,768]{1,0:T(1,128)}, u32[]{:S(2)}) copy-start(f32[1,768]{1,0:T(1,128)} %get-tuple-element.82) | copy-start | bytes 9220
  461.5 11.4 %copy-start.3 = (bf16[32,64,768]{2,1,0:T(8,128)(2,1)S(1)}, bf16[32,64,768]{2,1,0:T(8,128)(2,1)}, u32[]{:S(2)}) copy-start(bf16[32,64,768]{2,1,0:T(8,128)(2,1)} %get-tuple-element.75) | copy-start | bytes 9437188
  466.2 17.9 %all-to-all-start.2 = ((bf16[32,2,864]{2,1,0:T(2,128)(2,1)}), bf16[32,2,864]{2,1,0:T(2,128)(2,1)S(1)}, u32[]{:S(2)}, u32[]{:S(2)}) async-start(bf16[32,2,864]{2,1,0:T(2,128)(2,1)} %reshape.733), calls=%async_computation.2 | async-start | bytes 229376 | tf_op jit(solution)/shard_map/all_to_all | solution.py:715
  476.5 10.2 %copy-start.8 = (bf16[768,216]{1,0:T(8,128)(2,1)S(1)}, bf16[768,216]{1,0:T(8,128)(2,1)}, u32[]{:S(2)}) copy-start(bf16[768,216]{1,0:T(8,128)(2,1)} %copy-done.7) | copy-start | bytes 995332
  482.2 5.0 copy-start.6
  482.2 157.2 %collective-permute-start = (bf16[16,64,768]{2,1,0:T(8,128)(2,1)}, bf16[16,64,768]{2,1,0:T(8,128)(2,1)}, u32[]{:S(2)}, u32[]{:S(2)}) collective-permute-start(bf16[16,64,768]{2,1,0:T(8,128)(2,1)} %get-tuple-element.97), channel_id=1, source_target_pairs={{0,3},{1,0},{2,1},{3,2},{4,7},{5,4},{6,5},{7,6},{8,11},{9,8},{10,9... | collective-permute-start | bytes 4718600 | tf_op jit(solution)/shard_map/ppermute | solution.py:723
  483.4 156.0 %collective-permute-start.1 = (bf16[16,64,768]{2,1,0:T(8,128)(2,1)}, bf16[16,64,768]{2,1,0:T(8,128)(2,1)}, u32[]{:S(2)}, u32[]{:S(2)}) collective-permute-start(bf16[16,64,768]{2,1,0:T(8,128)(2,1)} %get-tuple-element.96), channel_id=1, source_target_pairs={{0,2},{1,3},{2,0},{3,1},{4,6},{5,7},{6,4},{7,5},{8,10},{9,11},{10,... | collective-permute-start | bytes 4718600 | tf_op jit(solution)/shard_map/ppermute | solution.py:723
  483.9 155.5 %collective-permute-start.2 = (bf16[16,64,768]{2,1,0:T(8,128)(2,1)}, bf16[16,64,768]{2,1,0:T(8,128)(2,1)}, u32[]{:S(2)}, u32[]{:S(2)}) collective-permute-start(bf16[16,64,768]{2,1,0:T(8,128)(2,1)} %get-tuple-element.98), channel_id=1, source_target_pairs={{0,1},{1,2},{2,3},{3,0},{4,5},{5,6},{6,7},{7,4},{8,9},{9,10},{10,1... | collective-permute-start | bytes 4718600 | tf_op jit(solution)/shard_map/ppermute | solution.py:723
  490.6 158.1 %all-to-all-start.3 = ((f32[32,1,11496]{2,1,0:T(1,128)}), f32[32,1,11496]{2,1,0:T(1,128)}, u32[]{:S(2)}, u32[]{:S(2)}) async-start(f32[32,1,11496]{2,1,0:T(1,128)} %all_to_all.35), calls=%async_computation.3 | async-start | bytes 2949120 | tf_op jit(solution)/shard_map/all_to_all | solution.py:715
  631.0 8.0 %copy-start.9 = (bf16[2,16,64,768]{3,2,1,0:T(8,128)(2,1)S(1)}, bf16[2,16,64,768]{3,2,1,0:T(8,128)(2,1)}, u32[]{:S(2)}) copy-start(bf16[2,16,64,768]{3,2,1,0:T(8,128)(2,1)} %get-tuple-element.73) | copy-start | bytes 9437188
  639.0 1.4 copy-start.4
  639.1 1.9 copy-start.11
  650.2 3.9 copy-start.15
  650.2 4.5 copy-start.14
  650.2 5.9 copy-start.1
  650.3 5.1 copy-start.13

commit v4 on v3

--- a/solution.py
+++ b/solution.py
@@ -231,7 +231,7 @@
     dx2[...] = (grad + back).reshape(PT, LIVE, D)
 
 
-def attn_back_tile(x, grad, shift, scale, gate, branch, qkv, o, wqkv, wo, gw, gbo, do, dqkv, mask):
+def attn_back_tile(x, grad, shift, scale, gate, branch, qkv, o, wqkv, wo, gw, gbo, do, dqkv, mask, tick):
     first = pl.program_id(0) == 0
 
     @pl.when(first)
@@ -243,7 +243,9 @@
     do[...] = dot_nt(da, wo[...]).astype(BF)
     gw[:, 3 * D :] += dot_tn(o[...], da)
     gbo[...] += jnp.sum(da.astype(F32), axis=0, keepdims=True)
+    tick(0)
     attend_back(qkv, do, dqkv, mask)
+    tick(1)
     xhat, rstd = normalise(x)
     h = (xhat * (1.0 + scale) + shift).astype(BF)
     dh = jnp.zeros((TILE, D), F32)
@@ -256,24 +258,28 @@
     return dx, dh, dh * xhat, grad * branch
 
 
-def time_back(x1, dx2, mod, seg, qkv, o, a2, wqkv, wo, dx1, gw, gbo, dmod, do, dqkv, scratch):
+def no_tick(place):
+    pass
+
+
+def time_back(x1, dx2, mod, seg, qkv, o, a2, wqkv, wo, dx1, gw, gbo, dmod, do, dqkv, scratch, tick=no_tick):
     @pl.when(pl.program_id(0) == 0)
     def _():
         dmod[...] = jnp.zeros_like(dmod)
 
     dx, d_shift, d_scale, d_gate = attn_back_tile(
         x1[...].reshape(TILE, D), dx2[...].reshape(TILE, D), per_patch(mod[0]), per_patch(mod[1]),
-        per_patch(mod[2]), a2[...], qkv, o, wqkv, wo, gw, gbo, do, dqkv, attn_mask(seg))
+        per_patch(mod[2]), a2[...], qkv, o, wqkv, wo, gw, gbo, do, dqkv, attn_mask(seg), tick)
     dmod[0] += sum_groups(d_shift)
     dmod[1] += sum_groups(d_scale)
     dmod[2] += sum_groups(d_gate)
     swap_major(dx, scratch, dx1, PT, LIVE)
 
 
-def frame_back(frames, dx1, mod, qkv, o, a1, wqkv, wo, dx0, gw, gbo, dmod, do, dqkv):
+def frame_back(frames, dx1, mod, qkv, o, a1, wqkv, wo, dx0, gw, gbo, dmod, do, dqkv, tick=no_tick):
     dx, d_shift, d_scale, d_gate = attn_back_tile(
         frames[...].reshape(TILE, D).astype(F32), dx1[...].reshape(TILE, D), per_frame(mod[0]), per_frame(mod[1]),
-        per_frame(mod[2]), a1[...], qkv, o, wqkv, wo, gw, gbo, do, dqkv, None)
+        per_frame(mod[2]), a1[...], qkv, o, wqkv, wo, gw, gbo, do, dqkv, None, tick)
     dmod[0] = sum_patches(d_shift)
     dmod[1] = sum_patches(d_scale)
     dmod[2] = sum_patches(d_gate)
@@ -319,21 +325,53 @@
     ]
 
 
-def carrying(kernel, count, n, js, back, *refs):
-    src, ins, dst, rest = refs[0], refs[1 : 1 + count], refs[1 + count], refs[2 + count : -2]
-    copies = clip_copies(n, js, back, src, dst, *refs[-2:])
-
-    @pl.when(pl.program_id(0) == 0)
+def carrying(kernel, count, n, js, back, plan, *refs):
+    sent = 0 if plan is None else plan.inputs
+    made = 0 if plan is None else plan.outputs
+    held = 0 if plan is None else plan.scratches
+    src, grads, ins = refs[0], refs[1 : 1 + sent], refs[1 + sent : 1 + sent + count]
+    at = 1 + sent + count
+    dst, results, rest = refs[at], refs[at + 1 : at + 1 + made], refs[at + 1 + made : len(refs) - 2 - held]
+    copies = clip_copies(n, js, back, src, dst, *refs[len(refs) - 2 - held : len(refs) - held])
+    step = pl.program_id(0)
+    sums = None if plan is None else plan.steps(grads + results + refs[len(refs) - held :])
+
+    @pl.when(step == 0)
     def _():
         w, k = lax.axis_index("wide"), lax.axis_index("narrow")
-        greet([(w, (k + j) % n) for j in js])
+        peers = [(w, (k + j) % n) for j in js]
+        greet(peers if sums is None else peers + list(sums.peers))
+        if sums is not None:
+            sums.begin()
         for copy in copies:
             copy.start()
 
-    kernel(*ins, *rest)
-
-    @pl.when(pl.program_id(0) == GRID - 1)
+    if sums is None:
+        kernel(*ins, *rest)
+    else:
+        @pl.when(step > 0)
+        def _():
+            sums.hop(2 * step - 1)
+
+        def tick(place):
+            @pl.when(step == 0)
+            def _():
+                if place == 0:
+                    sums.load_first()
+                else:
+                    sums.first_hop()
+
+            if place == 1:
+                @pl.when(step > 0)
+                def _():
+                    sums.hop(2 * step)
+
+        kernel(*ins, *rest, tick=tick)
+
+    @pl.when(step == GRID - 1)
     def _():
+        if sums is not None:
+            sums.finish()
         for copy in copies:
             copy.wait()
 
@@ -342,11 +380,16 @@
     moved = sum(a.size * a.dtype.itemsize for a in tuple(ins) + tuple(outs))
     params = {}
     if carry is not None:
-        src, n, js, back, number = carry
-        kernel = functools.partial(carrying, kernel, len(ins), n, js, back)
-        ins, in_specs = [src] + ins, [ANY] + in_specs
-        outs, out_specs = [shape_of((len(js),) + src.shape[1:], src.dtype)] + outs, [ANY] + out_specs
+        src, n, js, back, number, plan, grads = carry
+        kernel = functools.partial(carrying, kernel, len(ins), n, js, back, plan)
+        ins, in_specs = [src] + grads + ins, [ANY] * (1 + len(grads)) + in_specs
+        first = [shape_of((len(js),) + src.shape[1:], src.dtype)]
+        first_specs = [ANY]
         scratch = scratch + [pltpu.SemaphoreType.DMA((len(js),))] * 2
+        if plan is not None:
+            first, first_specs = first + plan.out_shapes, first_specs + plan.out_specs
+            scratch = scratch + plan.scratch
+        outs, out_specs = first + outs, first_specs + out_specs
         params = dict(collective_id=number, has_side_effects=True)
     grid_spec = pltpu.PrefetchScalarGridSpec(
         num_scalar_prefetch=0 if prefetch is None else 1,
@@ -564,143 +607,194 @@
     return got[0], got[1:]
 
 
-def scatter_kernel(ring, heights, ways, *refs):
-    count = len(heights)
-    grads, outs, stages = refs[:count], refs[count : 2 * count], refs[2 * count : 3 * count]
-    local, part, came, went, last, fin_s, fin_r = (
-        refs[(3 + i) * count : (4 + i) * count] for i in range(7)
-    )
-    ring_s, ring_r, core_s, core_r, x_s, x_r, load_sem, part_sem = refs[10 * count :]
-    w, k, r, x, c, wide_at = place_of(ring)
-    other_x = (w, 2 * (1 - x) + c)
-    other_c = (w, 2 * x + 1 - c)
-    steps = ((wide_at((r + 1) % ring), k), (wide_at((r + ring - 1) % ring), k))
-    greet(steps + (other_x, other_c))
-    final = ring - 1
-
-    def place(t, s):
-        return (r + 2 * ring - 1 - s) % ring if ways[t] == 0 else (r + 1 + s) % ring
-
-    def rows(t, s, column, core):
-        block = 4 * wide_at(place(t, s)) + 2 * column + core
-        return pl.ds(pl.multiple_of(block * heights[t], 8), heights[t])
-
-    def half(t, column):
-        return pl.ds(column * heights[t], heights[t])
-
-    def core_copy(t, s, column):
-        return send(grads[t].at[rows(t, s, column, 1 - c)], stages[t].at[s, half(t, column)],
-                    core_s.at[t, s, column], core_r.at[t, s, column], other_c)
-
-    def local_load(t, s, slot, column):
-        return pltpu.make_async_copy(grads[t].at[rows(t, s, column, c)], local[t].at[slot, half(t, column)],
-                                     load_sem.at[t, slot, column])
-
-    def part_load(t, s, slot):
-        return pltpu.make_async_copy(stages[t].at[s], part[t].at[slot], part_sem.at[t, slot])
-
-    def ring_copy(t, s):
-        return send(went[t].at[s], came[t].at[s], ring_s.at[t, s], ring_r.at[t, s], steps[ways[t]])
-
-    def x_copy(t):
-        return send(fin_s[t], fin_r[t], x_s.at[t], x_r.at[t], other_x)
-
-    order = (0, 2, 1, 3)
-
-    def fetch(t, s, slot):
+class Sums:
+    def __init__(self, plan, refs):
+        self.plan, count = plan, len(plan.pieces)
+        self.grads, refs = refs[: plan.inputs], refs[plan.inputs :]
+        self.outs, refs = refs[: len(plan.shapes)], refs[len(plan.shapes) :]
+        self.stages, refs = refs[:count], refs[count:]
+        self.own, self.part, self.came, self.went, self.last, self.fin_s, self.fin_r = (
+            refs[i * count : (i + 1) * count] for i in range(7)
+        )
+        (self.ring_s, self.ring_r, self.core_s, self.core_r, self.x_s, self.x_r, self.load_sem,
+         self.part_sem) = refs[7 * count :]
+        ring = plan.ring
+        self.w, self.k, self.r, self.x, self.c, self.wide_at = place_of(ring)
+        self.other_x = (self.w, 2 * (1 - self.x) + self.c)
+        self.other_c = (self.w, 2 * self.x + 1 - self.c)
+        self.next = ((self.wide_at((self.r + 1) % ring), self.k), (self.wide_at((self.r + ring - 1) % ring), self.k))
+        self.peers = self.next + (self.other_x, self.other_c)
+        self.final = ring - 1
+
+    def source(self, t, s, column, core):
+        ring = self.plan.ring
+        g, col, width, height, way = self.plan.pieces[t]
+        place = (self.r + 2 * ring - 1 - s) % ring if way == 0 else (self.r + 1 + s) % ring
+        block = 4 * self.wide_at(place) + 2 * column + core
+        return self.grads[g].at[pl.ds(pl.multiple_of(block * height, 8), height), pl.ds(col, width)]
+
+    def half(self, t, column):
+        height = self.plan.pieces[t][3]
+        return pl.ds(column * height, height)
+
+    def core_copy(self, t, s, column):
+        return send(self.source(t, s, column, 1 - self.c), self.stages[t].at[s, self.half(t, column)],
+                    self.core_s.at[t, s, column], self.core_r.at[t, s, column], self.other_c)
+
+    def own_load(self, t, s, slot, column):
+        return pltpu.make_async_copy(self.source(t, s, column, self.c), self.own[t].at[slot, self.half(t, column)],
+                                     self.load_sem.at[t, slot, column])
+
+    def part_load(self, t, s, slot):
+        return pltpu.make_async_copy(self.stages[t].at[s], self.part[t].at[slot], self.part_sem.at[t, slot])
+
+    def ring_copy(self, t, s):
+        return send(self.went[t].at[s], self.came[t].at[s], self.ring_s.at[t, s], self.ring_r.at[t, s],
+                    self.next[self.plan.pieces[t][4]])
+
+    def x_copy(self, t):
+        return send(self.fin_s[t], self.fin_r[t], self.x_s.at[t], self.x_r.at[t], self.other_x)
+
+    def each(self):
+        return range(len(self.plan.pieces))
+
+    def fetch(self, t, s, slot):
         for column in range(2):
-            core_copy(t, s, column).wait_recv()
-        part_load(t, s, slot).start()
+            self.core_copy(t, s, column).wait_recv()
+        self.part_load(t, s, slot).start()
         for column in range(2):
-            local_load(t, s, slot, column).start()
-
-    def total(t, s, slot):
+            self.own_load(t, s, slot, column).start()
+
+    def total(self, t, s, slot):
         for column in range(2):
-            local_load(t, s, slot, column).wait()
-        part_load(t, s, slot).wait()
-        return local[t][slot] + part[t][slot]
-
-    for t in order:
-        for column in range(2):
-            core_copy(t, 0, column).start()
-    for s in range(1, ring):
-        for t in order:
-            for column in range(2):
-                core_copy(t, s, column).start()
-    for t in order:
-        fetch(t, 0, 0)
-    for t in order:
-        fetch(t, 1, 1)
-        went[t][0] = total(t, 0, 0).astype(BF)
-        ring_copy(t, 0).start()
+            self.own_load(t, s, slot, column).wait()
+        self.part_load(t, s, slot).wait()
+        return self.own[t][slot] + self.part[t][slot]
+
+    def begin(self):
+        for s in range(self.plan.ring):
+            for t in self.each():
+                for column in range(2):
+                    self.core_copy(t, s, column).start()
+
+    def load_first(self):
+        for t in self.each():
+            self.fetch(t, 0, 0)
+
+    def first_hop(self):
+        for t in self.each():
+            self.fetch(t, 1, 1)
+            self.went[t][0] = self.total(t, 0, 0).astype(BF)
+            self.ring_copy(t, 0).start()
+
+    def hop(self, s):
+        slot = s % 2
+        for t in self.each():
+            self.fetch(t, s + 1, 1 - slot)
+            value = self.total(t, s, slot)
+            self.ring_copy(t, s - 1).wait_recv()
+            self.went[t][s] = (value + self.came[t][s - 1].astype(F32)).astype(BF)
+            self.ring_copy(t, s).start()
+
+    def finish(self):
+        final = self.final
+        for t in self.each():
+            height = self.plan.pieces[t][3]
+            value = self.total(t, final, final % 2)
+            self.ring_copy(t, final - 1).wait_recv()
+            value = value + self.came[t][final - 1].astype(F32)
+            self.last[t][0] = value[:height]
+            self.last[t][1] = value[height:]
+            self.fin_s[t][...] = self.last[t][1 - self.x].astype(BF)
+            self.x_copy(t).start()
+        for t in self.each():
+            self.x_copy(t).wait_recv()
+            value = self.last[t][self.x] + self.fin_r[t][...].astype(F32)
+            for o, out_col, col, width in self.plan.places[t]:
+                self.outs[o][:, out_col : out_col + width] = value[:, col : col + width]
+        for t in self.each():
+            self.x_copy(t).wait_send()
+            for s in range(final):
+                self.ring_copy(t, s).wait_send()
+            for s in range(self.plan.ring):
+                for column in range(2):
+                    self.core_copy(t, s, column).wait_send()
+
+
+class Plan:
+    def __init__(self, ring, inputs, pieces, shapes, places):
+        self.ring, self.inputs, self.pieces, self.shapes, self.places = ring, inputs, pieces, shapes, places
+        count = len(pieces)
+        sizes = [(height, width) for _, _, width, height, _ in pieces]
+        sems, vmem = pltpu.SemaphoreType.DMA, pltpu.VMEM
+        self.out_shapes = [shape_of(hw, F32) for hw in shapes]
+        self.out_shapes += [shape_of((ring, 2 * h, wd), F32) for h, wd in sizes]
+        self.out_specs = [pl.BlockSpec(memory_space=pltpu.VMEM)] * len(shapes) + [ANY] * count
+        self.outputs = len(self.out_shapes)
+        self.scratch = (
+            [vmem((2, 2 * h, wd), F32) for h, wd in sizes]
+            + [vmem((2, 2 * h, wd), F32) for h, wd in sizes]
+            + [vmem((ring - 1, 2 * h, wd), BF) for h, wd in sizes]
+            + [vmem((ring - 1, 2 * h, wd), BF) for h, wd in sizes]
+            + [vmem((2, h, wd), F32) for h, wd in sizes]
+            + [vmem((h, wd), BF) for h, wd in sizes]
+            + [vmem((h, wd), BF) for h, wd in sizes]
+            + [sems((count, ring))] * 2
+            + [sems((count, ring, 2))] * 2
+            + [sems((count,))] * 2
+            + [sems((count, 2, 2)), sems((count, 2))]
+        )
+        self.scratches = len(self.scratch)
+
+    def steps(self, refs):
+        return Sums(self, refs)
+
+
+def mlp_plan(ring, g_in, g_out, devices):
+    a, b = g_in.shape[0] // devices, g_out.shape[0] // devices
+    wa, wb = g_in.shape[1], g_out.shape[1]
+    return Plan(ring, 2, [(0, 0, wa, a, 0), (1, 0, wb, b, 1)], [(a, wa), (b, wb)], [[(0, 0, 0, wa)], [(1, 0, 0, wb)]])
+
+
+def attn_plan(ring, g, devices):
+    h, half, cut = g.shape[0] // devices, 2 * D, 3 * D
+    return Plan(ring, 1, [(0, 0, half, h, 0), (0, half, half, h, 1)], [(h, cut), (h, D)],
+                [[(0, 0, 0, half)], [(0, half, 0, cut - half), (1, 0, cut - half, D)]])
+
+
+def scatter_kernel(plan, *refs):
+    sums = plan.steps(refs)
+    greet(sums.peers)
+    sums.begin()
+    sums.load_first()
+    sums.first_hop()
 
     def body(s, carry):
-        slot = s % 2
-        for t in order:
-            fetch(t, s + 1, 1 - slot)
-            value = total(t, s, slot)
-            ring_copy(t, s - 1).wait_recv()
-            went[t][s] = (value + came[t][s - 1].astype(F32)).astype(BF)
-            ring_copy(t, s).start()
+        sums.hop(s)
         return carry
 
-    lax.fori_loop(1, final, body, 0)
-    for t in order:
-        value = total(t, final, final % 2)
-        ring_copy(t, final - 1).wait_recv()
-        value = value + came[t][final - 1].astype(F32)
-        last[t][0] = value[: heights[t]]
-        last[t][1] = value[heights[t] :]
-        fin_s[t][...] = last[t][1 - x].astype(BF)
-        x_copy(t).start()
-    for t in order:
-        x_copy(t).wait_recv()
-        outs[t][...] = last[t][x] + fin_r[t][...].astype(F32)
-    for t in order:
-        x_copy(t).wait_send()
-        for s in range(final):
-            ring_copy(t, s).wait_send()
-        for s in range(ring):
-            for column in range(2):
-                core_copy(t, s, column).wait_send()
-
-
-def scatter_all(grads, ways, ring, n):
-    count = len(grads)
-    devices = ring * n
-    heights = tuple(g.shape[0] // devices for g in grads)
-    widths = tuple(g.shape[1] for g in grads)
-    each = tuple(zip(heights, widths))
-    sems = pltpu.SemaphoreType.DMA
-    vmem = pltpu.VMEM
+    lax.fori_loop(1, sums.final, body, 0)
+    sums.finish()
+
+
+def scatter_last(g, plan):
     got = pl.pallas_call(
-        functools.partial(scatter_kernel, ring, heights, ways),
-        name="scatter_all",
-        out_shape=[shape_of(hw, F32) for hw in each]
-        + [shape_of((ring, 2 * h, wd), F32) for h, wd in each],
-        in_specs=[ANY] * count,
-        out_specs=[pl.BlockSpec(memory_space=pltpu.VMEM)] * count + [ANY] * count,
-        scratch_shapes=[vmem((2, 2 * h, wd), F32) for h, wd in each]
-        + [vmem((2, 2 * h, wd), F32) for h, wd in each]
-        + [vmem((ring - 1, 2 * h, wd), BF) for h, wd in each]
-        + [vmem((ring - 1, 2 * h, wd), BF) for h, wd in each]
-        + [vmem((2, h, wd), F32) for h, wd in each]
-        + [vmem((h, wd), BF) for h, wd in each]
-        + [vmem((h, wd), BF) for h, wd in each]
-        + [sems((count, ring))] * 2
-        + [sems((count, ring, 2))] * 2
-        + [sems((count,))] * 2
-        + [sems((count, 2, 2)), sems((count, 2))],
+        functools.partial(scatter_kernel, plan),
+        name="scatter_last",
+        out_shape=plan.out_shapes,
+        in_specs=[ANY],
+        out_specs=plan.out_specs,
+        scratch_shapes=plan.scratch,
         compiler_params=pltpu.CompilerParams(
             collective_id=1, has_side_effects=True, vmem_limit_bytes=VMEM_LIMIT
         ),
-    )(*grads)
-    return got[:count]
+    )(g)
+    return got[:2]
 
 
 def tuned(mesh):
     wide, n = mesh.shape["wide"], mesh.shape["narrow"]
-    if n != 4 or wide < 4 or wide % 2 or D % (8 * wide * n):
+    if n != 4 or wide != 2 * GRID or D % (8 * wide * n):
         return False
     for w in range(wide):
         for k in range(n):
@@ -787,8 +881,8 @@
     mod_rows = jnp.swapaxes(mod_rows, 0, 1).reshape(2 * n, 9, D)
     mod = jnp.swapaxes(mod_rows[row_choice], 0, 1)
 
-    def carry(clips, js, back, number):
-        return (clips, n, js, back, number) if fast else None
+    def carry(clips, js, back, number, plan=None, grads=()):
+        return (clips, n, js, back, number, plan, list(grads)) if fast else None
 
     def regroup(clips, back, half, odd):
         if fast:
@@ -815,17 +909,24 @@
         return lax.psum_scatter(g.astype(BF), ALL, scatter_dimension=0, tiled=True).astype(F32)
 
     out = spread(out)
-    *half, dx1, g_t, gb_t, dmod2 = run_time_back(
-        x1, dx2, mod, seg, qkv2, o2, a2, wqkv_t, wo_t, carry(out, (2,), True, 4))
-    *odd, dx0, g_s, gb_s, dmod1 = run_frame_back(
-        frames, dx1, mod, qkv1, o1, a1, wqkv_s, wo_s, carry(out, (1, 3), True, 5))
-    layer_out = only_live(regroup(out, True, *(half or [None]), *(odd or [None])))
+    if fast:
+        half, s_in, s_out, _, _, dx1, g_t, gb_t, dmod2 = run_time_back(
+            x1, dx2, mod, seg, qkv2, o2, a2, wqkv_t, wo_t,
+            carry(out, (2,), True, 4, mlp_plan(wide, g_in, g_out, devices), (g_in, g_out)))
+        odd, s_qkv_t, s_o_t, _, _, dx0, g_s, gb_s, dmod1 = run_frame_back(
+            frames, dx1, mod, qkv1, o1, a1, wqkv_s, wo_s,
+            carry(out, (1, 3), True, 5, attn_plan(wide, g_t, devices), (g_t,)))
+    else:
+        half = odd = None
+        dx1, g_t, gb_t, dmod2 = run_time_back(x1, dx2, mod, seg, qkv2, o2, a2, wqkv_t, wo_t)
+        dx0, g_s, gb_s, dmod1 = run_frame_back(frames, dx1, mod, qkv1, o1, a1, wqkv_s, wo_s)
+    layer_out = only_live(regroup(out, True, half, odd))
     grad_clips = only_live(shift_clips(spread(dx0), True))
-    grads = (g_in, g_out, g_t, g_s)
     if fast:
-        s_in, s_out, s_t, s_s = scatter_all(grads, (0, 0, 1, 1), wide, n)
+        s_qkv_s, s_o_s = scatter_last(g_s, attn_plan(wide, g_s, devices))
     else:
-        s_in, s_out, s_t, s_s = [scatter(g) for g in grads]
+        s_in, s_out, s_t, s_s = [scatter(g) for g in (g_in, g_out, g_t, g_s)]
+        s_qkv_t, s_o_t, s_qkv_s, s_o_s = s_t[:, : 3 * D], s_t[:, 3 * D :], s_s[:, : 3 * D], s_s[:, 3 * D :]
 
     grad_frames = jnp.swapaxes(jnp.concatenate([dmod1, dmod2, dmod3], axis=0), 0, 1).reshape(LIVE, 9 * D)
     chooser = (row_choice[:, None] == jnp.arange(2 * n, dtype=jnp.int32)[None, :]).astype(F32)
@@ -858,11 +959,11 @@
         grad_t_emb,
         grad_w_mod,
         grad_b_mod,
-        s_s[:, : 3 * D],
-        s_s[:, 3 * D :],
+        s_qkv_s,
+        s_o_s,
         gb[:b1],
-        s_t[:, : 3 * D],
-        s_t[:, 3 * D :],
+        s_qkv_t,
+        s_o_t,
         gb[b1 : 2 * b1],
         s_in,
         gb[2 * b1 : 2 * b1 + b_in.size],

time: 664 us -> 638 us (0.961)
  the two profiles are of different devices: /device:TPU:12 before, /device:TPU:1 now
where the time goes in v4:
time: 638 us; the launch traced here: 636 us
  Pallas kernels  514 us (81%)
  local copies, waits for them, and re-layouts  63.4 us (10%)
  other arithmetic  24.9 us (4%)
  starting transfers between devices  23.4 us (4%)
  waiting for transfers between devices  6.76 us (1%)
    pallas_call x6, Pallas kernels, call(): return fn(*ins) if prefetch is None else fn(prefetch, *ins)  334 us
    pallas_call x1, Pallas kernels, gather_all(): pl.pallas_call(functools.partial(gather_kernel, ring, n, heights, ways),...  104 us
    pallas_call x1, Pallas kernels, scatter_last(): pl.pallas_call(functools.partial(scatter_kernel, plan), name='scatter_las...  75.6 us
    all_to_all x4, starting transfers between devices, exchange(): return lax.all_to_all(x, ALL, split_axis=0, concat_axis=0, tiled=True)  19.8 us
  transfers between devices with their start and end apart: 7, of which 1 were waited for; matrix products, arithmetic and copies ran while one was open for 7% of the time, Pallas kernels for 28%

profile of v4, /device:TPU:1, one launch (start us, length us, event | category | flops | bytes accessed | tf_op | source)
XLA Modules:
  0.0 636.0 jit_solution(5360960006143959903)
XLA Ops:
  0.7 2.2 reshape.596
  3.5 0.7 broadcast_in_dim.25
  4.2 0.8 pad_maximum_fusion.3
  6.1 1.1 reduce.10
  7.2 1.7 reshape.731
  8.9 7.1 %all-to-all-start = ((bf16[32,2,5748]{2,1,0:T(2,128)(2,1)}), bf16[32,2,5748]{2,1,0:T(2,128)(2,1)S(1)}, u32[]{:S(2)}, u32[]{:S(2)}) async-start(bf16[32,2,5748]{2,1,0:T(2,128)(2,1)} %reshape.731), calls=%async_computation | async-start | bytes 1474560 | tf_op jit(solution)/shard_map/all_to_all | solution.py:809
  18.3 0.8 gather_fusion.5
  19.1 1.2 gather_fusion.6
  20.4 3.1 fusion.23
  23.5 0.8 gather_fusion.3
  24.3 104.3 %gather_all.1 = (bf16[4,16,64,768]{3,2,1,0:T(8,128)(2,1)}, bf16[768,3072]{1,0:T(8,128)(2,1)}, bf16[3072,768]{1,0:T(8,128)(2,1)}, bf16[768,2304]{1,0:T(8,128)(2,1...) custom-call(bf16[4,16,64,768]{3,2,1,0:T(8,128)(2,1)} %refs_0_.3, ...), custom_call_target="tpu_custom_call" | custom-call | tf_op jit(solution)/shard_map/gather_all/pallas_call | solution.py:592
  128.6 5.2 gather_fusion.1
  134.4 0.7 and_convert_fusion.refs_3_.refs_6_
  135.1 1.0 reshape.732
  138.4 1.3 all_to_all.38
  139.7 4.1 all-to-all-start.1
  146.0 0.7 reshape.620.bin_
  146.7 6.7 %all-to-all-done.1 = f32[32,1,1728]{2,1,0:T(1,128)S(1)} async-done(((f32[32,1,1728]{2,1,0:T(1,128)}), f32[32,1,1728]{2,1,0:T(1,128)S(1)}, u32[]{:S(2)}, u32[]{:S(2)}) %all-to-all-start.1) | async-done | bytes 221216 | tf_op jit(solution)/shard_map/all_to_all | solution.py:809
  155.3 1.5 copy.129
  156.8 41.3 %frame_forward.1 = (bf16[1,16,64,768]{3,2,1,0:T(8,128)(2,1)}, f32[64,32,768]{2,1,0:T(8,128)}, bf16[2048,2304]{1,0:T(8,128)(2,1)}, bf16[2048,768]{1,0:T(8,128)(2,1)}, f32[2048,768]{1,0:T(8,128)}) custom-call(bf16[4,16,64,768]{3,2,1,0:T(8,128)(2,1)} %refs_0_.5, bf16[32,64,768]{2,1,0:T(8,128)(2,1)} %gather_fusion.1, f32[9,32,768]{2,1,0:T(8,128)} %bitcast.146, ...), custom_call_target="tpu_custom_call" | custom-call | flops 9663676416 | bytes 33917952 | tf_op jit(solution)/shard_map/frame_forward/pallas_call | solution.py:411
  198.1 42.5 %time_forward.1 = (bf16[2,16,64,768]{3,2,1,0:T(8,128)(2,1)}, f32[64,32,768]{2,1,0:T(8,128)}, bf16[2048,2304]{1,0:T(8,128)(2,1)}, bf16[2048,768]{1,0:T(8,128)(2,1)}, f32[2048,768]{1,0:T(8,128)}) custom-call(bf16[4,16,64,768]{3,2,1,0:T(8,128)(2,1)} %refs_0_.5, f32[64,32,768]{2,1,0:T(8,128)} %get-tuple-element.58.refs_1_.refs_3_, f32[9,32,768]{2,1,0:T(8,128)} %bitcast.147, ...), custom_call_target="tpu_custom_call" | custom-call | flops 9663676416 | bytes 37096448 | tf_op jit(solution)/shard_map/time_forward/pallas_call | solution.py:411
  240.7 2.2 fusion.29
  243.5 3.2 pad_maximum_fusion
  246.6 6.9 %turn_frames.1.dy = f32[64,32,768]{2,1,0:T(8,128)} custom-call(s32[32]{0:T(128)} %get-tuple-element.97.rows_ref, bf16[64,64,768]{2,1,0:T(8,128)(2,1)} %bitcast.123, bf16[64,64,768]{2,1,0:T(8,128)(2,1)} %bitcast.124, bf16[64,64,768]{2,1,0:T(8,128)(2,1)} %bitcast.125, bf16[64,64,768]{2,1,0:T(8,128)(2,1)} %bitcast.126, bf16[64,64,768]{2,1,0:T(8,128)(2,1)} %bitcast.127, ...), custom_call_target="tpu_custom_call" | custom-call | flops 1000 | bytes 56623104 | tf_op jit(solution)/shard_map/turn_frames/pallas_call | solution.py:411
  253.6 97.8 %mlp_both.1 = (bf16[32,64,768]{2,1,0:T(8,128)(2,1)}, f32[64,32,768]{2,1,0:T(8,128)}, f32[768,3072]{1,0:T(8,128)}, f32[3072,768]{1,0:T(8,128)}, f32[1,3072]{1,0:T...) custom-call(f32[64,32,768]{2,1,0:T(8,128)} %get-tuple-element.61.x2, f32[64,32,768]{2,1,0:T(8,128)} %turn_frames.1.dy, ...), custom_call_target="tpu_custom_call" | custom-call | flops 57982058496 | bytes 51542016 | tf_op jit(solution)/shard_map/mlp_both/pallas_call | solution.py:411
  351.3 5.5 gather_fusion.7
  356.9 77.6 %time_back.1 = (bf16[1,16,64,768]{3,2,1,0:T(8,128)(2,1)}, f32[24,3072]{1,0:T(8,128)}, f32[96,768]{1,0:T(8,128)}, f32[8,48,3072]{2,1,0:T(8,128)}, f32[8,192,768]{...) custom-call(bf16[4,16,64,768]{3,2,1,0:T(8,128)(2,1)} %bitcast.131, ...), custom_call_target="tpu_custom_call" | custom-call | flops 19327352832 | bytes 53120000 | tf_op jit(solution)/shard_map/time_back/pallas_call | solution.py:411
  434.5 68.3 %frame_back.1 = (bf16[2,16,64,768]{3,2,1,0:T(8,128)(2,1)}, f32[24,2304]{1,0:T(8,128)}, f32[24,768]{1,0:T(8,128)}, f32[8,48,1536]{2,1,0:T(8,128)}, f32[8,48,1536]...) custom-call(bf16[4,16,64,768]{3,2,1,0:T(8,128)(2,1)} %bitcast.132, ...), custom_call_target="tpu_custom_call" | custom-call | flops 19327352832 | bytes 46795776 | tf_op jit(solution)/shard_map/frame_back/pallas_call | solution.py:411
  502.8 1.3 maximum_bitcast_fusion
  505.4 1.3 reduce.11
  506.7 0.8 reshape.733
  507.5 4.1 all-to-all-start.2
  513.2 3.7 gather_fusion.8
  516.8 5.7 slice_bitcast_fusion
  522.9 1.5 collective-permute-start.1
  524.3 1.8 collective-permute-start.2
  526.3 0.7 reduce.2
  527.7 0.8 convert_reduce_fusion
  530.5 2.2 all_to_all.35
  532.7 4.5 all-to-all-start.3
  538.1 75.6 %scatter_last.1 = (f32[24,2304]{1,0:T(8,128)}, f32[24,768]{1,0:T(8,128)}, f32[8,48,1536]{2,1,0:T(8,128)}, f32[8,48,1536]{2,1,0:T(8,128)}) custom-call(f32[768,3072]{1,0:T(8,128)} %get-tuple-element.88.refs_0_), custom_call_target="tpu_custom_call" | custom-call | tf_op jit(solution)/shard_map/scatter_last/pallas_call | solution.py:781
  613.7 1.7 slice_bitcast_fusion.1
  616.4 1.0 copy-done.4
  617.9 7.8 %maximum_select_fusion.1 = (bf16[4,16,64,768]{3,2,1,0:T(8,128)(2,1)}, bf16[4,16,64,768]{3,2,1,0:T(8,128)(2,1)}) fusion(bf16[1,16,64,768]{3,2,1,0:T(8,128)(2,1)} %bitcast.34, bf16[1,16,64,768]{3,2,1,0:T(8,128)(2,1)} %bitcast.33, bf16[1,16,64,768]{3,2,1,0:T(8,128)(2,1)} %bitcast.32, bf16[1,16,64,768]{3,2,1,0:T(8,128)(2,1)S(1)} %copy-done.4, ...), kind=kLoop, calls=%fused_computation.12 | loop fusion | flops 25165824 | bytes 25165888 | tf_op jit(solution)/shard_map/jit(_where)/select_n | solution.py:906
  625.7 1.5 copy.128
  629.8 1.3 reshape.617
  634.4 0.7 copy.145
  635.1 0.7 copy.146
  (167 shorter events, 25.2 us)
Async XLA Ops:
  0.6 17.1 %copy-start = (s32[16,16]{1,0:T(8,128)S(1)}, s32[16,16]{1,0:T(8,128)}, u32[]{:S(2)}) copy-start(s32[16,16]{1,0:T(8,128)} %param.20) | copy-start | bytes 3076
  5.0 11.0 %copy-start.25 = (s32[16]{0:T(128)S(1)}, s32[16]{0:T(128)}, u32[]{:S(2)}) copy-start(s32[16]{0:T(128)} %param.19) | copy-start | bytes 196
  5.0 12.6 %copy-start.26 = (bf16[216]{0:T(256)(128)(2,1)S(1)}, bf16[216]{0:T(256)(128)(2,1)}, u32[]{:S(2)}) copy-start(bf16[216]{0:T(256)(128)(2,1)} %param.22) | copy-start | bytes 1300
  8.9 126.2 %all-to-all-start = ((bf16[32,2,5748]{2,1,0:T(2,128)(2,1)}), bf16[32,2,5748]{2,1,0:T(2,128)(2,1)S(1)}, u32[]{:S(2)}, u32[]{:S(2)}) async-start(bf16[32,2,5748]{2,1,0:T(2,128)(2,1)} %reshape.731), calls=%async_computation | async-start | bytes 1474560 | tf_op jit(solution)/shard_map/all_to_all | solution.py:809
  16.1 1.5 copy-start.2
  136.7 17.4 %copy-start.5 = (bf16[256,768]{1,0:T(8,128)(2,1)}, bf16[256,768]{1,0:T(8,128)(2,1)S(1)}, u32[]{:S(2)}) copy-start(bf16[256,768]{1,0:T(8,128)(2,1)S(1)} %convert_element_type.58) | copy-start | bytes 1179652
  137.4 16.9 %copy-start.7 = (bf16[768,216]{1,0:T(8,128)(2,1)}, bf16[768,216]{1,0:T(8,128)(2,1)S(1)}, u32[]{:S(2)}) copy-start(bf16[768,216]{1,0:T(8,128)(2,1)S(1)} %reshape.598) | copy-start | bytes 995332
  139.7 13.7 %all-to-all-start.1 = ((f32[32,1,1728]{2,1,0:T(1,128)}), f32[32,1,1728]{2,1,0:T(1,128)S(1)}, u32[]{:S(2)}, u32[]{:S(2)}) async-start(f32[32,1,1728]{2,1,0:T(1,128)} %all_to_all.38), calls=%async_computation.1 | async-start | bytes 458752 | tf_op jit(solution)/shard_map/all_to_all | solution.py:809
  240.6 2.4 slice-start
  240.7 2.8 copy-start.10
  434.4 68.3 %copy-start.12 = (f32[3,32,768]{2,1,0:T(8,128)S(1)}, f32[3,32,768]{2,1,0:T(8,128)}, u32[]{:S(2)}) copy-start(f32[3,32,768]{2,1,0:T(8,128)} %get-tuple-element.83) | copy-start | bytes 884740
  502.7 1.4 copy-start.24
  502.7 8.8 %copy-start.23 = (f32[1,768]{1,0:T(1,128)S(1)}, f32[1,768]{1,0:T(1,128)}, u32[]{:S(2)}) copy-start(f32[1,768]{1,0:T(1,128)} %get-tuple-element.84) | copy-start | bytes 9220
  502.8 8.9 %copy-start.22 = (f32[1,768]{1,0:T(1,128)S(1)}, f32[1,768]{1,0:T(1,128)}, u32[]{:S(2)}) copy-start(f32[1,768]{1,0:T(1,128)} %get-tuple-element.85) | copy-start | bytes 9220
  502.8 9.6 %copy-start.20 = (f32[1,3072]{1,0:T(1,128)S(1)}, f32[1,3072]{1,0:T(1,128)}, u32[]{:S(2)}) copy-start(f32[1,3072]{1,0:T(1,128)} %get-tuple-element.86) | copy-start | bytes 36868
  502.8 10.3 %copy-start.21 = (f32[1,768]{1,0:T(1,128)S(1)}, f32[1,768]{1,0:T(1,128)}, u32[]{:S(2)}) copy-start(f32[1,768]{1,0:T(1,128)} %get-tuple-element.87) | copy-start | bytes 9220
  502.8 10.4 %copy-start.3 = (bf16[32,64,768]{2,1,0:T(8,128)(2,1)S(1)}, bf16[32,64,768]{2,1,0:T(8,128)(2,1)}, u32[]{:S(2)}) copy-start(bf16[32,64,768]{2,1,0:T(8,128)(2,1)} %get-tuple-element.80) | copy-start | bytes 9437188
  507.5 18.7 %all-to-all-start.2 = ((bf16[32,2,864]{2,1,0:T(2,128)(2,1)}), bf16[32,2,864]{2,1,0:T(2,128)(2,1)S(1)}, u32[]{:S(2)}, u32[]{:S(2)}) async-start(bf16[32,2,864]{2,1,0:T(2,128)(2,1)} %reshape.733), calls=%async_computation.2 | async-start | bytes 229376 | tf_op jit(solution)/shard_map/all_to_all | solution.py:809
  516.8 11.9 %copy-start.8 = (bf16[768,216]{1,0:T(8,128)(2,1)S(1)}, bf16[768,216]{1,0:T(8,128)(2,1)}, u32[]{:S(2)}) copy-start(bf16[768,216]{1,0:T(8,128)(2,1)} %copy-done.7) | copy-start | bytes 995332
  522.6 6.6 %copy-start.6 = (bf16[256,768]{1,0:T(8,128)(2,1)S(1)}, bf16[256,768]{1,0:T(8,128)(2,1)}, u32[]{:S(2)}) copy-start(bf16[256,768]{1,0:T(8,128)(2,1)} %copy-done.5) | copy-start | bytes 1179652
  522.6 93.8 %collective-permute-start = (bf16[16,64,768]{2,1,0:T(8,128)(2,1)}, bf16[16,64,768]{2,1,0:T(8,128)(2,1)}, u32[]{:S(2)}, u32[]{:S(2)}) collective-permute-start(bf16[16,64,768]{2,1,0:T(8,128)(2,1)} %get-tuple-element.101), channel_id=1, source_target_pairs={{0,3},{1,0},{2,1},{3,2},{4,7},{5,4},{6,5},{7,6},{8,11},{9,8},{10,9... | collective-permute-start | bytes 4718600 | tf_op jit(solution)/shard_map/ppermute | solution.py:817
  522.9 93.5 %collective-permute-start.1 = (bf16[16,64,768]{2,1,0:T(8,128)(2,1)}, bf16[16,64,768]{2,1,0:T(8,128)(2,1)}, u32[]{:S(2)}, u32[]{:S(2)}) collective-permute-start(bf16[16,64,768]{2,1,0:T(8,128)(2,1)} %get-tuple-element.100), channel_id=1, source_target_pairs={{0,2},{1,3},{2,0},{3,1},{4,6},{5,7},{6,4},{7,5},{8,10},{9,11},{10,... | collective-permute-start | bytes 4718600 | tf_op jit(solution)/shard_map/ppermute | solution.py:817
  524.3 92.1 %collective-permute-start.2 = (bf16[16,64,768]{2,1,0:T(8,128)(2,1)}, bf16[16,64,768]{2,1,0:T(8,128)(2,1)}, u32[]{:S(2)}, u32[]{:S(2)}) collective-permute-start(bf16[16,64,768]{2,1,0:T(8,128)(2,1)} %get-tuple-element.102), channel_id=1, source_target_pairs={{0,1},{1,2},{2,3},{3,0},{4,5},{5,6},{6,7},{7,4},{8,9},{9,10},{10,1... | collective-permute-start | bytes 4718600 | tf_op jit(solution)/shard_map/ppermute | solution.py:817
  532.7 93.0 %all-to-all-start.3 = ((f32[32,1,11496]{2,1,0:T(1,128)}), f32[32,1,11496]{2,1,0:T(1,128)}, u32[]{:S(2)}, u32[]{:S(2)}) async-start(f32[32,1,11496]{2,1,0:T(1,128)} %all_to_all.35), calls=%async_computation.3 | async-start | bytes 2949120 | tf_op jit(solution)/shard_map/all_to_all | solution.py:809
  613.7 2.4 copy-start.9
  616.0 1.4 copy-start.4
  616.1 1.9 copy-start.11
  627.2 3.9 copy-start.19
  627.2 4.5 copy-start.16
  627.3 5.2 copy-start.18
  627.3 5.8 copy-start.15
  627.3 6.5 %copy-start.17 = (f32[24,768]{1,0:T(8,128)S(1)}, f32[24,768]{1,0:T(8,128)}, u32[]{:S(2)}) copy-start(f32[24,768]{1,0:T(8,128)} %get-tuple-element.159) | copy-start | bytes 221188
  627.3 7.1 %copy-start.14 = (f32[24,3072]{1,0:T(8,128)S(1)}, f32[24,3072]{1,0:T(8,128)}, u32[]{:S(2)}) copy-start(f32[24,3072]{1,0:T(8,128)} %get-tuple-element.161) | copy-start | bytes 884740
  628.3 7.5 %copy-start.1 = (s32[16,16]{1,0:T(8,128)S(1)}, s32[16,16]{1,0:T(8,128)}, u32[]{:S(2)}) copy-start(s32[16,16]{1,0:T(8,128)} %param.20) | copy-start | bytes 3076
  628.9 6.2 copy-start.13

commit v5 on v4

--- a/solution.py
+++ b/solution.py
@@ -317,80 +317,21 @@
     return jax.ShapeDtypeStruct(shape, dtype)
 
 
-def clip_copies(n, js, back, src, dst, send_sem, recv_sem):
-    w, k = lax.axis_index("wide"), lax.axis_index("narrow")
-    return [
-        send(src.at[j], dst.at[i], send_sem.at[i], recv_sem.at[i], (w, (k + (n - j if back else j)) % n))
-        for i, j in enumerate(js)
-    ]
-
-
-def carrying(kernel, count, n, js, back, plan, *refs):
-    sent = 0 if plan is None else plan.inputs
-    made = 0 if plan is None else plan.outputs
-    held = 0 if plan is None else plan.scratches
-    src, grads, ins = refs[0], refs[1 : 1 + sent], refs[1 + sent : 1 + sent + count]
-    at = 1 + sent + count
-    dst, results, rest = refs[at], refs[at + 1 : at + 1 + made], refs[at + 1 + made : len(refs) - 2 - held]
-    copies = clip_copies(n, js, back, src, dst, *refs[len(refs) - 2 - held : len(refs) - held])
-    step = pl.program_id(0)
-    sums = None if plan is None else plan.steps(grads + results + refs[len(refs) - held :])
-
-    @pl.when(step == 0)
-    def _():
-        w, k = lax.axis_index("wide"), lax.axis_index("narrow")
-        peers = [(w, (k + j) % n) for j in js]
-        greet(peers if sums is None else peers + list(sums.peers))
-        if sums is not None:
-            sums.begin()
-        for copy in copies:
-            copy.start()
-
-    if sums is None:
-        kernel(*ins, *rest)
-    else:
-        @pl.when(step > 0)
-        def _():
-            sums.hop(2 * step - 1)
-
-        def tick(place):
-            @pl.when(step == 0)
-            def _():
-                if place == 0:
-                    sums.load_first()
-                else:
-                    sums.first_hop()
-
-            if place == 1:
-                @pl.when(step > 0)
-                def _():
-                    sums.hop(2 * step)
-
-        kernel(*ins, *rest, tick=tick)
-
-    @pl.when(step == GRID - 1)
-    def _():
-        if sums is not None:
-            sums.finish()
-        for copy in copies:
-            copy.wait()
-
-
-def call(kernel, name, ins, in_specs, outs, out_specs, scratch, flops, prefetch=None, carry=None):
+class Carrier:
+    def __init__(self, wrap, number, ins, outs, out_specs, scratch, aliases=None):
+        self.wrap, self.number, self.ins, self.outs = wrap, number, ins, outs
+        self.out_specs, self.scratch, self.aliases = out_specs, scratch, aliases or {}
+
+
+def call(kernel, name, ins, in_specs, outs, out_specs, scratch, flops, prefetch=None, carrier=None):
     moved = sum(a.size * a.dtype.itemsize for a in tuple(ins) + tuple(outs))
-    params = {}
-    if carry is not None:
-        src, n, js, back, number, plan, grads = carry
-        kernel = functools.partial(carrying, kernel, len(ins), n, js, back, plan)
-        ins, in_specs = [src] + grads + ins, [ANY] * (1 + len(grads)) + in_specs
-        first = [shape_of((len(js),) + src.shape[1:], src.dtype)]
-        first_specs = [ANY]
-        scratch = scratch + [pltpu.SemaphoreType.DMA((len(js),))] * 2
-        if plan is not None:
-            first, first_specs = first + plan.out_shapes, first_specs + plan.out_specs
-            scratch = scratch + plan.scratch
-        outs, out_specs = first + outs, first_specs + out_specs
-        params = dict(collective_id=number, has_side_effects=True)
+    params, aliases = {}, {}
+    if carrier is not None:
+        kernel = functools.partial(carrier.wrap, kernel, len(ins), len(outs), len(scratch))
+        ins, in_specs = carrier.ins + ins, [ANY] * len(carrier.ins) + in_specs
+        outs, out_specs = carrier.outs + outs, carrier.out_specs + out_specs
+        scratch = scratch + carrier.scratch
+        params, aliases = dict(collective_id=carrier.number, has_side_effects=True), carrier.aliases
     grid_spec = pltpu.PrefetchScalarGridSpec(
         num_scalar_prefetch=0 if prefetch is None else 1,
         grid=(GRID,),
@@ -403,6 +344,7 @@
         grid_spec=grid_spec,
         out_shape=outs,
         name=name,
+        input_output_aliases=aliases,
         cost_estimate=pl.CostEstimate(flops=flops, bytes_accessed=moved, transcendentals=0),
         compiler_params=pltpu.CompilerParams(
             dimension_semantics=("arbitrary",), vmem_limit_bytes=VMEM_LIMIT, **params
@@ -411,10 +353,156 @@
     return fn(*ins) if prefetch is None else fn(prefetch, *ins)
 
 
+def split_refs(refs, *counts):
+    parts = []
+    for count in counts:
+        parts.append(refs[:count])
+        refs = refs[count:]
+    return parts + [refs]
+
+
+def clips_carrier(clips, js, n, number):
+    def wrap(kernel, n_in, n_out, n_scratch, *refs):
+        (src,), ins, (dst,), outs, scratch, (send_sem, recv_sem) = split_refs(refs, 1, n_in, 1, n_out, n_scratch)
+        w, k = lax.axis_index("wide"), lax.axis_index("narrow")
+        peers = [(w, (k + j) % n) for j in js]
+        copies = [send(src.at[j], dst.at[i], send_sem.at[i], recv_sem.at[i], peers[i]) for i, j in enumerate(js)]
+
+        @pl.when(pl.program_id(0) == 0)
+        def _():
+            greet(peers)
+            for copy in copies:
+                copy.start()
+
+        kernel(*ins, *outs, *scratch)
+
+        @pl.when(pl.program_id(0) == GRID - 1)
+        def _():
+            for copy in copies:
+                copy.wait()
+
+    sems = pltpu.SemaphoreType.DMA((len(js),))
+    return Carrier(wrap, number, [clips], [shape_of((len(js),) + clips.shape[1:], clips.dtype)], [ANY], [sems, sems])
+
+
+def packed(slot, first=0, count=LIVE):
+    return pl.ds(pl.multiple_of(slot * LIVE + first, 8), count)
+
+
+def slot_for(k):
+    return 3 - 2 * (k % 2)
+
+
+def ticks(sums, step):
+    @pl.when(step > 0)
+    def _():
+        sums.hop(2 * step - 1)
+
+    def tick(place):
+        @pl.when(step == 0)
+        def _():
+            if place == 0:
+                sums.load_first()
+            else:
+                sums.first_hop()
+
+        if place == 1:
+            @pl.when(step > 0)
+            def _():
+                sums.hop(2 * step)
+
+    return tick
+
+
+def share_carrier(frames, grads, plan, number):
+    n_grads = len(grads)
+
+    def wrap(kernel, n_in, n_out, n_scratch, *refs):
+        (_,), grad_refs, ins, (dst,), left, outs, scratch, (send_sem, recv_sem), own = split_refs(
+            refs, 1, n_grads, n_in, 1, plan.outputs, n_out, n_scratch, 2)
+        step = pl.program_id(0)
+        sums = plan.steps(grad_refs + left + own)
+        targets = ((slot_for(sums.k), sums.other_c), (2, sums.other_x))
+        copies = [send(dst.at[packed(0)], dst.at[packed(slot)], send_sem.at[i], recv_sem.at[i], peer)
+                  for i, (slot, peer) in enumerate(targets)]
+
+        @pl.when(step == 0)
+        def _():
+            greet(sums.peers)
+            sums.begin()
+            for copy in copies:
+                copy.start()
+
+        kernel(*ins, *outs, *scratch, tick=ticks(sums, step))
+
+        @pl.when(step == GRID - 1)
+        def _():
+            sums.leave()
+            for copy in copies:
+                copy.wait()
+
+    sems = pltpu.SemaphoreType.DMA((2,))
+    return Carrier(wrap, number, [frames] + grads, [shape_of(frames.shape, frames.dtype)] + plan.out_shapes,
+                   [ANY] + plan.out_specs, [sems, sems] + plan.scratch, {0: 0})
+
+
+def tile_copies(k, other_c, other_x, src, dst, i, send_sem, recv_sem):
+    return [send(src, dst.at[packed(slot, i * FT, FT)], send_sem.at[a, i], recv_sem.at[a, i], peer)
+            for a, (slot, peer) in enumerate(((slot_for(k), other_c), (2, other_x)))]
+
+
+def relay_carrier(frames, grads, plan, number):
+    n_grads = len(grads)
+
+    def wrap(kernel, n_in, n_out, n_scratch, *refs):
+        (_,), grad_refs, ins, (dst, made), left, outs, scratch, (send_sem, recv_sem, tile_s, tile_r, keep, buf), own = (
+            split_refs(refs, 1, n_grads, n_in, 2, plan.outputs, n_out, n_scratch, 6))
+        step = pl.program_id(0)
+        sums = plan.steps(grad_refs + left + own)
+        relay = send(dst.at[packed(2)], dst.at[packed(4 - slot_for(sums.k))],
+                     send_sem.at[0], recv_sem.at[0], sums.other_c)
+
+        def tile(i):
+            return tile_copies(sums.k, sums.other_c, sums.other_x, buf.at[i], made, i, tile_s, tile_r)
+
+        def store(i):
+            return pltpu.make_async_copy(buf.at[i], made.at[packed(0, i * FT, FT)], keep.at[i])
+
+        @pl.when(step == 0)
+        def _():
+            greet(sums.peers)
+            sums.begin()
+            relay.start()
+
+        kernel(*ins, buf.at[step], *outs, *scratch, tick=ticks(sums, step))
+        store(step).start()
+
+        @pl.when(step < GRID - 1)
+        def _():
+            for copy in tile(step):
+                copy.start()
+
+        @pl.when(step == GRID - 1)
+        def _():
+            sums.leave()
+            relay.wait()
+            for i in range(GRID):
+                store(i).wait()
+            for i in range(GRID - 1):
+                for copy in tile(i):
+                    copy.wait()
+
+    sems = pltpu.SemaphoreType.DMA
+    shape = shape_of(frames.shape, frames.dtype)
+    return Carrier(wrap, number, [frames] + grads, [shape, shape] + plan.out_shapes, [ANY, ANY] + plan.out_specs,
+                   [sems((1,)), sems((1,)), sems((2, GRID - 1)), sems((2, GRID - 1)), sems((GRID,)),
+                    pltpu.VMEM((GRID, FT, PATCHES, D), BF)] + plan.scratch, {0: 0})
+
+
 TOKENS = LIVE * PATCHES
 
 
-def run_frame_forward(frames, mod, wqkv, wo, bo, carry=None):
+def run_frame_forward(frames, mod, wqkv, wo, bo, carrier=None):
     return call(
         frame_forward, "frame_forward",
         [frames, mod, wqkv, wo, bo],
@@ -423,7 +511,7 @@
          shape_of((TOKENS, D), F32)],
         [tiles((PATCHES, FT, D), 1), ROWS3, ROWS, ROWS],
         [TURN],
-        2 * TOKENS * D * 4 * D, carry=carry)
+        2 * TOKENS * D * 4 * D, carrier=carrier)
 
 
 def run_turn_frames(frames, rows):
@@ -433,7 +521,31 @@
         [TURN], 1000, rows)[0]
 
 
-def run_time_forward(x1, mod, seg, wqkv, wo, bo, carry=None):
+def unpack_frames(rows_ref, *refs):
+    x_refs, (out,) = refs[:FT], refs[FT:]
+    first = pl.program_id(0) * FT
+    for j in range(FT):
+        x = x_refs[j][0]
+        out[j] = jnp.where(rows_ref[first + j] >= 0, x, jnp.zeros_like(x))
+
+
+def run_unpack(frames, rows):
+    specs = [
+        pl.BlockSpec((1, PATCHES, D), functools.partial(lambda j, i, r: (jnp.maximum(r[FT * i + j], 0), 0, 0), j))
+        for j in range(FT)
+    ]
+    return pl.pallas_call(
+        unpack_frames,
+        grid_spec=pltpu.PrefetchScalarGridSpec(
+            num_scalar_prefetch=1, grid=(rows.shape[0] // FT,), in_specs=specs, out_specs=tiles((FT, PATCHES, D), 0)),
+        out_shape=shape_of((rows.shape[0], PATCHES, D), frames.dtype),
+        name="unpack_frames",
+        cost_estimate=pl.CostEstimate(flops=1000, bytes_accessed=4 * rows.shape[0] * PATCHES * D, transcendentals=0),
+        compiler_params=pltpu.CompilerParams(dimension_semantics=("arbitrary",)),
+    )(rows, *[frames] * FT)
+
+
+def run_time_forward(x1, mod, seg, wqkv, wo, bo, carrier=None):
     return call(
         time_forward, "time_forward",
         [x1, mod, seg, wqkv, wo, bo],
@@ -442,16 +554,16 @@
         [shape_of((PATCHES, LIVE, D), F32), shape_of((TOKENS, 3 * D), BF), shape_of((TOKENS, D), BF),
          shape_of((TOKENS, D), F32)],
         [TURNED, ROWS3, ROWS, ROWS],
-        [], 2 * TOKENS * D * 4 * D, carry=carry)
-
-
-def run_mlp(x2, dy, mod, win, bin_, wout, bout):
+        [], 2 * TOKENS * D * 4 * D, carrier=carrier)
+
+
+def run_mlp(x2, dy, mod, win, bin_, wout, bout, slots=1):
     return call(
         mlp_both, "mlp_both",
         [x2, dy, mod, win, bin_, wout, bout],
         [TURNED, TURNED, piece_spec(2, LIVE, False), whole((D, FF)), whole((1, FF)), whole((FF, D)),
          whole((1, D))],
-        [shape_of((LIVE, PATCHES, D), BF), shape_of((PATCHES, LIVE, D), F32), shape_of((D, FF), F32),
+        [shape_of((slots * LIVE, PATCHES, D), BF), shape_of((PATCHES, LIVE, D), F32), shape_of((D, FF), F32),
          shape_of((FF, D), F32), shape_of((1, FF), F32), shape_of((1, D), F32), shape_of((3, LIVE, D), F32)],
         [tiles((LIVE, PT, D), 1), TURNED, whole((D, FF)), whole((FF, D)), whole((1, FF)), whole((1, D)),
          whole((3, LIVE, D))],
@@ -459,7 +571,7 @@
         6 * 2 * TOKENS * D * FF)
 
 
-def run_time_back(x1, dx2, mod, seg, qkv, o, a2, wqkv, wo, carry=None):
+def run_time_back(x1, dx2, mod, seg, qkv, o, a2, wqkv, wo, carrier=None):
     return call(
         time_back, "time_back",
         [x1, dx2, mod, seg, qkv, o, a2, wqkv, wo],
@@ -468,19 +580,21 @@
         [shape_of((LIVE, PATCHES, D), F32), shape_of((D, 4 * D), F32), shape_of((1, D), F32), shape_of((3, LIVE, D), F32)],
         [tiles((LIVE, PT, D), 1), whole((D, 4 * D)), whole((1, D)), whole((3, LIVE, D))],
         [pltpu.VMEM((TILE, D), BF), pltpu.VMEM((TILE, 3 * D), BF), TURN],
-        2 * 2 * TOKENS * D * 4 * D, carry=carry)
-
-
-def run_frame_back(frames, dx1, mod, qkv, o, a1, wqkv, wo, carry=None):
+        2 * 2 * TOKENS * D * 4 * D, carrier=carrier)
+
+
+def run_frame_back(frames, dx1, mod, qkv, o, a1, wqkv, wo, carrier=None):
+    frames_out = [] if carrier else [shape_of((LIVE, PATCHES, D), BF)]
+    frames_spec = [] if carrier else [tiles((FT, PATCHES, D), 0)]
     return call(
         frame_back, "frame_back",
         [frames, dx1, mod, qkv, o, a1, wqkv, wo],
         [tiles((FT, PATCHES, D), 0), tiles((FT, PATCHES, D), 0), piece_spec(0, FT, True), ROWS3, ROWS, ROWS,
                          whole((D, 3 * D)), whole((D, D))],
-        [shape_of((LIVE, PATCHES, D), BF), shape_of((D, 4 * D), F32), shape_of((1, D), F32), shape_of((3, LIVE, D), F32)],
-        [tiles((FT, PATCHES, D), 0), whole((D, 4 * D)), whole((1, D)), piece_spec(0, FT, True)],
+        frames_out + [shape_of((D, 4 * D), F32), shape_of((1, D), F32), shape_of((3, LIVE, D), F32)],
+        frames_spec + [whole((D, 4 * D)), whole((1, D)), piece_spec(0, FT, True)],
         [pltpu.VMEM((TILE, D), BF), pltpu.VMEM((TILE, 3 * D), BF)],
-        2 * 2 * TOKENS * D * 4 * D, carry=carry)
+        2 * 2 * TOKENS * D * 4 * D, carrier=carrier)
 
 
 def place_of(wide):
@@ -607,11 +721,16 @@
     return got[0], got[1:]
 
 
+def put(outs, places, value):
+    for o, out_col, col, width in places:
+        outs[o][:, out_col : out_col + width] = value[:, col : col + width]
+
+
 class Sums:
     def __init__(self, plan, refs):
         self.plan, count = plan, len(plan.pieces)
         self.grads, refs = refs[: plan.inputs], refs[plan.inputs :]
-        self.outs, refs = refs[: len(plan.shapes)], refs[len(plan.shapes) :]
+        self.outs, refs = refs[: plan.results], refs[plan.results :]
         self.stages, refs = refs[:count], refs[count:]
         self.own, self.part, self.came, self.went, self.last, self.fin_s, self.fin_r = (
             refs[i * count : (i + 1) * count] for i in range(7)
@@ -696,25 +815,38 @@
             self.went[t][s] = (value + self.came[t][s - 1].astype(F32)).astype(BF)
             self.ring_copy(t, s).start()
 
+    def end_ring(self, t):
+        final, height = self.final, self.plan.pieces[t][3]
+        value = self.total(t, final, final % 2)
+        self.ring_copy(t, final - 1).wait_recv()
+        value = value + self.came[t][final - 1].astype(F32)
+        self.last[t][0] = value[:height]
+        self.last[t][1] = value[height:]
+
+    def leave(self):
+        count = len(self.plan.pieces)
+        for t in self.each():
+            self.end_ring(t)
+            self.outs[t][...] = self.last[t][self.x]
+            self.outs[count + t][...] = self.last[t][1 - self.x].astype(BF)
+        self.drain()
+
     def finish(self):
-        final = self.final
         for t in self.each():
-            height = self.plan.pieces[t][3]
-            value = self.total(t, final, final % 2)
-            self.ring_copy(t, final - 1).wait_recv()
-            value = value + self.came[t][final - 1].astype(F32)
-            self.last[t][0] = value[:height]
-            self.last[t][1] = value[height:]
+            self.end_ring(t)
             self.fin_s[t][...] = self.last[t][1 - self.x].astype(BF)
             self.x_copy(t).start()
         for t in self.each():
             self.x_copy(t).wait_recv()
             value = self.last[t][self.x] + self.fin_r[t][...].astype(F32)
-            for o, out_col, col, width in self.plan.places[t]:
-                self.outs[o][:, out_col : out_col + width] = value[:, col : col + width]
+            put(self.outs, self.plan.places[t], value)
         for t in self.each():
             self.x_copy(t).wait_send()
-            for s in range(final):
+        self.drain()
+
+    def drain(self):
+        for t in self.each():
+            for s in range(self.final):
                 self.ring_copy(t, s).wait_send()
             for s in range(self.plan.ring):
                 for column in range(2):
@@ -722,14 +854,17 @@
 
 
 class Plan:
-    def __init__(self, ring, inputs, pieces, shapes, places):
+    def __init__(self, ring, inputs, pieces, shapes, places, leave):
         self.ring, self.inputs, self.pieces, self.shapes, self.places = ring, inputs, pieces, shapes, places
         count = len(pieces)
         sizes = [(height, width) for _, _, width, height, _ in pieces]
         sems, vmem = pltpu.SemaphoreType.DMA, pltpu.VMEM
         self.out_shapes = [shape_of(hw, F32) for hw in shapes]
+        if leave:
+            self.out_shapes = [shape_of(hw, F32) for hw in sizes] + [shape_of(hw, BF) for hw in sizes]
+        self.results = len(self.out_shapes)
         self.out_shapes += [shape_of((ring, 2 * h, wd), F32) for h, wd in sizes]
-        self.out_specs = [pl.BlockSpec(memory_space=pltpu.VMEM)] * len(shapes) + [ANY] * count
+        self.out_specs = [pl.BlockSpec(memory_space=pltpu.VMEM)] * self.results + [ANY] * count
         self.outputs = len(self.out_shapes)
         self.scratch = (
             [vmem((2, 2 * h, wd), F32) for h, wd in sizes]
@@ -753,19 +888,43 @@
 def mlp_plan(ring, g_in, g_out, devices):
     a, b = g_in.shape[0] // devices, g_out.shape[0] // devices
     wa, wb = g_in.shape[1], g_out.shape[1]
-    return Plan(ring, 2, [(0, 0, wa, a, 0), (1, 0, wb, b, 1)], [(a, wa), (b, wb)], [[(0, 0, 0, wa)], [(1, 0, 0, wb)]])
-
-
-def attn_plan(ring, g, devices):
+    return Plan(ring, 2, [(0, 0, wa, a, 0), (1, 0, wb, b, 1)], [(a, wa), (b, wb)], [[(0, 0, 0, wa)], [(1, 0, 0, wb)]], True)
+
+
+def attn_plan(ring, g, devices, leave):
     h, half, cut = g.shape[0] // devices, 2 * D, 3 * D
     return Plan(ring, 1, [(0, 0, half, h, 0), (0, half, half, h, 1)], [(h, cut), (h, D)],
-                [[(0, 0, 0, half)], [(0, half, 0, cut - half), (1, 0, cut - half, D)]])
-
-
-def scatter_kernel(plan, *refs):
-    sums = plan.steps(refs)
+                [[(0, 0, 0, half)], [(0, half, 0, cut - half), (1, 0, cut - half, D)]], leave)
+
+
+def last_kernel(plan, left, shapes, *refs):
+    places = [part for p in left for part in p.places]
+    offsets = [sum(len(p.shapes) for p in left[:i]) for i, p in enumerate(left) for _ in p.pieces]
+    count, made = len(places), sum(len(p.shapes) for p in left)
+    ((_,), grads, keeps, fins, (frames,), left_outs, own_outs, fins_r,
+     (fin_send, fin_recv, tile_s, tile_r, relay_s, relay_r), own) = split_refs(
+        refs, 1, plan.inputs, count, count, 1, made, plan.outputs, count, 6)
+    sums = plan.steps(grads + own_outs + own)
+    final_tile = GRID - 1
+    tile = tile_copies(sums.k, sums.other_c, sums.other_x, frames.at[packed(0, final_tile * FT, FT)], frames, final_tile,
+                       tile_s, tile_r)
+
+    def fin_copy(t):
+        return send(fins[t], fins_r[t], fin_send.at[t], fin_recv.at[t], sums.other_x)
+
+    def relay(i, first, frames_count):
+        return send(frames.at[packed(2, first, frames_count)],
+                    frames.at[packed(4 - slot_for(sums.k), first, frames_count)],
+                    relay_s.at[i], relay_r.at[i], sums.other_c)
+
+    early, late = relay(0, 0, final_tile * FT), relay(1, final_tile * FT, FT)
     greet(sums.peers)
     sums.begin()
+    for copy in tile:
+        copy.start()
+    for t in range(count):
+        fin_copy(t).start()
+    early.start()
     sums.load_first()
     sums.first_hop()
 
@@ -775,21 +934,37 @@
 
     lax.fori_loop(1, sums.final, body, 0)
     sums.finish()
-
-
-def scatter_last(g, plan):
-    got = pl.pallas_call(
-        functools.partial(scatter_kernel, plan),
+    tile[1].wait_recv()
+    late.start()
+    for t in range(count):
+        fin_copy(t).wait_recv()
+        value = keeps[t][...] + fins_r[t][...].astype(F32)
+        put(left_outs[offsets[t] :], places[t], value)
+    for t in range(count):
+        fin_copy(t).wait_send()
+    tile[0].wait()
+    tile[1].wait_send()
+    early.wait()
+    late.wait()
+
+
+def scatter_last(frames, g, keeps, fins, plan, left):
+    shapes = [shape for p in left for shape in p.shapes]
+    sems = pltpu.SemaphoreType.DMA
+    vmem = pl.BlockSpec(memory_space=pltpu.VMEM)
+    return pl.pallas_call(
+        functools.partial(last_kernel, plan, left, shapes),
         name="scatter_last",
-        out_shape=plan.out_shapes,
-        in_specs=[ANY],
-        out_specs=plan.out_specs,
-        scratch_shapes=plan.scratch,
+        out_shape=[shape_of(frames.shape, frames.dtype)] + [shape_of(hw, F32) for hw in shapes] + plan.out_shapes,
+        in_specs=[ANY] * 2 + [vmem] * len(keeps) + [ANY] * len(fins),
+        out_specs=[ANY] + [vmem] * len(shapes) + plan.out_specs,
+        scratch_shapes=[pltpu.VMEM(f.shape, f.dtype) for f in fins]
+        + [sems((len(fins),))] * 2 + [sems((2, GRID))] * 2 + [sems((2,))] * 2 + plan.scratch,
+        input_output_aliases={0: 0},
         compiler_params=pltpu.CompilerParams(
             collective_id=1, has_side_effects=True, vmem_limit_bytes=VMEM_LIMIT
         ),
-    )(g)
-    return got[:2]
+    )(frames, g, *keeps, *fins)
 
 
 def tuned(mesh):
@@ -881,26 +1056,25 @@
     mod_rows = jnp.swapaxes(mod_rows, 0, 1).reshape(2 * n, 9, D)
     mod = jnp.swapaxes(mod_rows[row_choice], 0, 1)
 
-    def carry(clips, js, back, number, plan=None, grads=()):
-        return (clips, n, js, back, number, plan, list(grads)) if fast else None
-
-    def regroup(clips, back, half, odd):
-        if fast:
-            return jnp.stack([clips[0], odd[0], half[0], odd[1]])
-        return shift_clips(clips, back)
+    def carry(js, number):
+        return clips_carrier(cotangent, js, n, number) if fast else None
 
     *half, x1, qkv1, o1, a1 = run_frame_forward(
-        frames, mod, wqkv_s, wo_s, bias_s, carry(cotangent, (2,), False, 2))
+        frames, mod, wqkv_s, wo_s, bias_s, carry((2,), 2))
     *odd, x2, qkv2, o2, a2 = run_time_forward(
-        x1, mod, seg, wqkv_t, wo_t, bias_t, carry(cotangent, (1, 3), False, 3))
-    cots = regroup(cotangent, False, *(half or [None]), *(odd or [None]))
+        x1, mod, seg, wqkv_t, wo_t, bias_t, carry((1, 3), 3))
+    if fast:
+        cots = jnp.stack([cotangent[0], odd[0][0], half[0][0], odd[0][1]])
+    else:
+        cots = shift_clips(cotangent, False)
     dy = run_turn_frames(cots.reshape(n * FR, PATCHES, D), pack_rows)
-    out, dx2, g_in, g_out, gb_in, gb_out, dmod3 = run_mlp(x2, dy, mod, win, bias_in, wout, bias_out)
-
-    own_live = frame_ids[None, :] < lengths.reshape(n, n)[rank][:, None]
-
-    def spread(packed):
-        return jnp.take(packed, unpack_rows, axis=0, mode="clip").reshape(n, FR, PATCHES, D)
+    out, dx2, g_in, g_out, gb_in, gb_out, dmod3 = run_mlp(x2, dy, mod, win, bias_in, wout, bias_out, n if fast else 1)
+
+    own_len = lengths.reshape(n, n)[rank]
+    own_live = frame_ids[None, :] < own_len[:, None]
+
+    def spread(frames):
+        return jnp.take(frames, unpack_rows, axis=0, mode="clip").reshape(n, FR, PATCHES, D)
 
     def only_live(parts):
         return jnp.where(own_live[:, :, None, None], parts, jnp.zeros((), parts.dtype))
@@ -908,23 +1082,28 @@
     def scatter(g):
         return lax.psum_scatter(g.astype(BF), ALL, scatter_dimension=0, tiled=True).astype(F32)
 
-    out = spread(out)
     if fast:
-        half, s_in, s_out, _, _, dx1, g_t, gb_t, dmod2 = run_time_back(
-            x1, dx2, mod, seg, qkv2, o2, a2, wqkv_t, wo_t,
-            carry(out, (2,), True, 4, mlp_plan(wide, g_in, g_out, devices), (g_in, g_out)))
-        odd, s_qkv_t, s_o_t, _, _, dx0, g_s, gb_s, dmod1 = run_frame_back(
-            frames, dx1, mod, qkv1, o1, a1, wqkv_s, wo_s,
-            carry(out, (1, 3), True, 5, attn_plan(wide, g_t, devices), (g_t,)))
+        ahead = lengths.reshape(n, n)[(rank + slots[:, None] - slots[None, :]) % n, slots[None, :]]
+        own_start = jnp.sum(jnp.where(slots[None, :] < slots[:, None], ahead, 0), axis=1)
+        own_rows = slots[:, None] * LIVE + own_start[:, None] + frame_ids[None, :]
+        own_rows = jnp.where(own_live, own_rows, -1).reshape(-1)
+        plan_mlp = mlp_plan(wide, g_in, g_out, devices)
+        out, *got, dx1, g_t, gb_t, dmod2 = run_time_back(
+            x1, dx2, mod, seg, qkv2, o2, a2, wqkv_t, wo_t, share_carrier(out, [g_in, g_out], plan_mlp, 4))
+        keeps, fins = got[:2], got[2:4]
+        plan_t = attn_plan(wide, g_t, devices, True)
+        out, dx0, *got, g_s, gb_s, dmod1 = run_frame_back(
+            frames, dx1, mod, qkv1, o1, a1, wqkv_s, wo_s, relay_carrier(out, [g_t], plan_t, 5))
+        keeps, fins = keeps + got[:2], fins + got[2:4]
+        dx0, s_in, s_out, s_qkv_t, s_o_t, s_qkv_s, s_o_s, _, _ = scatter_last(
+            dx0, g_s, keeps, fins, attn_plan(wide, g_s, devices, False), (plan_mlp, plan_t))
+        layer_out = run_unpack(out, own_rows).reshape(n, FR, PATCHES, D)
+        grad_clips = run_unpack(dx0, own_rows).reshape(n, FR, PATCHES, D)
     else:
-        half = odd = None
         dx1, g_t, gb_t, dmod2 = run_time_back(x1, dx2, mod, seg, qkv2, o2, a2, wqkv_t, wo_t)
         dx0, g_s, gb_s, dmod1 = run_frame_back(frames, dx1, mod, qkv1, o1, a1, wqkv_s, wo_s)
-    layer_out = only_live(regroup(out, True, half, odd))
-    grad_clips = only_live(shift_clips(spread(dx0), True))
-    if fast:
-        s_qkv_s, s_o_s = scatter_last(g_s, attn_plan(wide, g_s, devices))
-    else:
+        layer_out = only_live(shift_clips(spread(out), True))
+        grad_clips = only_live(shift_clips(spread(dx0), True))
         s_in, s_out, s_t, s_s = [scatter(g) for g in (g_in, g_out, g_t, g_s)]
         s_qkv_t, s_o_t, s_qkv_s, s_o_s = s_t[:, : 3 * D], s_t[:, 3 * D :], s_s[:, : 3 * D], s_s[:, 3 * D :]
 

time: 638 us -> 627 us (0.983)
  local copies, waits for them, and re-layouts: 63.4 us -> 44.8 us
  Pallas kernels: 514 us -> 523 us
  other arithmetic: 24.9 us -> 16.7 us
    pallas_call x1 -> x3, Pallas kernels: 75.6 us -> 84.5 us  [the longest x1 67 us: scatter_last(): pl.pallas_call(functools.partial(last_kernel, plan, left, shapes), name='...]
    gather x2, local copies, waits for them, and re-layouts: 9.2 us -> 0.77 us  [local(): lengths.reshape(n, n)]
    select_n x2 -> x1, other arithmetic: 7.86 us -> 0.07 us  [local(): own_rows = jnp.where(own_live, own_rows, -1).reshape(-1)]
    slice x6 -> x3, local copies, waits for them, and re-layouts: 10.1 us -> 2.33 us  [local(): cots = jnp.stack([cotangent[0], odd[0][0], half[0][0], odd[0][1]])]
  transfers between devices with their start and end apart: 7 -> 4, of which waited for: 1 -> 2; matrix products, arithmetic and copies ran while one was open for 7% -> 3% of each run, Pallas kernels for 28% -> 31%
where the time goes in v5:
time: 627 us; the launch traced here: 619 us
  Pallas kernels  523 us (83%)
  local copies, waits for them, and re-layouts  44.8 us (7%)
  starting transfers between devices  18.5 us (3%)
  other arithmetic  16.7 us (3%)
  waiting for transfers between devices  12.9 us (2%)
    pallas_call x6, Pallas kernels, call(): return fn(*ins) if prefetch is None else fn(prefetch, *ins)  334 us
    pallas_call x1, Pallas kernels, gather_all(): pl.pallas_call(functools.partial(gather_kernel, ring, n, heights, ways),...  104 us
    pallas_call x1, Pallas kernels, scatter_last(): pl.pallas_call(functools.partial(last_kernel, plan, left, shapes), name='...  67 us
    all_to_all x4, starting transfers between devices, exchange(): return lax.all_to_all(x, ALL, split_axis=0, concat_axis=0, tiled=True)  18.5 us
    pallas_call x2, Pallas kernels, run_unpack(): pl.pallas_call(unpack_frames, grid_spec=pltpu.PrefetchScalarGridSpec(num_...  17.5 us
    all_to_all x4, waiting for transfers between devices, exchange(): return lax.all_to_all(x, ALL, split_axis=0, concat_axis=0, tiled=True)  12.9 us
  transfers between devices with their start and end apart: 4, of which 2 were waited for; matrix products, arithmetic and copies ran while one was open for 3% of the time, Pallas kernels for 31%

profile of v5, /device:TPU:1, one launch (start us, length us, event | category | flops | bytes accessed | tf_op | source)
XLA Modules:
  0.0 618.9 jit_solution(8553806961591130597)
XLA Ops:
  0.7 0.7 broadcast_in_dim.18
  1.4 2.2 reshape.614
  4.2 0.8 pad_maximum_fusion.3
  6.1 1.2 reduce.10
  7.3 1.7 reshape.738
  9.0 7.1 %all-to-all-start = ((bf16[32,2,5748]{2,1,0:T(2,128)(2,1)}), bf16[32,2,5748]{2,1,0:T(2,128)(2,1)S(1)}, u32[]{:S(2)}, u32[]{:S(2)}) async-start(bf16[32,2,5748]{2,1,0:T(2,128)(2,1)} %reshape.738), calls=%async_computation | async-start | bytes 1474560 | tf_op jit(solution)/shard_map/all_to_all | solution.py:984
  18.3 0.8 gather_fusion.6
  19.1 3.1 fusion.27
  22.2 1.2 gather_fusion.7
  23.5 0.8 gather_fusion.4
  24.2 104.4 %gather_all.1 = (bf16[4,16,64,768]{3,2,1,0:T(8,128)(2,1)}, bf16[768,3072]{1,0:T(8,128)(2,1)}, bf16[3072,768]{1,0:T(8,128)(2,1)}, bf16[768,2304]{1,0:T(8,128)(2,1...) custom-call(bf16[4,16,64,768]{3,2,1,0:T(8,128)(2,1)} %refs_0_.3, ...), custom_call_target="tpu_custom_call" | custom-call | tf_op jit(solution)/shard_map/gather_all/pallas_call | solution.py:706
  128.7 5.2 gather_fusion.2
  133.9 0.7 and_convert_fusion.refs_3_.refs_6_
  134.6 1.0 reshape.739
  137.9 1.3 all_to_all.38
  139.2 4.3 all-to-all-start.1
  143.6 0.7 reshape.639.bin_
  144.3 0.7 reshape.640.bout
  146.3 6.7 %all-to-all-done.1 = f32[32,1,1728]{2,1,0:T(1,128)S(1)} async-done(((f32[32,1,1728]{2,1,0:T(1,128)}), f32[32,1,1728]{2,1,0:T(1,128)S(1)}, u32[]{:S(2)}, u32[]{:S(2)}) %all-to-all-start.1) | async-done | bytes 221216 | tf_op jit(solution)/shard_map/all_to_all | solution.py:984
  154.9 1.4 copy.132
  156.3 41.3 %frame_forward.1 = (bf16[1,16,64,768]{3,2,1,0:T(8,128)(2,1)}, f32[64,32,768]{2,1,0:T(8,128)}, bf16[2048,2304]{1,0:T(8,128)(2,1)}, bf16[2048,768]{1,0:T(8,128)(2,1)}, f32[2048,768]{1,0:T(8,128)}) custom-call(bf16[4,16,64,768]{3,2,1,0:T(8,128)(2,1)} %refs_0_.5, bf16[32,64,768]{2,1,0:T(8,128)(2,1)} %gather_fusion.2, f32[9,32,768]{2,1,0:T(8,128)} %bitcast.142, ...), custom_call_target="tpu_custom_call" | custom-call | flops 9663676416 | bytes 33917952 | tf_op jit(solution)/shard_map/frame_forward/pallas_call | solution.py:353
  197.6 42.5 %time_forward.1 = (bf16[2,16,64,768]{3,2,1,0:T(8,128)(2,1)}, f32[64,32,768]{2,1,0:T(8,128)}, bf16[2048,2304]{1,0:T(8,128)(2,1)}, bf16[2048,768]{1,0:T(8,128)(2,1)}, f32[2048,768]{1,0:T(8,128)}) custom-call(bf16[4,16,64,768]{3,2,1,0:T(8,128)(2,1)} %refs_0_.5, f32[64,32,768]{2,1,0:T(8,128)} %get-tuple-element.67.refs_1_.refs_3_, f32[9,32,768]{2,1,0:T(8,128)} %bitcast.143, ...), custom_call_target="tpu_custom_call" | custom-call | flops 9663676416 | bytes 37096448 | tf_op jit(solution)/shard_map/time_forward/pallas_call | solution.py:353
  240.1 2.2 fusion.32
  242.9 3.2 pad_maximum_fusion
  246.1 6.9 %turn_frames.1.dy = f32[64,32,768]{2,1,0:T(8,128)} custom-call(s32[32]{0:T(128)} %get-tuple-element.115.rows_ref, bf16[64,64,768]{2,1,0:T(8,128)(2,1)} %bitcast.119, bf16[64,64,768]{2,1,0:T(8,128)(2,1)} %bitcast.120, bf16[64,64,768]{2,1,0:T(8,128)(2,1)} %bitcast.121, bf16[64,64,768]{2,1,0:T(8,128)(2,1)} %bitcast.122, bf16[64,64,768]{2,1,0:T(8,128)(2,1)} %bitcast.123, ...), custom_call_target="tpu_custom_call" | custom-call | flops 1000 | bytes 56623104 | tf_op jit(solution)/shard_map/turn_frames/pallas_call | solution.py:353
  253.0 85.5 %mlp_both.1 = (bf16[128,64,768]{2,1,0:T(8,128)(2,1)}, f32[64,32,768]{2,1,0:T(8,128)}, f32[768,3072]{1,0:T(8,128)}, f32[3072,768]{1,0:T(8,128)}, f32[1,3072]{1,0:...) custom-call(f32[64,32,768]{2,1,0:T(8,128)} %get-tuple-element.70.x2, f32[64,32,768]{2,1,0:T(8,128)} %turn_frames.1.dy, ...), custom_call_target="tpu_custom_call" | custom-call | flops 57982058496 | bytes 60979200 | tf_op jit(solution)/shard_map/mlp_both/pallas_call | solution.py:353
  338.5 80.8 %time_back.1 = (bf16[128,64,768]{2,1,0:T(8,128)(2,1)}, f32[24,3072]{1,0:T(8,128)}, f32[96,768]{1,0:T(8,128)}, bf16[24,3072]{1,0:T(8,128)(2,1)}, bf16[96,768]{1,0...) custom-call(bf16[128,64,768]{2,1,0:T(8,128)(2,1)} %get-tuple-element, ...), custom_call_target="tpu_custom_call", output_to_operand_aliasing={{0}: (0, {})} | custom-call | flops 19327352832 | bytes 53120000 | tf_op jit(solution)/shard_map/time_back/pallas_call | solution.py:353
  419.3 76.9 %frame_back.1 = (bf16[128,64,768]{2,1,0:T(8,128)(2,1)}, bf16[128,64,768]{2,1,0:T(8,128)(2,1)}, f32[24,1536]{1,0:T(8,128)}, f32[24,1536]{1,0:T(8,128)}, bf16[24,1...) custom-call(bf16[128,64,768]{2,1,0:T(8,128)(2,1)} %get-tuple-element, ...), custom_call_target="tpu_custom_call", output_to_operand_aliasing={{0}: (0, {})} | custom-call | flops 19327352832 | bytes 43650048 | tf_op jit(solution)/shard_map/frame_back/pallas_call | solution.py:353
  496.3 1.2 maximum_bitcast_fusion
  498.7 1.3 reduce.11
  500.1 0.8 reshape.740
  500.9 3.9 all-to-all-start.2
  505.4 0.7 reduce.9
  506.4 6.2 all-to-all-done.2
  512.7 0.7 reduce.2
  514.1 0.8 convert_reduce_fusion
  516.9 2.1 all_to_all.35
  519.0 3.3 all-to-all-start.3
  522.5 0.7 gather_fusion
  524.1 8.4 %unpack_frames.2 = bf16[64,64,768]{2,1,0:T(8,128)(2,1)} custom-call(s32[64]{0:T(128)} %select_n.185.rows_ref, bf16[128,64,768]{2,1,0:T(8,128)(2,1)} %get-tuple-element.88.refs_0_.refs_1_.refs_2_.refs_3_.refs_4_.refs_5_.refs_6_.refs_7_, bf16[128,64,768]{2,1,0:T(8,128)(2,1)} %get-tuple-element.88.refs_0_.refs_1_.refs_2_.refs_3_.refs_4_.refs_5_.refs_6_.refs_7_, ...), custom_call_target="tpu_custom_call" | custom-call | flops 1000 | bytes 12582912 | tf_op jit(solution)/shard_map/unpack_frames/pallas_call | solution.py:537
  532.5 67.0 %scatter_last.1 = (bf16[128,64,768]{2,1,0:T(8,128)(2,1)}, f32[24,3072]{1,0:T(8,128)}, f32[96,768]{1,0:T(8,128)}, f32[24,2304]{1,0:T(8,128)}, f32[24,768]{1,0:T(8...) custom-call(bf16[128,64,768]{2,1,0:T(8,128)(2,1)} %get-tuple-element, ...), custom_call_target="tpu_custom_call", output_to_operand_aliasing={{0}: (0, {})} | custom-call | tf_op jit(solution)/shard_map/scatter_last/pallas_call | solution.py:955
  599.5 9.1 %unpack_frames.3 = bf16[64,64,768]{2,1,0:T(8,128)(2,1)} custom-call(s32[64]{0:T(128)} %select_n.185.rows_ref, bf16[128,64,768]{2,1,0:T(8,128)(2,1)} %get-tuple-element.99.refs_0_.refs_1_.refs_2_.refs_3_.refs_4_.refs_5_.refs_6_.refs_7_, bf16[128,64,768]{2,1,0:T(8,128)(2,1)} %get-tuple-element.99.refs_0_.refs_1_.refs_2_.refs_3_.refs_4_.refs_5_.refs_6_.refs_7_, ...), custom_call_target="tpu_custom_call" | custom-call | flops 1000 | bytes 12582912 | tf_op jit(solution)/shard_map/unpack_frames/pallas_call | solution.py:537
  608.6 1.5 copy.131
  613.3 1.3 reshape.636
  614.6 0.7 copy.147
  615.9 0.7 copy.149
  617.2 0.7 copy.151
  618.0 0.7 copy.152
  (144 shorter events, 20.3 us)
Async XLA Ops:
  0.6 16.5 %copy-start = (s32[16,16]{1,0:T(8,128)S(1)}, s32[16,16]{1,0:T(8,128)}, u32[]{:S(2)}) copy-start(s32[16,16]{1,0:T(8,128)} %param.20) | copy-start | bytes 3076
  3.8 12.3 %copy-start.17 = (bf16[216]{0:T(256)(128)(2,1)S(1)}, bf16[216]{0:T(256)(128)(2,1)}, u32[]{:S(2)}) copy-start(bf16[216]{0:T(256)(128)(2,1)} %param.22) | copy-start | bytes 1300
  3.8 12.3 %copy-start.16 = (s32[16]{0:T(128)S(1)}, s32[16]{0:T(128)}, u32[]{:S(2)}) copy-start(s32[16]{0:T(128)} %param.19) | copy-start | bytes 196
  9.0 125.6 %all-to-all-start = ((bf16[32,2,5748]{2,1,0:T(2,128)(2,1)}), bf16[32,2,5748]{2,1,0:T(2,128)(2,1)S(1)}, u32[]{:S(2)}, u32[]{:S(2)}) async-start(bf16[32,2,5748]{2,1,0:T(2,128)(2,1)} %reshape.738), calls=%async_computation | async-start | bytes 1474560 | tf_op jit(solution)/shard_map/all_to_all | solution.py:984
  16.2 112.4 %copy-start.2 = (s32[4,4]{1,0:T(4,128)}, s32[4,4]{1,0:T(4,128)S(1)}, u32[]{:S(2)}) copy-start(s32[4,4]{1,0:T(4,128)S(1)} %reshape.610) | copy-start | bytes 196
  139.2 13.9 %all-to-all-start.1 = ((f32[32,1,1728]{2,1,0:T(1,128)}), f32[32,1,1728]{2,1,0:T(1,128)S(1)}, u32[]{:S(2)}, u32[]{:S(2)}) async-start(f32[32,1,1728]{2,1,0:T(1,128)} %all_to_all.38), calls=%async_computation.1 | async-start | bytes 458752 | tf_op jit(solution)/shard_map/all_to_all | solution.py:984
  240.1 2.4 slice-start
  240.1 2.8 copy-start.4
  496.2 8.6 %copy-start.15 = (f32[1,768]{1,0:T(1,128)S(1)}, f32[1,768]{1,0:T(1,128)}, u32[]{:S(2)}) copy-start(f32[1,768]{1,0:T(1,128)} %get-tuple-element.103) | copy-start | bytes 9220
  496.2 8.6 %copy-start.14 = (f32[1,768]{1,0:T(1,128)S(1)}, f32[1,768]{1,0:T(1,128)}, u32[]{:S(2)}) copy-start(f32[1,768]{1,0:T(1,128)} %get-tuple-element.104) | copy-start | bytes 9220
  496.2 8.6 %copy-start.13 = (f32[1,768]{1,0:T(1,128)S(1)}, f32[1,768]{1,0:T(1,128)}, u32[]{:S(2)}) copy-start(f32[1,768]{1,0:T(1,128)} %get-tuple-element.106) | copy-start | bytes 9220
  496.2 9.1 %copy-start.12 = (f32[1,3072]{1,0:T(1,128)S(1)}, f32[1,3072]{1,0:T(1,128)}, u32[]{:S(2)}) copy-start(f32[1,3072]{1,0:T(1,128)} %get-tuple-element.105) | copy-start | bytes 36868
  500.9 11.7 %all-to-all-start.2 = ((bf16[32,2,864]{2,1,0:T(2,128)(2,1)}), bf16[32,2,864]{2,1,0:T(2,128)(2,1)S(1)}, u32[]{:S(2)}, u32[]{:S(2)}) async-start(bf16[32,2,864]{2,1,0:T(2,128)(2,1)} %reshape.740), calls=%async_computation.2 | async-start | bytes 229376 | tf_op jit(solution)/shard_map/all_to_all | solution.py:984
  516.9 5.6 copy-start.3
  519.0 89.6 %all-to-all-start.3 = ((f32[32,1,11496]{2,1,0:T(1,128)}), f32[32,1,11496]{2,1,0:T(1,128)}, u32[]{:S(2)}, u32[]{:S(2)}) async-start(f32[32,1,11496]{2,1,0:T(1,128)} %all_to_all.35), calls=%async_computation.3 | async-start | bytes 2949120 | tf_op jit(solution)/shard_map/all_to_all | solution.py:984
  608.6 3.2 copy-start.11
  610.1 4.5 copy-start.8
  611.3 3.9 copy-start.10
  611.3 4.6 copy-start.7
  611.6 5.0 copy-start.9
  611.6 5.6 copy-start.6
  611.7 6.3 %copy-start.5 = (f32[96,768]{1,0:T(8,128)S(1)}, f32[96,768]{1,0:T(8,128)}, u32[]{:S(2)}) copy-start(f32[96,768]{1,0:T(8,128)} %get-tuple-element.173) | copy-start | bytes 884740
  611.7 7.0 %copy-start.1 = (s32[16,16]{1,0:T(8,128)S(1)}, s32[16,16]{1,0:T(8,128)}, u32[]{:S(2)}) copy-start(s32[16,16]{1,0:T(8,128)} %param.20) | copy-start | bytes 3076

commit v6 on v5

--- a/solution.py
+++ b/solution.py
@@ -26,6 +26,7 @@
 PT = TILE // LIVE
 GRID = LIVE * PATCHES // TILE
 GROUPS = TILE // 64
+EARLY_TILES = GRID // 2
 GELU_C = 0.7978845608028654
 GELU_A = 0.044715
 VMEM_LIMIT = 66 * 1000 * 1000
@@ -161,12 +162,18 @@
     return seg_ref[...] > 0.0
 
 
-def frame_forward(frames, mod, wqkv, wo, bo, x1t, qkv, o, a1, scratch):
+def no_tick(place):
+    pass
+
+
+def frame_forward(frames, mod, wqkv, wo, bo, x1t, qkv, o, a1, scratch, tick=no_tick):
     x = frames[...].reshape(TILE, D).astype(F32)
     xhat, _ = normalise(x)
     h = (xhat * (1.0 + per_frame(mod[1])) + per_frame(mod[0])).astype(BF)
     qkv[...] = dot(h, wqkv[...]).astype(BF)
+    tick(0)
     attend(qkv, o, None)
+    tick(1)
     branch = dot(o[...], wo[...]) + bo[...]
     a1[...] = branch
     x1 = x + per_frame(mod[2]) * branch
@@ -178,12 +185,14 @@
     swap_major(frames_of(x_refs), scratch, out, FT, PATCHES)
 
 
-def time_forward(x1, mod, seg, wqkv, wo, bo, x2, qkv, o, a2):
+def time_forward(x1, mod, seg, wqkv, wo, bo, x2, qkv, o, a2, tick=no_tick):
     x = x1[...].reshape(TILE, D)
     xhat, _ = normalise(x)
     h = (xhat * (1.0 + per_patch(mod[1])) + per_patch(mod[0])).astype(BF)
     qkv[...] = dot(h, wqkv[...]).astype(BF)
+    tick(0)
     attend(qkv, o, attn_mask(seg))
+    tick(1)
     branch = dot(o[...], wo[...]) + bo[...]
     a2[...] = branch
     x2[...] = (x + per_patch(mod[2]) * branch).reshape(PT, LIVE, D)
@@ -258,10 +267,6 @@
     return dx, dh, dh * xhat, grad * branch
 
 
-def no_tick(place):
-    pass
-
-
 def time_back(x1, dx2, mod, seg, qkv, o, a2, wqkv, wo, dx1, gw, gbo, dmod, do, dqkv, scratch, tick=no_tick):
     @pl.when(pl.program_id(0) == 0)
     def _():
@@ -361,28 +366,48 @@
     return parts + [refs]
 
 
-def clips_carrier(clips, js, n, number):
+def forward_carrier(clips, js, shard, ring, n, number):
+    held = Gather.scratch([shard], ring)
+
     def wrap(kernel, n_in, n_out, n_scratch, *refs):
-        (src,), ins, (dst,), outs, scratch, (send_sem, recv_sem) = split_refs(refs, 1, n_in, 1, n_out, n_scratch)
-        w, k = lax.axis_index("wide"), lax.axis_index("narrow")
-        peers = [(w, (k + j) % n) for j in js]
-        copies = [send(src.at[j], dst.at[i], send_sem.at[i], recv_sem.at[i], peers[i]) for i, j in enumerate(js)]
-
-        @pl.when(pl.program_id(0) == 0)
+        (src, part), ins, (dst, full), outs, scratch, (send_sem, recv_sem), own = split_refs(
+            refs, 2, n_in, 2, n_out, n_scratch, 2)
+        step = pl.program_id(0)
+        gather = Gather(ring, (shard.shape[0],), (part, full) + own)
+        targets = [(gather.w, (gather.k + j) % n) for j in js]
+        copies = [send(src.at[j], dst.at[i], send_sem.at[i], recv_sem.at[i], targets[i]) for i, j in enumerate(js)]
+
+        @pl.when(step == 0)
         def _():
-            greet(peers)
+            greet(tuple(targets) + gather.peers)
+            gather.begin()
             for copy in copies:
                 copy.start()
 
-        kernel(*ins, *outs, *scratch)
-
-        @pl.when(pl.program_id(0) == GRID - 1)
+        def tick(place):
+            if place == 0:
+                @pl.when(step == 0)
+                def _():
+                    gather.second()
+
+                @pl.when(step > 0)
+                def _():
+                    gather.hop(2 * step)
+            else:
+                gather.hop(2 * step + 1)
+
+        kernel(*ins, *outs, *scratch, tick=tick)
+
+        @pl.when(step == GRID - 1)
         def _():
+            gather.finish()
             for copy in copies:
                 copy.wait()
 
     sems = pltpu.SemaphoreType.DMA((len(js),))
-    return Carrier(wrap, number, [clips], [shape_of((len(js),) + clips.shape[1:], clips.dtype)], [ANY], [sems, sems])
+    return Carrier(wrap, number, [clips, shard],
+                   [shape_of((len(js),) + clips.shape[1:], clips.dtype)] + Gather.shapes([shard], ring * n),
+                   [ANY, ANY], [sems, sems] + held)
 
 
 def packed(slot, first=0, count=LIVE):
@@ -394,10 +419,6 @@
 
 
 def ticks(sums, step):
-    @pl.when(step > 0)
-    def _():
-        sums.hop(2 * step - 1)
-
     def tick(place):
         @pl.when(step == 0)
         def _():
@@ -406,10 +427,9 @@
             else:
                 sums.first_hop()
 
-        if place == 1:
-            @pl.when(step > 0)
-            def _():
-                sums.hop(2 * step)
+        @pl.when(step > 0)
+        def _():
+            sums.hop(2 * step - 1 + place)
 
     return tick
 
@@ -477,7 +497,7 @@
         kernel(*ins, buf.at[step], *outs, *scratch, tick=ticks(sums, step))
         store(step).start()
 
-        @pl.when(step < GRID - 1)
+        @pl.when(step < EARLY_TILES)
         def _():
             for copy in tile(step):
                 copy.start()
@@ -488,14 +508,14 @@
             relay.wait()
             for i in range(GRID):
                 store(i).wait()
-            for i in range(GRID - 1):
+            for i in range(EARLY_TILES):
                 for copy in tile(i):
                     copy.wait()
 
     sems = pltpu.SemaphoreType.DMA
     shape = shape_of(frames.shape, frames.dtype)
     return Carrier(wrap, number, [frames] + grads, [shape, shape] + plan.out_shapes, [ANY, ANY] + plan.out_specs,
-                   [sems((1,)), sems((1,)), sems((2, GRID - 1)), sems((2, GRID - 1)), sems((GRID,)),
+                   [sems((1,)), sems((1,)), sems((2, EARLY_TILES)), sems((2, EARLY_TILES)), sems((GRID,)),
                     pltpu.VMEM((GRID, FT, PATCHES, D), BF)] + plan.scratch, {0: 0})
 
 
@@ -625,100 +645,119 @@
     )
 
 
-def gather_kernel(ring, n, heights, ways, *refs):
-    count = len(heights)
-    clips, shards = refs[0], refs[1 : 1 + count]
-    frames, full = refs[1 + count], refs[2 + count : 2 + 2 * count]
-    clip_buf, bufs = refs[2 + 2 * count], refs[3 + 2 * count : 3 + 3 * count]
-    ring_s, ring_r, core_s, core_r, x_s, x_r, clip_s, clip_r, load_sem, keep_sem = refs[3 + 3 * count :]
-    w, k, r, x, c, wide_at = place_of(ring)
-    other_x = (w, 2 * (1 - x) + c)
-    other_c = (w, 2 * x + 1 - c)
-    steps = ((wide_at((r + 1) % ring), k), (wide_at((r + ring - 1) % ring), k))
-    greet(steps + tuple((w, (k + j) % n) for j in range(1, n)))
-
-    def rows(t, position, column):
-        block = 4 * wide_at(position) + 2 * column + c
-        return pl.ds(pl.multiple_of(block * heights[t], 8), heights[t])
-
-    def ring_copy(t, b, s, src=None):
-        place = (r + ring - s) % ring if ways[t] == 0 else (r + s) % ring
-        dst = full[t].at[rows(t, place, x if b == 0 else 1 - x)]
-        return send(dst if src is None else src, dst, ring_s.at[t, b, s], ring_r.at[t, b, s], steps[ways[t]])
-
-    def core_copy(t, b, s, src=None):
-        place = (r + ring - s) % ring if ways[t] == 0 else (r + s) % ring
-        dst = full[t].at[rows(t, place, x if b == 0 else 1 - x)]
-        return send(dst if src is None else src, dst, core_s.at[t, b, s], core_r.at[t, b, s], other_c)
-
-    def x_copy(t):
-        dst = full[t].at[rows(t, r, x)]
-        return send(shards[t], dst, x_s.at[t], x_r.at[t], other_x)
-
-    def clip_copy(j):
-        return send(clips.at[j], frames.at[j], clip_s.at[j], clip_r.at[j], (w, (k + j) % n))
-
-    for t in range(count):
-        x_copy(t).start()
-        ring_copy(t, 0, 0, shards[t]).start()
-    for j in range(1, n):
-        clip_copy(j).start()
-    for t in range(count):
-        core_copy(t, 0, 0, shards[t]).start()
-    loads = [pltpu.make_async_copy(clips.at[0], clip_buf, load_sem.at[count])]
-    loads += [pltpu.make_async_copy(shards[t], bufs[t], load_sem.at[t]) for t in range(count)]
-    keeps = [pltpu.make_async_copy(clip_buf, frames.at[0], keep_sem.at[count])]
-    keeps += [pltpu.make_async_copy(bufs[t], full[t].at[rows(t, r, x)], keep_sem.at[t]) for t in range(count)]
-    for copy in loads:
-        copy.start()
-    for copy, keep in zip(loads, keeps):
-        copy.wait()
-        keep.start()
-    for t in range(count):
-        x_copy(t).wait_recv()
-        ring_copy(t, 1, 0).start()
-        core_copy(t, 1, 0).start()
-    for s in range(1, ring):
+class Gather:
+    def __init__(self, ring, heights, refs):
+        count = len(heights)
+        self.ring, self.heights, self.count = ring, heights, count
+        self.shards, self.full, self.bufs, sems = split_refs(refs, count, count, count)
+        (self.ring_s, self.ring_r, self.core_s, self.core_r, self.x_s, self.x_r, self.load_sem, self.keep_sem) = sems
+        self.w, self.k, self.r, self.x, self.c, self.wide_at = place_of(ring)
+        self.other_x = (self.w, 2 * (1 - self.x) + self.c)
+        self.other_c = (self.w, 2 * self.x + 1 - self.c)
+        self.next = ((self.wide_at((self.r + 1) % ring), self.k), (self.wide_at((self.r + ring - 1) % ring), self.k))
+        self.peers = self.next + (self.other_x, self.other_c)
+
+    @staticmethod
+    def scratch(shards, ring):
+        count, sems = len(shards), pltpu.SemaphoreType.DMA
+        return ([pltpu.VMEM(a.shape, a.dtype) for a in shards] + [sems((count, 2, ring))] * 4 + [sems((count,))] * 4)
+
+    @staticmethod
+    def shapes(shards, devices):
+        return [shape_of((a.shape[0] * devices, a.shape[1]), a.dtype) for a in shards]
+
+    def way(self, t, b):
+        return (t + b) % 2
+
+    def block(self, t, b, s):
+        r, ring = self.r, self.ring
+        place = (r + ring - s) % ring if self.way(t, b) == 0 else (r + s) % ring
+        column = self.x if b == 0 else 1 - self.x
+        block = 4 * self.wide_at(place) + 2 * column + self.c
+        return self.full[t].at[pl.ds(pl.multiple_of(block * self.heights[t], 8), self.heights[t])]
+
+    def ring_copy(self, t, b, s, src=None):
+        dst = self.block(t, b, s)
+        return send(dst if src is None else src, dst, self.ring_s.at[t, b, s], self.ring_r.at[t, b, s],
+                    self.next[self.way(t, b)])
+
+    def core_copy(self, t, b, s, src=None):
+        dst = self.block(t, b, s)
+        return send(dst if src is None else src, dst, self.core_s.at[t, b, s], self.core_r.at[t, b, s], self.other_c)
+
+    def x_copy(self, t):
+        return send(self.shards[t], self.block(t, 0, 0), self.x_s.at[t], self.x_r.at[t], self.other_x)
+
+    def load(self, t):
+        return pltpu.make_async_copy(self.shards[t], self.bufs[t], self.load_sem.at[t])
+
+    def keep(self, t):
+        return pltpu.make_async_copy(self.bufs[t], self.block(t, 0, 0), self.keep_sem.at[t])
+
+    def begin(self):
+        for t in range(self.count):
+            self.x_copy(t).start()
+            self.ring_copy(t, 0, 0, self.shards[t]).start()
+        for t in range(self.count):
+            self.core_copy(t, 0, 0, self.shards[t]).start()
+            self.load(t).start()
+
+    def second(self):
+        for t in range(self.count):
+            self.load(t).wait()
+            self.keep(t).start()
+        for t in range(self.count):
+            self.x_copy(t).wait_recv()
+            self.ring_copy(t, 1, 0).start()
+            self.core_copy(t, 1, 0).start()
+
+    def hop(self, s):
         for b in range(2):
-            for t in range(count):
-                ring_copy(t, b, s - 1).wait_recv()
-                if s < ring - 1:
-                    ring_copy(t, b, s).start()
-                core_copy(t, b, s).start()
-    for copy in keeps:
-        copy.wait()
-    for t in range(count):
-        x_copy(t).wait_send()
-        for b in range(2):
-            for s in range(ring):
-                if s < ring - 1:
-                    ring_copy(t, b, s).wait_send()
-                core_copy(t, b, s).wait()
-    for j in range(1, n):
-        clip_copy(j).wait()
-
-
-def gather_all(clips, shards, ways, ring, n):
-    count = len(shards)
-    devices = ring * n
+            for t in range(self.count):
+                self.ring_copy(t, b, s - 1).wait_recv()
+
+                @pl.when(s < self.ring - 1)
+                def _():
+                    self.ring_copy(t, b, s).start()
+
+                self.core_copy(t, b, s).start()
+
+    def finish(self):
+        for t in range(self.count):
+            self.keep(t).wait()
+            self.x_copy(t).wait_send()
+            for b in range(2):
+                for s in range(self.ring):
+                    if s < self.ring - 1:
+                        self.ring_copy(t, b, s).wait_send()
+                    self.core_copy(t, b, s).wait()
+
+
+def gather_kernel(ring, heights, *refs):
+    gather = Gather(ring, heights, refs)
+    greet(gather.peers)
+    gather.begin()
+    gather.second()
+
+    def body(s, carry):
+        gather.hop(s)
+        return carry
+
+    lax.fori_loop(1, ring, body, 0)
+    gather.finish()
+
+
+def gather_first(shards, ring, n):
     heights = tuple(a.shape[0] for a in shards)
-    sems = pltpu.SemaphoreType.DMA
-    got = pl.pallas_call(
-        functools.partial(gather_kernel, ring, n, heights, ways),
-        name="gather_all",
-        out_shape=[shape_of(clips.shape, clips.dtype)]
-        + [shape_of((a.shape[0] * devices, a.shape[1]), a.dtype) for a in shards],
-        in_specs=[ANY] * (1 + count),
-        out_specs=[ANY] * (1 + count),
-        scratch_shapes=[pltpu.VMEM(clips.shape[1:], clips.dtype)]
-        + [pltpu.VMEM(a.shape, a.dtype) for a in shards]
-        + [sems((count, 2, ring))] * 4
-        + [sems((count,))] * 2
-        + [sems((n,))] * 2
-        + [sems((count + 1,))] * 2,
+    return pl.pallas_call(
+        functools.partial(gather_kernel, ring, heights),
+        name="gather_first",
+        out_shape=Gather.shapes(shards, ring * n),
+        in_specs=[ANY] * len(shards),
+        out_specs=[ANY] * len(shards),
+        scratch_shapes=Gather.scratch(shards, ring),
         compiler_params=pltpu.CompilerParams(collective_id=0, has_side_effects=True),
-    )(clips, *shards)
-    return got[0], got[1:]
+    )(*shards)
 
 
 def put(outs, places, value):
@@ -881,20 +920,25 @@
         )
         self.scratches = len(self.scratch)
 
+    def left(self, results):
+        count = len(self.pieces)
+        return results[:count], results[count : 2 * count]
+
     def steps(self, refs):
         return Sums(self, refs)
 
 
 def mlp_plan(ring, g_in, g_out, devices):
     a, b = g_in.shape[0] // devices, g_out.shape[0] // devices
-    wa, wb = g_in.shape[1], g_out.shape[1]
-    return Plan(ring, 2, [(0, 0, wa, a, 0), (1, 0, wb, b, 1)], [(a, wa), (b, wb)], [[(0, 0, 0, wa)], [(1, 0, 0, wb)]], True)
+    wa, wb = g_in.shape[1] // 2, g_out.shape[1] // 2
+    return Plan(ring, 2, [(0, 0, wa, a, 0), (1, 0, wb, b, 1), (0, wa, wa, a, 0), (1, wb, wb, b, 1)],
+                [(a, 2 * wa), (b, 2 * wb)], [[(0, 0, 0, wa)], [(1, 0, 0, wb)], [(0, wa, 0, wa)], [(1, wb, 0, wb)]], True)
 
 
 def attn_plan(ring, g, devices, leave):
-    h, half, cut = g.shape[0] // devices, 2 * D, 3 * D
-    return Plan(ring, 1, [(0, 0, half, h, 0), (0, half, half, h, 1)], [(h, cut), (h, D)],
-                [[(0, 0, 0, half)], [(0, half, 0, cut - half), (1, 0, cut - half, D)]], leave)
+    h = g.shape[0] // devices
+    return Plan(ring, 1, [(0, i * D, D, h, i % 2) for i in range(4)], [(h, 3 * D), (h, D)],
+                [[(0, i * D, 0, D)] for i in range(3)] + [[(1, 0, 0, D)]], leave)
 
 
 def last_kernel(plan, left, shapes, *refs):
@@ -905,9 +949,9 @@
      (fin_send, fin_recv, tile_s, tile_r, relay_s, relay_r), own) = split_refs(
         refs, 1, plan.inputs, count, count, 1, made, plan.outputs, count, 6)
     sums = plan.steps(grads + own_outs + own)
-    final_tile = GRID - 1
-    tile = tile_copies(sums.k, sums.other_c, sums.other_x, frames.at[packed(0, final_tile * FT, FT)], frames, final_tile,
-                       tile_s, tile_r)
+    late_tiles = range(EARLY_TILES, GRID)
+    tile = {i: tile_copies(sums.k, sums.other_c, sums.other_x, frames.at[packed(0, i * FT, FT)], frames, i, tile_s, tile_r)
+            for i in late_tiles}
 
     def fin_copy(t):
         return send(fins[t], fins_r[t], fin_send.at[t], fin_recv.at[t], sums.other_x)
@@ -917,11 +961,13 @@
                     frames.at[packed(4 - slot_for(sums.k), first, frames_count)],
                     relay_s.at[i], relay_r.at[i], sums.other_c)
 
-    early, late = relay(0, 0, final_tile * FT), relay(1, final_tile * FT, FT)
+    early = relay(0, 0, EARLY_TILES * FT)
+    late = {i: relay(i, i * FT, FT) for i in late_tiles}
     greet(sums.peers)
     sums.begin()
-    for copy in tile:
-        copy.start()
+    for i in late_tiles:
+        for copy in tile[i]:
+            copy.start()
     for t in range(count):
         fin_copy(t).start()
     early.start()
@@ -934,18 +980,20 @@
 
     lax.fori_loop(1, sums.final, body, 0)
     sums.finish()
-    tile[1].wait_recv()
-    late.start()
+    for i in late_tiles:
+        tile[i][1].wait_recv()
+        late[i].start()
     for t in range(count):
         fin_copy(t).wait_recv()
         value = keeps[t][...] + fins_r[t][...].astype(F32)
         put(left_outs[offsets[t] :], places[t], value)
     for t in range(count):
         fin_copy(t).wait_send()
-    tile[0].wait()
-    tile[1].wait_send()
     early.wait()
-    late.wait()
+    for i in late_tiles:
+        tile[i][0].wait()
+        tile[i][1].wait_send()
+        late[i].wait()
 
 
 def scatter_last(frames, g, keeps, fins, plan, left):
@@ -959,7 +1007,7 @@
         in_specs=[ANY] * 2 + [vmem] * len(keeps) + [ANY] * len(fins),
         out_specs=[ANY] + [vmem] * len(shapes) + plan.out_specs,
         scratch_shapes=[pltpu.VMEM(f.shape, f.dtype) for f in fins]
-        + [sems((len(fins),))] * 2 + [sems((2, GRID))] * 2 + [sems((2,))] * 2 + plan.scratch,
+        + [sems((len(fins),))] * 2 + [sems((2, GRID))] * 2 + [sems((GRID,))] * 2 + plan.scratch,
         input_output_aliases={0: 0},
         compiler_params=pltpu.CompilerParams(
             collective_id=1, has_side_effects=True, vmem_limit_bytes=VMEM_LIMIT
@@ -1025,13 +1073,11 @@
     def gather(w):
         return lax.all_gather(w, ALL, axis=0, tiled=True)
 
-    weights = (w_in, w_out, w_qkv_t, w_o_t, w_qkv_s, w_o_s)
+    frames = shift_clips(clips, False)
     if fast:
-        frames, weights = gather_all(clips, weights, (0, 0, 1, 1, 1, 1), wide, n)
+        wqkv_s, wo_s, wqkv_t, wo_t = gather_first((w_qkv_s, w_o_s, w_qkv_t, w_o_t), wide, n)
     else:
-        frames = shift_clips(clips, False)
-        weights = [gather(w) for w in weights]
-    win, wout, wqkv_t, wo_t, wqkv_s, wo_s = weights
+        win, wout, wqkv_t, wo_t, wqkv_s, wo_s = [gather(w) for w in (w_in, w_out, w_qkv_t, w_o_t, w_qkv_s, w_o_s)]
     frames = jnp.take(frames.reshape(n * FR, PATCHES, D), pack_rows, axis=0, mode="clip")
 
     wm = jnp.swapaxes(w_mod.reshape(part, devices, mod_cols), 0, 1).reshape(devices, -1)
@@ -1056,15 +1102,16 @@
     mod_rows = jnp.swapaxes(mod_rows, 0, 1).reshape(2 * n, 9, D)
     mod = jnp.swapaxes(mod_rows[row_choice], 0, 1)
 
-    def carry(js, number):
-        return clips_carrier(cotangent, js, n, number) if fast else None
+    def carry(js, shard, number):
+        return forward_carrier(cotangent, js, shard, wide, n, number) if fast else None
 
     *half, x1, qkv1, o1, a1 = run_frame_forward(
-        frames, mod, wqkv_s, wo_s, bias_s, carry((2,), 2))
+        frames, mod, wqkv_s, wo_s, bias_s, carry((2,), w_in, 2))
     *odd, x2, qkv2, o2, a2 = run_time_forward(
-        x1, mod, seg, wqkv_t, wo_t, bias_t, carry((1, 3), 3))
+        x1, mod, seg, wqkv_t, wo_t, bias_t, carry((1, 3), w_out, 3))
     if fast:
-        cots = jnp.stack([cotangent[0], odd[0][0], half[0][0], odd[0][1]])
+        (half, win), (odd, wout) = half, odd
+        cots = jnp.stack([cotangent[0], odd[0], half[0], odd[1]])
     else:
         cots = shift_clips(cotangent, False)
     dy = run_turn_frames(cots.reshape(n * FR, PATCHES, D), pack_rows)
@@ -1090,13 +1137,14 @@
         plan_mlp = mlp_plan(wide, g_in, g_out, devices)
         out, *got, dx1, g_t, gb_t, dmod2 = run_time_back(
             x1, dx2, mod, seg, qkv2, o2, a2, wqkv_t, wo_t, share_carrier(out, [g_in, g_out], plan_mlp, 4))
-        keeps, fins = got[:2], got[2:4]
+        keeps, fins = plan_mlp.left(got)
         plan_t = attn_plan(wide, g_t, devices, True)
         out, dx0, *got, g_s, gb_s, dmod1 = run_frame_back(
             frames, dx1, mod, qkv1, o1, a1, wqkv_s, wo_s, relay_carrier(out, [g_t], plan_t, 5))
-        keeps, fins = keeps + got[:2], fins + got[2:4]
-        dx0, s_in, s_out, s_qkv_t, s_o_t, s_qkv_s, s_o_s, _, _ = scatter_last(
-            dx0, g_s, keeps, fins, attn_plan(wide, g_s, devices, False), (plan_mlp, plan_t))
+        more_keeps, more_fins = plan_t.left(got)
+        keeps, fins = keeps + more_keeps, fins + more_fins
+        dx0, s_in, s_out, s_qkv_t, s_o_t, s_qkv_s, s_o_s = scatter_last(
+            dx0, g_s, keeps, fins, attn_plan(wide, g_s, devices, False), (plan_mlp, plan_t))[:7]
         layer_out = run_unpack(out, own_rows).reshape(n, FR, PATCHES, D)
         grad_clips = run_unpack(dx0, own_rows).reshape(n, FR, PATCHES, D)
     else:

time: 627 us -> 665 us (1.061)
  Pallas kernels: 523 us -> 551 us
  local copies, waits for them, and re-layouts: 44.8 us -> 56.6 us
  other arithmetic: 16.7 us -> 24.4 us
  waiting for transfers between devices: 12.9 us -> 6.18 us
    pallas_call x6, Pallas kernels: 334 us -> 353 us  [call(): return fn(*ins) if prefetch is None else fn(prefetch, *ins)]
    pallas_call x1, Pallas kernels: 104 us -> 117 us  [gather_first(): pl.pallas_call(functools.partial(gather_kernel, ring, heights), name='gat...]
    all_to_all x4, waiting for transfers between devices: 12.9 us -> 6.17 us  [exchange(): return lax.all_to_all(x, ALL, split_axis=0, concat_axis=0, tiled=True)]
    unnamed x50 -> x66, local copies, waits for them, and re-layouts: 9.98 us -> 14.8 us
  transfers between devices with their start and end apart: 4 -> 7, of which waited for: 2 -> 1; matrix products, arithmetic and copies ran while one was open for 3% -> 6% of each run, Pallas kernels for 31% -> 30%
where the time goes in v6:
time: 665 us; the launch traced here: 662 us
  Pallas kernels  551 us (83%)
  local copies, waits for them, and re-layouts  56.6 us (9%)
  other arithmetic  24.4 us (4%)
  starting transfers between devices  19.8 us (3%)
    pallas_call x6, Pallas kernels, call(): return fn(*ins) if prefetch is None else fn(prefetch, *ins)  353 us
    pallas_call x1, Pallas kernels, gather_first(): pl.pallas_call(functools.partial(gather_kernel, ring, heights), name='gat...  117 us
    pallas_call x1, Pallas kernels, scatter_last(): pl.pallas_call(functools.partial(last_kernel, plan, left, shapes), name='...  64.4 us
    all_to_all x4, starting transfers between devices, exchange(): return lax.all_to_all(x, ALL, split_axis=0, concat_axis=0, tiled=True)  18 us
    pallas_call x2, Pallas kernels, run_unpack(): pl.pallas_call(unpack_frames, grid_spec=pltpu.PrefetchScalarGridSpec(num_...  17.7 us
    unnamed x66, local copies, waits for them, and re-layouts  14.8 us
  transfers between devices with their start and end apart: 7, of which 1 were waited for; matrix products, arithmetic and copies ran while one was open for 6% of the time, Pallas kernels for 30%

profile of v6, /device:TPU:1, one launch (start us, length us, event | category | flops | bytes accessed | tf_op | source)
XLA Modules:
  0.0 661.7 jit_solution(3964304347088800128)
XLA Ops:
  0.7 0.7 broadcast_in_dim.18
  1.4 2.2 reshape.614
  4.2 0.8 pad_maximum_fusion.4
  6.1 1.1 reduce.10
  7.2 1.7 reshape.738
  8.9 7.1 %all-to-all-start = ((bf16[32,2,5748]{2,1,0:T(2,128)(2,1)}), bf16[32,2,5748]{2,1,0:T(2,128)(2,1)}, u32[]{:S(2)}, u32[]{:S(2)}) async-start(bf16[32,2,5748]{2,1,0:T(2,128)(2,1)} %reshape.738), calls=%async_computation | async-start | bytes 1474560 | tf_op jit(solution)/shard_map/all_to_all | solution.py:1032
  16.1 5.2 fusion.32
  21.3 1.6 collective-permute-start
  25.4 0.8 gather_fusion.6
  26.2 3.1 fusion.27
  29.3 1.2 gather_fusion.7
  30.5 0.8 gather_fusion.4
  31.3 116.6 %gather_first.1 = (bf16[768,2304]{1,0:T(8,128)(2,1)}, bf16[768,768]{1,0:T(8,128)(2,1)}, bf16[768,2304]{1,0:T(8,128)(2,1)}, bf16[768,768]{1,0:T(8,128)(2,1)}) custom-call(bf16[24,2304]{1,0:T(8,128)(2,1)} %refs_0_.3, bf16[24,768]{1,0:T(8,128)(2,1)} %refs_1_.3, bf16[24,2304]{1,0:T(8,128)(2,1)} %refs_2_.1, bf16[24,768]{1,0:T(8,128)(2,1)} %refs_3_.1), custom_call_target="tpu_custom_call" | custom-call | tf_op jit(solution)/shard_map/gather_first/pallas_call | solution.py:752
  148.5 0.7 and_convert_fusion.refs_4_.refs_6_
  149.2 5.1 reshape.739
  156.9 0.8 slice_convert_fusion.1
  158.4 0.8 slice_convert_fusion
  161.6 1.3 all_to_all.38
  162.9 4.0 all-to-all-start.1
  166.9 5.9 pad_maximum_fusion
  172.8 5.3 gather_fusion.2
  179.9 1.4 copy.132
  181.4 51.5 %frame_forward.1 = (bf16[1,16,64,768]{3,2,1,0:T(8,128)(2,1)}, bf16[768,3072]{1,0:T(8,128)(2,1)}, f32[64,32,768]{2,1,0:T(8,128)}, bf16[2048,2304]{1,0:T(8,128)(2,...) custom-call(bf16[4,16,64,768]{3,2,1,0:T(8,128)(2,1)} %refs_0_.5, bf16[24,3072]{1,0:T(8,128)(2,1)} %refs_1_.4, ...), custom_call_target="tpu_custom_call" | custom-call | flops 9663676416 | bytes 33917952 | tf_op jit(solution)/shard_map/frame_forward/pallas_call | solution.py:358
  232.9 50.8 %time_forward.1 = (bf16[2,16,64,768]{3,2,1,0:T(8,128)(2,1)}, bf16[3072,768]{1,0:T(8,128)(2,1)}, f32[64,32,768]{2,1,0:T(8,128)}, bf16[2048,2304]{1,0:T(8,128)(2,1...) custom-call(bf16[4,16,64,768]{3,2,1,0:T(8,128)(2,1)} %refs_0_.5, bf16[96,768]{1,0:T(8,128)(2,1)} %refs_1_.5, ...), custom_call_target="tpu_custom_call" | custom-call | flops 9663676416 | bytes 37096448 | tf_op jit(solution)/shard_map/time_forward/pallas_call | solution.py:358
  283.8 2.2 fusion.33
  286.6 3.2 pad_maximum_fusion.1
  289.8 6.9 %turn_frames.1.dy = f32[64,32,768]{2,1,0:T(8,128)} custom-call(s32[32]{0:T(128)} %get-tuple-element.129.rows_ref, bf16[64,64,768]{2,1,0:T(8,128)(2,1)} %bitcast.128, bf16[64,64,768]{2,1,0:T(8,128)(2,1)} %bitcast.129, bf16[64,64,768]{2,1,0:T(8,128)(2,1)} %bitcast.130, bf16[64,64,768]{2,1,0:T(8,128)(2,1)} %bitcast.131, bf16[64,64,768]{2,1,0:T(8,128)(2,1)} %bitcast.132, ...), custom_call_target="tpu_custom_call" | custom-call | flops 1000 | bytes 56623104 | tf_op jit(solution)/shard_map/turn_frames/pallas_call | solution.py:358
  296.7 97.6 %mlp_both.1 = (bf16[128,64,768]{2,1,0:T(8,128)(2,1)}, f32[64,32,768]{2,1,0:T(8,128)}, f32[768,3072]{1,0:T(8,128)}, f32[3072,768]{1,0:T(8,128)}, f32[1,3072]{1,0:...) custom-call(f32[64,32,768]{2,1,0:T(8,128)} %get-tuple-element.76.x2, f32[64,32,768]{2,1,0:T(8,128)} %turn_frames.1.dy, ...), custom_call_target="tpu_custom_call" | custom-call | flops 57982058496 | bytes 60979200 | tf_op jit(solution)/shard_map/mlp_both/pallas_call | solution.py:358
  394.3 82.0 %time_back.1 = (bf16[128,64,768]{2,1,0:T(8,128)(2,1)}, f32[24,1536]{1,0:T(8,128)}, f32[96,384]{1,0:T(8,128)}, f32[24,1536]{1,0:T(8,128)}, f32[96,384]{1,0:T(8,12...) custom-call(bf16[128,64,768]{2,1,0:T(8,128)(2,1)} %get-tuple-element, ...), custom_call_target="tpu_custom_call", output_to_operand_aliasing={{0}: (0, {})} | custom-call | flops 19327352832 | bytes 53120000 | tf_op jit(solution)/shard_map/time_back/pallas_call | solution.py:358
  476.3 63.8 %frame_back.1 = (bf16[128,64,768]{2,1,0:T(8,128)(2,1)}, bf16[128,64,768]{2,1,0:T(8,128)(2,1)}, f32[24,768]{1,0:T(8,128)}, f32[24,768]{1,0:T(8,128)}, f32[24,768]...) custom-call(bf16[128,64,768]{2,1,0:T(8,128)(2,1)} %get-tuple-element, ...), custom_call_target="tpu_custom_call", output_to_operand_aliasing={{0}: (0, {})} | custom-call | flops 19327352832 | bytes 43650048 | tf_op jit(solution)/shard_map/frame_back/pallas_call | solution.py:358
  540.2 1.0 maximum_bitcast_fusion
  542.5 1.3 reduce.11
  543.9 0.8 reshape.740
  544.7 3.6 all-to-all-start.2
  549.9 6.2 all-to-all-done.2
  556.2 0.7 reduce.2
  557.6 0.8 convert_reduce_fusion
  559.4 1.2 reshape.628
  560.5 1.5 concatenate.58
  562.1 2.1 all_to_all.35
  564.2 3.3 all-to-all-start.3
  569.3 8.8 %unpack_frames.2 = bf16[64,64,768]{2,1,0:T(8,128)(2,1)} custom-call(s32[64]{0:T(128)} %select_n.185.rows_ref, bf16[128,64,768]{2,1,0:T(8,128)(2,1)} %get-tuple-element.94.refs_0_.refs_1_.refs_2_.refs_3_.refs_4_.refs_5_.refs_6_.refs_7_, bf16[128,64,768]{2,1,0:T(8,128)(2,1)} %get-tuple-element.94.refs_0_.refs_1_.refs_2_.refs_3_.refs_4_.refs_5_.refs_6_.refs_7_, ...), custom_call_target="tpu_custom_call" | custom-call | flops 1000 | bytes 12582912 | tf_op jit(solution)/shard_map/unpack_frames/pallas_call | solution.py:557
  578.0 64.4 %scatter_last.1 = (bf16[128,64,768]{2,1,0:T(8,128)(2,1)}, f32[24,3072]{1,0:T(8,128)}, f32[96,768]{1,0:T(8,128)}, f32[24,2304]{1,0:T(8,128)}, f32[24,768]{1,0:T(8...) custom-call(bf16[128,64,768]{2,1,0:T(8,128)(2,1)} %get-tuple-element, ...), custom_call_target="tpu_custom_call", output_to_operand_aliasing={{0}: (0, {})} | custom-call | tf_op jit(solution)/shard_map/scatter_last/pallas_call | solution.py:1003
  642.4 8.9 %unpack_frames.3 = bf16[64,64,768]{2,1,0:T(8,128)(2,1)} custom-call(s32[64]{0:T(128)} %select_n.185.rows_ref, bf16[128,64,768]{2,1,0:T(8,128)(2,1)} %get-tuple-element.113.refs_0_.refs_1_.refs_2_.refs_3_.refs_4_.refs_5_.refs_6_.refs_7_, bf16[128,64,768]{2,1,0:T(8,128)(2,1)} %get-tuple-element.113.refs_0_.refs_1_.refs_2_.refs_3_.refs_4_.refs_5_.refs_6_.refs_7_, ...), custom_call_target="tpu_custom_call" | custom-call | flops 1000 | bytes 12582912 | tf_op jit(solution)/shard_map/unpack_frames/pallas_call | solution.py:557
  651.4 1.5 copy.131
  656.1 1.3 reshape.636
  660.0 0.7 copy.151
  660.8 0.7 copy.152
  (168 shorter events, 24.7 us)
Async XLA Ops:
  0.6 23.6 %copy-start = (s32[16,16]{1,0:T(8,128)S(1)}, s32[16,16]{1,0:T(8,128)}, u32[]{:S(2)}) copy-start(s32[16,16]{1,0:T(8,128)} %param.20) | copy-start | bytes 3076
  8.9 140.3 %all-to-all-start = ((bf16[32,2,5748]{2,1,0:T(2,128)(2,1)}), bf16[32,2,5748]{2,1,0:T(2,128)(2,1)}, u32[]{:S(2)}, u32[]{:S(2)}) async-start(bf16[32,2,5748]{2,1,0:T(2,128)(2,1)} %reshape.738), calls=%async_computation | async-start | bytes 1474560 | tf_op jit(solution)/shard_map/all_to_all | solution.py:1032
  16.1 7.1 %copy-start.25 = (bf16[216]{0:T(256)(128)(2,1)S(1)}, bf16[216]{0:T(256)(128)(2,1)}, u32[]{:S(2)}) copy-start(bf16[216]{0:T(256)(128)(2,1)} %param.22) | copy-start | bytes 1300
  16.1 7.1 %copy-start.24 = (s32[16]{0:T(128)S(1)}, s32[16]{0:T(128)}, u32[]{:S(2)}) copy-start(s32[16]{0:T(128)} %param.19) | copy-start | bytes 196
  21.3 145.6 %collective-permute-start = (bf16[16,64,768]{2,1,0:T(8,128)(2,1)}, bf16[16,64,768]{2,1,0:T(8,128)(2,1)}, u32[]{:S(2)}, u32[]{:S(2)}) collective-permute-start(bf16[16,64,768]{2,1,0:T(8,128)(2,1)} %get-tuple-element.132), channel_id=1, source_target_pairs={{0,1},{1,2},{2,3},{3,0},{4,5},{5,6},{6,7},{7,4},{8,9},{9,10},{10,1... | collective-permute-start | bytes 4718600 | tf_op jit(solution)/shard_map/ppermute | solution.py:1040
  22.9 144.0 %collective-permute-start.2 = (bf16[16,64,768]{2,1,0:T(8,128)(2,1)}, bf16[16,64,768]{2,1,0:T(8,128)(2,1)}, u32[]{:S(2)}, u32[]{:S(2)}) collective-permute-start(bf16[16,64,768]{2,1,0:T(8,128)(2,1)} %get-tuple-element.133), channel_id=1, source_target_pairs={{0,3},{1,0},{2,1},{3,2},{4,7},{5,4},{6,5},{7,6},{8,11},{9,8},{10,9... | collective-permute-start | bytes 4718600 | tf_op jit(solution)/shard_map/ppermute | solution.py:1040
  22.9 144.0 %collective-permute-start.1 = (bf16[16,64,768]{2,1,0:T(8,128)(2,1)}, bf16[16,64,768]{2,1,0:T(8,128)(2,1)}, u32[]{:S(2)}, u32[]{:S(2)}) collective-permute-start(bf16[16,64,768]{2,1,0:T(8,128)(2,1)} %get-tuple-element.134), channel_id=1, source_target_pairs={{0,2},{1,3},{2,0},{3,1},{4,6},{5,7},{6,4},{7,5},{8,10},{9,11},{10,... | collective-permute-start | bytes 4718600 | tf_op jit(solution)/shard_map/ppermute | solution.py:1040
  23.3 131.0 %copy-start.2 = (s32[4,4]{1,0:T(4,128)}, s32[4,4]{1,0:T(4,128)S(1)}, u32[]{:S(2)}) copy-start(s32[4,4]{1,0:T(4,128)S(1)} %reshape.610) | copy-start | bytes 196
  154.4 0.9 copy-start.8
  155.5 17.3 %copy-start.4 = (bf16[256,768]{1,0:T(8,128)(2,1)}, bf16[256,768]{1,0:T(8,128)(2,1)S(1)}, u32[]{:S(2)}) copy-start(bf16[256,768]{1,0:T(8,128)(2,1)S(1)} %convert_element_type.58) | copy-start | bytes 1179652
  156.2 16.6 %copy-start.6 = (bf16[768,216]{1,0:T(8,128)(2,1)}, bf16[768,216]{1,0:T(8,128)(2,1)S(1)}, u32[]{:S(2)}) copy-start(bf16[768,216]{1,0:T(8,128)(2,1)S(1)} %reshape.616) | copy-start | bytes 995332
  162.9 15.3 %all-to-all-start.1 = ((f32[32,1,1728]{2,1,0:T(1,128)}), f32[32,1,1728]{2,1,0:T(1,128)S(1)}, u32[]{:S(2)}, u32[]{:S(2)}) async-start(f32[32,1,1728]{2,1,0:T(1,128)} %all_to_all.38), calls=%async_computation.1 | async-start | bytes 458752 | tf_op jit(solution)/shard_map/all_to_all | solution.py:1032
  283.8 2.4 slice-start
  283.8 2.8 copy-start.9
  476.2 63.9 %copy-start.10 = (f32[3,32,768]{2,1,0:T(8,128)S(1)}, f32[3,32,768]{2,1,0:T(8,128)}, u32[]{:S(2)}) copy-start(f32[3,32,768]{2,1,0:T(8,128)} %get-tuple-element.116) | copy-start | bytes 884740
  476.3 63.9 %copy-start.11 = (f32[3,32,768]{2,1,0:T(8,128)S(1)}, f32[3,32,768]{2,1,0:T(8,128)}, u32[]{:S(2)}) copy-start(f32[3,32,768]{2,1,0:T(8,128)} %get-tuple-element.115) | copy-start | bytes 884740
  540.1 1.2 copy-start.23
  540.1 8.1 %copy-start.22 = (f32[1,768]{1,0:T(1,128)S(1)}, f32[1,768]{1,0:T(1,128)}, u32[]{:S(2)}) copy-start(f32[1,768]{1,0:T(1,128)} %get-tuple-element.117) | copy-start | bytes 9220
  540.1 8.1 %copy-start.21 = (f32[1,768]{1,0:T(1,128)S(1)}, f32[1,768]{1,0:T(1,128)}, u32[]{:S(2)}) copy-start(f32[1,768]{1,0:T(1,128)} %get-tuple-element.118) | copy-start | bytes 9220
  540.1 8.2 %copy-start.20 = (f32[1,768]{1,0:T(1,128)S(1)}, f32[1,768]{1,0:T(1,128)}, u32[]{:S(2)}) copy-start(f32[1,768]{1,0:T(1,128)} %get-tuple-element.120) | copy-start | bytes 9220
  540.2 8.7 %copy-start.19 = (f32[1,3072]{1,0:T(1,128)S(1)}, f32[1,3072]{1,0:T(1,128)}, u32[]{:S(2)}) copy-start(f32[1,3072]{1,0:T(1,128)} %get-tuple-element.119) | copy-start | bytes 36868
  541.2 17.4 %copy-start.7 = (bf16[768,216]{1,0:T(8,128)(2,1)S(1)}, bf16[768,216]{1,0:T(8,128)(2,1)}, u32[]{:S(2)}) copy-start(bf16[768,216]{1,0:T(8,128)(2,1)} %copy-done.6) | copy-start | bytes 995332
  541.3 17.6 %copy-start.5 = (bf16[256,768]{1,0:T(8,128)(2,1)S(1)}, bf16[256,768]{1,0:T(8,128)(2,1)}, u32[]{:S(2)}) copy-start(bf16[256,768]{1,0:T(8,128)(2,1)} %copy-done.4) | copy-start | bytes 1179652
  544.7 11.4 %all-to-all-start.2 = ((bf16[32,2,864]{2,1,0:T(2,128)(2,1)}), bf16[32,2,864]{2,1,0:T(2,128)(2,1)S(1)}, u32[]{:S(2)}, u32[]{:S(2)}) async-start(bf16[32,2,864]{2,1,0:T(2,128)(2,1)} %reshape.740), calls=%async_computation.2 | async-start | bytes 229376 | tf_op jit(solution)/shard_map/all_to_all | solution.py:1032
  562.1 5.6 copy-start.3
  564.2 87.2 %all-to-all-start.3 = ((f32[32,1,11496]{2,1,0:T(1,128)}), f32[32,1,11496]{2,1,0:T(1,128)}, u32[]{:S(2)}, u32[]{:S(2)}) async-start(f32[32,1,11496]{2,1,0:T(1,128)} %all_to_all.35), calls=%async_computation.3 | async-start | bytes 2949120 | tf_op jit(solution)/shard_map/all_to_all | solution.py:1032
  651.4 3.2 copy-start.18
  654.4 3.0 copy-start.15
  654.4 3.7 copy-start.17
  654.4 4.3 copy-start.14
  654.5 4.9 copy-start.16
  654.5 5.6 copy-start.13
  654.5 6.2 copy-start.12
  654.5 6.9 %copy-start.1 = (s32[16,16]{1,0:T(8,128)S(1)}, s32[16,16]{1,0:T(8,128)}, u32[]{:S(2)}) copy-start(s32[16,16]{1,0:T(8,128)} %param.20) | copy-start | bytes 3076

commit v7 on v6

--- a/solution.py
+++ b/solution.py
@@ -26,7 +26,7 @@
 PT = TILE // LIVE
 GRID = LIVE * PATCHES // TILE
 GROUPS = TILE // 64
-EARLY_TILES = GRID // 2
+EARLY_TILES = GRID - 1
 GELU_C = 0.7978845608028654
 GELU_A = 0.044715
 VMEM_LIMIT = 66 * 1000 * 1000
@@ -366,14 +366,14 @@
     return parts + [refs]
 
 
-def forward_carrier(clips, js, shard, ring, n, number):
+def forward_carrier(clips, js, shard, far, ring, n, number):
     held = Gather.scratch([shard], ring)
 
     def wrap(kernel, n_in, n_out, n_scratch, *refs):
-        (src, part), ins, (dst, full), outs, scratch, (send_sem, recv_sem), own = split_refs(
-            refs, 2, n_in, 2, n_out, n_scratch, 2)
+        (src, part, other), ins, (dst, full), outs, scratch, (send_sem, recv_sem), own = split_refs(
+            refs, 3, n_in, 2, n_out, n_scratch, 2)
         step = pl.program_id(0)
-        gather = Gather(ring, (shard.shape[0],), (part, full) + own)
+        gather = Gather(ring, (shard.shape[0],), (part, other, full) + own)
         targets = [(gather.w, (gather.k + j) % n) for j in js]
         copies = [send(src.at[j], dst.at[i], send_sem.at[i], recv_sem.at[i], targets[i]) for i, j in enumerate(js)]
 
@@ -405,7 +405,7 @@
                 copy.wait()
 
     sems = pltpu.SemaphoreType.DMA((len(js),))
-    return Carrier(wrap, number, [clips, shard],
+    return Carrier(wrap, number, [clips, shard, far],
                    [shape_of((len(js),) + clips.shape[1:], clips.dtype)] + Gather.shapes([shard], ring * n),
                    [ANY, ANY], [sems, sems] + held)
 
@@ -649,18 +649,19 @@
     def __init__(self, ring, heights, refs):
         count = len(heights)
         self.ring, self.heights, self.count = ring, heights, count
-        self.shards, self.full, self.bufs, sems = split_refs(refs, count, count, count)
-        (self.ring_s, self.ring_r, self.core_s, self.core_r, self.x_s, self.x_r, self.load_sem, self.keep_sem) = sems
+        near, far, self.full, near_bufs, far_bufs, sems = split_refs(refs, count, count, count, count, count)
+        self.shards, self.bufs = (near, far), (near_bufs, far_bufs)
+        (self.ring_s, self.ring_r, self.core_s, self.core_r, self.load_sem, self.keep_sem) = sems
         self.w, self.k, self.r, self.x, self.c, self.wide_at = place_of(ring)
-        self.other_x = (self.w, 2 * (1 - self.x) + self.c)
         self.other_c = (self.w, 2 * self.x + 1 - self.c)
         self.next = ((self.wide_at((self.r + 1) % ring), self.k), (self.wide_at((self.r + ring - 1) % ring), self.k))
-        self.peers = self.next + (self.other_x, self.other_c)
+        self.peers = self.next + (self.other_c,)
 
     @staticmethod
     def scratch(shards, ring):
         count, sems = len(shards), pltpu.SemaphoreType.DMA
-        return ([pltpu.VMEM(a.shape, a.dtype) for a in shards] + [sems((count, 2, ring))] * 4 + [sems((count,))] * 4)
+        bufs = [pltpu.VMEM(a.shape, a.dtype) for a in shards]
+        return bufs + bufs + [sems((count, 2, ring))] * 4 + [sems((count, 2))] * 2
 
     @staticmethod
     def shapes(shards, devices):
@@ -685,31 +686,26 @@
         dst = self.block(t, b, s)
         return send(dst if src is None else src, dst, self.core_s.at[t, b, s], self.core_r.at[t, b, s], self.other_c)
 
-    def x_copy(self, t):
-        return send(self.shards[t], self.block(t, 0, 0), self.x_s.at[t], self.x_r.at[t], self.other_x)
-
-    def load(self, t):
-        return pltpu.make_async_copy(self.shards[t], self.bufs[t], self.load_sem.at[t])
-
-    def keep(self, t):
-        return pltpu.make_async_copy(self.bufs[t], self.block(t, 0, 0), self.keep_sem.at[t])
+    def load(self, t, b):
+        return pltpu.make_async_copy(self.shards[b][t], self.bufs[b][t], self.load_sem.at[t, b])
+
+    def keep(self, t, b):
+        return pltpu.make_async_copy(self.bufs[b][t], self.block(t, b, 0), self.keep_sem.at[t, b])
+
+    def each(self):
+        return [(t, b) for b in range(2) for t in range(self.count)]
 
     def begin(self):
-        for t in range(self.count):
-            self.x_copy(t).start()
-            self.ring_copy(t, 0, 0, self.shards[t]).start()
-        for t in range(self.count):
-            self.core_copy(t, 0, 0, self.shards[t]).start()
-            self.load(t).start()
+        for t, b in self.each():
+            self.ring_copy(t, b, 0, self.shards[b][t]).start()
+        for t, b in self.each():
+            self.core_copy(t, b, 0, self.shards[b][t]).start()
+            self.load(t, b).start()
 
     def second(self):
-        for t in range(self.count):
-            self.load(t).wait()
-            self.keep(t).start()
-        for t in range(self.count):
-            self.x_copy(t).wait_recv()
-            self.ring_copy(t, 1, 0).start()
-            self.core_copy(t, 1, 0).start()
+        for t, b in self.each():
+            self.load(t, b).wait()
+            self.keep(t, b).start()
 
     def hop(self, s):
         for b in range(2):
@@ -723,14 +719,12 @@
                 self.core_copy(t, b, s).start()
 
     def finish(self):
-        for t in range(self.count):
-            self.keep(t).wait()
-            self.x_copy(t).wait_send()
-            for b in range(2):
-                for s in range(self.ring):
-                    if s < self.ring - 1:
-                        self.ring_copy(t, b, s).wait_send()
-                    self.core_copy(t, b, s).wait()
+        for t, b in self.each():
+            self.keep(t, b).wait()
+            for s in range(self.ring):
+                if s < self.ring - 1:
+                    self.ring_copy(t, b, s).wait_send()
+                self.core_copy(t, b, s).wait()
 
 
 def gather_kernel(ring, heights, *refs):
@@ -747,17 +741,17 @@
     gather.finish()
 
 
-def gather_first(shards, ring, n):
+def gather_first(shards, far, ring, n):
     heights = tuple(a.shape[0] for a in shards)
     return pl.pallas_call(
         functools.partial(gather_kernel, ring, heights),
         name="gather_first",
         out_shape=Gather.shapes(shards, ring * n),
-        in_specs=[ANY] * len(shards),
+        in_specs=[ANY] * (2 * len(shards)),
         out_specs=[ANY] * len(shards),
         scratch_shapes=Gather.scratch(shards, ring),
         compiler_params=pltpu.CompilerParams(collective_id=0, has_side_effects=True),
-    )(*shards)
+    )(*shards, *far)
 
 
 def put(outs, places, value):
@@ -893,8 +887,8 @@
 
 
 class Plan:
-    def __init__(self, ring, inputs, pieces, shapes, places, leave):
-        self.ring, self.inputs, self.pieces, self.shapes, self.places = ring, inputs, pieces, shapes, places
+    def __init__(self, ring, inputs, pieces, places, leave, shapes=()):
+        self.ring, self.inputs, self.pieces, self.places = ring, inputs, pieces, places
         count = len(pieces)
         sizes = [(height, width) for _, _, width, height, _ in pieces]
         sems, vmem = pltpu.SemaphoreType.DMA, pltpu.VMEM
@@ -928,49 +922,63 @@
         return Sums(self, refs)
 
 
-def mlp_plan(ring, g_in, g_out, devices):
+def time_plan(ring, g_in, g_out, devices):
     a, b = g_in.shape[0] // devices, g_out.shape[0] // devices
-    wa, wb = g_in.shape[1] // 2, g_out.shape[1] // 2
+    wa, wb = g_in.shape[1] // 3, g_out.shape[1] // 3
     return Plan(ring, 2, [(0, 0, wa, a, 0), (1, 0, wb, b, 1), (0, wa, wa, a, 0), (1, wb, wb, b, 1)],
-                [(a, 2 * wa), (b, 2 * wb)], [[(0, 0, 0, wa)], [(1, 0, 0, wb)], [(0, wa, 0, wa)], [(1, wb, 0, wb)]], True)
-
-
-def attn_plan(ring, g, devices, leave):
-    h = g.shape[0] // devices
-    return Plan(ring, 1, [(0, i * D, D, h, i % 2) for i in range(4)], [(h, 3 * D), (h, D)],
-                [[(0, i * D, 0, D)] for i in range(3)] + [[(1, 0, 0, D)]], leave)
-
-
-def last_kernel(plan, left, shapes, *refs):
+                [[(0, 0, 0, wa)], [(1, 0, 0, wb)], [(0, wa, 0, wa)], [(1, wb, 0, wb)]], True)
+
+
+def attn_pieces(g, number, devices):
+    return [(number, i * D, D, g.shape[0] // devices, i % 2) for i in range(4)]
+
+
+def attn_places(first):
+    return [[(first, i * D, 0, D)] for i in range(3)] + [[(first + 1, 0, 0, D)]]
+
+
+def frame_plan(ring, g_t, g_in, g_out, devices):
+    a, b = g_in.shape[0] // devices, g_out.shape[0] // devices
+    wa, wb = g_in.shape[1] // 3, g_out.shape[1] // 3
+    return Plan(ring, 3, attn_pieces(g_t, 0, devices) + [(1, 2 * wa, wa, a, 0), (2, 2 * wb, wb, b, 1)],
+                attn_places(2) + [[(0, 2 * wa, 0, wa)], [(1, 2 * wb, 0, wb)]], True)
+
+
+def last_plan(ring, g_s, devices):
+    return Plan(ring, 1, attn_pieces(g_s, 0, devices), attn_places(0), False, attn_shapes(g_s, devices))
+
+
+def attn_shapes(g, devices):
+    return [(g.shape[0] // devices, 3 * D), (g.shape[0] // devices, D)]
+
+
+def last_kernel(plan, left, made, *refs):
     places = [part for p in left for part in p.places]
-    offsets = [sum(len(p.shapes) for p in left[:i]) for i, p in enumerate(left) for _ in p.pieces]
-    count, made = len(places), sum(len(p.shapes) for p in left)
+    count = len(places)
     ((_,), grads, keeps, fins, (frames,), left_outs, own_outs, fins_r,
-     (fin_send, fin_recv, tile_s, tile_r, relay_s, relay_r), own) = split_refs(
-        refs, 1, plan.inputs, count, count, 1, made, plan.outputs, count, 6)
+     (fin_send, fin_recv, send_sem, recv_sem), own) = split_refs(
+        refs, 1, plan.inputs, count, count, 1, made, plan.outputs, count, 4)
     sums = plan.steps(grads + own_outs + own)
-    late_tiles = range(EARLY_TILES, GRID)
-    tile = {i: tile_copies(sums.k, sums.other_c, sums.other_x, frames.at[packed(0, i * FT, FT)], frames, i, tile_s, tile_r)
-            for i in late_tiles}
+    early, late = EARLY_TILES * FT, LIVE - EARLY_TILES * FT
+    mine, theirs = slot_for(sums.k), 4 - slot_for(sums.k)
+    moves = (
+        (packed(0, early, late), packed(2, early, late), sums.other_x),
+        (packed(0, early, late), packed(mine, early, late), sums.other_c),
+        (packed(2, 0, early), packed(theirs, 0, early), sums.other_c),
+        (packed(2, early, late), packed(theirs, early, late), sums.other_c),
+    )
+    copies = [send(frames.at[src], frames.at[dst], send_sem.at[i], recv_sem.at[i], peer)
+              for i, (src, dst, peer) in enumerate(moves)]
 
     def fin_copy(t):
         return send(fins[t], fins_r[t], fin_send.at[t], fin_recv.at[t], sums.other_x)
 
-    def relay(i, first, frames_count):
-        return send(frames.at[packed(2, first, frames_count)],
-                    frames.at[packed(4 - slot_for(sums.k), first, frames_count)],
-                    relay_s.at[i], relay_r.at[i], sums.other_c)
-
-    early = relay(0, 0, EARLY_TILES * FT)
-    late = {i: relay(i, i * FT, FT) for i in late_tiles}
     greet(sums.peers)
     sums.begin()
-    for i in late_tiles:
-        for copy in tile[i]:
-            copy.start()
+    for copy in copies[:3]:
+        copy.start()
     for t in range(count):
         fin_copy(t).start()
-    early.start()
     sums.load_first()
     sums.first_hop()
 
@@ -979,35 +987,31 @@
         return carry
 
     lax.fori_loop(1, sums.final, body, 0)
+    copies[0].wait_recv()
+    copies[3].start()
     sums.finish()
-    for i in late_tiles:
-        tile[i][1].wait_recv()
-        late[i].start()
     for t in range(count):
         fin_copy(t).wait_recv()
         value = keeps[t][...] + fins_r[t][...].astype(F32)
-        put(left_outs[offsets[t] :], places[t], value)
+        put(left_outs, places[t], value)
     for t in range(count):
         fin_copy(t).wait_send()
-    early.wait()
-    for i in late_tiles:
-        tile[i][0].wait()
-        tile[i][1].wait_send()
-        late[i].wait()
-
-
-def scatter_last(frames, g, keeps, fins, plan, left):
-    shapes = [shape for p in left for shape in p.shapes]
+    copies[0].wait_send()
+    for copy in copies[1:]:
+        copy.wait()
+
+
+def scatter_last(frames, g, keeps, fins, plan, left, shapes):
     sems = pltpu.SemaphoreType.DMA
     vmem = pl.BlockSpec(memory_space=pltpu.VMEM)
     return pl.pallas_call(
-        functools.partial(last_kernel, plan, left, shapes),
+        functools.partial(last_kernel, plan, left, len(shapes)),
         name="scatter_last",
         out_shape=[shape_of(frames.shape, frames.dtype)] + [shape_of(hw, F32) for hw in shapes] + plan.out_shapes,
         in_specs=[ANY] * 2 + [vmem] * len(keeps) + [ANY] * len(fins),
         out_specs=[ANY] + [vmem] * len(shapes) + plan.out_specs,
         scratch_shapes=[pltpu.VMEM(f.shape, f.dtype) for f in fins]
-        + [sems((len(fins),))] * 2 + [sems((2, GRID))] * 2 + [sems((GRID,))] * 2 + plan.scratch,
+        + [sems((len(fins),))] * 2 + [sems((4,))] * 2 + plan.scratch,
         input_output_aliases={0: 0},
         compiler_params=pltpu.CompilerParams(
             collective_id=1, has_side_effects=True, vmem_limit_bytes=VMEM_LIMIT
@@ -1073,10 +1077,20 @@
     def gather(w):
         return lax.all_gather(w, ALL, axis=0, tiled=True)
 
-    frames = shift_clips(clips, False)
+    def across(value):
+        return lax.ppermute(value, "narrow", [(k, (k + n // 2) % n) for k in range(n)])
+
     if fast:
-        wqkv_s, wo_s, wqkv_t, wo_t = gather_first((w_qkv_s, w_o_s, w_qkv_t, w_o_t), wide, n)
+        flat = (w_qkv_s, w_o_s, w_qkv_t, w_o_t, w_in)
+        far, far_out = across(jnp.concatenate(flat, axis=1)), across(w_out)
+        clips, far, far_out = lax.optimization_barrier((clips, far, far_out))
+        cuts = [sum(a.shape[1] for a in flat[: i + 1]) for i in range(len(flat) - 1)]
+        *far_attn, far_in = jnp.split(far, cuts, axis=1)
+        frames = shift_clips(clips, False)
+        wqkv_s, wo_s, wqkv_t, wo_t = gather_first(flat[:4], far_attn, wide, n)
     else:
+        far_in = far_out = None
+        frames = shift_clips(clips, False)
         win, wout, wqkv_t, wo_t, wqkv_s, wo_s = [gather(w) for w in (w_in, w_out, w_qkv_t, w_o_t, w_qkv_s, w_o_s)]
     frames = jnp.take(frames.reshape(n * FR, PATCHES, D), pack_rows, axis=0, mode="clip")
 
@@ -1102,13 +1116,13 @@
     mod_rows = jnp.swapaxes(mod_rows, 0, 1).reshape(2 * n, 9, D)
     mod = jnp.swapaxes(mod_rows[row_choice], 0, 1)
 
-    def carry(js, shard, number):
-        return forward_carrier(cotangent, js, shard, wide, n, number) if fast else None
+    def carry(js, shard, other, number):
+        return forward_carrier(cotangent, js, shard, other, wide, n, number) if fast else None
 
     *half, x1, qkv1, o1, a1 = run_frame_forward(
-        frames, mod, wqkv_s, wo_s, bias_s, carry((2,), w_in, 2))
+        frames, mod, wqkv_s, wo_s, bias_s, carry((2,), w_in, far_in, 2))
     *odd, x2, qkv2, o2, a2 = run_time_forward(
-        x1, mod, seg, wqkv_t, wo_t, bias_t, carry((1, 3), w_out, 3))
+        x1, mod, seg, wqkv_t, wo_t, bias_t, carry((1, 3), w_out, far_out, 3))
     if fast:
         (half, win), (odd, wout) = half, odd
         cots = jnp.stack([cotangent[0], odd[0], half[0], odd[1]])
@@ -1134,17 +1148,17 @@
         own_start = jnp.sum(jnp.where(slots[None, :] < slots[:, None], ahead, 0), axis=1)
         own_rows = slots[:, None] * LIVE + own_start[:, None] + frame_ids[None, :]
         own_rows = jnp.where(own_live, own_rows, -1).reshape(-1)
-        plan_mlp = mlp_plan(wide, g_in, g_out, devices)
+        plan_a = time_plan(wide, g_in, g_out, devices)
         out, *got, dx1, g_t, gb_t, dmod2 = run_time_back(
-            x1, dx2, mod, seg, qkv2, o2, a2, wqkv_t, wo_t, share_carrier(out, [g_in, g_out], plan_mlp, 4))
-        keeps, fins = plan_mlp.left(got)
-        plan_t = attn_plan(wide, g_t, devices, True)
+            x1, dx2, mod, seg, qkv2, o2, a2, wqkv_t, wo_t, share_carrier(out, [g_in, g_out], plan_a, 4))
+        keeps, fins = plan_a.left(got)
+        plan_b = frame_plan(wide, g_t, g_in, g_out, devices)
         out, dx0, *got, g_s, gb_s, dmod1 = run_frame_back(
-            frames, dx1, mod, qkv1, o1, a1, wqkv_s, wo_s, relay_carrier(out, [g_t], plan_t, 5))
-        more_keeps, more_fins = plan_t.left(got)
-        keeps, fins = keeps + more_keeps, fins + more_fins
+            frames, dx1, mod, qkv1, o1, a1, wqkv_s, wo_s, relay_carrier(out, [g_t, g_in, g_out], plan_b, 5))
+        more_keeps, more_fins = plan_b.left(got)
         dx0, s_in, s_out, s_qkv_t, s_o_t, s_qkv_s, s_o_s = scatter_last(
-            dx0, g_s, keeps, fins, attn_plan(wide, g_s, devices, False), (plan_mlp, plan_t))[:7]
+            dx0, g_s, keeps + more_keeps, fins + more_fins, last_plan(wide, g_s, devices), (plan_a, plan_b),
+            [w_in.shape, w_out.shape] + attn_shapes(g_t, devices))[:7]
         layer_out = run_unpack(out, own_rows).reshape(n, FR, PATCHES, D)
         grad_clips = run_unpack(dx0, own_rows).reshape(n, FR, PATCHES, D)
     else:

time: 665 us -> 614 us (0.923)
  Pallas kernels: 551 us -> 475 us
  waiting for transfers between devices: 6.18 us -> 20 us
    pallas_call x1, Pallas kernels: 117 us -> 52.2 us  [gather_first(): pl.pallas_call(functools.partial(gather_kernel, ring, heights), name='gat...]
    pallas_call x1, Pallas kernels: 64.4 us -> 54.2 us  [scatter_last(): pl.pallas_call(functools.partial(last_kernel, plan, left, len(shapes)), n...]
    ppermute x0 -> x2, waiting for transfers between devices: none -> 8.53 us  [across(): lax.ppermute(value, 'narrow', [(k, (k + n // 2) % n) for k in range(n)])]
    unnamed x66 -> x82, local copies, waits for them, and re-layouts: 14.8 us -> 14.9 us
  transfers between devices with their start and end apart: 7 -> 9, of which waited for: 1 -> 3; matrix products, arithmetic and copies ran while one was open for 6% -> 7% of each run, Pallas kernels for 30% -> 20%
where the time goes in v7:
time: 614 us; the launch traced here: 605 us
  Pallas kernels  475 us (77%)
  local copies, waits for them, and re-layouts  58.8 us (10%)
  other arithmetic  24.2 us (4%)
  starting transfers between devices  23.5 us (4%)
  waiting for transfers between devices  20 us (3%)
    pallas_call x6, Pallas kernels, call(): return fn(*ins) if prefetch is None else fn(prefetch, *ins)  353 us
    pallas_call x1, Pallas kernels, scatter_last(): pl.pallas_call(functools.partial(last_kernel, plan, left, len(shapes)), n...  54.2 us
    pallas_call x1, Pallas kernels, gather_first(): pl.pallas_call(functools.partial(gather_kernel, ring, heights), name='gat...  52.2 us
    all_to_all x4, starting transfers between devices, exchange(): return lax.all_to_all(x, ALL, split_axis=0, concat_axis=0, tiled=True)  17.3 us
    pallas_call x2, Pallas kernels, run_unpack(): pl.pallas_call(unpack_frames, grid_spec=pltpu.PrefetchScalarGridSpec(num_...  16 us
    unnamed x82, local copies, waits for them, and re-layouts  14.9 us
  transfers between devices with their start and end apart: 9, of which 3 were waited for; matrix products, arithmetic and copies ran while one was open for 7% of the time, Pallas kernels for 20%

profile of v7, /device:TPU:1, one launch (start us, length us, event | category | flops | bytes accessed | tf_op | source)
XLA Modules:
  0.0 605.2 jit_solution(12355877702076554314)
XLA Ops:
  0.7 2.1 collective-permute-start.1
  3.5 2.2 reshape.614
  6.3 0.8 pad_maximum_fusion.4
  8.2 1.1 reduce.10
  9.2 1.7 reshape.738
  11.0 5.7 all-to-all-start
  16.8 1.4 collective-permute-start
  20.5 3.1 fusion.27
  23.6 1.2 gather_fusion.7
  24.8 0.8 gather_fusion.6
  25.6 0.8 gather_fusion.4
  27.6 8.5 %collective-permute-done = bf16[24,9216]{1,0:T(8,128)(2,1)S(1)} collective-permute-done((bf16[24,9216]{1,0:T(8,128)(2,1)S(1)}, bf16[24,9216]{1,0:T(8,128)(2,1)S(1)}, u32[]{:S(2)}, u32[]{:S(2)}) %collective-permute-start) | collective-permute-done | bytes 442400 | tf_op jit(solution)/shard_map/ppermute | solution.py:1081
  36.8 5.2 fusion.32
  42.0 1.0 collective-permute-start.4
  43.1 1.6 collective-permute-start.2
  46.0 52.2 %gather_first.1 = (bf16[768,2304]{1,0:T(8,128)(2,1)}, bf16[768,768]{1,0:T(8,128)(2,1)}, bf16[768,2304]{1,0:T(8,128)(2,1)}, bf16[768,768]{1,0:T(8,128)(2,1)}) custom-call(bf16[24,2304]{1,0:T(8,128)(2,1)} %refs_0_.3, bf16[24,768]{1,0:T(8,128)(2,1)} %refs_1_.3, bf16[24,2304]{1,0:T(8,128)(2,1)} %refs_2_.1, bf16[24,768]{1,0:T(8,128)(2,1)} %refs_3_.1, ...), custom_call_target="tpu_custom_call" | custom-call | tf_op jit(solution)/shard_map/gather_first/pallas_call | solution.py:746
  98.2 5.1 reshape.739
  106.3 1.3 all_to_all.38
  107.6 4.4 all-to-all-start.1
  112.0 0.8 slice_convert_fusion.1
  113.5 0.8 slice_convert_fusion
  116.3 5.3 all-to-all-done.1
  123.4 1.4 copy.132
  124.9 5.9 pad_maximum_fusion
  130.7 5.3 gather_fusion.2
  136.1 43.0 %frame_forward.1 = (bf16[1,16,64,768]{3,2,1,0:T(8,128)(2,1)}, bf16[768,3072]{1,0:T(8,128)(2,1)}, f32[64,32,768]{2,1,0:T(8,128)}, bf16[2048,2304]{1,0:T(8,128)(2,...) custom-call(bf16[4,16,64,768]{3,2,1,0:T(8,128)(2,1)} %refs_0_.5, bf16[24,3072]{1,0:T(8,128)(2,1)} %refs_1_.4, ...), custom_call_target="tpu_custom_call" | custom-call | flops 9663676416 | bytes 33917952 | tf_op jit(solution)/shard_map/frame_forward/pallas_call | solution.py:358
  179.0 44.3 %time_forward.1 = (bf16[2,16,64,768]{3,2,1,0:T(8,128)(2,1)}, bf16[3072,768]{1,0:T(8,128)(2,1)}, f32[64,32,768]{2,1,0:T(8,128)}, bf16[2048,2304]{1,0:T(8,128)(2,1...) custom-call(bf16[4,16,64,768]{3,2,1,0:T(8,128)(2,1)} %refs_0_.5, bf16[96,768]{1,0:T(8,128)(2,1)} %refs_1_.5, ...), custom_call_target="tpu_custom_call" | custom-call | flops 9663676416 | bytes 37096448 | tf_op jit(solution)/shard_map/time_forward/pallas_call | solution.py:358
  223.4 2.2 fusion.33
  226.2 3.2 pad_maximum_fusion.1
  229.3 6.9 %turn_frames.1.dy = f32[64,32,768]{2,1,0:T(8,128)} custom-call(s32[32]{0:T(128)} %get-tuple-element.143.rows_ref, bf16[64,64,768]{2,1,0:T(8,128)(2,1)} %bitcast.128, bf16[64,64,768]{2,1,0:T(8,128)(2,1)} %bitcast.129, bf16[64,64,768]{2,1,0:T(8,128)(2,1)} %bitcast.130, bf16[64,64,768]{2,1,0:T(8,128)(2,1)} %bitcast.131, bf16[64,64,768]{2,1,0:T(8,128)(2,1)} %bitcast.132, ...), custom_call_target="tpu_custom_call" | custom-call | flops 1000 | bytes 56623104 | tf_op jit(solution)/shard_map/turn_frames/pallas_call | solution.py:358
  236.3 97.5 %mlp_both.1 = (bf16[128,64,768]{2,1,0:T(8,128)(2,1)}, f32[64,32,768]{2,1,0:T(8,128)}, f32[768,3072]{1,0:T(8,128)}, f32[3072,768]{1,0:T(8,128)}, f32[1,3072]{1,0:...) custom-call(f32[64,32,768]{2,1,0:T(8,128)} %get-tuple-element.86.x2, f32[64,32,768]{2,1,0:T(8,128)} %turn_frames.1.dy, ...), custom_call_target="tpu_custom_call" | custom-call | flops 57982058496 | bytes 60979200 | tf_op jit(solution)/shard_map/mlp_both/pallas_call | solution.py:358
  333.7 82.0 %time_back.1 = (bf16[128,64,768]{2,1,0:T(8,128)(2,1)}, f32[24,1024]{1,0:T(8,128)}, f32[96,256]{1,0:T(8,128)}, f32[24,1024]{1,0:T(8,128)}, f32[96,256]{1,0:T(8,12...) custom-call(bf16[128,64,768]{2,1,0:T(8,128)(2,1)} %get-tuple-element, ...), custom_call_target="tpu_custom_call", output_to_operand_aliasing={{0}: (0, {})} | custom-call | flops 19327352832 | bytes 53120000 | tf_op jit(solution)/shard_map/time_back/pallas_call | solution.py:358
  415.8 79.4 %frame_back.1 = (bf16[128,64,768]{2,1,0:T(8,128)(2,1)}, bf16[128,64,768]{2,1,0:T(8,128)(2,1)}, f32[24,768]{1,0:T(8,128)}, f32[24,768]{1,0:T(8,128)}, f32[24,768]...) custom-call(bf16[128,64,768]{2,1,0:T(8,128)(2,1)} %get-tuple-element, ...), custom_call_target="tpu_custom_call", output_to_operand_aliasing={{0}: (0, {})} | custom-call | flops 19327352832 | bytes 43650048 | tf_op jit(solution)/shard_map/frame_back/pallas_call | solution.py:358
  495.3 1.0 maximum_bitcast_fusion
  497.6 1.3 reduce.11
  498.9 0.8 reshape.740
  499.7 4.0 all-to-all-start.2
  505.3 6.2 %all-to-all-done.2 = bf16[32,2,864]{2,1,0:T(2,128)(2,1)S(1)} async-done(((bf16[32,2,864]{2,1,0:T(2,128)(2,1)}), bf16[32,2,864]{2,1,0:T(2,128)(2,1)S(1)}, u32[]{:S(2)}, u32[]{:S(2)}) %all-to-all-start.2) | async-done | bytes 110624 | tf_op jit(solution)/shard_map/all_to_all | solution.py:1036
  513.0 0.8 convert_reduce_fusion
  514.8 1.2 reshape.628
  516.0 1.5 concatenate.62
  517.5 2.1 all_to_all.35
  519.7 3.3 all-to-all-start.3
  524.7 8.0 %unpack_frames.2 = bf16[64,64,768]{2,1,0:T(8,128)(2,1)} custom-call(s32[64]{0:T(128)} %select_n.185.rows_ref, bf16[128,64,768]{2,1,0:T(8,128)(2,1)} %get-tuple-element.104.refs_0_.refs_1_.refs_2_.refs_3_.refs_4_.refs_5_.refs_6_.refs_7_, bf16[128,64,768]{2,1,0:T(8,128)(2,1)} %get-tuple-element.104.refs_0_.refs_1_.refs_2_.refs_3_.refs_4_.refs_5_.refs_6_.refs_7_, ...), custom_call_target="tpu_custom_call" | custom-call | flops 1000 | bytes 12582912 | tf_op jit(solution)/shard_map/unpack_frames/pallas_call | solution.py:557
  532.7 54.2 %scatter_last.1 = (bf16[128,64,768]{2,1,0:T(8,128)(2,1)}, f32[24,3072]{1,0:T(8,128)}, f32[96,768]{1,0:T(8,128)}, f32[24,2304]{1,0:T(8,128)}, f32[24,768]{1,0:T(8...) custom-call(bf16[128,64,768]{2,1,0:T(8,128)(2,1)} %get-tuple-element, ...), custom_call_target="tpu_custom_call", output_to_operand_aliasing={{0}: (0, {})} | custom-call | tf_op jit(solution)/shard_map/scatter_last/pallas_call | solution.py:1007
  586.9 8.0 %unpack_frames.3 = bf16[64,64,768]{2,1,0:T(8,128)(2,1)} custom-call(s32[64]{0:T(128)} %select_n.185.rows_ref, bf16[128,64,768]{2,1,0:T(8,128)(2,1)} %get-tuple-element.127.refs_0_.refs_1_.refs_2_.refs_3_.refs_4_.refs_5_.refs_6_.refs_7_, bf16[128,64,768]{2,1,0:T(8,128)(2,1)} %get-tuple-element.127.refs_0_.refs_1_.refs_2_.refs_3_.refs_4_.refs_5_.refs_6_.refs_7_, ...), custom_call_target="tpu_custom_call" | custom-call | flops 1000 | bytes 12582912 | tf_op jit(solution)/shard_map/unpack_frames/pallas_call | solution.py:557
  594.9 1.5 copy.131
  599.6 1.3 reshape.636
  (190 shorter events, 30.1 us)
Async XLA Ops:
  0.6 18.6 %copy-start = (s32[16,16]{1,0:T(8,128)S(1)}, s32[16,16]{1,0:T(8,128)}, u32[]{:S(2)}) copy-start(s32[16,16]{1,0:T(8,128)} %param.20) | copy-start | bytes 3076
  0.7 26.9 %collective-permute-start.1 = (bf16[96,768]{1,0:T(8,128)(2,1)}, bf16[96,768]{1,0:T(8,128)(2,1)S(1)}, u32[]{:S(2)}, u32[]{:S(2)}) collective-permute-start(bf16[96,768]{1,0:T(8,128)(2,1)} %refs_1_.5), channel_id=1, source_target_pairs={{0,2},{1,3},{2,0},{3,1},{4,6},{5,7},{6,4},{7,5},{8,10},{9,11},{10,... | collective-permute-start | bytes 442376 | tf_op jit(solution)/shard_map/ppermute | solution.py:1081
  7.1 9.6 %copy-start.10 = (bf16[24,2304]{1,0:T(8,128)(2,1)S(1)}, bf16[24,2304]{1,0:T(8,128)(2,1)}, u32[]{:S(2)}) copy-start(bf16[24,2304]{1,0:T(8,128)(2,1)} %refs_0_.3) | copy-start | bytes 331780
  7.1 9.6 %copy-start.18 = (bf16[24,768]{1,0:T(8,128)(2,1)S(1)}, bf16[24,768]{1,0:T(8,128)(2,1)}, u32[]{:S(2)}) copy-start(bf16[24,768]{1,0:T(8,128)(2,1)} %refs_1_.3) | copy-start | bytes 110596
  7.1 9.6 %copy-start.11 = (bf16[24,2304]{1,0:T(8,128)(2,1)S(1)}, bf16[24,2304]{1,0:T(8,128)(2,1)}, u32[]{:S(2)}) copy-start(bf16[24,2304]{1,0:T(8,128)(2,1)} %refs_2_.1) | copy-start | bytes 331780
  7.1 9.6 %copy-start.19 = (bf16[24,768]{1,0:T(8,128)(2,1)S(1)}, bf16[24,768]{1,0:T(8,128)(2,1)}, u32[]{:S(2)}) copy-start(bf16[24,768]{1,0:T(8,128)(2,1)} %refs_3_.1) | copy-start | bytes 110596
  7.1 9.6 %copy-start.20 = (bf16[24,3072]{1,0:T(8,128)(2,1)S(1)}, bf16[24,3072]{1,0:T(8,128)(2,1)}, u32[]{:S(2)}) copy-start(bf16[24,3072]{1,0:T(8,128)(2,1)} %refs_1_.4) | copy-start | bytes 442372
  7.2 11.1 %copy-start.29 = (s32[16]{0:T(128)S(1)}, s32[16]{0:T(128)}, u32[]{:S(2)}) copy-start(s32[16]{0:T(128)} %param.19) | copy-start | bytes 196
  9.2 18.3 %copy-start.31 = (bf16[216]{0:T(256)(128)(2,1)S(1)}, bf16[216]{0:T(256)(128)(2,1)}, u32[]{:S(2)}) copy-start(bf16[216]{0:T(256)(128)(2,1)} %param.22) | copy-start | bytes 1300
  11.0 87.2 %all-to-all-start = ((bf16[32,2,5748]{2,1,0:T(2,128)(2,1)}), bf16[32,2,5748]{2,1,0:T(2,128)(2,1)}, u32[]{:S(2)}, u32[]{:S(2)}) async-start(bf16[32,2,5748]{2,1,0:T(2,128)(2,1)} %reshape.738), calls=%async_computation | async-start | bytes 1474560 | tf_op jit(solution)/shard_map/all_to_all | solution.py:1036
  16.8 19.3 %collective-permute-start = (bf16[24,9216]{1,0:T(8,128)(2,1)S(1)}, bf16[24,9216]{1,0:T(8,128)(2,1)S(1)}, u32[]{:S(2)}, u32[]{:S(2)}) collective-permute-start(bf16[24,9216]{1,0:T(8,128)(2,1)S(1)} %constant_dynamic-update-slice_fusion), channel_id=1, source_target_pairs={{0,2},{1,3},{2,0},{3,1},{4,6},{5,7},{6,4},{7,5},{8,10},{9,11},{10,... | collective-permute-start | bytes 1327112 | tf_op jit(solution)/shard_map/ppermute | solution.py:1081
  18.4 23.6 %copy-start.2 = (s32[4,4]{1,0:T(4,128)}, s32[4,4]{1,0:T(4,128)S(1)}, u32[]{:S(2)}) copy-start(s32[4,4]{1,0:T(4,128)S(1)} %reshape.610) | copy-start | bytes 196
  27.6 14.4 %copy-start.30 = (bf16[96,768]{1,0:T(8,128)(2,1)}, bf16[96,768]{1,0:T(8,128)(2,1)S(1)}, u32[]{:S(2)}) copy-start(bf16[96,768]{1,0:T(8,128)(2,1)S(1)} %collective-permute-done.1.refs_2_) | copy-start | bytes 442372
  42.0 82.9 %collective-permute-start.4 = (bf16[16,64,768]{2,1,0:T(8,128)(2,1)}, bf16[16,64,768]{2,1,0:T(8,128)(2,1)}, u32[]{:S(2)}, u32[]{:S(2)}) collective-permute-start(bf16[16,64,768]{2,1,0:T(8,128)(2,1)} %get-tuple-element.146), channel_id=1, source_target_pairs={{0,3},{1,0},{2,1},{3,2},{4,7},{5,4},{6,5},{7,6},{8,11},{9,8},{10,9... | collective-permute-start | bytes 4718600 | tf_op jit(solution)/shard_map/ppermute | solution.py:1044
  43.0 81.9 %collective-permute-start.3 = (bf16[16,64,768]{2,1,0:T(8,128)(2,1)}, bf16[16,64,768]{2,1,0:T(8,128)(2,1)}, u32[]{:S(2)}, u32[]{:S(2)}) collective-permute-start(bf16[16,64,768]{2,1,0:T(8,128)(2,1)} %get-tuple-element.147), channel_id=1, source_target_pairs={{0,2},{1,3},{2,0},{3,1},{4,6},{5,7},{6,4},{7,5},{8,10},{9,11},{10,... | collective-permute-start | bytes 4718600 | tf_op jit(solution)/shard_map/ppermute | solution.py:1044
  43.1 81.8 %collective-permute-start.2 = (bf16[16,64,768]{2,1,0:T(8,128)(2,1)}, bf16[16,64,768]{2,1,0:T(8,128)(2,1)}, u32[]{:S(2)}, u32[]{:S(2)}) collective-permute-start(bf16[16,64,768]{2,1,0:T(8,128)(2,1)} %get-tuple-element.148), channel_id=1, source_target_pairs={{0,1},{1,2},{2,3},{3,0},{4,5},{5,6},{6,7},{7,4},{8,9},{9,10},{10,1... | collective-permute-start | bytes 4718600 | tf_op jit(solution)/shard_map/ppermute | solution.py:1044
  103.4 0.9 copy-start.8
  104.5 17.6 %copy-start.4 = (bf16[256,768]{1,0:T(8,128)(2,1)}, bf16[256,768]{1,0:T(8,128)(2,1)S(1)}, u32[]{:S(2)}) copy-start(bf16[256,768]{1,0:T(8,128)(2,1)S(1)} %convert_element_type.58) | copy-start | bytes 1179652
  105.2 17.1 %copy-start.6 = (bf16[768,216]{1,0:T(8,128)(2,1)}, bf16[768,216]{1,0:T(8,128)(2,1)S(1)}, u32[]{:S(2)}) copy-start(bf16[768,216]{1,0:T(8,128)(2,1)S(1)} %reshape.616) | copy-start | bytes 995332
  107.6 14.0 %all-to-all-start.1 = ((f32[32,1,1728]{2,1,0:T(1,128)}), f32[32,1,1728]{2,1,0:T(1,128)S(1)}, u32[]{:S(2)}, u32[]{:S(2)}) async-start(f32[32,1,1728]{2,1,0:T(1,128)} %all_to_all.38), calls=%async_computation.1 | async-start | bytes 458752 | tf_op jit(solution)/shard_map/all_to_all | solution.py:1036
  223.4 2.4 slice-start
  223.4 2.8 copy-start.9
  415.8 79.5 %copy-start.12 = (f32[3,32,768]{2,1,0:T(8,128)S(1)}, f32[3,32,768]{2,1,0:T(8,128)}, u32[]{:S(2)}) copy-start(f32[3,32,768]{2,1,0:T(8,128)} %get-tuple-element.130) | copy-start | bytes 884740
  415.8 79.5 %copy-start.13 = (f32[3,32,768]{2,1,0:T(8,128)S(1)}, f32[3,32,768]{2,1,0:T(8,128)}, u32[]{:S(2)}) copy-start(f32[3,32,768]{2,1,0:T(8,128)} %get-tuple-element.129) | copy-start | bytes 884740
  495.2 1.2 copy-start.28
  495.2 8.4 %copy-start.27 = (f32[1,768]{1,0:T(1,128)S(1)}, f32[1,768]{1,0:T(1,128)}, u32[]{:S(2)}) copy-start(f32[1,768]{1,0:T(1,128)} %get-tuple-element.131) | copy-start | bytes 9220
  495.2 8.5 %copy-start.26 = (f32[1,768]{1,0:T(1,128)S(1)}, f32[1,768]{1,0:T(1,128)}, u32[]{:S(2)}) copy-start(f32[1,768]{1,0:T(1,128)} %get-tuple-element.132) | copy-start | bytes 9220
  495.3 8.5 %copy-start.25 = (f32[1,768]{1,0:T(1,128)S(1)}, f32[1,768]{1,0:T(1,128)}, u32[]{:S(2)}) copy-start(f32[1,768]{1,0:T(1,128)} %get-tuple-element.134) | copy-start | bytes 9220
  495.3 9.0 %copy-start.24 = (f32[1,3072]{1,0:T(1,128)S(1)}, f32[1,3072]{1,0:T(1,128)}, u32[]{:S(2)}) copy-start(f32[1,3072]{1,0:T(1,128)} %get-tuple-element.133) | copy-start | bytes 36868
  496.3 17.7 %copy-start.7 = (bf16[768,216]{1,0:T(8,128)(2,1)S(1)}, bf16[768,216]{1,0:T(8,128)(2,1)}, u32[]{:S(2)}) copy-start(bf16[768,216]{1,0:T(8,128)(2,1)} %copy-done.6) | copy-start | bytes 995332
  496.4 17.9 %copy-start.5 = (bf16[256,768]{1,0:T(8,128)(2,1)S(1)}, bf16[256,768]{1,0:T(8,128)(2,1)}, u32[]{:S(2)}) copy-start(bf16[256,768]{1,0:T(8,128)(2,1)} %copy-done.4) | copy-start | bytes 1179652
  499.7 11.8 %all-to-all-start.2 = ((bf16[32,2,864]{2,1,0:T(2,128)(2,1)}), bf16[32,2,864]{2,1,0:T(2,128)(2,1)S(1)}, u32[]{:S(2)}, u32[]{:S(2)}) async-start(bf16[32,2,864]{2,1,0:T(2,128)(2,1)} %reshape.740), calls=%async_computation.2 | async-start | bytes 229376 | tf_op jit(solution)/shard_map/all_to_all | solution.py:1036
  517.5 5.6 copy-start.3
  519.7 75.2 %all-to-all-start.3 = ((f32[32,1,11496]{2,1,0:T(1,128)}), f32[32,1,11496]{2,1,0:T(1,128)}, u32[]{:S(2)}, u32[]{:S(2)}) async-start(f32[32,1,11496]{2,1,0:T(1,128)} %all_to_all.35), calls=%async_computation.3 | async-start | bytes 2949120 | tf_op jit(solution)/shard_map/all_to_all | solution.py:1036
  594.9 3.2 copy-start.23
  597.9 3.0 copy-start.17
  597.9 3.7 copy-start.22
  597.9 4.3 copy-start.16
  598.0 4.9 copy-start.21
  598.0 5.6 copy-start.15
  598.1 6.2 %copy-start.14 = (f32[96,768]{1,0:T(8,128)S(1)}, f32[96,768]{1,0:T(8,128)}, u32[]{:S(2)}) copy-start(f32[96,768]{1,0:T(8,128)} %get-tuple-element.213) | copy-start | bytes 884740
  598.1 6.9 %copy-start.1 = (s32[16,16]{1,0:T(8,128)S(1)}, s32[16,16]{1,0:T(8,128)}, u32[]{:S(2)}) copy-start(s32[16,16]{1,0:T(8,128)} %param.20) | copy-start | bytes 3076

commit v8 on v7

--- a/solution.py
+++ b/solution.py
@@ -26,7 +26,7 @@
 PT = TILE // LIVE
 GRID = LIVE * PATCHES // TILE
 GROUPS = TILE // 64
-EARLY_TILES = GRID - 1
+EARLY_TILES = GRID // 2
 GELU_C = 0.7978845608028654
 GELU_A = 0.044715
 VMEM_LIMIT = 66 * 1000 * 1000
@@ -434,6 +434,49 @@
     return tick
 
 
+def patches_of(frames, slot, i):
+    return frames.at[packed(slot), pl.ds(pl.multiple_of(i * PT, PT), PT)]
+
+
+def out_carrier(slots, number):
+    def wrap(kernel, n_in, n_out, n_scratch, *refs):
+        ins, (dst,), outs, scratch, (send_sem, recv_sem, keep, buf) = split_refs(refs, n_in, 1, n_out, n_scratch)
+        step = pl.program_id(0)
+        w, k = lax.axis_index("wide"), lax.axis_index("narrow")
+        other_x, other_c = (w, (k + 2) % 4), (w, k + 1 - 2 * (k % 2))
+
+        def tile(i):
+            return [send(buf.at[i], patches_of(dst, slot, i), send_sem.at[a, i], recv_sem.at[a, i], peer)
+                    for a, (slot, peer) in enumerate(((slot_for(k), other_c), (2, other_x)))]
+
+        def store(i):
+            return pltpu.make_async_copy(buf.at[i], patches_of(dst, 0, i), keep.at[i])
+
+        @pl.when(step == 0)
+        def _():
+            greet((other_x, other_c))
+
+        kernel(*ins, buf.at[step], *outs, *scratch)
+        store(step).start()
+
+        @pl.when(step < GRID - 1)
+        def _():
+            for copy in tile(step):
+                copy.start()
+
+        @pl.when(step == GRID - 1)
+        def _():
+            for i in range(GRID):
+                store(i).wait()
+            for i in range(GRID - 1):
+                for copy in tile(i):
+                    copy.wait()
+
+    sems = pltpu.SemaphoreType.DMA
+    return Carrier(wrap, number, [], [shape_of((slots * LIVE, PATCHES, D), BF)], [ANY],
+                   [sems((2, GRID - 1)), sems((2, GRID - 1)), sems((GRID,)), pltpu.VMEM((GRID, LIVE, PT, D), BF)])
+
+
 def share_carrier(frames, grads, plan, number):
     n_grads = len(grads)
 
@@ -443,7 +486,8 @@
         step = pl.program_id(0)
         sums = plan.steps(grad_refs + left + own)
         targets = ((slot_for(sums.k), sums.other_c), (2, sums.other_x))
-        copies = [send(dst.at[packed(0)], dst.at[packed(slot)], send_sem.at[i], recv_sem.at[i], peer)
+        final = GRID - 1
+        copies = [send(patches_of(dst, 0, final), patches_of(dst, slot, final), send_sem.at[i], recv_sem.at[i], peer)
                   for i, (slot, peer) in enumerate(targets)]
 
         @pl.when(step == 0)
@@ -577,18 +621,20 @@
         [], 2 * TOKENS * D * 4 * D, carrier=carrier)
 
 
-def run_mlp(x2, dy, mod, win, bin_, wout, bout, slots=1):
+def run_mlp(x2, dy, mod, win, bin_, wout, bout, carrier=None):
+    frames_out = [] if carrier else [shape_of((LIVE, PATCHES, D), BF)]
+    frames_spec = [] if carrier else [tiles((LIVE, PT, D), 1)]
     return call(
         mlp_both, "mlp_both",
         [x2, dy, mod, win, bin_, wout, bout],
         [TURNED, TURNED, piece_spec(2, LIVE, False), whole((D, FF)), whole((1, FF)), whole((FF, D)),
          whole((1, D))],
-        [shape_of((slots * LIVE, PATCHES, D), BF), shape_of((PATCHES, LIVE, D), F32), shape_of((D, FF), F32),
+        frames_out + [shape_of((PATCHES, LIVE, D), F32), shape_of((D, FF), F32),
          shape_of((FF, D), F32), shape_of((1, FF), F32), shape_of((1, D), F32), shape_of((3, LIVE, D), F32)],
-        [tiles((LIVE, PT, D), 1), TURNED, whole((D, FF)), whole((FF, D)), whole((1, FF)), whole((1, D)),
+        frames_spec + [TURNED, whole((D, FF)), whole((FF, D)), whole((1, FF)), whole((1, D)),
          whole((3, LIVE, D))],
         [TURN],
-        6 * 2 * TOKENS * D * FF)
+        6 * 2 * TOKENS * D * FF, carrier=carrier)
 
 
 def run_time_back(x1, dx2, mod, seg, qkv, o, a2, wqkv, wo, carrier=None):
@@ -922,11 +968,28 @@
         return Sums(self, refs)
 
 
+def mlp_cuts(g):
+    lanes = g.shape[1] // LANES
+    last = lanes - lanes // 6
+    return [0, (last + 1) // 2 * LANES, last * LANES, g.shape[1]]
+
+
+def mlp_pieces(numbers, grads, parts, devices):
+    pieces = []
+    for i in parts:
+        for way, (number, g) in enumerate(zip(numbers, grads)):
+            cuts = mlp_cuts(g)
+            pieces.append((number, cuts[i], cuts[i + 1] - cuts[i], g.shape[0] // devices, way))
+    return pieces
+
+
+def mlp_places(pieces):
+    return [[(way, col, 0, width)] for _, col, width, _, way in pieces]
+
+
 def time_plan(ring, g_in, g_out, devices):
-    a, b = g_in.shape[0] // devices, g_out.shape[0] // devices
-    wa, wb = g_in.shape[1] // 3, g_out.shape[1] // 3
-    return Plan(ring, 2, [(0, 0, wa, a, 0), (1, 0, wb, b, 1), (0, wa, wa, a, 0), (1, wb, wb, b, 1)],
-                [[(0, 0, 0, wa)], [(1, 0, 0, wb)], [(0, wa, 0, wa)], [(1, wb, 0, wb)]], True)
+    pieces = mlp_pieces((0, 1), (g_in, g_out), (0, 1), devices)
+    return Plan(ring, 2, pieces, mlp_places(pieces), True)
 
 
 def attn_pieces(g, number, devices):
@@ -938,10 +1001,8 @@
 
 
 def frame_plan(ring, g_t, g_in, g_out, devices):
-    a, b = g_in.shape[0] // devices, g_out.shape[0] // devices
-    wa, wb = g_in.shape[1] // 3, g_out.shape[1] // 3
-    return Plan(ring, 3, attn_pieces(g_t, 0, devices) + [(1, 2 * wa, wa, a, 0), (2, 2 * wb, wb, b, 1)],
-                attn_places(2) + [[(0, 2 * wa, 0, wa)], [(1, 2 * wb, 0, wb)]], True)
+    pieces = mlp_pieces((1, 2), (g_in, g_out), (2,), devices)
+    return Plan(ring, 3, attn_pieces(g_t, 0, devices) + pieces, attn_places(2) + mlp_places(pieces), True)
 
 
 def last_plan(ring, g_s, devices):
@@ -1129,7 +1190,7 @@
     else:
         cots = shift_clips(cotangent, False)
     dy = run_turn_frames(cots.reshape(n * FR, PATCHES, D), pack_rows)
-    out, dx2, g_in, g_out, gb_in, gb_out, dmod3 = run_mlp(x2, dy, mod, win, bias_in, wout, bias_out, n if fast else 1)
+    out, dx2, g_in, g_out, gb_in, gb_out, dmod3 = run_mlp(x2, dy, mod, win, bias_in, wout, bias_out, out_carrier(n, 6) if fast else None)
 
     own_len = lengths.reshape(n, n)[rank]
     own_live = frame_ids[None, :] < own_len[:, None]

time: 614 us -> 594 us (0.967)
  Pallas kernels: 475 us -> 459 us
    pallas_call x6, Pallas kernels: 353 us -> 329 us  [call(): return fn(*ins) if prefetch is None else fn(prefetch, *ins)]
    pallas_call x1, Pallas kernels: 54.2 us -> 60.9 us  [scatter_last(): pl.pallas_call(functools.partial(last_kernel, plan, left, len(shapes)), n...]
  transfers between devices with their start and end apart: 9 -> 9, of which waited for: 3 -> 3; matrix products, arithmetic and copies ran while one was open for 7% -> 7% of each run, Pallas kernels for 20% -> 22%
where the time goes in v8:
time: 594 us; the launch traced here: 589 us
  Pallas kernels  459 us (77%)
  local copies, waits for them, and re-layouts  58.5 us (10%)
  other arithmetic  24.4 us (4%)
  starting transfers between devices  24 us (4%)
  waiting for transfers between devices  19.9 us (3%)
    pallas_call x6, Pallas kernels, call(): return fn(*ins) if prefetch is None else fn(prefetch, *ins)  329 us
    pallas_call x1, Pallas kernels, scatter_last(): pl.pallas_call(functools.partial(last_kernel, plan, left, len(shapes)), n...  60.9 us
    pallas_call x1, Pallas kernels, gather_first(): pl.pallas_call(functools.partial(gather_kernel, ring, heights), name='gat...  52.2 us
    all_to_all x4, starting transfers between devices, exchange(): return lax.all_to_all(x, ALL, split_axis=0, concat_axis=0, tiled=True)  17.8 us
    pallas_call x2, Pallas kernels, run_unpack(): pl.pallas_call(unpack_frames, grid_spec=pltpu.PrefetchScalarGridSpec(num_...  16.8 us
    unnamed x82, local copies, waits for them, and re-layouts  14.8 us
  transfers between devices with their start and end apart: 9, of which 3 were waited for; matrix products, arithmetic and copies ran while one was open for 7% of the time, Pallas kernels for 22%

profile of v8, /device:TPU:1, one launch (start us, length us, event | category | flops | bytes accessed | tf_op | source)
XLA Modules:
  0.0 589.5 jit_solution(6945416539951982070)
XLA Ops:
  0.7 2.1 collective-permute-start.1
  3.5 2.2 reshape.614
  6.3 0.8 pad_maximum_fusion.4
  8.2 1.1 reduce.10
  9.4 1.7 reshape.738
  11.0 5.7 all-to-all-start
  16.8 1.4 collective-permute-start
  20.5 3.1 fusion.27
  23.6 1.2 gather_fusion.7
  24.9 0.8 gather_fusion.6
  25.6 0.8 gather_fusion.4
  27.7 8.5 %collective-permute-done = bf16[24,9216]{1,0:T(8,128)(2,1)S(1)} collective-permute-done((bf16[24,9216]{1,0:T(8,128)(2,1)S(1)}, bf16[24,9216]{1,0:T(8,128)(2,1)S(1)}, u32[]{:S(2)}, u32[]{:S(2)}) %collective-permute-start) | collective-permute-done | bytes 442400 | tf_op jit(solution)/shard_map/ppermute | solution.py:1142
  36.8 5.2 fusion.32
  42.0 1.0 collective-permute-start.4
  43.1 1.6 collective-permute-start.2
  46.0 52.2 %gather_first.1 = (bf16[768,2304]{1,0:T(8,128)(2,1)}, bf16[768,768]{1,0:T(8,128)(2,1)}, bf16[768,2304]{1,0:T(8,128)(2,1)}, bf16[768,768]{1,0:T(8,128)(2,1)}) custom-call(bf16[24,2304]{1,0:T(8,128)(2,1)} %refs_0_.3, bf16[24,768]{1,0:T(8,128)(2,1)} %refs_1_.3, bf16[24,2304]{1,0:T(8,128)(2,1)} %refs_2_.1, bf16[24,768]{1,0:T(8,128)(2,1)} %refs_3_.1, ...), custom_call_target="tpu_custom_call" | custom-call | tf_op jit(solution)/shard_map/gather_first/pallas_call | solution.py:792
  98.3 5.1 reshape.739
  106.3 1.3 all_to_all.38
  107.6 4.4 all-to-all-start.1
  112.0 0.8 slice_convert_fusion.1
  113.5 0.9 slice_convert_fusion
  116.3 5.3 all-to-all-done.1
  123.4 1.4 copy.132
  124.9 5.9 pad_maximum_fusion
  130.8 5.2 gather_fusion.2
  135.9 43.0 %frame_forward.1 = (bf16[1,16,64,768]{3,2,1,0:T(8,128)(2,1)}, bf16[768,3072]{1,0:T(8,128)(2,1)}, f32[64,32,768]{2,1,0:T(8,128)}, bf16[2048,2304]{1,0:T(8,128)(2,...) custom-call(bf16[4,16,64,768]{3,2,1,0:T(8,128)(2,1)} %refs_0_.5, bf16[24,3072]{1,0:T(8,128)(2,1)} %refs_1_.4, ...), custom_call_target="tpu_custom_call" | custom-call | flops 9663676416 | bytes 33917952 | tf_op jit(solution)/shard_map/frame_forward/pallas_call | solution.py:358
  178.9 44.2 %time_forward.1 = (bf16[2,16,64,768]{3,2,1,0:T(8,128)(2,1)}, bf16[3072,768]{1,0:T(8,128)(2,1)}, f32[64,32,768]{2,1,0:T(8,128)}, bf16[2048,2304]{1,0:T(8,128)(2,1...) custom-call(bf16[4,16,64,768]{3,2,1,0:T(8,128)(2,1)} %refs_0_.5, bf16[96,768]{1,0:T(8,128)(2,1)} %refs_1_.5, ...), custom_call_target="tpu_custom_call" | custom-call | flops 9663676416 | bytes 37096448 | tf_op jit(solution)/shard_map/time_forward/pallas_call | solution.py:358
  223.1 2.2 fusion.33
  226.0 3.2 pad_maximum_fusion.1
  229.1 6.9 %turn_frames.1.refs_1_ = f32[64,32,768]{2,1,0:T(8,128)} custom-call(s32[32]{0:T(128)} %get-tuple-element.143.rows_ref, bf16[64,64,768]{2,1,0:T(8,128)(2,1)} %bitcast.128, bf16[64,64,768]{2,1,0:T(8,128)(2,1)} %bitcast.129, bf16[64,64,768]{2,1,0:T(8,128)(2,1)} %bitcast.130, bf16[64,64,768]{2,1,0:T(8,128)(2,1)} %bitcast.131, bf16[64,64,768]{2,1,0:T(8,128)(2,1)} %bitcast.132, ...), custom_call_target="tpu_custom_call" | custom-call | flops 1000 | bytes 56623104 | tf_op jit(solution)/shard_map/turn_frames/pallas_call | solution.py:358
  236.1 98.4 %mlp_both.1 = (bf16[128,64,768]{2,1,0:T(8,128)(2,1)}, f32[64,32,768]{2,1,0:T(8,128)}, f32[768,3072]{1,0:T(8,128)}, f32[3072,768]{1,0:T(8,128)}, f32[1,3072]{1,0:...) custom-call(f32[64,32,768]{2,1,0:T(8,128)} %get-tuple-element.86.refs_0_, f32[64,32,768]{2,1,0:T(8,128)} %turn_frames.1.refs_1_, ...), custom_call_target="tpu_custom_call" | custom-call | flops 57982058496 | bytes 48396288 | tf_op jit(solution)/shard_map/mlp_both/pallas_call | solution.py:358
  334.5 70.5 %time_back.1 = (bf16[128,64,768]{2,1,0:T(8,128)(2,1)}, f32[24,1280]{1,0:T(8,128)}, f32[96,384]{1,0:T(8,128)}, f32[24,1280]{1,0:T(8,128)}, f32[96,256]{1,0:T(8,12...) custom-call(bf16[128,64,768]{2,1,0:T(8,128)(2,1)} %get-tuple-element, ...), custom_call_target="tpu_custom_call", output_to_operand_aliasing={{0}: (0, {})} | custom-call | flops 19327352832 | bytes 53120000 | tf_op jit(solution)/shard_map/time_back/pallas_call | solution.py:358
  405.0 66.4 %frame_back.1 = (bf16[128,64,768]{2,1,0:T(8,128)(2,1)}, bf16[128,64,768]{2,1,0:T(8,128)(2,1)}, f32[24,768]{1,0:T(8,128)}, f32[24,768]{1,0:T(8,128)}, f32[24,768]...) custom-call(bf16[128,64,768]{2,1,0:T(8,128)(2,1)} %get-tuple-element, ...), custom_call_target="tpu_custom_call", output_to_operand_aliasing={{0}: (0, {})} | custom-call | flops 19327352832 | bytes 43650048 | tf_op jit(solution)/shard_map/frame_back/pallas_call | solution.py:358
  471.4 1.0 maximum_bitcast_fusion
  473.7 1.3 reduce.11
  475.1 0.8 reshape.740
  475.9 4.5 all-to-all-start.2
  482.0 6.2 %all-to-all-done.2 = bf16[32,2,864]{2,1,0:T(2,128)(2,1)S(1)} async-done(((bf16[32,2,864]{2,1,0:T(2,128)(2,1)}), bf16[32,2,864]{2,1,0:T(2,128)(2,1)S(1)}, u32[]{:S(2)}, u32[]{:S(2)}) %all-to-all-start.2) | async-done | bytes 110624 | tf_op jit(solution)/shard_map/all_to_all | solution.py:1097
  489.7 0.8 convert_reduce_fusion
  491.5 1.2 reshape.628
  492.7 1.5 concatenate.62
  494.2 2.1 all_to_all.35
  496.4 3.3 all-to-all-start.3
  501.4 8.4 %unpack_frames.2 = bf16[64,64,768]{2,1,0:T(8,128)(2,1)} custom-call(s32[64]{0:T(128)} %select_n.185.rows_ref, bf16[128,64,768]{2,1,0:T(8,128)(2,1)} %get-tuple-element.104.refs_0_.refs_1_.refs_2_.refs_3_.refs_4_.refs_5_.refs_6_.refs_7_, bf16[128,64,768]{2,1,0:T(8,128)(2,1)} %get-tuple-element.104.refs_0_.refs_1_.refs_2_.refs_3_.refs_4_.refs_5_.refs_6_.refs_7_, ...), custom_call_target="tpu_custom_call" | custom-call | flops 1000 | bytes 12582912 | tf_op jit(solution)/shard_map/unpack_frames/pallas_call | solution.py:601
  509.8 60.9 %scatter_last.1 = (bf16[128,64,768]{2,1,0:T(8,128)(2,1)}, f32[24,3072]{1,0:T(8,128)}, f32[96,768]{1,0:T(8,128)}, f32[24,2304]{1,0:T(8,128)}, f32[24,768]{1,0:T(8...) custom-call(bf16[128,64,768]{2,1,0:T(8,128)(2,1)} %get-tuple-element, ...), custom_call_target="tpu_custom_call", output_to_operand_aliasing={{0}: (0, {})} | custom-call | tf_op jit(solution)/shard_map/scatter_last/pallas_call | solution.py:1068
  570.8 8.3 %unpack_frames.3 = bf16[64,64,768]{2,1,0:T(8,128)(2,1)} custom-call(s32[64]{0:T(128)} %select_n.185.rows_ref, bf16[128,64,768]{2,1,0:T(8,128)(2,1)} %get-tuple-element.127.refs_0_.refs_1_.refs_2_.refs_3_.refs_4_.refs_5_.refs_6_.refs_7_, bf16[128,64,768]{2,1,0:T(8,128)(2,1)} %get-tuple-element.127.refs_0_.refs_1_.refs_2_.refs_3_.refs_4_.refs_5_.refs_6_.refs_7_, ...), custom_call_target="tpu_custom_call" | custom-call | flops 1000 | bytes 12582912 | tf_op jit(solution)/shard_map/unpack_frames/pallas_call | solution.py:601
  579.1 1.5 copy.131
  583.9 1.3 reshape.636
  (190 shorter events, 30.2 us)
Async XLA Ops:
  0.6 18.7 %copy-start = (s32[16,16]{1,0:T(8,128)S(1)}, s32[16,16]{1,0:T(8,128)}, u32[]{:S(2)}) copy-start(s32[16,16]{1,0:T(8,128)} %param.20) | copy-start | bytes 3076
  0.7 27.0 %collective-permute-start.1 = (bf16[96,768]{1,0:T(8,128)(2,1)}, bf16[96,768]{1,0:T(8,128)(2,1)S(1)}, u32[]{:S(2)}, u32[]{:S(2)}) collective-permute-start(bf16[96,768]{1,0:T(8,128)(2,1)} %refs_1_.5), channel_id=1, source_target_pairs={{0,2},{1,3},{2,0},{3,1},{4,6},{5,7},{6,4},{7,5},{8,10},{9,11},{10,... | collective-permute-start | bytes 442376 | tf_op jit(solution)/shard_map/ppermute | solution.py:1142
  7.1 9.7 %copy-start.10 = (bf16[24,2304]{1,0:T(8,128)(2,1)S(1)}, bf16[24,2304]{1,0:T(8,128)(2,1)}, u32[]{:S(2)}) copy-start(bf16[24,2304]{1,0:T(8,128)(2,1)} %refs_0_.3) | copy-start | bytes 331780
  7.1 9.6 %copy-start.18 = (bf16[24,768]{1,0:T(8,128)(2,1)S(1)}, bf16[24,768]{1,0:T(8,128)(2,1)}, u32[]{:S(2)}) copy-start(bf16[24,768]{1,0:T(8,128)(2,1)} %refs_1_.3) | copy-start | bytes 110596
  7.1 9.7 %copy-start.11 = (bf16[24,2304]{1,0:T(8,128)(2,1)S(1)}, bf16[24,2304]{1,0:T(8,128)(2,1)}, u32[]{:S(2)}) copy-start(bf16[24,2304]{1,0:T(8,128)(2,1)} %refs_2_.1) | copy-start | bytes 331780
  7.1 9.7 %copy-start.19 = (bf16[24,768]{1,0:T(8,128)(2,1)S(1)}, bf16[24,768]{1,0:T(8,128)(2,1)}, u32[]{:S(2)}) copy-start(bf16[24,768]{1,0:T(8,128)(2,1)} %refs_3_.1) | copy-start | bytes 110596
  7.1 9.7 %copy-start.20 = (bf16[24,3072]{1,0:T(8,128)(2,1)S(1)}, bf16[24,3072]{1,0:T(8,128)(2,1)}, u32[]{:S(2)}) copy-start(bf16[24,3072]{1,0:T(8,128)(2,1)} %refs_1_.4) | copy-start | bytes 442372
  7.2 11.2 %copy-start.29 = (s32[16]{0:T(128)S(1)}, s32[16]{0:T(128)}, u32[]{:S(2)}) copy-start(s32[16]{0:T(128)} %param.19) | copy-start | bytes 196
  9.4 18.3 %copy-start.31 = (bf16[216]{0:T(256)(128)(2,1)S(1)}, bf16[216]{0:T(256)(128)(2,1)}, u32[]{:S(2)}) copy-start(bf16[216]{0:T(256)(128)(2,1)} %param.22) | copy-start | bytes 1300
  11.0 87.2 %all-to-all-start = ((bf16[32,2,5748]{2,1,0:T(2,128)(2,1)}), bf16[32,2,5748]{2,1,0:T(2,128)(2,1)}, u32[]{:S(2)}, u32[]{:S(2)}) async-start(bf16[32,2,5748]{2,1,0:T(2,128)(2,1)} %reshape.738), calls=%async_computation | async-start | bytes 1474560 | tf_op jit(solution)/shard_map/all_to_all | solution.py:1097
  16.8 19.3 %collective-permute-start = (bf16[24,9216]{1,0:T(8,128)(2,1)S(1)}, bf16[24,9216]{1,0:T(8,128)(2,1)S(1)}, u32[]{:S(2)}, u32[]{:S(2)}) collective-permute-start(bf16[24,9216]{1,0:T(8,128)(2,1)S(1)} %constant_dynamic-update-slice_fusion), channel_id=1, source_target_pairs={{0,2},{1,3},{2,0},{3,1},{4,6},{5,7},{6,4},{7,5},{8,10},{9,11},{10,... | collective-permute-start | bytes 1327112 | tf_op jit(solution)/shard_map/ppermute | solution.py:1142
  18.4 23.6 %copy-start.2 = (s32[4,4]{1,0:T(4,128)}, s32[4,4]{1,0:T(4,128)S(1)}, u32[]{:S(2)}) copy-start(s32[4,4]{1,0:T(4,128)S(1)} %reshape.610) | copy-start | bytes 196
  27.6 14.4 %copy-start.30 = (bf16[96,768]{1,0:T(8,128)(2,1)}, bf16[96,768]{1,0:T(8,128)(2,1)S(1)}, u32[]{:S(2)}) copy-start(bf16[96,768]{1,0:T(8,128)(2,1)S(1)} %collective-permute-done.1.refs_2_) | copy-start | bytes 442372
  42.0 82.8 %collective-permute-start.4 = (bf16[16,64,768]{2,1,0:T(8,128)(2,1)}, bf16[16,64,768]{2,1,0:T(8,128)(2,1)}, u32[]{:S(2)}, u32[]{:S(2)}) collective-permute-start(bf16[16,64,768]{2,1,0:T(8,128)(2,1)} %get-tuple-element.146), channel_id=1, source_target_pairs={{0,3},{1,0},{2,1},{3,2},{4,7},{5,4},{6,5},{7,6},{8,11},{9,8},{10,9... | collective-permute-start | bytes 4718600 | tf_op jit(solution)/shard_map/ppermute | solution.py:1105
  43.0 81.9 %collective-permute-start.3 = (bf16[16,64,768]{2,1,0:T(8,128)(2,1)}, bf16[16,64,768]{2,1,0:T(8,128)(2,1)}, u32[]{:S(2)}, u32[]{:S(2)}) collective-permute-start(bf16[16,64,768]{2,1,0:T(8,128)(2,1)} %get-tuple-element.147), channel_id=1, source_target_pairs={{0,2},{1,3},{2,0},{3,1},{4,6},{5,7},{6,4},{7,5},{8,10},{9,11},{10,... | collective-permute-start | bytes 4718600 | tf_op jit(solution)/shard_map/ppermute | solution.py:1105
  43.1 81.7 %collective-permute-start.2 = (bf16[16,64,768]{2,1,0:T(8,128)(2,1)}, bf16[16,64,768]{2,1,0:T(8,128)(2,1)}, u32[]{:S(2)}, u32[]{:S(2)}) collective-permute-start(bf16[16,64,768]{2,1,0:T(8,128)(2,1)} %get-tuple-element.148), channel_id=1, source_target_pairs={{0,1},{1,2},{2,3},{3,0},{4,5},{5,6},{6,7},{7,4},{8,9},{9,10},{10,1... | collective-permute-start | bytes 4718600 | tf_op jit(solution)/shard_map/ppermute | solution.py:1105
  103.5 0.9 copy-start.8
  104.6 17.6 %copy-start.4 = (bf16[256,768]{1,0:T(8,128)(2,1)}, bf16[256,768]{1,0:T(8,128)(2,1)S(1)}, u32[]{:S(2)}) copy-start(bf16[256,768]{1,0:T(8,128)(2,1)S(1)} %convert_element_type.58) | copy-start | bytes 1179652
  105.2 17.1 %copy-start.6 = (bf16[768,216]{1,0:T(8,128)(2,1)}, bf16[768,216]{1,0:T(8,128)(2,1)S(1)}, u32[]{:S(2)}) copy-start(bf16[768,216]{1,0:T(8,128)(2,1)S(1)} %reshape.616) | copy-start | bytes 995332
  107.6 14.0 %all-to-all-start.1 = ((f32[32,1,1728]{2,1,0:T(1,128)}), f32[32,1,1728]{2,1,0:T(1,128)S(1)}, u32[]{:S(2)}, u32[]{:S(2)}) async-start(f32[32,1,1728]{2,1,0:T(1,128)} %all_to_all.38), calls=%async_computation.1 | async-start | bytes 458752 | tf_op jit(solution)/shard_map/all_to_all | solution.py:1097
  223.1 2.4 slice-start
  223.1 2.8 copy-start.9
  405.0 66.4 %copy-start.12 = (f32[3,32,768]{2,1,0:T(8,128)S(1)}, f32[3,32,768]{2,1,0:T(8,128)}, u32[]{:S(2)}) copy-start(f32[3,32,768]{2,1,0:T(8,128)} %get-tuple-element.130) | copy-start | bytes 884740
  405.0 66.4 %copy-start.13 = (f32[3,32,768]{2,1,0:T(8,128)S(1)}, f32[3,32,768]{2,1,0:T(8,128)}, u32[]{:S(2)}) copy-start(f32[3,32,768]{2,1,0:T(8,128)} %get-tuple-element.129) | copy-start | bytes 884740
  471.4 1.2 copy-start.28
  471.4 9.0 %copy-start.27 = (f32[1,768]{1,0:T(1,128)S(1)}, f32[1,768]{1,0:T(1,128)}, u32[]{:S(2)}) copy-start(f32[1,768]{1,0:T(1,128)} %get-tuple-element.131) | copy-start | bytes 9220
  471.4 9.0 %copy-start.26 = (f32[1,768]{1,0:T(1,128)S(1)}, f32[1,768]{1,0:T(1,128)}, u32[]{:S(2)}) copy-start(f32[1,768]{1,0:T(1,128)} %get-tuple-element.132) | copy-start | bytes 9220
  471.4 9.0 %copy-start.25 = (f32[1,768]{1,0:T(1,128)S(1)}, f32[1,768]{1,0:T(1,128)}, u32[]{:S(2)}) copy-start(f32[1,768]{1,0:T(1,128)} %get-tuple-element.134) | copy-start | bytes 9220
  471.4 9.6 %copy-start.24 = (f32[1,3072]{1,0:T(1,128)S(1)}, f32[1,3072]{1,0:T(1,128)}, u32[]{:S(2)}) copy-start(f32[1,3072]{1,0:T(1,128)} %get-tuple-element.133) | copy-start | bytes 36868
  472.5 18.3 %copy-start.7 = (bf16[768,216]{1,0:T(8,128)(2,1)S(1)}, bf16[768,216]{1,0:T(8,128)(2,1)}, u32[]{:S(2)}) copy-start(bf16[768,216]{1,0:T(8,128)(2,1)} %copy-done.6) | copy-start | bytes 995332
  472.6 18.5 %copy-start.5 = (bf16[256,768]{1,0:T(8,128)(2,1)S(1)}, bf16[256,768]{1,0:T(8,128)(2,1)}, u32[]{:S(2)}) copy-start(bf16[256,768]{1,0:T(8,128)(2,1)} %copy-done.4) | copy-start | bytes 1179652
  475.9 12.3 %all-to-all-start.2 = ((bf16[32,2,864]{2,1,0:T(2,128)(2,1)}), bf16[32,2,864]{2,1,0:T(2,128)(2,1)S(1)}, u32[]{:S(2)}, u32[]{:S(2)}) async-start(bf16[32,2,864]{2,1,0:T(2,128)(2,1)} %reshape.740), calls=%async_computation.2 | async-start | bytes 229376 | tf_op jit(solution)/shard_map/all_to_all | solution.py:1097
  494.2 5.6 copy-start.3
  496.4 82.8 %all-to-all-start.3 = ((f32[32,1,11496]{2,1,0:T(1,128)}), f32[32,1,11496]{2,1,0:T(1,128)}, u32[]{:S(2)}, u32[]{:S(2)}) async-start(f32[32,1,11496]{2,1,0:T(1,128)} %all_to_all.35), calls=%async_computation.3 | async-start | bytes 2949120 | tf_op jit(solution)/shard_map/all_to_all | solution.py:1097
  579.1 3.2 copy-start.23
  582.2 3.0 copy-start.17
  582.2 3.7 copy-start.22
  582.2 4.3 copy-start.16
  582.2 4.9 copy-start.21
  582.3 5.6 copy-start.15
  582.3 6.2 %copy-start.14 = (f32[96,768]{1,0:T(8,128)S(1)}, f32[96,768]{1,0:T(8,128)}, u32[]{:S(2)}) copy-start(f32[96,768]{1,0:T(8,128)} %get-tuple-element.213) | copy-start | bytes 884740
  582.3 6.9 %copy-start.1 = (s32[16,16]{1,0:T(8,128)S(1)}, s32[16,16]{1,0:T(8,128)}, u32[]{:S(2)}) copy-start(s32[16,16]{1,0:T(8,128)} %param.20) | copy-start | bytes 3076

commit v9 on v8

--- a/solution.py
+++ b/solution.py
@@ -27,6 +27,7 @@
 GRID = LIVE * PATCHES // TILE
 GROUPS = TILE // 64
 EARLY_TILES = GRID // 2
+UNPACK = FR
 GELU_C = 0.7978845608028654
 GELU_A = 0.044715
 VMEM_LIMIT = 66 * 1000 * 1000
@@ -586,27 +587,27 @@
 
 
 def unpack_frames(rows_ref, *refs):
-    x_refs, (out,) = refs[:FT], refs[FT:]
-    first = pl.program_id(0) * FT
-    for j in range(FT):
+    x_refs, (out,) = refs[:UNPACK], refs[UNPACK:]
+    first = pl.program_id(0) * UNPACK
+    for j in range(UNPACK):
         x = x_refs[j][0]
         out[j] = jnp.where(rows_ref[first + j] >= 0, x, jnp.zeros_like(x))
 
 
 def run_unpack(frames, rows):
     specs = [
-        pl.BlockSpec((1, PATCHES, D), functools.partial(lambda j, i, r: (jnp.maximum(r[FT * i + j], 0), 0, 0), j))
-        for j in range(FT)
+        pl.BlockSpec((1, PATCHES, D), functools.partial(lambda j, i, r: (jnp.maximum(r[UNPACK * i + j], 0), 0, 0), j))
+        for j in range(UNPACK)
     ]
     return pl.pallas_call(
         unpack_frames,
         grid_spec=pltpu.PrefetchScalarGridSpec(
-            num_scalar_prefetch=1, grid=(rows.shape[0] // FT,), in_specs=specs, out_specs=tiles((FT, PATCHES, D), 0)),
+            num_scalar_prefetch=1, grid=(rows.shape[0] // UNPACK,), in_specs=specs, out_specs=tiles((UNPACK, PATCHES, D), 0)),
         out_shape=shape_of((rows.shape[0], PATCHES, D), frames.dtype),
         name="unpack_frames",
         cost_estimate=pl.CostEstimate(flops=1000, bytes_accessed=4 * rows.shape[0] * PATCHES * D, transcendentals=0),
         compiler_params=pltpu.CompilerParams(dimension_semantics=("arbitrary",)),
-    )(rows, *[frames] * FT)
+    )(rows, *[frames] * UNPACK)
 
 
 def run_time_forward(x1, mod, seg, wqkv, wo, bo, carrier=None):
@@ -1143,8 +1144,8 @@
 
     if fast:
         flat = (w_qkv_s, w_o_s, w_qkv_t, w_o_t, w_in)
-        far, far_out = across(jnp.concatenate(flat, axis=1)), across(w_out)
-        clips, far, far_out = lax.optimization_barrier((clips, far, far_out))
+        side, clips = lax.optimization_barrier((jnp.concatenate(flat, axis=1), clips))
+        far, far_out = across(side), across(w_out)
         cuts = [sum(a.shape[1] for a in flat[: i + 1]) for i in range(len(flat) - 1)]
         *far_attn, far_in = jnp.split(far, cuts, axis=1)
         frames = shift_clips(clips, False)

time: 594 us -> 581 us (0.978)
  waiting for transfers between devices: 19.9 us -> 7.17 us
    ppermute x2, waiting for transfers between devices: 8.51 us -> 1 us  [across(): lax.ppermute(value, 'narrow', [(k, (k + n // 2) % n) for k in range(n)])]
  transfers between devices with their start and end apart: 9 -> 9, of which waited for: 3 -> 2; matrix products, arithmetic and copies ran while one was open for 7% -> 9% of each run, Pallas kernels for 22% -> 30%
where the time goes in v9:
time: 581 us; the launch traced here: 577 us
  Pallas kernels  460 us (79%)
  local copies, waits for them, and re-layouts  59.1 us (10%)
  other arithmetic  24.3 us (4%)
  starting transfers between devices  23.2 us (4%)
  waiting for transfers between devices  7.17 us (1%)
    pallas_call x6, Pallas kernels, call(): return fn(*ins) if prefetch is None else fn(prefetch, *ins)  332 us
    pallas_call x1, Pallas kernels, scatter_last(): pl.pallas_call(functools.partial(last_kernel, plan, left, len(shapes)), n...  61.3 us
    pallas_call x1, Pallas kernels, gather_first(): pl.pallas_call(functools.partial(gather_kernel, ring, heights), name='gat...  52.5 us
    all_to_all x4, starting transfers between devices, exchange(): return lax.all_to_all(x, ALL, split_axis=0, concat_axis=0, tiled=True)  17.4 us
    unnamed x82, local copies, waits for them, and re-layouts  15.4 us
    pallas_call x2, Pallas kernels, run_unpack(): pl.pallas_call(unpack_frames, grid_spec=pltpu.PrefetchScalarGridSpec(num_...  14.5 us
  transfers between devices with their start and end apart: 9, of which 2 were waited for; matrix products, arithmetic and copies ran while one was open for 9% of the time, Pallas kernels for 30%

profile of v9, /device:TPU:1, one launch (start us, length us, event | category | flops | bytes accessed | tf_op | source)
XLA Modules:
  0.0 577.3 jit_solution(4412844838765556750)
XLA Ops:
  0.7 2.1 collective-permute-start
  2.8 0.7 broadcast_in_dim.18
  3.5 2.2 reshape.614
  6.3 0.8 pad_maximum_fusion.4
  8.2 1.1 reduce.10
  9.2 1.7 reshape.738
  10.9 5.7 all-to-all-start
  16.7 1.4 collective-permute-start.1
  18.1 5.2 fusion.32
  24.0 1.6 collective-permute-start.2
  27.9 3.1 fusion.27
  31.0 0.8 gather_fusion.4
  31.8 1.2 gather_fusion.7
  33.0 0.8 gather_fusion.6
  35.0 1.0 collective-permute-done.1
  37.3 52.5 %gather_first.1 = (bf16[768,2304]{1,0:T(8,128)(2,1)}, bf16[768,768]{1,0:T(8,128)(2,1)}, bf16[768,2304]{1,0:T(8,128)(2,1)}, bf16[768,768]{1,0:T(8,128)(2,1)}) custom-call(bf16[24,2304]{1,0:T(8,128)(2,1)} %refs_0_.3, bf16[24,768]{1,0:T(8,128)(2,1)} %refs_1_.3, bf16[24,2304]{1,0:T(8,128)(2,1)} %refs_2_.1, bf16[24,768]{1,0:T(8,128)(2,1)} %refs_3_.1, ...), custom_call_target="tpu_custom_call" | custom-call | tf_op jit(solution)/shard_map/gather_first/pallas_call | solution.py:793
  90.6 5.1 reshape.739
  98.3 0.8 slice_convert_fusion.1
  99.8 0.8 slice_convert_fusion
  103.0 1.3 all_to_all.38
  104.3 3.9 all-to-all-start.1
  108.2 5.9 %pad_maximum_fusion = bf16[4,16,64,768]{3,2,1,0:T(8,128)(2,1)} fusion(bf16[1,16,64,768]{3,2,1,0:T(8,128)(2,1)} %bitcast.6, bf16[1,16,64,768]{3,2,1,0:T(8,128)(2,1)} %bitcast.4, bf16[1,16,64,768]{3,2,1,0:T(8,128)(2,1)} %bitcast.2, bf16[1,16,64,768]{3,2,1,0:T(8,128)(2,1)S(1)} %get-tuple-element.143), kind=kLoop, calls=%fused_computation.9 | loop fusion | flops 9437184 | bytes 12582912 | tf_op jit(solution)/shard_map/stack | solution.py:1107
  114.1 5.2 gather_fusion.2
  121.1 1.4 copy.132
  122.5 46.0 %frame_forward.1 = (bf16[1,16,64,768]{3,2,1,0:T(8,128)(2,1)}, bf16[768,3072]{1,0:T(8,128)(2,1)}, f32[64,32,768]{2,1,0:T(8,128)}, bf16[2048,2304]{1,0:T(8,128)(2,...) custom-call(bf16[4,16,64,768]{3,2,1,0:T(8,128)(2,1)} %refs_0_.5, bf16[24,3072]{1,0:T(8,128)(2,1)} %refs_1_.4, ...), custom_call_target="tpu_custom_call" | custom-call | flops 9663676416 | bytes 33917952 | tf_op jit(solution)/shard_map/frame_forward/pallas_call | solution.py:359
  169.2 43.4 %time_forward.1 = (bf16[2,16,64,768]{3,2,1,0:T(8,128)(2,1)}, bf16[3072,768]{1,0:T(8,128)(2,1)}, f32[64,32,768]{2,1,0:T(8,128)}, bf16[2048,2304]{1,0:T(8,128)(2,1...) custom-call(bf16[4,16,64,768]{3,2,1,0:T(8,128)(2,1)} %refs_0_.5, bf16[96,768]{1,0:T(8,128)(2,1)} %refs_1_.5, ...), custom_call_target="tpu_custom_call" | custom-call | flops 9663676416 | bytes 37096448 | tf_op jit(solution)/shard_map/time_forward/pallas_call | solution.py:359
  212.6 2.2 fusion.33
  215.4 3.2 pad_maximum_fusion.1
  218.5 6.9 %turn_frames.1.refs_1_ = f32[64,32,768]{2,1,0:T(8,128)} custom-call(s32[32]{0:T(128)} %get-tuple-element.141.rows_ref, bf16[64,64,768]{2,1,0:T(8,128)(2,1)} %bitcast.128, bf16[64,64,768]{2,1,0:T(8,128)(2,1)} %bitcast.129, bf16[64,64,768]{2,1,0:T(8,128)(2,1)} %bitcast.130, bf16[64,64,768]{2,1,0:T(8,128)(2,1)} %bitcast.131, bf16[64,64,768]{2,1,0:T(8,128)(2,1)} %bitcast.132, ...), custom_call_target="tpu_custom_call" | custom-call | flops 1000 | bytes 56623104 | tf_op jit(solution)/shard_map/turn_frames/pallas_call | solution.py:359
  225.5 98.8 %mlp_both.1 = (bf16[128,64,768]{2,1,0:T(8,128)(2,1)}, f32[64,32,768]{2,1,0:T(8,128)}, f32[768,3072]{1,0:T(8,128)}, f32[3072,768]{1,0:T(8,128)}, f32[1,3072]{1,0:...) custom-call(f32[64,32,768]{2,1,0:T(8,128)} %get-tuple-element.84.refs_0_, f32[64,32,768]{2,1,0:T(8,128)} %turn_frames.1.refs_1_, ...), custom_call_target="tpu_custom_call" | custom-call | flops 57982058496 | bytes 48396288 | tf_op jit(solution)/shard_map/mlp_both/pallas_call | solution.py:359
  324.3 70.3 %time_back.1 = (bf16[128,64,768]{2,1,0:T(8,128)(2,1)}, f32[24,1280]{1,0:T(8,128)}, f32[96,384]{1,0:T(8,128)}, f32[24,1280]{1,0:T(8,128)}, f32[96,256]{1,0:T(8,12...) custom-call(bf16[128,64,768]{2,1,0:T(8,128)(2,1)} %get-tuple-element, ...), custom_call_target="tpu_custom_call", output_to_operand_aliasing={{0}: (0, {})} | custom-call | flops 19327352832 | bytes 53120000 | tf_op jit(solution)/shard_map/time_back/pallas_call | solution.py:359
  394.6 66.5 %frame_back.1 = (bf16[128,64,768]{2,1,0:T(8,128)(2,1)}, bf16[128,64,768]{2,1,0:T(8,128)(2,1)}, f32[24,768]{1,0:T(8,128)}, f32[24,768]{1,0:T(8,128)}, f32[24,768]...) custom-call(bf16[128,64,768]{2,1,0:T(8,128)(2,1)} %get-tuple-element, ...), custom_call_target="tpu_custom_call", output_to_operand_aliasing={{0}: (0, {})} | custom-call | flops 19327352832 | bytes 43650048 | tf_op jit(solution)/shard_map/frame_back/pallas_call | solution.py:359
  461.2 1.0 maximum_bitcast_fusion
  463.5 1.3 reduce.11
  464.8 0.8 reshape.740
  465.6 4.5 all-to-all-start.2
  471.7 6.2 %all-to-all-done.2 = bf16[32,2,864]{2,1,0:T(2,128)(2,1)S(1)} async-done(((bf16[32,2,864]{2,1,0:T(2,128)(2,1)}), bf16[32,2,864]{2,1,0:T(2,128)(2,1)S(1)}, u32[]{:S(2)}, u32[]{:S(2)}) %all-to-all-start.2) | async-done | bytes 110624 | tf_op jit(solution)/shard_map/all_to_all | solution.py:1098
  479.4 0.8 convert_reduce_fusion
  481.2 1.2 reshape.628
  482.4 1.5 concatenate.62
  484.0 2.1 all_to_all.35
  486.1 3.3 all-to-all-start.3
  491.2 7.2 %unpack_frames.2 = bf16[64,64,768]{2,1,0:T(8,128)(2,1)} custom-call(s32[64]{0:T(128)} %select_n.185.rows_ref, bf16[128,64,768]{2,1,0:T(8,128)(2,1)} %get-tuple-element.102.refs_0_.refs_1_.refs_2_.refs_3_.refs_4_.refs_5_.refs_6_.refs_7_.refs_8_.refs_9_.refs_10_.refs_11_.refs_12_.refs_13_.refs_14_.refs_15_, ...), custom_call_target="tpu_custom_call" | custom-call | flops 1000 | bytes 12582912 | tf_op jit(solution)/shard_map/unpack_frames/pallas_call | solution.py:602
  498.4 61.3 %scatter_last.1 = (bf16[128,64,768]{2,1,0:T(8,128)(2,1)}, f32[24,3072]{1,0:T(8,128)}, f32[96,768]{1,0:T(8,128)}, f32[24,2304]{1,0:T(8,128)}, f32[24,768]{1,0:T(8...) custom-call(bf16[128,64,768]{2,1,0:T(8,128)(2,1)} %get-tuple-element, ...), custom_call_target="tpu_custom_call", output_to_operand_aliasing={{0}: (0, {})} | custom-call | tf_op jit(solution)/shard_map/scatter_last/pallas_call | solution.py:1069
  559.7 7.3 %unpack_frames.3 = bf16[64,64,768]{2,1,0:T(8,128)(2,1)} custom-call(s32[64]{0:T(128)} %select_n.185.rows_ref, bf16[128,64,768]{2,1,0:T(8,128)(2,1)} %get-tuple-element.125.refs_0_.refs_1_.refs_2_.refs_3_.refs_4_.refs_5_.refs_6_.refs_7_.refs_8_.refs_9_.refs_10_.refs_11_.refs_12_.refs_13_.refs_14_.refs_15_, ...), custom_call_target="tpu_custom_call" | custom-call | flops 1000 | bytes 12582912 | tf_op jit(solution)/shard_map/unpack_frames/pallas_call | solution.py:602
  567.0 1.5 copy.131
  571.7 1.3 reshape.636
  575.7 0.7 copy.155
  (191 shorter events, 29.9 us)
Async XLA Ops:
  0.6 26.1 %copy-start = (s32[16,16]{1,0:T(8,128)S(1)}, s32[16,16]{1,0:T(8,128)}, u32[]{:S(2)}) copy-start(s32[16,16]{1,0:T(8,128)} %param.20) | copy-start | bytes 3076
  0.7 167.8 %collective-permute-start = (bf16[96,768]{1,0:T(8,128)(2,1)}, bf16[96,768]{1,0:T(8,128)(2,1)S(1)}, u32[]{:S(2)}, u32[]{:S(2)}) collective-permute-start(bf16[96,768]{1,0:T(8,128)(2,1)} %refs_1_.5), channel_id=1, source_target_pairs={{0,2},{1,3},{2,0},{3,1},{4,6},{5,7},{6,4},{7,5},{8,10},{9,11},{10,... | collective-permute-start | bytes 442376 | tf_op jit(solution)/shard_map/ppermute | solution.py:1143
  7.1 9.5 %copy-start.10 = (bf16[24,2304]{1,0:T(8,128)(2,1)S(1)}, bf16[24,2304]{1,0:T(8,128)(2,1)}, u32[]{:S(2)}) copy-start(bf16[24,2304]{1,0:T(8,128)(2,1)} %refs_0_.3) | copy-start | bytes 331780
  7.1 9.5 %copy-start.18 = (bf16[24,768]{1,0:T(8,128)(2,1)S(1)}, bf16[24,768]{1,0:T(8,128)(2,1)}, u32[]{:S(2)}) copy-start(bf16[24,768]{1,0:T(8,128)(2,1)} %refs_1_.3) | copy-start | bytes 110596
  7.1 9.5 %copy-start.11 = (bf16[24,2304]{1,0:T(8,128)(2,1)S(1)}, bf16[24,2304]{1,0:T(8,128)(2,1)}, u32[]{:S(2)}) copy-start(bf16[24,2304]{1,0:T(8,128)(2,1)} %refs_2_.1) | copy-start | bytes 331780
  7.1 9.5 %copy-start.19 = (bf16[24,768]{1,0:T(8,128)(2,1)S(1)}, bf16[24,768]{1,0:T(8,128)(2,1)}, u32[]{:S(2)}) copy-start(bf16[24,768]{1,0:T(8,128)(2,1)} %refs_3_.1) | copy-start | bytes 110596
  7.1 9.5 %copy-start.20 = (bf16[24,3072]{1,0:T(8,128)(2,1)S(1)}, bf16[24,3072]{1,0:T(8,128)(2,1)}, u32[]{:S(2)}) copy-start(bf16[24,3072]{1,0:T(8,128)(2,1)} %refs_1_.4) | copy-start | bytes 442372
  10.9 79.7 %all-to-all-start = ((bf16[32,2,5748]{2,1,0:T(2,128)(2,1)}), bf16[32,2,5748]{2,1,0:T(2,128)(2,1)}, u32[]{:S(2)}, u32[]{:S(2)}) async-start(bf16[32,2,5748]{2,1,0:T(2,128)(2,1)} %reshape.738), calls=%async_computation | async-start | bytes 1474560 | tf_op jit(solution)/shard_map/all_to_all | solution.py:1098
  16.7 9.0 %copy-start.31 = (bf16[216]{0:T(256)(128)(2,1)S(1)}, bf16[216]{0:T(256)(128)(2,1)}, u32[]{:S(2)}) copy-start(bf16[216]{0:T(256)(128)(2,1)} %param.22) | copy-start | bytes 1300
  16.7 9.0 %copy-start.29 = (s32[16]{0:T(128)S(1)}, s32[16]{0:T(128)}, u32[]{:S(2)}) copy-start(s32[16]{0:T(128)} %param.19) | copy-start | bytes 196
  16.7 19.3 %collective-permute-start.1 = (bf16[24,9216]{1,0:T(8,128)(2,1)S(1)}, bf16[24,9216]{1,0:T(8,128)(2,1)S(1)}, u32[]{:S(2)}, u32[]{:S(2)}) collective-permute-start(bf16[24,9216]{1,0:T(8,128)(2,1)S(1)} %constant_dynamic-update-slice_fusion), channel_id=1, source_target_pairs={{0,2},{1,3},{2,0},{3,1},{4,6},{5,7},{6,4},{7,5},{8,10},{9,11},{10,... | collective-permute-start | bytes 1327112 | tf_op jit(solution)/shard_map/ppermute | solution.py:1143
  23.3 84.9 %collective-permute-start.4 = (bf16[16,64,768]{2,1,0:T(8,128)(2,1)}, bf16[16,64,768]{2,1,0:T(8,128)(2,1)}, u32[]{:S(2)}, u32[]{:S(2)}) collective-permute-start(bf16[16,64,768]{2,1,0:T(8,128)(2,1)} %get-tuple-element.144), channel_id=1, source_target_pairs={{0,3},{1,0},{2,1},{3,2},{4,7},{5,4},{6,5},{7,6},{8,11},{9,8},{10,9... | collective-permute-start | bytes 4718600 | tf_op jit(solution)/shard_map/ppermute | solution.py:1106
  24.0 84.2 %collective-permute-start.3 = (bf16[16,64,768]{2,1,0:T(8,128)(2,1)}, bf16[16,64,768]{2,1,0:T(8,128)(2,1)}, u32[]{:S(2)}, u32[]{:S(2)}) collective-permute-start(bf16[16,64,768]{2,1,0:T(8,128)(2,1)} %get-tuple-element.145), channel_id=1, source_target_pairs={{0,2},{1,3},{2,0},{3,1},{4,6},{5,7},{6,4},{7,5},{8,10},{9,11},{10,... | collective-permute-start | bytes 4718600 | tf_op jit(solution)/shard_map/ppermute | solution.py:1106
  24.0 84.2 %collective-permute-start.2 = (bf16[16,64,768]{2,1,0:T(8,128)(2,1)}, bf16[16,64,768]{2,1,0:T(8,128)(2,1)}, u32[]{:S(2)}, u32[]{:S(2)}) collective-permute-start(bf16[16,64,768]{2,1,0:T(8,128)(2,1)} %get-tuple-element.146), channel_id=1, source_target_pairs={{0,1},{1,2},{2,3},{3,0},{4,5},{5,6},{6,7},{7,4},{8,9},{9,10},{10,1... | collective-permute-start | bytes 4718600 | tf_op jit(solution)/shard_map/ppermute | solution.py:1106
  25.8 64.1 %copy-start.2 = (s32[4,4]{1,0:T(4,128)}, s32[4,4]{1,0:T(4,128)S(1)}, u32[]{:S(2)}) copy-start(s32[4,4]{1,0:T(4,128)S(1)} %reshape.610) | copy-start | bytes 196
  95.8 0.9 copy-start.8
  96.9 17.2 %copy-start.4 = (bf16[256,768]{1,0:T(8,128)(2,1)}, bf16[256,768]{1,0:T(8,128)(2,1)S(1)}, u32[]{:S(2)}) copy-start(bf16[256,768]{1,0:T(8,128)(2,1)S(1)} %convert_element_type.58) | copy-start | bytes 1179652
  97.6 16.5 %copy-start.6 = (bf16[768,216]{1,0:T(8,128)(2,1)}, bf16[768,216]{1,0:T(8,128)(2,1)S(1)}, u32[]{:S(2)}) copy-start(bf16[768,216]{1,0:T(8,128)(2,1)S(1)} %reshape.616) | copy-start | bytes 995332
  104.3 15.0 %all-to-all-start.1 = ((f32[32,1,1728]{2,1,0:T(1,128)}), f32[32,1,1728]{2,1,0:T(1,128)S(1)}, u32[]{:S(2)}, u32[]{:S(2)}) async-start(f32[32,1,1728]{2,1,0:T(1,128)} %all_to_all.38), calls=%async_computation.1 | async-start | bytes 458752 | tf_op jit(solution)/shard_map/all_to_all | solution.py:1098
  168.5 0.7 copy-start.30
  212.5 2.4 slice-start
  212.6 2.8 copy-start.9
  394.6 66.6 %copy-start.12 = (f32[3,32,768]{2,1,0:T(8,128)S(1)}, f32[3,32,768]{2,1,0:T(8,128)}, u32[]{:S(2)}) copy-start(f32[3,32,768]{2,1,0:T(8,128)} %get-tuple-element.128) | copy-start | bytes 884740
  394.6 66.6 %copy-start.13 = (f32[3,32,768]{2,1,0:T(8,128)S(1)}, f32[3,32,768]{2,1,0:T(8,128)}, u32[]{:S(2)}) copy-start(f32[3,32,768]{2,1,0:T(8,128)} %get-tuple-element.127) | copy-start | bytes 884740
  461.1 1.2 copy-start.28
  461.1 9.0 %copy-start.27 = (f32[1,768]{1,0:T(1,128)S(1)}, f32[1,768]{1,0:T(1,128)}, u32[]{:S(2)}) copy-start(f32[1,768]{1,0:T(1,128)} %get-tuple-element.129) | copy-start | bytes 9220
  461.1 9.0 %copy-start.26 = (f32[1,768]{1,0:T(1,128)S(1)}, f32[1,768]{1,0:T(1,128)}, u32[]{:S(2)}) copy-start(f32[1,768]{1,0:T(1,128)} %get-tuple-element.130) | copy-start | bytes 9220
  461.1 9.0 %copy-start.25 = (f32[1,768]{1,0:T(1,128)S(1)}, f32[1,768]{1,0:T(1,128)}, u32[]{:S(2)}) copy-start(f32[1,768]{1,0:T(1,128)} %get-tuple-element.132) | copy-start | bytes 9220
  461.2 9.6 %copy-start.24 = (f32[1,3072]{1,0:T(1,128)S(1)}, f32[1,3072]{1,0:T(1,128)}, u32[]{:S(2)}) copy-start(f32[1,3072]{1,0:T(1,128)} %get-tuple-element.131) | copy-start | bytes 36868
  462.2 18.2 %copy-start.7 = (bf16[768,216]{1,0:T(8,128)(2,1)S(1)}, bf16[768,216]{1,0:T(8,128)(2,1)}, u32[]{:S(2)}) copy-start(bf16[768,216]{1,0:T(8,128)(2,1)} %copy-done.6) | copy-start | bytes 995332
  462.3 18.5 %copy-start.5 = (bf16[256,768]{1,0:T(8,128)(2,1)S(1)}, bf16[256,768]{1,0:T(8,128)(2,1)}, u32[]{:S(2)}) copy-start(bf16[256,768]{1,0:T(8,128)(2,1)} %copy-done.4) | copy-start | bytes 1179652
  465.6 12.3 %all-to-all-start.2 = ((bf16[32,2,864]{2,1,0:T(2,128)(2,1)}), bf16[32,2,864]{2,1,0:T(2,128)(2,1)S(1)}, u32[]{:S(2)}, u32[]{:S(2)}) async-start(bf16[32,2,864]{2,1,0:T(2,128)(2,1)} %reshape.740), calls=%async_computation.2 | async-start | bytes 229376 | tf_op jit(solution)/shard_map/all_to_all | solution.py:1098
  483.9 5.6 copy-start.3
  486.1 80.9 %all-to-all-start.3 = ((f32[32,1,11496]{2,1,0:T(1,128)}), f32[32,1,11496]{2,1,0:T(1,128)}, u32[]{:S(2)}, u32[]{:S(2)}) async-start(f32[32,1,11496]{2,1,0:T(1,128)} %all_to_all.35), calls=%async_computation.3 | async-start | bytes 2949120 | tf_op jit(solution)/shard_map/all_to_all | solution.py:1098
  567.0 3.2 copy-start.23
  570.0 3.0 copy-start.17
  570.0 3.7 copy-start.22
  570.1 4.3 copy-start.16
  570.1 4.9 copy-start.21
  570.1 5.6 copy-start.15
  570.2 6.2 %copy-start.14 = (f32[96,768]{1,0:T(8,128)S(1)}, f32[96,768]{1,0:T(8,128)}, u32[]{:S(2)}) copy-start(f32[96,768]{1,0:T(8,128)} %get-tuple-element.209) | copy-start | bytes 884740
  570.2 6.9 %copy-start.1 = (s32[16,16]{1,0:T(8,128)S(1)}, s32[16,16]{1,0:T(8,128)}, u32[]{:S(2)}) copy-start(s32[16,16]{1,0:T(8,128)} %param.20) | copy-start | bytes 3076
